TPU v7x, 32 devices: a whole 2x2x4 slice. The times are simulated.
32 devices in a mesh: var: 2 (over y), gx: 4 (over z), gy: 2 (over x), nd: 2 (over core).
Axes of the slice: x: 2, y: 2, z: 4, core: 2. Of those that a mesh axis runs over, the one named last changes fastest.
Arguments:
- right_side: float32 [8192, 256], P(('var', 'gx', 'gy', 'nd')), parts along dimension 0, may hold values from -8 to 8
- node_diag: float32 [8192], P(('var', 'gx', 'gy', 'nd')), parts along dimension 0, may hold values from 1 to 10
- local_coup: float32 [64, 7, 128, 128], P(('var', 'gx', 'gy', 'nd')), parts along dimension 0, may hold values from -0.01 to 0.01
- block_cols: int32 [32, 7], P(('gx', 'gy', 'nd')), may hold values from 0 to 3
- border_coup: float32 [32, 8, 128, 128], P(('var', 'gx', 'gy', 'nd')), parts along dimension 0, may hold values from -0.01 to 0.01
- border_send: int32 [16, 8], P(('gx', 'gy', 'nd')), may hold values from 0 to 1
- border_rows: int32 [16, 8], P(('gx', 'gy', 'nd')), may hold values from 0 to 1
Outputs:
- solution_field: float32 [8192, 256], P(('var', 'gx', 'gy', 'nd')), parts along dimension 0
There are 2 independent parts, one for each index of `var`. A program takes and returns all parts, laid end to end along the dimension named above; an argument that names none is the same for every part. Nothing has to cross between parts.
Inputs may be any that keep to these rules, and one draw needn't show every extreme that they name: `block_cols`: block numbers within a patch. `border_send`: block numbers within the sending device. `border_rows`: block numbers within the receiving device.
All inputs are finite; a program needn't handle non-finite values.
Results may differ from a plain program's by a relative error of at most 0.0003.
Values sent between devices are 32-bit elements; how exact they have to be, the bound alone decides.
No kernel may reach another device: no remote copies, remote signals or barrier semaphores. Data moves between devices by JAX's collectives and lax.ppermute only.
A program may use at most 64 MiB of HBM per device.

v0:
```python
import jax
import jax.numpy as jnp
from jax import lax
from jax.sharding import PartitionSpec as P

ITERS = 2


def with_halo(cells, sides, width, closed):
    for axis, dim in sides:
        count = lax.axis_size(axis)
        ends = count if closed else count - 1
        head = lax.slice_in_dim(cells, 0, width, axis=dim)
        tail = lax.slice_in_dim(cells, cells.shape[dim] - width, cells.shape[dim], axis=dim)
        cells = jnp.concatenate(
            [
                lax.ppermute(tail, axis, [(i, (i + 1) % count) for i in range(ends)]),
                cells,
                lax.ppermute(head, axis, [((i + 1) % count, i) for i in range(ends)]),
            ],
            axis=dim,
        )
    return cells


def apply_prec(field, node_diag, local_coup, block_cols, border_coup, border_send, border_rows):
    hp = lax.Precision.HIGHEST
    nblocks = local_coup.shape[0]
    nonzeros = local_coup.shape[1]
    bsize = local_coup.shape[2]
    width = field.shape[1]
    blocks = field.reshape(nblocks, bsize, width)
    patch = lax.all_gather(blocks, "nd", axis=0, tiled=True)
    picked = jnp.take(patch, block_cols, axis=0)
    result = node_diag.reshape(nblocks, bsize, 1) * blocks
    result = result + jnp.einsum("bkij,bkjc->bic", local_coup, picked, precision=hp)
    patch_len = patch.shape[0]
    tterms = jnp.einsum("bkji,bjc->bkic", local_coup, blocks, precision=hp).reshape(
        nblocks * nonzeros, bsize, width
    )
    tonehot = (
        block_cols.reshape(nblocks * nonzeros)[None, :]
        == jnp.arange(patch_len, dtype=jnp.int32)[:, None]
    ).astype(jnp.float32)
    spread = jnp.einsum("pq,qic->pic", tonehot, tterms, precision=hp)
    result = result + lax.psum_scatter(spread, "nd", scatter_dimension=0, tiled=True)
    chosen = jnp.take(blocks, border_send[0], axis=0)
    per_side = chosen.shape[0] // 4
    slots = chosen.reshape(4, per_side, bsize, width)
    own_rows = jnp.take(blocks, border_rows[0], axis=0)
    back = jnp.einsum("mji,mjc->mic", border_coup[0], own_rows, precision=hp)
    back_sides = back.reshape(4, per_side, bsize, width)
    along = with_halo(jnp.stack([slots[1], slots[0]]), (("gx", 0),), 1, True)
    across = with_halo(jnp.stack([slots[3], slots[2]]), (("gy", 0),), 1, False)
    received = jnp.concatenate([along[0], along[3], across[0], across[3]], axis=0)
    back_x = with_halo(jnp.stack([back_sides[0], back_sides[1]]), (("gx", 0),), 1, True)
    back_y = with_halo(jnp.stack([back_sides[2], back_sides[3]]), (("gy", 0),), 1, False)
    returned = jnp.concatenate([back_x[3], back_x[0], back_y[3], back_y[0]], axis=0)
    contrib = jnp.einsum("mij,mjc->mic", border_coup[0], received, precision=hp)
    onehot = (border_rows[0][None, :] == jnp.arange(nblocks, dtype=jnp.int32)[:, None]).astype(
        jnp.float32
    )
    result = result + jnp.einsum("nm,mic->nic", onehot, contrib, precision=hp)
    sonehot = (border_send[0][None, :] == jnp.arange(nblocks, dtype=jnp.int32)[:, None]).astype(
        jnp.float32
    )
    result = result + jnp.einsum("nm,mic->nic", sonehot, returned, precision=hp)
    return result.reshape(nblocks * bsize, width)


def squares(residual):
    return lax.psum(jnp.sum(residual * residual, axis=0), ("gx", "gy", "nd"))


def shards(right_side, node_diag, local_coup, block_cols, border_coup, border_send, border_rows):
    operands = (node_diag, local_coup, block_cols, border_coup, border_send, border_rows)
    solution_field = jnp.zeros_like(right_side)
    residual = right_side
    direction = right_side
    norm_now = squares(residual)
    for step in range(ITERS):
        image = apply_prec(direction, *operands)
        curve = lax.psum(jnp.sum(direction * image, axis=0), ("gx", "gy", "nd"))
        alpha = norm_now / curve
        solution_field = solution_field + alpha * direction
        if step + 1 < ITERS:
            residual = residual - alpha * image
            norm_next = squares(residual)
            direction = residual + norm_next / norm_now * direction
            norm_now = norm_next
    return solution_field


def solution(mesh):
    in_specs = (
        P(("var", "gx", "gy", "nd"), None),
        P(("var", "gx", "gy", "nd")),
        P(("var", "gx", "gy", "nd"), None, None, None),
        P(("gx", "gy", "nd"), None),
        P(("var", "gx", "gy", "nd"), None, None, None),
        P(("gx", "gy", "nd"), None),
        P(("gx", "gy", "nd"), None),
    )
    out_specs = P(("var", "gx", "gy", "nd"), None)
    return jax.shard_map(shards, mesh=mesh, in_specs=in_specs, out_specs=out_specs, check_vma=False)
```

profile of v0, /device:TPU:0, one launch (start us, length us, event | category | flops | bytes accessed | tf_op | source)
XLA Modules:
  0.0 218.6 jit_solution(11470286495793710172)
XLA Ops:
  7.7 2.6 %fusion.95 = f32[2,7,128,256]{3,2,1,0:T(8,128)S(1)} fusion(f32[2,7,128,128]{3,2,1,0:T(8,128)S(1)} %copy-done, f32[2,128,256,1]{2,1,3,0:T(8,128)} %bitcast.156), kind=kOutput, calls=%fused_computation.120 | convolution fusion | flops 704643072 | bytes 3014656 | tf_op jit(solution)/shard_map/bkji,bjc->bkic/dot_general | solution.py:38
  13.9 2.0 convolution_bitcast_fusion.1
  16.9 4.8 %collective-permute-start.7 = (f32[1,2,128,256]{2,3,1,0:T(8,128)}, f32[1,2,128,256]{2,3,1,0:T(8,128)S(1)}, u32[]{:S(2)}, u32[]{:S(2)}) collective-permute-start(f32[1,2,128,256]{2,3,1,0:T(8,128)} %get-tuple-element.24), channel_id=1, source_target_pairs={{0,2},{1,3},{4,6},{5,7},{8,10},{9,11},{12,14},{13,15},{16,18},{17,... | collective-permute-start | bytes 786440 | tf_op jit(solution)/shard_map/ppermute | solution.py:17
  24.7 2.2 %collective-permute-start.4 = (f32[1,2,128,256]{2,3,1,0:T(8,128)}, f32[1,2,128,256]{2,3,1,0:T(8,128)}, u32[]{:S(2)}, u32[]{:S(2)}) collective-permute-start(f32[1,2,128,256]{2,3,1,0:T(8,128)} %get-tuple-element.23), channel_id=1, source_target_pairs={{4,0},{8,4},{12,8},{0,12},{5,1},{9,5},{13,9},{1,13},{6,2},{10,6},{... | collective-permute-start | bytes 786440 | tf_op jit(solution)/shard_map/ppermute | solution.py:19
  30.2 2.2 all_gather.6
  35.0 4.6 %collective-permute-start.2 = (f32[1,2,128,256]{3,2,1,0:T(8,128)}, f32[1,2,128,256]{3,2,1,0:T(8,128)S(1)}, u32[]{:S(2)}, u32[]{:S(2)}) collective-permute-start(f32[1,2,128,256]{3,2,1,0:T(8,128)} %get-tuple-element.21), channel_id=1, source_target_pairs={{0,2},{1,3},{4,6},{5,7},{8,10},{9,11},{12,14},{13,15},{16,18},{17,... | collective-permute-start | bytes 786440 | tf_op jit(solution)/shard_map/ppermute | solution.py:17
  45.8 3.8 %collective-permute-done.1 = f32[1,2,128,256]{3,2,1,0:T(8,128)S(1)} collective-permute-done((f32[1,2,128,256]{3,2,1,0:T(8,128)}, f32[1,2,128,256]{3,2,1,0:T(8,128)S(1)}, u32[]{:S(2)}, u32[]{:S(2)}) %collective-permute-start.1) | collective-permute-done | bytes 262176 | tf_op jit(solution)/shard_map/ppermute | solution.py:19
  49.6 5.0 %collective-permute-done = f32[1,2,128,256]{3,2,1,0:T(8,128)} collective-permute-done((f32[1,2,128,256]{3,2,1,0:T(8,128)}, f32[1,2,128,256]{3,2,1,0:T(8,128)}, u32[]{:S(2)}, u32[]{:S(2)}) %collective-permute-start) | collective-permute-done | bytes 262176 | tf_op jit(solution)/shard_map/ppermute | solution.py:17
  54.6 2.9 %fusion.36 = f32[8,256,128]{2,1,0:T(8,128)S(1)} fusion(f32[2,128,256]{2,1,0:T(8,128)S(1)} %bitcast.170, f32[2,128,256]{2,1,0:T(8,128)S(1)} %bitcast.173, f32[2,128,256]{2,1,0:T(8,128)S(1)} %bitcast.174, f32[2,128,256]{2,1,0:T(8,128)} %bitcast.14, f32[1,8,128,128]{3,2,1,0:T(8,128)S(1)} %copy-done.2), kind=kOutput, calls=%fused_computation.24 | convolution fusion | flops 403439616 | bytes 2621440 | tf_op jit(solution)/shard_map/mij,mjc->mic/dot_general | solution.py:59
  60.9 2.5 %fusion.54 = f32[2,128,256]{2,0,1:T(2,128)} fusion(f32[8,256,128]{1,0,2:T(8,128)} %copy.39, s32[8]{0:T(128)S(1)} %bitcast.185), kind=kOutput, calls=%fused_computation.44 | convolution fusion | flops 6291472 | bytes 1310752 | tf_op jit(solution)/shard_map/nm,mic->nic/dot_general | solution.py:63
  63.4 2.5 %fusion.33 = f32[2,128,256]{2,1,0:T(8,128)S(1)} fusion(f32[2,128,256]{2,1,0:T(8,128)} %reduce-scatter.3.cloned.1.call-done, f32[2,7,128,128]{3,2,1,0:T(8,128)S(1)} %copy-done, f32[2,7,128,256]{3,2,1,0:T(8,128)S(1)} %bitcast.167, pred[2,7]{1,0:T(4,128)(4,1)} %compare_and_fusion.2, f32[2,128,256]{2,0,1:T(2,128)S(1)} %fusion.76, f32[2,128,256]{2,0,1:T(2,128)} %fusion.54, ...), kind=kOutput, calls=%fused_computation.23 | convolution fusion | flops 705429504 | bytes 4064270 | tf_op jit(solution)/shard_map/bkij,bkjc->bic/dot_general | solution.py:36
  66.0 29.5 %all-reduce = (f32[256]{0:T(256)S(1)}, f32[256]{0:T(256)S(1)}) all-reduce(f32[256]{0:T(256)S(1)} %get-tuple-element.8, f32[256]{0:T(256)S(1)} %get-tuple-element.6), channel_id=1, replica_groups=mesh['var'=2,'gx'=4,'gy'=2,'nd'=2] {'gx','gy','nd'}, use_global_device_ids=true, to_apply=%region_1.0 | all-reduce | flops 512 | bytes 4096 | tf_op jit(solution)/shard_map/psum | solution.py:72
  95.6 29.5 %psum.30 = f32[256]{0:T(256)S(1)} all-reduce(f32[256]{0:T(256)S(1)} %multiply_reduce_fusion), channel_id=1, replica_groups=mesh['var'=2,'gx'=4,'gy'=2,'nd'=2] {'gx','gy','nd'}, use_global_device_ids=true, to_apply=%region_6.9 | all-reduce | flops 256 | bytes 2048 | tf_op jit(solution)/shard_map/psum | solution.py:72
  128.5 2.9 %fusion.96 = f32[2,256,7,128]{3,1,2,0:T(8,128)} fusion(f32[2,128,256,1]{2,1,3,0:T(8,128)S(1)} %bitcast.163, f32[2,7,128,128]{3,2,1,0:T(8,128)S(1)} %copy-done), kind=kOutput, calls=%fused_computation.121 | convolution fusion | flops 704643072 | bytes 3014656 | tf_op jit(solution)/shard_map/bkji,bjc->bkic/dot_general | solution.py:38
  131.4 2.3 %copy.30 = f32[14,128,256]{2,0,1:T(8,128)S(1)} copy(f32[14,128,256]{1,2,0:T(8,128)} %bitcast.169) | data formatting | bytes 3670016 | tf_op jit(solution)/shard_map/reshape | solution.py:38
  136.0 2.7 %convolution_bitcast_fusion = f32[8,128,256]{1,2,0:T(8,128)S(1)} fusion(f32[8,128,256]{2,1,0:T(8,128)S(1)} %copy-done.7, f32[1,8,128,128]{3,2,1,0:T(8,128)S(1)} %copy-done.3, pred[8]{0:T(512)(128)(4,1)} %copy-done.24), kind=kOutput, calls=%fused_computation.12 | convolution fusion | flops 402915328 | bytes 2621448 | tf_op jit(solution)/shard_map/mji,mjc->mic/dot_general | solution.py:51
  141.5 3.8 %collective-permute-start.12 = (f32[1,2,128,256]{2,3,1,0:T(8,128)S(1)}, f32[1,2,128,256]{2,3,1,0:T(8,128)}, u32[]{:S(2)}, u32[]{:S(2)}) collective-permute-start(f32[1,2,128,256]{2,3,1,0:T(8,128)S(1)} %get-tuple-element.15), channel_id=1, source_target_pairs={{4,0},{8,4},{12,8},{0,12},{5,1},{9,5},{13,9},{1,13},{6,2},{10,6},{... | collective-permute-start | bytes 786440 | tf_op jit(solution)/shard_map/ppermute | solution.py:19
  147.8 4.6 %collective-permute-start.10 = (f32[1,2,128,256]{3,2,1,0:T(8,128)}, f32[1,2,128,256]{3,2,1,0:T(8,128)S(1)}, u32[]{:S(2)}, u32[]{:S(2)}) collective-permute-start(f32[1,2,128,256]{3,2,1,0:T(8,128)} %get-tuple-element.13), channel_id=1, source_target_pairs={{0,2},{1,3},{4,6},{5,7},{8,10},{9,11},{12,14},{13,15},{16,18},{17,... | collective-permute-start | bytes 786440 | tf_op jit(solution)/shard_map/ppermute | solution.py:17
  155.2 2.4 %all_gather.7 = f32[4,128,256]{2,1,0:T(8,128)S(1)} all-gather(f32[2,128,256]{2,1,0:T(8,128)S(1)} %bitcast.164), channel_id=1, replica_groups=mesh['var'=2,'gx'=4,'gy'=2,'nd'=2] {'nd'}, dimensions={0}, use_global_device_ids=true | all-gather | bytes 786432 | tf_op jit(solution)/shard_map/all_gather | solution.py:33
  162.2 6.2 %collective-permute-done.8 = f32[1,2,128,256]{3,2,1,0:T(8,128)} collective-permute-done((f32[1,2,128,256]{3,2,1,0:T(8,128)}, f32[1,2,128,256]{3,2,1,0:T(8,128)}, u32[]{:S(2)}, u32[]{:S(2)}) %collective-permute-start.8) | collective-permute-done | bytes 262176 | tf_op jit(solution)/shard_map/ppermute | solution.py:17
  168.4 3.0 %fusion.44 = f32[8,256,128]{2,1,0:T(8,128)S(1)} fusion(f32[2,128,256]{2,1,0:T(8,128)S(1)} %bitcast.171, f32[2,128,256]{2,1,0:T(8,128)S(1)} %bitcast.172, f32[2,128,256]{2,1,0:T(8,128)} %bitcast.45, f32[2,128,256]{2,1,0:T(8,128)} %bitcast.43, f32[1,8,128,128]{3,2,1,0:T(8,128)S(1)} %copy-done.3), kind=kOutput, calls=%fused_computation.33 | convolution fusion | flops 403439616 | bytes 2621440 | tf_op jit(solution)/shard_map/mij,mjc->mic/dot_general | solution.py:59
  174.7 2.5 %fusion.52 = f32[2,128,256]{2,0,1:T(2,128)} fusion(f32[8,256,128]{1,0,2:T(8,128)} %copy.43, s32[8]{0:T(128)} %bitcast.184), kind=kOutput, calls=%fused_computation.42 | convolution fusion | flops 6291472 | bytes 1310752 | tf_op jit(solution)/shard_map/nm,mic->nic/dot_general | solution.py:63
  177.3 2.6 %fusion.21 = f32[2,128,256]{2,1,0:T(8,128)S(1)} fusion(f32[2,128,256]{2,1,0:T(8,128)} %reduce-scatter.5.cloned.1.call-done, f32[2,7,128,128]{3,2,1,0:T(8,128)S(1)} %copy-done, f32[2,7,128,256]{3,2,1,0:T(8,128)S(1)} %bitcast.168, pred[2,7]{1,0:T(4,128)(4,1)} %compare_and_fusion.2, f32[2,128,256]{2,0,1:T(2,128)S(1)} %fusion.74, f32[2,128,256]{2,0,1:T(2,128)} %fusion.52, ...), kind=kOutput, calls=%fused_computation.19 | convolution fusion | flops 705429504 | bytes 4064270 | tf_op jit(solution)/shard_map/bkij,bkjc->bic/dot_general | solution.py:36
  179.9 31.1 %psum.31 = f32[256]{0:T(256)S(1)} all-reduce(f32[256]{0:T(256)S(1)} %fusion.70), channel_id=1, replica_groups=mesh['var'=2,'gx'=4,'gy'=2,'nd'=2] {'gx','gy','nd'}, use_global_device_ids=true, to_apply=%region_9.12 | all-reduce | flops 256 | bytes 2048 | tf_op jit(solution)/shard_map/psum | solution.py:83
  (127 shorter events, 46.5 us)
Async XLA Ops:
  6.5 56.9 %reduce-scatter.3.cloned.1.call-start = ((), (), s32[]{:S(2)}) async-start(), calls=%async_computation.2 | async-start | bytes 786432 | tf_op jit(solution)/shard_map/reduce_scatter | solution.py:46
  13.1 164.1 %reduce-scatter.5.cloned.1.call-start = ((), (), s32[]{:S(2)}) async-start(), calls=%async_computation.3 | async-start | bytes 786432 | tf_op jit(solution)/shard_map/reduce_scatter | solution.py:46
  13.9 13.1 %copy-start.16 = (s32[1,8]{1,0:T(1,128)S(1)}, s32[1,8]{1,0:T(1,128)}, u32[]{:S(2)}) copy-start(s32[1,8]{1,0:T(1,128)} %param.16) | copy-start | bytes 100
  16.9 17.4 %collective-permute-start.7 = (f32[1,2,128,256]{2,3,1,0:T(8,128)}, f32[1,2,128,256]{2,3,1,0:T(8,128)S(1)}, u32[]{:S(2)}, u32[]{:S(2)}) collective-permute-start(f32[1,2,128,256]{2,3,1,0:T(8,128)} %get-tuple-element.24), channel_id=1, source_target_pairs={{0,2},{1,3},{4,6},{5,7},{8,10},{9,11},{12,14},{13,15},{16,18},{17,... | collective-permute-start | bytes 786440 | tf_op jit(solution)/shard_map/ppermute | solution.py:17
  21.8 17.9 %collective-permute-start.6 = (f32[1,2,128,256]{2,3,1,0:T(8,128)}, f32[1,2,128,256]{2,3,1,0:T(8,128)S(1)}, u32[]{:S(2)}, u32[]{:S(2)}) collective-permute-start(f32[1,2,128,256]{2,3,1,0:T(8,128)} %get-tuple-element.25), channel_id=1, source_target_pairs={{2,0},{3,1},{6,4},{7,5},{10,8},{11,9},{14,12},{15,13},{18,16},{19,... | collective-permute-start | bytes 786440 | tf_op jit(solution)/shard_map/ppermute | solution.py:19
  23.1 19.1 %collective-permute-start.5 = (f32[1,2,128,256]{2,3,1,0:T(8,128)}, f32[1,2,128,256]{2,3,1,0:T(8,128)}, u32[]{:S(2)}, u32[]{:S(2)}) collective-permute-start(f32[1,2,128,256]{2,3,1,0:T(8,128)} %get-tuple-element.26), channel_id=1, source_target_pairs={{0,4},{4,8},{8,12},{12,0},{1,5},{5,9},{9,13},{13,1},{2,6},{6,10},{... | collective-permute-start | bytes 786440 | tf_op jit(solution)/shard_map/ppermute | solution.py:17
  24.7 18.2 %collective-permute-start.4 = (f32[1,2,128,256]{2,3,1,0:T(8,128)}, f32[1,2,128,256]{2,3,1,0:T(8,128)}, u32[]{:S(2)}, u32[]{:S(2)}) collective-permute-start(f32[1,2,128,256]{2,3,1,0:T(8,128)} %get-tuple-element.23), channel_id=1, source_target_pairs={{4,0},{8,4},{12,8},{0,12},{5,1},{9,5},{13,9},{1,13},{6,2},{10,6},{... | collective-permute-start | bytes 786440 | tf_op jit(solution)/shard_map/ppermute | solution.py:19
  28.8 16.8 %collective-permute-start.3 = (f32[1,2,128,256]{3,2,1,0:T(8,128)}, f32[1,2,128,256]{3,2,1,0:T(8,128)S(1)}, u32[]{:S(2)}, u32[]{:S(2)}) collective-permute-start(f32[1,2,128,256]{3,2,1,0:T(8,128)} %get-tuple-element.20), channel_id=1, source_target_pairs={{2,0},{3,1},{6,4},{7,5},{10,8},{11,9},{14,12},{15,13},{18,16},{19,... | collective-permute-start | bytes 786440 | tf_op jit(solution)/shard_map/ppermute | solution.py:19
  32.4 10.0 %copy-start.26 = (s32[2,7]{1,0:T(2,128)S(1)}, s32[2,7]{1,0:T(2,128)}, u32[]{:S(2)}) copy-start(s32[2,7]{1,0:T(2,128)} %param.14) | copy-start | bytes 172
  35.0 10.7 %collective-permute-start.2 = (f32[1,2,128,256]{3,2,1,0:T(8,128)}, f32[1,2,128,256]{3,2,1,0:T(8,128)S(1)}, u32[]{:S(2)}, u32[]{:S(2)}) collective-permute-start(f32[1,2,128,256]{3,2,1,0:T(8,128)} %get-tuple-element.21), channel_id=1, source_target_pairs={{0,2},{1,3},{4,6},{5,7},{8,10},{9,11},{12,14},{13,15},{16,18},{17,... | collective-permute-start | bytes 786440 | tf_op jit(solution)/shard_map/ppermute | solution.py:17
  40.4 9.2 %collective-permute-start.1 = (f32[1,2,128,256]{3,2,1,0:T(8,128)}, f32[1,2,128,256]{3,2,1,0:T(8,128)S(1)}, u32[]{:S(2)}, u32[]{:S(2)}) collective-permute-start(f32[1,2,128,256]{3,2,1,0:T(8,128)} %get-tuple-element.22), channel_id=1, source_target_pairs={{4,0},{8,4},{12,8},{0,12},{5,1},{9,5},{13,9},{1,13},{6,2},{10,6},{... | collective-permute-start | bytes 786440 | tf_op jit(solution)/shard_map/ppermute | solution.py:19
  42.2 12.4 %collective-permute-start = (f32[1,2,128,256]{3,2,1,0:T(8,128)}, f32[1,2,128,256]{3,2,1,0:T(8,128)}, u32[]{:S(2)}, u32[]{:S(2)}) collective-permute-start(f32[1,2,128,256]{3,2,1,0:T(8,128)} %get-tuple-element.19), channel_id=1, source_target_pairs={{0,4},{4,8},{8,12},{12,0},{1,5},{5,9},{9,13},{13,1},{2,6},{6,10},{... | collective-permute-start | bytes 786440 | tf_op jit(solution)/shard_map/ppermute | solution.py:17
  136.0 9.3 %copy-start.6 = (f32[8,128,256]{2,1,0:T(8,128)S(1)}, f32[8,128,256]{2,1,0:T(8,128)}, u32[]{:S(2)}) copy-start(f32[8,128,256]{2,1,0:T(8,128)} %gather_fusion.4) | copy-start | bytes 3145732
  136.0 9.3 %copy-start.21 = (pred[8]{0:T(512)(128)(4,1)S(1)}, pred[8]{0:T(512)(128)(4,1)}, u32[]{:S(2)}) copy-start(pred[8]{0:T(512)(128)(4,1)} %copy-done.20) | copy-start | bytes 28
  138.8 9.0 %collective-permute-start.15 = (f32[1,2,128,256]{2,3,1,0:T(8,128)S(1)}, f32[1,2,128,256]{2,3,1,0:T(8,128)S(1)}, u32[]{:S(2)}, u32[]{:S(2)}) collective-permute-start(f32[1,2,128,256]{2,3,1,0:T(8,128)S(1)} %get-tuple-element.16), channel_id=1, source_target_pairs={{0,2},{1,3},{4,6},{5,7},{8,10},{9,11},{12,14},{13,15},{16,18},{17,... | collective-permute-start | bytes 786440 | tf_op jit(solution)/shard_map/ppermute | solution.py:17
  140.1 12.3 %collective-permute-start.14 = (f32[1,2,128,256]{2,3,1,0:T(8,128)S(1)}, f32[1,2,128,256]{2,3,1,0:T(8,128)S(1)}, u32[]{:S(2)}, u32[]{:S(2)}) collective-permute-start(f32[1,2,128,256]{2,3,1,0:T(8,128)S(1)} %get-tuple-element.17), channel_id=1, source_target_pairs={{2,0},{3,1},{6,4},{7,5},{10,8},{11,9},{14,12},{15,13},{18,16},{19,... | collective-permute-start | bytes 786440 | tf_op jit(solution)/shard_map/ppermute | solution.py:19
  141.4 11.1 %collective-permute-start.13 = (f32[1,2,128,256]{2,3,1,0:T(8,128)S(1)}, f32[1,2,128,256]{2,3,1,0:T(8,128)S(1)}, u32[]{:S(2)}, u32[]{:S(2)}) collective-permute-start(f32[1,2,128,256]{2,3,1,0:T(8,128)S(1)} %get-tuple-element.18), channel_id=1, source_target_pairs={{0,4},{4,8},{8,12},{12,0},{1,5},{5,9},{9,13},{13,1},{2,6},{6,10},{... | collective-permute-start | bytes 786440 | tf_op jit(solution)/shard_map/ppermute | solution.py:17
  141.5 18.0 %collective-permute-start.12 = (f32[1,2,128,256]{2,3,1,0:T(8,128)S(1)}, f32[1,2,128,256]{2,3,1,0:T(8,128)}, u32[]{:S(2)}, u32[]{:S(2)}) collective-permute-start(f32[1,2,128,256]{2,3,1,0:T(8,128)S(1)} %get-tuple-element.15), channel_id=1, source_target_pairs={{4,0},{8,4},{12,8},{0,12},{5,1},{9,5},{13,9},{1,13},{6,2},{10,6},{... | collective-permute-start | bytes 786440 | tf_op jit(solution)/shard_map/ppermute | solution.py:19
  146.5 15.7 %collective-permute-start.11 = (f32[1,2,128,256]{3,2,1,0:T(8,128)}, f32[1,2,128,256]{3,2,1,0:T(8,128)S(1)}, u32[]{:S(2)}, u32[]{:S(2)}) collective-permute-start(f32[1,2,128,256]{3,2,1,0:T(8,128)} %get-tuple-element.12), channel_id=1, source_target_pairs={{2,0},{3,1},{6,4},{7,5},{10,8},{11,9},{14,12},{15,13},{18,16},{19,... | collective-permute-start | bytes 786440 | tf_op jit(solution)/shard_map/ppermute | solution.py:19
  147.8 11.7 %copy-start.10 = (f32[1,2,128,256]{2,3,1,0:T(8,128)}, f32[1,2,128,256]{2,3,1,0:T(8,128)S(1)}, u32[]{:S(2)}) copy-start(f32[1,2,128,256]{2,3,1,0:T(8,128)S(1)} %collective-permute-done.15) | copy-start | bytes 786436
  147.8 14.4 %collective-permute-start.10 = (f32[1,2,128,256]{3,2,1,0:T(8,128)}, f32[1,2,128,256]{3,2,1,0:T(8,128)S(1)}, u32[]{:S(2)}, u32[]{:S(2)}) collective-permute-start(f32[1,2,128,256]{3,2,1,0:T(8,128)} %get-tuple-element.13), channel_id=1, source_target_pairs={{0,2},{1,3},{4,6},{5,7},{8,10},{9,11},{12,14},{13,15},{16,18},{17,... | collective-permute-start | bytes 786440 | tf_op jit(solution)/shard_map/ppermute | solution.py:17
  152.4 9.8 %collective-permute-start.9 = (f32[1,2,128,256]{3,2,1,0:T(8,128)}, f32[1,2,128,256]{3,2,1,0:T(8,128)}, u32[]{:S(2)}, u32[]{:S(2)}) collective-permute-start(f32[1,2,128,256]{3,2,1,0:T(8,128)} %get-tuple-element.14), channel_id=1, source_target_pairs={{4,0},{8,4},{12,8},{0,12},{5,1},{9,5},{13,9},{1,13},{6,2},{10,6},{... | collective-permute-start | bytes 786440 | tf_op jit(solution)/shard_map/ppermute | solution.py:19
  153.2 15.2 %collective-permute-start.8 = (f32[1,2,128,256]{3,2,1,0:T(8,128)}, f32[1,2,128,256]{3,2,1,0:T(8,128)}, u32[]{:S(2)}, u32[]{:S(2)}) collective-permute-start(f32[1,2,128,256]{3,2,1,0:T(8,128)} %get-tuple-element.11), channel_id=1, source_target_pairs={{0,4},{4,8},{8,12},{12,0},{1,5},{5,9},{9,13},{13,1},{2,6},{6,10},{... | collective-permute-start | bytes 786440 | tf_op jit(solution)/shard_map/ppermute | solution.py:17
  172.8 4.5 %copy-start.15 = (f32[256]{0:T(256)S(1)}, f32[256]{0:T(256)}, u32[]{:S(2)}) copy-start(f32[256]{0:T(256)} %param.12) | copy-start | bytes 3076
  (21 other events, 47.6 us)
Sparse Core Ops, SparseCore 0:
  13.3 10.6 reduce-scatter.2
  135.5 5.2 reduce-scatter.4
where the time goes:
time: 219 us
  blocking collectives  94.6 us (43%)
  matrix products  32.8 us (15%)
  starting transfers between devices  32.3 us (15%)
  local copies, waits for them, and re-layouts  25.3 us (12%)
  waiting for transfers between devices  15.3 us (7%)
  between operations  13.9 us (6%)
  other arithmetic  4.4 us (2%)
    psum x2, blocking collectives, squares(): return lax.psum(jnp.sum(residual * residual, axis=0), ('gx', 'gy', 'nd'))  59 us
    psum x1, blocking collectives, shards(): curve = lax.psum(jnp.sum(direction * image, axis=0), ('gx', 'gy', 'nd'))  31.1 us
    ppermute x8, starting transfers between devices, with_halo(): lax.ppermute(tail, axis, [(i, (i + 1) % count) for i in range(ends)])  19.2 us
    ppermute x8, starting transfers between devices, with_halo(): lax.ppermute(head, axis, [((i + 1) % count, i) for i in range(ends)])  13.1 us
    ppermute x8, waiting for transfers between devices, with_halo(): lax.ppermute(tail, axis, [(i, (i + 1) % count) for i in range(ends)])  11.4 us
    dot_general x2, matrix products, apply_prec(): contrib = jnp.einsum('mij,mjc->mic', border_coup[0], received, precision=hp)  5.89 us
    dot_general x2, matrix products, apply_prec(): jnp.einsum('bkji,bjc->bkic', local_coup, blocks, precision=hp)  5.47 us
    dot_general x2, matrix products, apply_prec(): jnp.einsum('bkij,bkjc->bic', local_coup, picked, precision=hp)  5.09 us
  transfers between devices with their start and end apart: 18, of which 4 were waited for; matrix products, arithmetic and copies ran while one was open for 17% of the time, Pallas kernels for 0%

commit v1 on v0

v1 whole, which is shorter than its diff:
```python
import jax
import jax.numpy as jnp
from jax import lax
from jax.experimental import pallas as pl
from jax.experimental.pallas import tpu as pltpu
from jax.sharding import PartitionSpec as P

F32 = jnp.float32
HP = lax.Precision.HIGHEST
AXES = ("gx", "gy", "nd")
SIDE = 2
TAIL = 8


def vmem():
    return pl.BlockSpec(memory_space=pltpu.VMEM)


def smem():
    return pl.BlockSpec(memory_space=pltpu.SMEM)


def axis_sum(part):
    for axis in ("nd", "gy", "gx"):
        count = lax.axis_size(axis)
        if count & (count - 1):
            part = lax.psum(part, axis)
            continue
        step = 1
        while step < count:
            part = part + lax.ppermute(part, axis, [(i, i ^ step) for i in range(count)])
            step *= 2
    return part


def prep_kernel(cols, send, rows, sides, field, diag, local, border, own, pair, *pays):
    nblocks, nonzeros, bs, _ = local.shape
    width = nblocks * bs
    patch_len = 2 * nblocks
    base = sides[0] * nblocks
    own[...] = jnp.zeros(own.shape, F32)
    pair[...] = jnp.zeros(pair.shape, F32)
    pair[pl.ds(0, width), :] = field[...]
    for b in range(nblocks):
        for k in range(nonzeros):
            spot = lax.rem(cols[b, k] - base + patch_len, patch_len)
            block = local[b, k]
            for c in range(nblocks):

                @pl.when(spot == c)
                def _():
                    own[pl.ds(b * bs, bs), pl.ds(c * bs, bs)] += block

                @pl.when(spot == c + nblocks)
                def _():
                    pair[pl.ds(width + b * bs, bs), pl.ds(c * bs, bs)] += block

    lower = own[...]
    here = lax.broadcasted_iota(jnp.int32, (width, width), 0)
    there = lax.broadcasted_iota(jnp.int32, (width, width), 1)
    own[...] = lower + lower.T + jnp.where(here == there, diag[...], 0.0)
    lane = lax.broadcasted_iota(jnp.int32, (TAIL, bs), 1)
    for n, pay in enumerate(pays):
        give = sides[1 + n]
        tail = jnp.zeros((TAIL, bs), F32)
        for s in range(SIDE):
            pay[pl.ds(s * bs, bs), :] = border[give * SIDE + s]
            tail = jnp.where(lane == s, rows[0, give * SIDE + s].astype(F32), tail)
            back = (give ^ 1) * SIDE + s
            tail = jnp.where(lane == SIDE + s, send[0, back].astype(F32), tail)
        pay[pl.ds(SIDE * bs, TAIL), :] = tail


def apply_kernel(nslots, send, rows, sides, field, own, pair, mate, border, *refs):
    fields = refs[:nslots]
    pays = refs[nslots : 2 * nslots]
    image, coup, sums = refs[2 * nslots :]
    width = field.shape[0]
    bs = border.shape[1]
    coup[0] = pair[pl.ds(width, width), :] + mate[pl.ds(width, width), :].T
    for n in range(nslots):
        take = sides[1 + n]
        other = take ^ 1
        coup[1 + n] = jnp.zeros((width, width), F32)
        pay = pays[n]
        tail = pay[pl.ds(SIDE * bs, TAIL), :]
        for s in range(SIDE):
            from_row = tail[0:1, s : s + 1]
            from_send = tail[0:1, SIDE + s : SIDE + s + 1]
            block = border[take * SIDE + s]
            turned = pay[pl.ds(s * bs, bs), :].T
            at = pl.multiple_of(rows[0, take * SIDE + s] * bs, bs)
            bt = pl.multiple_of(send[0, other * SIDE + s] * bs, bs)
            for c in range(width // bs):
                coup[1 + n, pl.ds(at, bs), pl.ds(c * bs, bs)] += jnp.where(from_send == c, block, 0.0)
                coup[1 + n, pl.ds(bt, bs), pl.ds(c * bs, bs)] += jnp.where(from_row == c, turned, 0.0)
    acc = jnp.dot(own[...], field[...], precision=HP, preferred_element_type=F32)
    acc += jnp.dot(coup[0], mate[pl.ds(0, width), :], precision=HP, preferred_element_type=F32)
    for n in range(nslots):
        acc += jnp.dot(coup[1 + n], fields[n][...], precision=HP, preferred_element_type=F32)
    image[...] = acc
    sums[0:1, :] = jnp.sum(field[...] * field[...], axis=0, keepdims=True)
    sums[1:2, :] = jnp.sum(field[...] * acc, axis=0, keepdims=True)


def form_kernel(weights, step, field, image, mate_b, mate_w, own, coup, *refs):
    nused = len(weights)
    fields = refs[:nused]
    images = refs[nused : 2 * nused]
    sums = refs[2 * nused]
    width = field.shape[0]
    a = step[...]
    res = field[...] - a * image[...]
    acc = jnp.dot(own[...], res, precision=HP, preferred_element_type=F32)
    far = mate_b[pl.ds(0, width), :] - a * mate_w[...]
    acc += jnp.dot(coup[0], far, precision=HP, preferred_element_type=F32)
    for n, (slot, weight) in enumerate(weights):
        far = weight * (fields[n][...] - a * images[n][...])
        acc += jnp.dot(coup[1 + slot], far, precision=HP, preferred_element_type=F32)
    sums[0:1, :] = jnp.sum(res * res, axis=0, keepdims=True)
    sums[1:2, :] = jnp.sum(res * acc, axis=0, keepdims=True)


def shards(right_side, node_diag, local_coup, block_cols, border_coup, border_send, border_rows):
    width, ncols = right_side.shape
    nblocks, _, bs, _ = local_coup.shape
    n_gx, n_gy, n_nd = (lax.axis_size(a) for a in AXES)
    assert n_nd == 2 and border_coup.shape[1] == 4 * SIDE
    gyi = lax.axis_index("gy")
    swap = [(0, 1), (1, 0)]
    right = [(i, (i + 1) % n_gx) for i in range(n_gx)]
    left = [(j, i) for i, j in right]
    up = [(i, i + 1) for i in range(n_gy - 1)]
    down = [(j, i) for i, j in up]
    slots = [("gx", right, 0), ("gx", left, 1)]
    if n_gy == 2:
        slots.insert(1, ("gy", swap, jnp.where(gyi == 0, 3, 2)))
        weights = [(0, 2.0), (1, 1.0)]
    elif n_gy > 2:
        slots.insert(1, ("gy", up, 2))
        slots.append(("gy", down, 3))
        weights = [(0, 2.0), (1, 2.0)]
    else:
        weights = [(0, 2.0)]
    nslots = len(slots)
    take = [jnp.asarray(t, jnp.int32) for _, _, t in slots]
    ndi = lax.axis_index("nd").astype(jnp.int32)
    give = [jnp.where(gyi == 0, 3, 2).astype(jnp.int32) if n_gy == 2 and a == "gy" else t ^ 1 for (a, _, _), t in zip(slots, take)]
    sides_out = jnp.stack([ndi] + give)
    sides_in = jnp.stack([ndi] + take)

    fields = [lax.ppermute(right_side, axis, perm) for axis, perm, _ in slots]
    pay_shape = jax.ShapeDtypeStruct((SIDE * bs + TAIL, bs), F32)
    border = border_coup[0]
    own, pair, *pays = pl.pallas_call(
        prep_kernel,
        name="prep",
        in_specs=[smem()] * 4 + [vmem()] * 4,
        out_specs=[vmem()] * (2 + nslots),
        out_shape=[jax.ShapeDtypeStruct((width, width), F32), jax.ShapeDtypeStruct((2 * width, ncols), F32)]
        + [pay_shape] * nslots,
    )(block_cols, border_send, border_rows, sides_out, right_side, node_diag.reshape(1, width), local_coup, border)
    mate = lax.ppermute(pair, "nd", swap)
    pays = [lax.ppermute(pay, axis, perm) for pay, (axis, perm, _) in zip(pays, slots)]

    image, coup, sums = pl.pallas_call(
        lambda *refs: apply_kernel(nslots, *refs),
        name="apply",
        in_specs=[smem()] * 3 + [vmem()] * (5 + 2 * nslots),
        out_specs=[vmem()] * 3,
        out_shape=[
            jax.ShapeDtypeStruct((width, ncols), F32),
            jax.ShapeDtypeStruct((1 + nslots, width, width), F32),
            jax.ShapeDtypeStruct((2, ncols), F32),
        ],
    )(border_send, border_rows, sides_in, right_side, own, pair, mate, border, *fields, *pays)

    images = [lax.ppermute(image, slots[n][0], slots[n][1]) for n, _ in weights]
    mate_w = lax.ppermute(image, "nd", swap)
    sums = axis_sum(sums)
    norm, curve = sums[0:1], sums[1:2]
    step = norm / curve

    sums = pl.pallas_call(
        lambda *refs: form_kernel(weights, *refs),
        name="form",
        in_specs=[vmem()] * (7 + 2 * len(weights)),
        out_specs=vmem(),
        out_shape=jax.ShapeDtypeStruct((2, ncols), F32),
    )(step, right_side, image, mate, mate_w, own, coup, *[fields[n] for n, _ in weights], *images)
    sums = axis_sum(sums)
    ratio = sums[0:1] / norm
    last = sums[0:1] / (sums[1:2] - ratio * ratio * curve)
    residual = right_side - step * image
    return step * right_side + last * (residual + ratio * right_side)


def solution(mesh):
    blocks = P(("var", "gx", "gy", "nd"))
    tables = P(AXES)
    in_specs = (blocks, blocks, blocks, tables, blocks, tables, tables)
    return jax.shard_map(shards, mesh=mesh, in_specs=in_specs, out_specs=blocks, check_vma=False)
```

time: 219 us -> 70 us (0.32)
  blocking collectives: 94.6 us -> 0 us
  matrix products: 32.8 us -> 0 us
  local copies, waits for them, and re-layouts: 25.3 us -> 2.58 us
  waiting for transfers between devices: 15.3 us -> 36.1 us
  starting transfers between devices: 32.3 us -> 16.6 us
  between operations: 13.9 us -> 0.16 us
  Pallas kernels: 0 us -> 11 us
    psum x3 -> x0, blocking collectives: 90.1 us -> none  [the longest x2 59 us: squares(): return lax.psum(jnp.sum(residual * residual, axis=0), ('gx', 'gy', 'nd'))]
    dot_general x14 -> x0, matrix products: 32.8 us -> none  [the longest x2 5.89 us: apply_prec(): contrib = jnp.einsum('mij,mjc->mic', border_coup[0], received, precision=hp)]
    ppermute x16 -> x18, waiting for transfers between devices: 15.2 us -> 36.1 us  [the longest x8 24.1 us: axis_sum(): lax.ppermute(part, axis, [(i, i ^ step) for i in range(count)])]
    ppermute x16 -> x18, starting transfers between devices: 32.3 us -> 16.6 us  [the longest x3 7.93 us: shards(): lax.ppermute(pay, axis, perm)]
    pallas_call x0 -> x3, Pallas kernels: none -> 11 us  [the longest x1 4.32 us: shards(): pl.pallas_call(lambda *refs: apply_kernel(nslots, *refs), name='apply', i...]
    gather x6 -> x0, local copies, waits for them, and re-layouts: 8.39 us -> none  [the longest x2 3.84 us: apply_prec(): picked = jnp.take(patch, block_cols, axis=0)]
    dot_general x4 -> x0, local copies, waits for them, and re-layouts: 4.6 us -> none  [the longest x2 2.81 us: apply_prec(): contrib = jnp.einsum('mij,mjc->mic', border_coup[0], received, precision=hp)]
    all_gather x2 -> x0, blocking collectives: 4.56 us -> none  [apply_prec(): patch = lax.all_gather(blocks, 'nd', axis=0, tiled=True)]
  transfers between devices with their start and end apart: 18 -> 18, of which waited for: 4 -> 10; matrix products, arithmetic and copies ran while one was open for 17% -> 2% of each run, Pallas kernels for 0% -> 0%
where the time goes in v1:
time: 70 us; the launch traced here: 69.8 us
  waiting for transfers between devices  36.1 us (52%)
  starting transfers between devices  16.6 us (24%)
  Pallas kernels  11 us (16%)
  other arithmetic  3.34 us (5%)
  local copies, waits for them, and re-layouts  2.58 us (4%)
    ppermute x8, waiting for transfers between devices, axis_sum(): lax.ppermute(part, axis, [(i, i ^ step) for i in range(count)])  24.1 us
    ppermute x3, waiting for transfers between devices, shards(): lax.ppermute(pay, axis, perm)  12 us
    ppermute x3, starting transfers between devices, shards(): lax.ppermute(pay, axis, perm)  7.93 us
    pallas_call x1, Pallas kernels, shards(): pl.pallas_call(lambda *refs: apply_kernel(nslots, *refs), name='apply', i...  4.32 us
    pallas_call x1, Pallas kernels, shards(): pl.pallas_call(lambda *refs: form_kernel(weights, *refs), name='form', in...  3.81 us
    ppermute x8, starting transfers between devices, axis_sum(): lax.ppermute(part, axis, [(i, i ^ step) for i in range(count)])  3.46 us
    pallas_call x1, Pallas kernels, shards(): pl.pallas_call(prep_kernel, name='prep', in_specs=[smem()] * 4 + [vmem()]...  2.91 us
    ppermute x3, starting transfers between devices, shards(): fields = [lax.ppermute(right_side, axis, perm) for axis, perm, _ in slots]  2.65 us
  transfers between devices with their start and end apart: 18, of which 10 were waited for; matrix products, arithmetic and copies ran while one was open for 2% of the time, Pallas kernels for 0%

profile of v1, /device:TPU:0, one launch (start us, length us, event | category | flops | bytes accessed | tf_op | source)
XLA Modules:
  0.0 69.8 jit_solution(14198976983362247098)
XLA Ops:
  0.0 0.7 pad_add_fusion.1.sides
  0.7 2.9 %prep.1 = (f32[256,256]{1,0:T(8,128)}, f32[512,256]{1,0:T(8,128)}, f32[264,128]{1,0:T(8,128)}, f32[264,128]{1,0:T(8,128)}, f32[264,128]{1,0:T(8,128)}) custom-call(s32[2,7]{1,0:T(2,128)} %cols.1, s32[1,8]{1,0:T(1,128)} %refs_0_.1, s32[1,8]{1,0:T(1,128)} %refs_1_.2, s32[4]{0:T(128)} %pad_add_fusion.1.sides, f32[256,256]{1,0:T(8,128)} %refs_1_.3, ...), custom_call_target="tpu_custom_call" | custom-call | tf_op jit(solution)/shard_map/prep/pallas_call | solution.py:155
  4.0 2.6 %collective-permute-start.4 = (f32[264,128]{1,0:T(8,128)}, f32[264,128]{1,0:T(8,128)S(1)}, u32[]{:S(2)}, u32[]{:S(2)}) collective-permute-start(f32[264,128]{1,0:T(8,128)} %get-tuple-element.15), channel_id=1, source_target_pairs={{0,4},{4,8},{8,12},{12,0},{1,5},{5,9},{9,13},{13,1},{2,6},{6,10},{... | collective-permute-start | bytes 405512 | tf_op jit(solution)/shard_map/ppermute | solution.py:164
  6.7 1.5 %collective-permute-start.5 = (f32[264,128]{1,0:T(8,128)}, f32[264,128]{1,0:T(8,128)S(1)}, u32[]{:S(2)}, u32[]{:S(2)}) collective-permute-start(f32[264,128]{1,0:T(8,128)} %get-tuple-element.16), channel_id=1, source_target_pairs={{0,2},{2,0},{1,3},{3,1},{4,6},{6,4},{5,7},{7,5},{8,10},{10,8},{9,1... | collective-permute-start | bytes 405512 | tf_op jit(solution)/shard_map/ppermute | solution.py:164
  8.2 2.2 %collective-permute-start.3 = (f32[256,256]{1,0:T(8,128)S(1)}, f32[256,256]{1,0:T(8,128)S(1)}, u32[]{:S(2)}, u32[]{:S(2)}) collective-permute-start(f32[256,256]{1,0:T(8,128)S(1)} %copy-done), channel_id=1, source_target_pairs={{4,0},{8,4},{12,8},{0,12},{5,1},{9,5},{13,9},{1,13},{6,2},{10,6},{... | collective-permute-start | bytes 786440 | tf_op jit(solution)/shard_map/ppermute | solution.py:152
  10.8 2.5 %collective-permute-done.4.refs_11_ = f32[264,128]{1,0:T(8,128)S(1)} collective-permute-done((f32[264,128]{1,0:T(8,128)}, f32[264,128]{1,0:T(8,128)S(1)}, u32[]{:S(2)}, u32[]{:S(2)}) %collective-permute-start.4) | collective-permute-done | bytes 135200 | tf_op jit(solution)/shard_map/ppermute | solution.py:164
  13.4 3.8 %collective-permute-start.6 = (f32[264,128]{1,0:T(8,128)}, f32[264,128]{1,0:T(8,128)S(1)}, u32[]{:S(2)}, u32[]{:S(2)}) collective-permute-start(f32[264,128]{1,0:T(8,128)} %get-tuple-element.17), channel_id=1, source_target_pairs={{4,0},{8,4},{12,8},{0,12},{5,1},{9,5},{13,9},{1,13},{6,2},{10,6},{... | collective-permute-start | bytes 405512 | tf_op jit(solution)/shard_map/ppermute | solution.py:164
  17.8 9.5 %collective-permute-done.6.refs_13_ = f32[264,128]{1,0:T(8,128)S(1)} collective-permute-done((f32[264,128]{1,0:T(8,128)}, f32[264,128]{1,0:T(8,128)S(1)}, u32[]{:S(2)}, u32[]{:S(2)}) %collective-permute-start.6) | collective-permute-done | bytes 135200 | tf_op jit(solution)/shard_map/ppermute | solution.py:164
  28.4 4.3 %apply.1 = (f32[256,256]{1,0:T(8,128)}, f32[4,256,256]{2,1,0:T(8,128)}, f32[2,256]{1,0:T(2,128)}) custom-call(s32[1,8]{1,0:T(1,128)} %refs_0_.1, s32[1,8]{1,0:T(1,128)} %refs_1_.2, s32[4]{0:T(128)} %pad_add_fusion.refs_2_, f32[256,256]{1,0:T(8,128)} %refs_1_.3, f32[256,256]{1,0:T(8,128)} %get-tuple-element.13.refs_4_.refs_5_, ...), custom_call_target="tpu_custom_call" | custom-call | tf_op jit(solution)/shard_map/apply/pallas_call | solution.py:166
  32.7 1.0 %collective-permute-start.13 = (f32[256,256]{1,0:T(8,128)}, f32[256,256]{1,0:T(8,128)S(1)}, u32[]{:S(2)}, u32[]{:S(2)}) collective-permute-start(f32[256,256]{1,0:T(8,128)} %get-tuple-element.19.refs_2_), channel_id=1, source_target_pairs={{0,2},{2,0},{1,3},{3,1},{4,6},{6,4},{5,7},{7,5},{8,10},{10,8},{9,1... | collective-permute-start | bytes 786440 | tf_op jit(solution)/shard_map/ppermute | solution.py:178
  33.7 1.1 %collective-permute-start.12 = (f32[256,256]{1,0:T(8,128)}, f32[256,256]{1,0:T(8,128)S(1)}, u32[]{:S(2)}, u32[]{:S(2)}) collective-permute-start(f32[256,256]{1,0:T(8,128)} %get-tuple-element.19.refs_2_), channel_id=1, source_target_pairs={{0,4},{4,8},{8,12},{12,0},{1,5},{5,9},{9,13},{13,1},{2,6},{6,10},{... | collective-permute-start | bytes 786440 | tf_op jit(solution)/shard_map/ppermute | solution.py:178
  35.3 0.8 %collective-permute-done.7 = f32[2,256]{1,0:T(2,128)S(1)} collective-permute-done((f32[2,256]{1,0:T(2,128)S(1)}, f32[2,256]{1,0:T(2,128)S(1)}, u32[]{:S(2)}, u32[]{:S(2)}) %collective-permute-start.7) | collective-permute-done | bytes 2080 | tf_op jit(solution)/shard_map/ppermute | solution.py:31
  36.7 4.5 %collective-permute-done.8 = f32[2,256]{1,0:T(2,128)S(1)} collective-permute-done((f32[2,256]{1,0:T(2,128)S(1)}, f32[2,256]{1,0:T(2,128)S(1)}, u32[]{:S(2)}, u32[]{:S(2)}) %collective-permute-start.8) | collective-permute-done | bytes 2080 | tf_op jit(solution)/shard_map/ppermute | solution.py:31
  41.8 3.0 %collective-permute-done.9 = f32[2,256]{1,0:T(2,128)S(1)} collective-permute-done((f32[2,256]{1,0:T(2,128)S(1)}, f32[2,256]{1,0:T(2,128)S(1)}, u32[]{:S(2)}, u32[]{:S(2)}) %collective-permute-start.9) | collective-permute-done | bytes 2080 | tf_op jit(solution)/shard_map/ppermute | solution.py:31
  45.3 4.0 %collective-permute-done.10 = f32[2,256]{1,0:T(2,128)S(1)} collective-permute-done((f32[2,256]{1,0:T(2,128)S(1)}, f32[2,256]{1,0:T(2,128)S(1)}, u32[]{:S(2)}, u32[]{:S(2)}) %collective-permute-start.10) | collective-permute-done | bytes 2080 | tf_op jit(solution)/shard_map/ppermute | solution.py:31
  50.0 0.7 copy-done.7
  50.8 3.8 %form.1 = f32[2,256]{1,0:T(2,128)} custom-call(f32[1,256]{1,0:T(1,128)} %slice_divide_fusion.1.refs_0_, f32[256,256]{1,0:T(8,128)} %refs_1_.3, f32[256,256]{1,0:T(8,128)} %get-tuple-element.19.refs_2_, f32[512,256]{1,0:T(8,128)} %copy-done.2, f32[256,256]{1,0:T(8,128)} %copy-done.9, f32[256,256]{1,0:T(8,128)} %get-tuple-element.13.refs_4_.refs_5_, ...), custom_call_target="tpu_custom_call" | custom-call | tf_op jit(solution)/shard_map/form/pallas_call | solution.py:184
  54.6 1.4 %collective-permute-done.14 = f32[2,256]{1,0:T(2,128)S(1)} collective-permute-done((f32[2,256]{1,0:T(2,128)}, f32[2,256]{1,0:T(2,128)S(1)}, u32[]{:S(2)}, u32[]{:S(2)}) %collective-permute-start.14) | collective-permute-done | bytes 2080 | tf_op jit(solution)/shard_map/ppermute | solution.py:31
  56.0 0.7 add.34
  56.9 3.3 %collective-permute-done.15 = f32[2,256]{1,0:T(2,128)S(1)} collective-permute-done((f32[2,256]{1,0:T(2,128)S(1)}, f32[2,256]{1,0:T(2,128)S(1)}, u32[]{:S(2)}, u32[]{:S(2)}) %collective-permute-start.15) | collective-permute-done | bytes 2080 | tf_op jit(solution)/shard_map/ppermute | solution.py:31
  60.8 3.0 %collective-permute-done.16 = f32[2,256]{1,0:T(2,128)S(1)} collective-permute-done((f32[2,256]{1,0:T(2,128)S(1)}, f32[2,256]{1,0:T(2,128)S(1)}, u32[]{:S(2)}, u32[]{:S(2)}) %collective-permute-start.16) | collective-permute-done | bytes 2080 | tf_op jit(solution)/shard_map/ppermute | solution.py:31
  64.4 4.0 %collective-permute-done.17 = f32[2,256]{1,0:T(2,128)S(1)} collective-permute-done((f32[2,256]{1,0:T(2,128)S(1)}, f32[2,256]{1,0:T(2,128)S(1)}, u32[]{:S(2)}, u32[]{:S(2)}) %collective-permute-start.17) | collective-permute-done | bytes 2080 | tf_op jit(solution)/shard_map/ppermute | solution.py:31
  68.4 0.7 copy-done.13
  69.0 0.8 %multiply_add_fusion = f32[256,256]{1,0:T(8,128)} fusion(f32[256,256]{1,0:T(8,128)S(1)} %copy-done.1, f32[256,256]{1,0:T(8,128)S(1)} %copy-done.5, f32[256]{0:T(256)S(1)} %bitcast.11, f32[256]{0:T(256)S(1)} %bitcast.10, f32[256]{0:T(256)S(1)} %bitcast.9), kind=kLoop, calls=%fused_computation | loop fusion | flops 458752 | bytes 789504 | tf_op jit(solution)/shard_map/add | solution.py:195
  (58 shorter events, 6.8 us)
Async XLA Ops:
  0.7 7.5 %copy-start = (f32[256,256]{1,0:T(8,128)S(1)}, f32[256,256]{1,0:T(8,128)}, u32[]{:S(2)}) copy-start(f32[256,256]{1,0:T(8,128)} %refs_1_.3) | copy-start | bytes 786436
  3.6 23.7 %collective-permute-start = (f32[512,256]{1,0:T(8,128)}, f32[512,256]{1,0:T(8,128)S(1)}, u32[]{:S(2)}, u32[]{:S(2)}) collective-permute-start(f32[512,256]{1,0:T(8,128)} %get-tuple-element.14.refs_5_), channel_id=1, source_target_pairs={{0,1},{1,0},{2,3},{3,2},{4,5},{5,4},{6,7},{7,6},{8,9},{9,8},{10,11... | collective-permute-start | bytes 1572872 | tf_op jit(solution)/shard_map/ppermute | solution.py:163
  4.0 9.3 %collective-permute-start.4 = (f32[264,128]{1,0:T(8,128)}, f32[264,128]{1,0:T(8,128)S(1)}, u32[]{:S(2)}, u32[]{:S(2)}) collective-permute-start(f32[264,128]{1,0:T(8,128)} %get-tuple-element.15), channel_id=1, source_target_pairs={{0,4},{4,8},{8,12},{12,0},{1,5},{5,9},{9,13},{13,1},{2,6},{6,10},{... | collective-permute-start | bytes 405512 | tf_op jit(solution)/shard_map/ppermute | solution.py:164
  6.7 6.7 %collective-permute-start.5 = (f32[264,128]{1,0:T(8,128)}, f32[264,128]{1,0:T(8,128)S(1)}, u32[]{:S(2)}, u32[]{:S(2)}) collective-permute-start(f32[264,128]{1,0:T(8,128)} %get-tuple-element.16), channel_id=1, source_target_pairs={{0,2},{2,0},{1,3},{3,1},{4,6},{6,4},{5,7},{7,5},{8,10},{10,8},{9,1... | collective-permute-start | bytes 405512 | tf_op jit(solution)/shard_map/ppermute | solution.py:164
  8.2 19.1 %collective-permute-start.3 = (f32[256,256]{1,0:T(8,128)S(1)}, f32[256,256]{1,0:T(8,128)S(1)}, u32[]{:S(2)}, u32[]{:S(2)}) collective-permute-start(f32[256,256]{1,0:T(8,128)S(1)} %copy-done), channel_id=1, source_target_pairs={{4,0},{8,4},{12,8},{0,12},{5,1},{9,5},{13,9},{1,13},{6,2},{10,6},{... | collective-permute-start | bytes 786440 | tf_op jit(solution)/shard_map/ppermute | solution.py:152
  10.4 16.8 %collective-permute-start.2 = (f32[256,256]{1,0:T(8,128)S(1)}, f32[256,256]{1,0:T(8,128)S(1)}, u32[]{:S(2)}, u32[]{:S(2)}) collective-permute-start(f32[256,256]{1,0:T(8,128)S(1)} %copy-done), channel_id=1, source_target_pairs={{0,2},{2,0},{1,3},{3,1},{4,6},{6,4},{5,7},{7,5},{8,10},{10,8},{9,1... | collective-permute-start | bytes 786440 | tf_op jit(solution)/shard_map/ppermute | solution.py:152
  13.3 14.0 %copy-start.10 = (f32[264,128]{1,0:T(8,128)}, f32[264,128]{1,0:T(8,128)S(1)}, u32[]{:S(2)}) copy-start(f32[264,128]{1,0:T(8,128)S(1)} %collective-permute-done.4.refs_11_) | copy-start | bytes 405508
  13.3 13.9 %collective-permute-start.1 = (f32[256,256]{1,0:T(8,128)S(1)}, f32[256,256]{1,0:T(8,128)S(1)}, u32[]{:S(2)}, u32[]{:S(2)}) collective-permute-start(f32[256,256]{1,0:T(8,128)S(1)} %copy-done), channel_id=1, source_target_pairs={{0,4},{4,8},{8,12},{12,0},{1,5},{5,9},{9,13},{13,1},{2,6},{6,10},{... | collective-permute-start | bytes 786440 | tf_op jit(solution)/shard_map/ppermute | solution.py:152
  13.3 14.0 %copy-start.11 = (f32[264,128]{1,0:T(8,128)}, f32[264,128]{1,0:T(8,128)S(1)}, u32[]{:S(2)}) copy-start(f32[264,128]{1,0:T(8,128)S(1)} %collective-permute-done.5.refs_12_) | copy-start | bytes 405508
  13.4 13.9 %collective-permute-start.6 = (f32[264,128]{1,0:T(8,128)}, f32[264,128]{1,0:T(8,128)S(1)}, u32[]{:S(2)}, u32[]{:S(2)}) collective-permute-start(f32[264,128]{1,0:T(8,128)} %get-tuple-element.17), channel_id=1, source_target_pairs={{4,0},{8,4},{12,8},{0,12},{5,1},{9,5},{13,9},{1,13},{6,2},{10,6},{... | collective-permute-start | bytes 405512 | tf_op jit(solution)/shard_map/ppermute | solution.py:164
  32.7 2.1 %copy-start.14 = (f32[2,256]{1,0:T(2,128)S(1)}, f32[2,256]{1,0:T(2,128)}, u32[]{:S(2)}) copy-start(f32[2,256]{1,0:T(2,128)} %get-tuple-element.18) | copy-start | bytes 6148
  32.7 17.2 %collective-permute-start.13 = (f32[256,256]{1,0:T(8,128)}, f32[256,256]{1,0:T(8,128)S(1)}, u32[]{:S(2)}, u32[]{:S(2)}) collective-permute-start(f32[256,256]{1,0:T(8,128)} %get-tuple-element.19.refs_2_), channel_id=1, source_target_pairs={{0,2},{2,0},{1,3},{3,1},{4,6},{6,4},{5,7},{7,5},{8,10},{10,8},{9,1... | collective-permute-start | bytes 786440 | tf_op jit(solution)/shard_map/ppermute | solution.py:178
  33.7 16.2 %collective-permute-start.12 = (f32[256,256]{1,0:T(8,128)}, f32[256,256]{1,0:T(8,128)S(1)}, u32[]{:S(2)}, u32[]{:S(2)}) collective-permute-start(f32[256,256]{1,0:T(8,128)} %get-tuple-element.19.refs_2_), channel_id=1, source_target_pairs={{0,4},{4,8},{8,12},{12,0},{1,5},{5,9},{9,13},{13,1},{2,6},{6,10},{... | collective-permute-start | bytes 786440 | tf_op jit(solution)/shard_map/ppermute | solution.py:178
  34.8 15.2 %collective-permute-start.11 = (f32[256,256]{1,0:T(8,128)}, f32[256,256]{1,0:T(8,128)S(1)}, u32[]{:S(2)}, u32[]{:S(2)}) collective-permute-start(f32[256,256]{1,0:T(8,128)} %get-tuple-element.19.refs_2_), channel_id=1, source_target_pairs={{0,1},{1,0},{2,3},{3,2},{4,5},{5,4},{6,7},{7,6},{8,9},{9,8},{10,11... | collective-permute-start | bytes 786440 | tf_op jit(solution)/shard_map/ppermute | solution.py:179
  34.8 1.3 %collective-permute-start.7 = (f32[2,256]{1,0:T(2,128)S(1)}, f32[2,256]{1,0:T(2,128)S(1)}, u32[]{:S(2)}, u32[]{:S(2)}) collective-permute-start(f32[2,256]{1,0:T(2,128)S(1)} %copy-done.14), channel_id=1, source_target_pairs={{0,1},{1,0},{2,3},{3,2},{4,5},{5,4},{6,7},{7,6},{8,9},{9,8},{10,11... | collective-permute-start | bytes 6152 | tf_op jit(solution)/shard_map/ppermute | solution.py:31
  36.1 5.1 %collective-permute-start.8 = (f32[2,256]{1,0:T(2,128)S(1)}, f32[2,256]{1,0:T(2,128)S(1)}, u32[]{:S(2)}, u32[]{:S(2)}) collective-permute-start(f32[2,256]{1,0:T(2,128)S(1)} %add.30), channel_id=1, source_target_pairs={{0,2},{2,0},{1,3},{3,1},{4,6},{6,4},{5,7},{7,5},{8,10},{10,8},{9,1... | collective-permute-start | bytes 6152 | tf_op jit(solution)/shard_map/ppermute | solution.py:31
  41.2 3.6 %collective-permute-start.9 = (f32[2,256]{1,0:T(2,128)S(1)}, f32[2,256]{1,0:T(2,128)S(1)}, u32[]{:S(2)}, u32[]{:S(2)}) collective-permute-start(f32[2,256]{1,0:T(2,128)S(1)} %add.31), channel_id=1, source_target_pairs={{0,4},{4,0},{8,12},{12,8},{1,5},{5,1},{9,13},{13,9},{2,6},{6,2},{1... | collective-permute-start | bytes 6152 | tf_op jit(solution)/shard_map/ppermute | solution.py:31
  44.8 4.5 %collective-permute-start.10 = (f32[2,256]{1,0:T(2,128)S(1)}, f32[2,256]{1,0:T(2,128)S(1)}, u32[]{:S(2)}, u32[]{:S(2)}) collective-permute-start(f32[2,256]{1,0:T(2,128)S(1)} %add.32), channel_id=1, source_target_pairs={{0,8},{4,12},{8,0},{12,4},{1,9},{5,13},{9,1},{13,5},{2,10},{6,14},... | collective-permute-start | bytes 6152 | tf_op jit(solution)/shard_map/ppermute | solution.py:31
  50.8 17.6 %copy-start.1 = (f32[256,256]{1,0:T(8,128)S(1)}, f32[256,256]{1,0:T(8,128)}, u32[]{:S(2)}) copy-start(f32[256,256]{1,0:T(8,128)} %refs_1_.3) | copy-start | bytes 786436
  50.8 17.6 %copy-start.5 = (f32[256,256]{1,0:T(8,128)S(1)}, f32[256,256]{1,0:T(8,128)}, u32[]{:S(2)}) copy-start(f32[256,256]{1,0:T(8,128)} %get-tuple-element.19.refs_2_) | copy-start | bytes 786436
  54.6 1.4 %collective-permute-start.14 = (f32[2,256]{1,0:T(2,128)}, f32[2,256]{1,0:T(2,128)S(1)}, u32[]{:S(2)}, u32[]{:S(2)}) collective-permute-start(f32[2,256]{1,0:T(2,128)} %form.1), channel_id=1, source_target_pairs={{0,1},{1,0},{2,3},{3,2},{4,5},{5,4},{6,7},{7,6},{8,9},{9,8},{10,11... | collective-permute-start | bytes 6152 | tf_op jit(solution)/shard_map/ppermute | solution.py:31
  56.7 3.6 %collective-permute-start.15 = (f32[2,256]{1,0:T(2,128)S(1)}, f32[2,256]{1,0:T(2,128)S(1)}, u32[]{:S(2)}, u32[]{:S(2)}) collective-permute-start(f32[2,256]{1,0:T(2,128)S(1)} %add.34), channel_id=1, source_target_pairs={{0,2},{2,0},{1,3},{3,1},{4,6},{6,4},{5,7},{7,5},{8,10},{10,8},{9,1... | collective-permute-start | bytes 6152 | tf_op jit(solution)/shard_map/ppermute | solution.py:31
  60.3 3.6 %collective-permute-start.16 = (f32[2,256]{1,0:T(2,128)S(1)}, f32[2,256]{1,0:T(2,128)S(1)}, u32[]{:S(2)}, u32[]{:S(2)}) collective-permute-start(f32[2,256]{1,0:T(2,128)S(1)} %add.35), channel_id=1, source_target_pairs={{0,4},{4,0},{8,12},{12,8},{1,5},{5,1},{9,13},{13,9},{2,6},{6,2},{1... | collective-permute-start | bytes 6152 | tf_op jit(solution)/shard_map/ppermute | solution.py:31
  63.8 4.5 %collective-permute-start.17 = (f32[2,256]{1,0:T(2,128)S(1)}, f32[2,256]{1,0:T(2,128)S(1)}, u32[]{:S(2)}, u32[]{:S(2)}) collective-permute-start(f32[2,256]{1,0:T(2,128)S(1)} %add.36), channel_id=1, source_target_pairs={{0,8},{4,12},{8,0},{12,4},{1,9},{5,13},{9,1},{13,5},{2,10},{6,14},... | collective-permute-start | bytes 6152 | tf_op jit(solution)/shard_map/ppermute | solution.py:31
  (9 other events, 7.3 us)

commit v2 on v1

v2 whole, which is shorter than its diff:
```python
import jax
import jax.numpy as jnp
from jax import lax
from jax.experimental import pallas as pl
from jax.experimental.pallas import tpu as pltpu
from jax.sharding import PartitionSpec as P

F32 = jnp.float32
HP = lax.Precision.HIGHEST
AXES = ("gx", "gy", "nd")
SIDE = 2
TAIL = 8


def vmem():
    return pl.BlockSpec(memory_space=pltpu.VMEM)


def smem():
    return pl.BlockSpec(memory_space=pltpu.SMEM)


def call(kernel, name, tables, shapes, flops=None):
    def run(*args):
        args = list(args[:tables]) + [pltpu.with_memory_space_constraint(a, pltpu.VMEM) for a in args[tables:]]
        return pl.pallas_call(
            kernel,
            name=name,
            in_specs=[smem()] * tables + [vmem()] * (len(args) - tables),
            out_specs=[vmem()] * len(shapes),
            out_shape=[pltpu.VMEM(shape, F32) for shape in shapes],
            compiler_params=pltpu.CompilerParams(vmem_limit_bytes=16 << 20),
            cost_estimate=flops and pl.CostEstimate(flops=flops, bytes_accessed=1 << 20, transcendentals=0),
        )(*args)

    return run


def axis_sum(part, axes):
    count = lax.axis_size(axes)
    if count & (count - 1):
        return lax.psum(part, axes)
    step = 1
    while step < count:
        masks = [m * step for m in (1, 2, 3) if m * step < count]
        part = part + sum(lax.ppermute(part, axes, [(i, i ^ m) for i in range(count)]) for m in masks)
        step *= 4
    return part


def prep_kernel(cols, sides, packed, diag, local, own, pair):
    nblocks, nonzeros, bs, _ = local.shape
    width = nblocks * bs
    patch_len = 2 * nblocks
    base = sides[0] * nblocks
    own[...] = jnp.zeros(own.shape, F32)
    pair[...] = jnp.zeros((width, width), F32)
    for b in range(nblocks):
        for k in range(nonzeros):
            spot = lax.rem(cols[b, k] - base + patch_len, patch_len)
            block = local[b, k]
            for c in range(nblocks):

                @pl.when(spot == c)
                def _():
                    own[pl.ds(b * bs, bs), pl.ds(c * bs, bs)] += block

                @pl.when(spot == c + nblocks)
                def _():
                    pair[pl.ds(b * bs, bs), pl.ds(c * bs, bs)] += block

    lower = own[...]
    here = lax.broadcasted_iota(jnp.int32, (width, width), 0)
    there = lax.broadcasted_iota(jnp.int32, (width, width), 1)
    own[...] = lower + lower.T + jnp.where(here == there, diag[...], 0.0)


def pack_kernel(send, rows, gives, field, border, *pays):
    width = field.shape[0]
    bs = border.shape[1]
    lane = lax.broadcasted_iota(jnp.int32, (TAIL, SIDE * bs), 1)
    for n, pay in enumerate(pays):
        give = gives[n]
        pay[pl.ds(0, width), :] = field[...]
        tail = jnp.zeros(lane.shape, F32)
        for s in range(SIDE):
            pay[pl.ds(width, bs), pl.ds(s * bs, bs)] = border[give * SIDE + s]
            tail = jnp.where(lane == s, rows[0, give * SIDE + s].astype(F32), tail)
            sent = send[0, (give ^ 1) * SIDE + s].astype(F32)
            tail = jnp.where(lane == SIDE + s, sent, tail)
        pay[pl.ds(width + bs, TAIL), :] = tail


def apply_kernel(send, rows, takes, field, own, pair, mate, mate_pair, border, *refs):
    *pays, image, coup = refs
    width = field.shape[0]
    bs = border.shape[1]
    coup[0] = pair[...] + mate_pair[...].T
    for n, pay in enumerate(pays):
        take = takes[n]
        other = take ^ 1
        coup[1 + n] = jnp.zeros((width, width), F32)
        tail = pay[pl.ds(width + bs, TAIL), :]
        for s in range(SIDE):
            from_row = tail[0:1, s : s + 1]
            from_send = tail[0:1, SIDE + s : SIDE + s + 1]
            block = border[take * SIDE + s]
            turned = pay[pl.ds(width, bs), pl.ds(s * bs, bs)].T
            at = pl.multiple_of(rows[0, take * SIDE + s] * bs, bs)
            bt = pl.multiple_of(send[0, other * SIDE + s] * bs, bs)
            for c in range(width // bs):
                coup[1 + n, pl.ds(at, bs), pl.ds(c * bs, bs)] += jnp.where(from_send == c, block, 0.0)
                coup[1 + n, pl.ds(bt, bs), pl.ds(c * bs, bs)] += jnp.where(from_row == c, turned, 0.0)
    acc = jnp.dot(own[...], field[...], precision=HP, preferred_element_type=F32)
    acc += jnp.dot(coup[0], mate[...], precision=HP, preferred_element_type=F32)
    for n, pay in enumerate(pays):
        acc += jnp.dot(coup[1 + n], pay[pl.ds(0, width), :], precision=HP, preferred_element_type=F32)
    image[pl.ds(0, width), :] = acc
    norm = jnp.sum(field[...] * field[...], axis=0, keepdims=True)
    curve = jnp.sum(field[...] * acc, axis=0, keepdims=True)
    line = lax.broadcasted_iota(jnp.int32, (TAIL, acc.shape[1]), 0)
    image[pl.ds(width, TAIL), :] = jnp.where(line == 0, norm, jnp.where(line == 1, curve, 0.0))


def form_kernel(weights, sums_in, field, image, mate, mate_w, own, coup, *refs):
    nused = len(weights)
    pays = refs[:nused]
    images = refs[nused : 2 * nused]
    sums = refs[2 * nused]
    width = field.shape[0]
    a = sums_in[0:1, :] / sums_in[1:2, :]
    res = field[...] - a * image[pl.ds(0, width), :]
    acc = jnp.dot(own[...], res, precision=HP, preferred_element_type=F32)
    far = mate[...] - a * mate_w[pl.ds(0, width), :]
    acc += jnp.dot(coup[0], far, precision=HP, preferred_element_type=F32)
    for n, (slot, weight) in enumerate(weights):
        far = weight * (pays[n][pl.ds(0, width), :] - a * images[n][pl.ds(0, width), :])
        acc += jnp.dot(coup[1 + slot], far, precision=HP, preferred_element_type=F32)
    sums[0:1, :] = jnp.sum(res * res, axis=0, keepdims=True)
    sums[1:2, :] = jnp.sum(res * acc, axis=0, keepdims=True)


def last_kernel(first, second, field, image, out):
    norm, curve = first[0:1, :], first[1:2, :]
    a = norm / curve
    ratio = second[0:1, :] / norm
    b = second[0:1, :] / (second[1:2, :] - ratio * ratio * curve)
    out[...] = (a + b * (1.0 + ratio)) * field[...] - (b * a) * image[pl.ds(0, field.shape[0]), :]


def shards(right_side, node_diag, local_coup, block_cols, border_coup, border_send, border_rows):
    width, ncols = right_side.shape
    nblocks, _, bs, _ = local_coup.shape
    n_gx, n_gy, n_nd = (lax.axis_size(a) for a in AXES)
    assert n_nd == 2 and border_coup.shape[1] == 4 * SIDE
    gyi = lax.axis_index("gy")
    swap = [(0, 1), (1, 0)]
    right = [(i, (i + 1) % n_gx) for i in range(n_gx)]
    left = [(j, i) for i, j in right]
    up = [(i, i + 1) for i in range(n_gy - 1)]
    down = [(j, i) for i, j in up]
    slots = [("gx", right, 0), ("gx", left, 1)]
    if n_gy == 2:
        slots.insert(1, ("gy", swap, jnp.where(gyi == 0, 3, 2)))
        weights = [(0, 2.0), (1, 1.0)]
    elif n_gy > 2:
        slots.insert(1, ("gy", up, 2))
        slots.append(("gy", down, 3))
        weights = [(0, 2.0), (1, 2.0)]
    else:
        weights = [(0, 2.0)]
    nslots = len(slots)
    take = [jnp.asarray(t, jnp.int32) for _, _, t in slots]
    ndi = lax.axis_index("nd").astype(jnp.int32)
    give = [jnp.where(gyi == 0, 3, 2).astype(jnp.int32) if n_gy == 2 and a == "gy" else t ^ 1 for (a, _, _), t in zip(slots, take)]
    gives = jnp.stack(give)
    takes = jnp.stack(take)
    border = border_coup[0]

    packed = call(pack_kernel, "pack", 3, [(width + bs + TAIL, ncols)] * nslots)(border_send, border_rows, gives, right_side, border)
    pays = [lax.ppermute(pay, axis, perm) for pay, (axis, perm, _) in zip(packed, slots)]
    own, pair = call(prep_kernel, "prep", 2, [(width, width)] * 2, 1 << 24)(
        block_cols, ndi[None], packed[0], node_diag.reshape(1, width), local_coup
    )
    mate = lax.ppermute(right_side, "nd", swap)
    mate_pair = lax.ppermute(pair, "nd", swap)

    image, coup = call(apply_kernel, "apply", 3, [(width + TAIL, ncols), (1 + nslots, width, width)])(
        border_send, border_rows, takes, right_side, own, pair, mate, mate_pair, border, *pays
    )
    images = [lax.ppermute(image, slots[n][0], slots[n][1]) for n, _ in weights]
    mate_w = lax.ppermute(image, "nd", swap)
    first = axis_sum(image[width:] + mate_w[width:], ("gx", "gy"))

    (second,) = call(lambda *refs: form_kernel(weights, *refs), "form", 0, [(2, ncols)])(
        first, right_side, image, mate, mate_w, own, coup, *[pays[n] for n, _ in weights], *images
    )
    second = axis_sum(second, AXES)
    return pl.pallas_call(
        last_kernel,
        name="last",
        in_specs=[vmem()] * 4,
        out_specs=vmem(),
        out_shape=jax.ShapeDtypeStruct((width, ncols), F32),
        compiler_params=pltpu.CompilerParams(vmem_limit_bytes=16 << 20),
    )(first, second, right_side, image)


def solution(mesh):
    blocks = P(("var", "gx", "gy", "nd"))
    tables = P(AXES)
    in_specs = (blocks, blocks, blocks, tables, blocks, tables, tables)
    return jax.shard_map(shards, mesh=mesh, in_specs=in_specs, out_specs=blocks, check_vma=False)
```

time: 70 us -> 60.2 us (0.86)
  waiting for transfers between devices: 36.1 us -> 26.6 us
  starting transfers between devices: 16.6 us -> 20.7 us
  other arithmetic: 3.34 us -> 0.17 us
  Pallas kernels: 11 us -> 8.76 us
  local copies, waits for them, and re-layouts: 2.58 us -> 3.56 us
    ppermute x12, waiting for transfers between devices: 24.1 us -> 13.5 us  [the longest x10 12.4 us: axis_sum(): lax.ppermute(part, axes, [(i, i ^ m) for i in range(count)])]
    ppermute x12, starting transfers between devices: 6.56 us -> 11.8 us  [the longest x10 11.2 us: axis_sum(): lax.ppermute(part, axes, [(i, i ^ m) for i in range(count)])]
    pallas_call x3 -> x5, Pallas kernels: 11 us -> 8.76 us  [the longest x4 7.06 us: run(): pl.pallas_call(kernel, name=name, in_specs=[smem()] * tables + [vmem()] *...]
    add x9 -> x5, other arithmetic: 1.46 us -> 0.02 us  [the longest x4 0.02 us: axis_sum(): part + sum((lax.ppermute(part, axes, [(i, i ^ m) for i in range(count)])...]
    ppermute x3, starting transfers between devices: 7.93 us -> 6.61 us  [shards(): lax.ppermute(pay, axis, perm)]
    another operation x2, other arithmetic: 1.26 us -> 0.15 us  [the longest x1 0.08 us: shards(): gives = jnp.stack(give)]
    ppermute x3, waiting for transfers between devices: 12 us -> 13.1 us  [shards(): lax.ppermute(pay, axis, perm)]
    unnamed x30 -> x14, local copies, waits for them, and re-layouts: 2.58 us -> 3.56 us
  transfers between devices with their start and end apart: 18 -> 18, of which waited for: 10 -> 10; matrix products, arithmetic and copies ran while one was open for 2% -> 0% of each run, Pallas kernels for 0% -> 2%
where the time goes in v2:
time: 60.2 us; the launch traced here: 59.9 us
  waiting for transfers between devices  26.6 us (44%)
  starting transfers between devices  20.7 us (34%)
  Pallas kernels  8.76 us (15%)
  local copies, waits for them, and re-layouts  3.56 us (6%)
    ppermute x3, waiting for transfers between devices, shards(): lax.ppermute(pay, axis, perm)  13.1 us
    ppermute x10, waiting for transfers between devices, axis_sum(): lax.ppermute(part, axes, [(i, i ^ m) for i in range(count)])  12.4 us
    ppermute x10, starting transfers between devices, axis_sum(): lax.ppermute(part, axes, [(i, i ^ m) for i in range(count)])  11.2 us
    pallas_call x4, Pallas kernels, run(): pl.pallas_call(kernel, name=name, in_specs=[smem()] * tables + [vmem()] *...  7.06 us
    ppermute x3, starting transfers between devices, shards(): lax.ppermute(pay, axis, perm)  6.61 us
    unnamed x14, local copies, waits for them, and re-layouts  3.56 us
    ppermute x2, starting transfers between devices, shards(): images = [lax.ppermute(image, slots[n][0], slots[n][1]) for n, _ in weights]  2.23 us
    pallas_call x1, Pallas kernels, shards(): pl.pallas_call(last_kernel, name='last', in_specs=[vmem()] * 4, out_specs...  1.7 us
  transfers between devices with their start and end apart: 18, of which 10 were waited for; matrix products, arithmetic and copies ran while one was open for 0% of the time, Pallas kernels for 2%

profile of v2, /device:TPU:0, one launch (start us, length us, event | category | flops | bytes accessed | tf_op | source)
XLA Modules:
  0.0 59.9 jit_solution(818633936859280987)
XLA Ops:
  0.8 1.0 %copy-done = f32[1,8,128,128]{3,2,1,0:T(8,128)S(1)} copy-done((f32[1,8,128,128]{3,2,1,0:T(8,128)S(1)}, f32[1,8,128,128]{3,2,1,0:T(8,128)}, u32[]{:S(2)}) %copy-start) | copy-done | bytes 524312
  1.8 1.0 %pack.1 = (f32[392,256]{1,0:T(8,128)S(1)}, f32[392,256]{1,0:T(8,128)S(1)}, f32[392,256]{1,0:T(8,128)S(1)}) custom-call(s32[1,8]{1,0:T(1,128)S(1)} %copy-done.3, s32[1,8]{1,0:T(1,128)S(1)} %copy-done.4, s32[3]{0:T(128)S(1)} %pad_add_fusion.1.gives, f32[256,256]{1,0:T(8,128)} %field.5, f32[8,128,128]{2,1,0:T(8,128)S(1)} %bitcast.4), custom_call_target="tpu_custom_call" | custom-call | tf_op jit(solution)/shard_map/pack/pallas_call | solution.py:26
  2.8 3.0 %collective-permute-start.3 = (f32[392,256]{1,0:T(8,128)S(1)}, f32[392,256]{1,0:T(8,128)S(1)}, u32[]{:S(2)}, u32[]{:S(2)}) collective-permute-start(f32[392,256]{1,0:T(8,128)S(1)} %get-tuple-element.15), channel_id=1, source_target_pairs={{0,2},{2,0},{1,3},{3,1},{4,6},{6,4},{5,7},{7,5},{8,10},{10,8},{9,1... | collective-permute-start | bytes 1204232 | tf_op jit(solution)/shard_map/ppermute | solution.py:181
  5.8 3.6 %collective-permute-start.4 = (f32[392,256]{1,0:T(8,128)S(1)}, f32[392,256]{1,0:T(8,128)S(1)}, u32[]{:S(2)}, u32[]{:S(2)}) collective-permute-start(f32[392,256]{1,0:T(8,128)S(1)} %get-tuple-element.16), channel_id=1, source_target_pairs={{4,0},{8,4},{12,8},{0,12},{5,1},{9,5},{13,9},{1,13},{6,2},{10,6},{... | collective-permute-start | bytes 1204232 | tf_op jit(solution)/shard_map/ppermute | solution.py:181
  10.1 1.2 %copy-done.2 = f32[2,7,128,128]{3,2,1,0:T(8,128)S(1)} copy-done((f32[2,7,128,128]{3,2,1,0:T(8,128)S(1)}, f32[2,7,128,128]{3,2,1,0:T(8,128)}, u32[]{:S(2)}) %copy-start.2) | copy-done | bytes 917528
  11.3 1.1 %prep.1 = (f32[256,256]{1,0:T(8,128)S(1)}, f32[256,256]{1,0:T(8,128)S(1)}) custom-call(s32[2,7]{1,0:T(2,128)S(1)} %copy-done.5, s32[1]{0:T(128)} %bitcast.1.sides, f32[392,256]{1,0:T(8,128)S(1)} %get-tuple-element.12.packed, f32[1,256]{1,0:T(1,128)S(1)} %bitcast.6, f32[2,7,128,128]{3,2,1,0:T(8,128)S(1)} %copy-done.2), custom_call_target="tpu_custom_call" | custom-call | flops 16777216 | bytes 1048576 | tf_op jit(solution)/shard_map/prep/pallas_call | solution.py:26
  13.1 1.1 %collective-permute-done.1.mate_pair = f32[256,256]{1,0:T(8,128)S(1)} collective-permute-done((f32[256,256]{1,0:T(8,128)S(1)}, f32[256,256]{1,0:T(8,128)S(1)}, u32[]{:S(2)}, u32[]{:S(2)}) %collective-permute-start.1) | collective-permute-done | bytes 262176 | tf_op jit(solution)/shard_map/ppermute | solution.py:186
  14.1 1.0 %collective-permute-done.3.refs_1_.refs_8_ = f32[392,256]{1,0:T(8,128)S(1)} collective-permute-done((f32[392,256]{1,0:T(8,128)S(1)}, f32[392,256]{1,0:T(8,128)S(1)}, u32[]{:S(2)}, u32[]{:S(2)}) %collective-permute-start.3) | collective-permute-done | bytes 401440 | tf_op jit(solution)/shard_map/ppermute | solution.py:181
  15.1 4.0 %collective-permute-done.4.refs_2_ = f32[392,256]{1,0:T(8,128)S(1)} collective-permute-done((f32[392,256]{1,0:T(8,128)S(1)}, f32[392,256]{1,0:T(8,128)S(1)}, u32[]{:S(2)}, u32[]{:S(2)}) %collective-permute-start.4) | collective-permute-done | bytes 401440 | tf_op jit(solution)/shard_map/ppermute | solution.py:181
  19.2 8.0 %collective-permute-done.2.refs_0_.refs_7_ = f32[392,256]{1,0:T(8,128)S(1)} collective-permute-done((f32[392,256]{1,0:T(8,128)S(1)}, f32[392,256]{1,0:T(8,128)S(1)}, u32[]{:S(2)}, u32[]{:S(2)}) %collective-permute-start.2) | collective-permute-done | bytes 401440 | tf_op jit(solution)/shard_map/ppermute | solution.py:181
  27.2 2.7 %apply.1 = (f32[264,256]{1,0:T(8,128)S(1)}, f32[4,256,256]{2,1,0:T(8,128)S(1)}) custom-call(s32[1,8]{1,0:T(1,128)S(1)} %copy-done.3, s32[1,8]{1,0:T(1,128)S(1)} %copy-done.4, s32[3]{0:T(128)S(1)} %pad_add_fusion.takes, f32[256,256]{1,0:T(8,128)} %field.5, f32[256,256]{1,0:T(8,128)S(1)} %get-tuple-element.13.own.refs_5_, ...), custom_call_target="tpu_custom_call" | custom-call | tf_op jit(solution)/shard_map/apply/pallas_call | solution.py:26
  30.7 1.6 %collective-permute-start.10 = (f32[264,256]{1,0:T(8,128)S(1)}, f32[264,256]{1,0:T(8,128)S(1)}, u32[]{:S(2)}, u32[]{:S(2)}) collective-permute-start(f32[264,256]{1,0:T(8,128)S(1)} %get-tuple-element.17.refs_2_.image), channel_id=1, source_target_pairs={{0,4},{4,8},{8,12},{12,0},{1,5},{5,9},{9,13},{13,1},{2,6},{6,10},{... | collective-permute-start | bytes 811016 | tf_op jit(solution)/shard_map/ppermute | solution.py:191
  32.3 1.0 %collective-permute-start.8 = (f32[8,256]{1,0:T(8,128)S(1)}, f32[8,256]{1,0:T(8,128)S(1)}, u32[]{:S(2)}, u32[]{:S(2)}) collective-permute-start(f32[8,256]{1,0:T(8,128)S(1)} %slice_add_fusion), channel_id=1, source_target_pairs={{0,6},{2,4},{4,2},{6,0},{8,14},{10,12},{12,10},{14,8},{1,7},{3,5},... | collective-permute-start | bytes 24584 | tf_op jit(solution)/shard_map/ppermute | solution.py:46
  33.3 2.0 %collective-permute-start.7 = (f32[8,256]{1,0:T(8,128)S(1)}, f32[8,256]{1,0:T(8,128)S(1)}, u32[]{:S(2)}, u32[]{:S(2)}) collective-permute-start(f32[8,256]{1,0:T(8,128)S(1)} %slice_add_fusion), channel_id=1, source_target_pairs={{0,4},{2,6},{4,0},{6,2},{8,12},{10,14},{12,8},{14,10},{1,5},{3,7},... | collective-permute-start | bytes 24584 | tf_op jit(solution)/shard_map/ppermute | solution.py:46
  35.8 5.7 %collective-permute-done.8 = f32[8,256]{1,0:T(8,128)S(1)} collective-permute-done((f32[8,256]{1,0:T(8,128)S(1)}, f32[8,256]{1,0:T(8,128)S(1)}, u32[]{:S(2)}, u32[]{:S(2)}) %collective-permute-start.8) | collective-permute-done | bytes 8224 | tf_op jit(solution)/shard_map/ppermute | solution.py:46
  41.5 1.3 %collective-permute-start.9 = (f32[8,256]{1,0:T(8,128)S(1)}, f32[8,256]{1,0:T(8,128)S(1)}, u32[]{:S(2)}, u32[]{:S(2)}) collective-permute-start(f32[8,256]{1,0:T(8,128)S(1)} %add_add_fusion), channel_id=1, source_target_pairs={{0,8},{2,10},{4,12},{6,14},{8,0},{10,2},{12,4},{14,6},{1,9},{3,11}... | collective-permute-start | bytes 24584 | tf_op jit(solution)/shard_map/ppermute | solution.py:46
  42.8 3.3 %collective-permute-done.9 = f32[8,256]{1,0:T(8,128)S(1)} collective-permute-done((f32[8,256]{1,0:T(8,128)S(1)}, f32[8,256]{1,0:T(8,128)S(1)}, u32[]{:S(2)}, u32[]{:S(2)}) %collective-permute-start.9) | collective-permute-done | bytes 8224 | tf_op jit(solution)/shard_map/ppermute | solution.py:46
  46.2 2.2 %form.1 = f32[2,256]{1,0:T(2,128)S(1)} custom-call(f32[8,256]{1,0:T(8,128)S(1)} %add.37.refs_0_.first, f32[256,256]{1,0:T(8,128)} %field.5, f32[264,256]{1,0:T(8,128)S(1)} %get-tuple-element.17.refs_2_.image, f32[256,256]{1,0:T(8,128)S(1)} %collective-permute-done.mate.refs_3_, f32[264,256]{1,0:T(8,128)S(1)} %collective-permute-done.5.refs_4_, ...), custom_call_target="tpu_custom_call" | custom-call | tf_op jit(solution)/shard_map/form/pallas_call | solution.py:26
  48.5 1.3 %collective-permute-start.13 = (f32[2,256]{1,0:T(2,128)S(1)}, f32[2,256]{1,0:T(2,128)S(1)}, u32[]{:S(2)}, u32[]{:S(2)}) collective-permute-start(f32[2,256]{1,0:T(2,128)S(1)} %form.1), channel_id=1, source_target_pairs={{0,2},{1,3},{2,0},{3,1},{4,6},{5,7},{6,4},{7,5},{8,10},{9,11},{10,... | collective-permute-start | bytes 6152 | tf_op jit(solution)/shard_map/ppermute | solution.py:46
  50.3 1.1 %collective-permute-done.14 = f32[2,256]{1,0:T(2,128)S(1)} collective-permute-done((f32[2,256]{1,0:T(2,128)S(1)}, f32[2,256]{1,0:T(2,128)S(1)}, u32[]{:S(2)}, u32[]{:S(2)}) %collective-permute-start.14) | collective-permute-done | bytes 2080 | tf_op jit(solution)/shard_map/ppermute | solution.py:46
  52.8 1.3 %collective-permute-start.16 = (f32[2,256]{1,0:T(2,128)S(1)}, f32[2,256]{1,0:T(2,128)S(1)}, u32[]{:S(2)}, u32[]{:S(2)}) collective-permute-start(f32[2,256]{1,0:T(2,128)S(1)} %add_add_fusion.2), channel_id=1, source_target_pairs={{0,8},{1,9},{2,10},{3,11},{4,12},{5,13},{6,14},{7,15},{8,0},{9,1},... | collective-permute-start | bytes 6152 | tf_op jit(solution)/shard_map/ppermute | solution.py:46
  54.1 2.4 %collective-permute-start.15 = (f32[2,256]{1,0:T(2,128)S(1)}, f32[2,256]{1,0:T(2,128)S(1)}, u32[]{:S(2)}, u32[]{:S(2)}) collective-permute-start(f32[2,256]{1,0:T(2,128)S(1)} %add_add_fusion.2), channel_id=1, source_target_pairs={{0,4},{1,5},{2,6},{3,7},{4,0},{5,1},{6,2},{7,3},{8,12},{9,13},{10,... | collective-permute-start | bytes 6152 | tf_op jit(solution)/shard_map/ppermute | solution.py:46
  56.6 1.0 %collective-permute-done.17 = f32[2,256]{1,0:T(2,128)S(1)} collective-permute-done((f32[2,256]{1,0:T(2,128)S(1)}, f32[2,256]{1,0:T(2,128)S(1)}, u32[]{:S(2)}, u32[]{:S(2)}) %collective-permute-start.17) | collective-permute-done | bytes 2080 | tf_op jit(solution)/shard_map/ppermute | solution.py:46
  58.1 1.7 %last.1 = f32[256,256]{1,0:T(8,128)} custom-call(f32[8,256]{1,0:T(8,128)S(1)} %add.37.refs_0_.first, f32[2,256]{1,0:T(2,128)S(1)} %add_add_fusion.1.second, f32[256,256]{1,0:T(8,128)} %field.5, f32[264,256]{1,0:T(8,128)S(1)} %get-tuple-element.17.refs_2_.image), custom_call_target="tpu_custom_call" | custom-call | tf_op jit(solution)/shard_map/last/pallas_call | solution.py:199
  (38 shorter events, 5.9 us)
Async XLA Ops:
  0.1 0.7 %copy-start.4 = (s32[1,8]{1,0:T(1,128)S(1)}, s32[1,8]{1,0:T(1,128)}, u32[]{:S(2)}) copy-start(s32[1,8]{1,0:T(1,128)} %rows.3) | copy-start | bytes 100
  0.7 1.0 %copy-start = (f32[1,8,128,128]{3,2,1,0:T(8,128)S(1)}, f32[1,8,128,128]{3,2,1,0:T(8,128)}, u32[]{:S(2)}) copy-start(f32[1,8,128,128]{3,2,1,0:T(8,128)} %param.11) | copy-start | bytes 1572868
  2.8 12.3 %collective-permute-start.3 = (f32[392,256]{1,0:T(8,128)S(1)}, f32[392,256]{1,0:T(8,128)S(1)}, u32[]{:S(2)}, u32[]{:S(2)}) collective-permute-start(f32[392,256]{1,0:T(8,128)S(1)} %get-tuple-element.15), channel_id=1, source_target_pairs={{0,2},{2,0},{1,3},{3,1},{4,6},{6,4},{5,7},{7,5},{8,10},{10,8},{9,1... | collective-permute-start | bytes 1204232 | tf_op jit(solution)/shard_map/ppermute | solution.py:181
  5.8 3.6 %copy-start.6 = (f32[256]{0:T(256)S(1)}, f32[256]{0:T(256)}, u32[]{:S(2)}) copy-start(f32[256]{0:T(256)} %param.8) | copy-start | bytes 3076
  5.8 13.3 %collective-permute-start.4 = (f32[392,256]{1,0:T(8,128)S(1)}, f32[392,256]{1,0:T(8,128)S(1)}, u32[]{:S(2)}, u32[]{:S(2)}) collective-permute-start(f32[392,256]{1,0:T(8,128)S(1)} %get-tuple-element.16), channel_id=1, source_target_pairs={{4,0},{8,4},{12,8},{0,12},{5,1},{9,5},{13,9},{1,13},{6,2},{10,6},{... | collective-permute-start | bytes 1204232 | tf_op jit(solution)/shard_map/ppermute | solution.py:181
  9.4 17.8 %collective-permute-start.2 = (f32[392,256]{1,0:T(8,128)S(1)}, f32[392,256]{1,0:T(8,128)S(1)}, u32[]{:S(2)}, u32[]{:S(2)}) collective-permute-start(f32[392,256]{1,0:T(8,128)S(1)} %get-tuple-element.12.packed), channel_id=1, source_target_pairs={{0,4},{4,8},{8,12},{12,0},{1,5},{5,9},{9,13},{13,1},{2,6},{6,10},{... | collective-permute-start | bytes 1204232 | tf_op jit(solution)/shard_map/ppermute | solution.py:181
  9.4 3.6 %collective-permute-start = (f32[256,256]{1,0:T(8,128)}, f32[256,256]{1,0:T(8,128)S(1)}, u32[]{:S(2)}, u32[]{:S(2)}) collective-permute-start(f32[256,256]{1,0:T(8,128)} %field.5), channel_id=1, source_target_pairs={{0,1},{1,0},{2,3},{3,2},{4,5},{5,4},{6,7},{7,6},{8,9},{9,8},{10,11... | collective-permute-start | bytes 786440 | tf_op jit(solution)/shard_map/ppermute | solution.py:185
  9.5 0.7 %copy-start.5 = (s32[2,7]{1,0:T(2,128)S(1)}, s32[2,7]{1,0:T(2,128)}, u32[]{:S(2)}) copy-start(s32[2,7]{1,0:T(2,128)} %cols.1) | copy-start | bytes 172
  10.1 1.2 %copy-start.2 = (f32[2,7,128,128]{3,2,1,0:T(8,128)S(1)}, f32[2,7,128,128]{3,2,1,0:T(8,128)}, u32[]{:S(2)}) copy-start(f32[2,7,128,128]{3,2,1,0:T(8,128)} %local.1) | copy-start | bytes 2752516
  11.3 15.9 %copy-start.1 = (f32[1,8,128,128]{3,2,1,0:T(8,128)S(1)}, f32[1,8,128,128]{3,2,1,0:T(8,128)}, u32[]{:S(2)}) copy-start(f32[1,8,128,128]{3,2,1,0:T(8,128)} %param.11) | copy-start | bytes 1572868
  12.4 1.7 %collective-permute-start.1 = (f32[256,256]{1,0:T(8,128)S(1)}, f32[256,256]{1,0:T(8,128)S(1)}, u32[]{:S(2)}, u32[]{:S(2)}) collective-permute-start(f32[256,256]{1,0:T(8,128)S(1)} %get-tuple-element.14.pair), channel_id=1, source_target_pairs={{0,1},{1,0},{2,3},{3,2},{4,5},{5,4},{6,7},{7,6},{8,9},{9,8},{10,11... | collective-permute-start | bytes 786440 | tf_op jit(solution)/shard_map/ppermute | solution.py:186
  30.0 2.3 %collective-permute-start.5 = (f32[264,256]{1,0:T(8,128)S(1)}, f32[264,256]{1,0:T(8,128)S(1)}, u32[]{:S(2)}, u32[]{:S(2)}) collective-permute-start(f32[264,256]{1,0:T(8,128)S(1)} %get-tuple-element.17.refs_2_.image), channel_id=1, source_target_pairs={{0,1},{1,0},{2,3},{3,2},{4,5},{5,4},{6,7},{7,6},{8,9},{9,8},{10,11... | collective-permute-start | bytes 811016 | tf_op jit(solution)/shard_map/ppermute | solution.py:192
  30.1 16.1 %collective-permute-start.11 = (f32[264,256]{1,0:T(8,128)S(1)}, f32[264,256]{1,0:T(8,128)S(1)}, u32[]{:S(2)}, u32[]{:S(2)}) collective-permute-start(f32[264,256]{1,0:T(8,128)S(1)} %get-tuple-element.17.refs_2_.image), channel_id=1, source_target_pairs={{0,2},{2,0},{1,3},{3,1},{4,6},{6,4},{5,7},{7,5},{8,10},{10,8},{9,1... | collective-permute-start | bytes 811016 | tf_op jit(solution)/shard_map/ppermute | solution.py:191
  30.7 15.5 %collective-permute-start.10 = (f32[264,256]{1,0:T(8,128)S(1)}, f32[264,256]{1,0:T(8,128)S(1)}, u32[]{:S(2)}, u32[]{:S(2)}) collective-permute-start(f32[264,256]{1,0:T(8,128)S(1)} %get-tuple-element.17.refs_2_.image), channel_id=1, source_target_pairs={{0,4},{4,8},{8,12},{12,0},{1,5},{5,9},{9,13},{13,1},{2,6},{6,10},{... | collective-permute-start | bytes 811016 | tf_op jit(solution)/shard_map/ppermute | solution.py:191
  32.3 9.2 %collective-permute-start.8 = (f32[8,256]{1,0:T(8,128)S(1)}, f32[8,256]{1,0:T(8,128)S(1)}, u32[]{:S(2)}, u32[]{:S(2)}) collective-permute-start(f32[8,256]{1,0:T(8,128)S(1)} %slice_add_fusion), channel_id=1, source_target_pairs={{0,6},{2,4},{4,2},{6,0},{8,14},{10,12},{12,10},{14,8},{1,7},{3,5},... | collective-permute-start | bytes 24584 | tf_op jit(solution)/shard_map/ppermute | solution.py:46
  33.3 8.2 %collective-permute-start.7 = (f32[8,256]{1,0:T(8,128)S(1)}, f32[8,256]{1,0:T(8,128)S(1)}, u32[]{:S(2)}, u32[]{:S(2)}) collective-permute-start(f32[8,256]{1,0:T(8,128)S(1)} %slice_add_fusion), channel_id=1, source_target_pairs={{0,4},{2,6},{4,0},{6,2},{8,12},{10,14},{12,8},{14,10},{1,5},{3,7},... | collective-permute-start | bytes 24584 | tf_op jit(solution)/shard_map/ppermute | solution.py:46
  35.2 6.3 %collective-permute-start.6 = (f32[8,256]{1,0:T(8,128)S(1)}, f32[8,256]{1,0:T(8,128)S(1)}, u32[]{:S(2)}, u32[]{:S(2)}) collective-permute-start(f32[8,256]{1,0:T(8,128)S(1)} %slice_add_fusion), channel_id=1, source_target_pairs={{0,2},{2,0},{4,6},{6,4},{8,10},{10,8},{12,14},{14,12},{1,3},{3,1},... | collective-permute-start | bytes 24584 | tf_op jit(solution)/shard_map/ppermute | solution.py:46
  41.5 4.7 %collective-permute-start.9 = (f32[8,256]{1,0:T(8,128)S(1)}, f32[8,256]{1,0:T(8,128)S(1)}, u32[]{:S(2)}, u32[]{:S(2)}) collective-permute-start(f32[8,256]{1,0:T(8,128)S(1)} %add_add_fusion), channel_id=1, source_target_pairs={{0,8},{2,10},{4,12},{6,14},{8,0},{10,2},{12,4},{14,6},{1,9},{3,11}... | collective-permute-start | bytes 24584 | tf_op jit(solution)/shard_map/ppermute | solution.py:46
  48.4 3.1 %collective-permute-start.14 = (f32[2,256]{1,0:T(2,128)S(1)}, f32[2,256]{1,0:T(2,128)S(1)}, u32[]{:S(2)}, u32[]{:S(2)}) collective-permute-start(f32[2,256]{1,0:T(2,128)S(1)} %form.1), channel_id=1, source_target_pairs={{0,3},{1,2},{2,1},{3,0},{4,7},{5,6},{6,5},{7,4},{8,11},{9,10},{10,... | collective-permute-start | bytes 6152 | tf_op jit(solution)/shard_map/ppermute | solution.py:46
  48.5 3.7 %collective-permute-start.13 = (f32[2,256]{1,0:T(2,128)S(1)}, f32[2,256]{1,0:T(2,128)S(1)}, u32[]{:S(2)}, u32[]{:S(2)}) collective-permute-start(f32[2,256]{1,0:T(2,128)S(1)} %form.1), channel_id=1, source_target_pairs={{0,2},{1,3},{2,0},{3,1},{4,6},{5,7},{6,4},{7,5},{8,10},{9,11},{10,... | collective-permute-start | bytes 6152 | tf_op jit(solution)/shard_map/ppermute | solution.py:46
  49.7 2.4 %collective-permute-start.12 = (f32[2,256]{1,0:T(2,128)S(1)}, f32[2,256]{1,0:T(2,128)S(1)}, u32[]{:S(2)}, u32[]{:S(2)}) collective-permute-start(f32[2,256]{1,0:T(2,128)S(1)} %form.1), channel_id=1, source_target_pairs={{0,1},{1,0},{2,3},{3,2},{4,5},{5,4},{6,7},{7,6},{8,9},{9,8},{10,11... | collective-permute-start | bytes 6152 | tf_op jit(solution)/shard_map/ppermute | solution.py:46
  52.1 5.4 %collective-permute-start.17 = (f32[2,256]{1,0:T(2,128)S(1)}, f32[2,256]{1,0:T(2,128)S(1)}, u32[]{:S(2)}, u32[]{:S(2)}) collective-permute-start(f32[2,256]{1,0:T(2,128)S(1)} %add_add_fusion.2), channel_id=1, source_target_pairs={{0,12},{1,13},{2,14},{3,15},{4,8},{5,9},{6,10},{7,11},{8,4},{9,5},... | collective-permute-start | bytes 6152 | tf_op jit(solution)/shard_map/ppermute | solution.py:46
  52.8 4.8 %collective-permute-start.16 = (f32[2,256]{1,0:T(2,128)S(1)}, f32[2,256]{1,0:T(2,128)S(1)}, u32[]{:S(2)}, u32[]{:S(2)}) collective-permute-start(f32[2,256]{1,0:T(2,128)S(1)} %add_add_fusion.2), channel_id=1, source_target_pairs={{0,8},{1,9},{2,10},{3,11},{4,12},{5,13},{6,14},{7,15},{8,0},{9,1},... | collective-permute-start | bytes 6152 | tf_op jit(solution)/shard_map/ppermute | solution.py:46
  54.1 4.0 %collective-permute-start.15 = (f32[2,256]{1,0:T(2,128)S(1)}, f32[2,256]{1,0:T(2,128)S(1)}, u32[]{:S(2)}, u32[]{:S(2)}) collective-permute-start(f32[2,256]{1,0:T(2,128)S(1)} %add_add_fusion.2), channel_id=1, source_target_pairs={{0,4},{1,5},{2,6},{3,7},{4,0},{5,1},{6,2},{7,3},{8,12},{9,13},{10,... | collective-permute-start | bytes 6152 | tf_op jit(solution)/shard_map/ppermute | solution.py:46
  (1 other events, 0.7 us)

commit v3 on v2

v3 whole, which is shorter than its diff:
```python
from functools import partial

import jax
import jax.numpy as jnp
from jax import lax
from jax.experimental import pallas as pl
from jax.experimental.pallas import tpu as pltpu
from jax.sharding import PartitionSpec as P

F32 = jnp.float32
HP = lax.Precision.HIGHEST
AXES = ("gx", "gy", "nd")
SIDE = 2
LIMIT = 8 << 20
TAIL = 8


def vmem():
    return pl.BlockSpec(memory_space=pltpu.VMEM)


def smem():
    return pl.BlockSpec(memory_space=pltpu.SMEM)


def call(kernel, name, tables, shapes, flops=None, scratch=()):
    def run(*args):
        args = list(args[:tables]) + [pltpu.with_memory_space_constraint(a, pltpu.VMEM) for a in args[tables:]]
        return pl.pallas_call(
            kernel,
            name=name,
            in_specs=[smem()] * tables + [vmem()] * (len(args) - tables),
            out_specs=[vmem()] * len(shapes),
            out_shape=[pltpu.VMEM(shape, F32) for shape in shapes],
            scratch_shapes=scratch,
            compiler_params=pltpu.CompilerParams(vmem_limit_bytes=LIMIT),
            cost_estimate=flops and pl.CostEstimate(flops=flops, bytes_accessed=1 << 20, transcendentals=0),
        )(*args)

    return run


def axis_sum(part, axes):
    count = lax.axis_size(axes)
    if count & (count - 1):
        return lax.psum(part, axes)
    step = 1
    while step < count:
        masks = [m * step for m in (1, 2, 3) if m * step < count]
        part = part + sum(lax.ppermute(part, axes, [(i, i ^ m) for i in range(count)]) for m in masks)
        step *= 4
    return part


def prep_kernel(cols, sides, packed, diag, local, own, pair):
    nblocks, nonzeros, bs, _ = local.shape
    width = nblocks * bs
    patch_len = 2 * nblocks
    base = sides[0] * nblocks
    own[...] = jnp.zeros(own.shape, F32)
    pair[...] = jnp.zeros((width, width), F32)
    for b in range(nblocks):
        for k in range(nonzeros):
            spot = lax.rem(cols[b, k] - base + patch_len, patch_len)
            block = local[b, k]
            for c in range(nblocks):

                @pl.when(spot == c)
                def _():
                    own[pl.ds(b * bs, bs), pl.ds(c * bs, bs)] += block

                @pl.when(spot == c + nblocks)
                def _():
                    pair[pl.ds(b * bs, bs), pl.ds(c * bs, bs)] += block

    lower = own[...]
    here = lax.broadcasted_iota(jnp.int32, (width, width), 0)
    there = lax.broadcasted_iota(jnp.int32, (width, width), 1)
    own[...] = lower + lower.T + jnp.where(here == there, diag[...], 0.0)


def pack_kernel(send, rows, gives, field, border, *refs):
    *pays, sems = refs
    width = field.shape[0]
    bs = border.shape[1]
    copies = []
    for n, pay in enumerate(pays):
        copies.append(pltpu.make_async_copy(field, pay.at[pl.ds(0, width), :], sems.at[n, SIDE]))
        for s in range(SIDE):
            block = pay.at[pl.ds(width, bs), pl.ds(s * bs, bs)]
            copies.append(pltpu.make_async_copy(border.at[gives[n] * SIDE + s], block, sems.at[n, s]))
    for copy in copies:
        copy.start()
    lane = lax.broadcasted_iota(jnp.int32, (TAIL, SIDE * bs), 1)
    for n, pay in enumerate(pays):
        give = gives[n]
        tail = jnp.zeros(lane.shape, F32)
        for s in range(SIDE):
            tail = jnp.where(lane == s, rows[0, give * SIDE + s].astype(F32), tail)
            sent = send[0, (give ^ 1) * SIDE + s].astype(F32)
            tail = jnp.where(lane == SIDE + s, sent, tail)
        pay[pl.ds(width + bs, TAIL), :] = tail
    for copy in copies:
        copy.wait()


def build_edge(coup, take, send, rows, border, pay):
    bs = border.shape[1]
    width = coup.shape[0]
    other = take ^ 1
    coup[...] = jnp.zeros((width, width), F32)
    tail = pay[pl.ds(width + bs, TAIL), :]
    for s in range(SIDE):
        from_row = tail[0:1, s : s + 1]
        from_send = tail[0:1, SIDE + s : SIDE + s + 1]
        block = border[take * SIDE + s]
        turned = pay[pl.ds(width, bs), pl.ds(s * bs, bs)].T
        at = pl.multiple_of(rows[0, take * SIDE + s] * bs, bs)
        bt = pl.multiple_of(send[0, other * SIDE + s] * bs, bs)
        for c in range(width // bs):
            coup[pl.ds(at, bs), pl.ds(c * bs, bs)] += jnp.where(from_send == c, block, 0.0)
            coup[pl.ds(bt, bs), pl.ds(c * bs, bs)] += jnp.where(from_row == c, turned, 0.0)


def dot(a, b):
    return jnp.dot(a, b, precision=HP, preferred_element_type=F32)


def two_rows(first, second):
    line = lax.broadcasted_iota(jnp.int32, (TAIL, first.shape[1]), 0)
    return jnp.where(line == 0, first, jnp.where(line == 1, second, 0.0))


def half_kernel(weights, send, rows, takes, field, own, pair, mate, mate_pair, border, *refs):
    *pays, image, coup, sums = refs
    width = field.shape[0]
    here = field[...]
    coup[0] = pair[...] + mate_pair[...].T
    acc = dot(own[...], here) + dot(coup[0], mate[...])
    half = acc
    for n, pay in enumerate(pays):
        build_edge(coup.at[1 + n], takes[n], send, rows, border, pay)
        edge = dot(coup[1 + n], pay[pl.ds(0, width), :])
        acc += edge
        half += weights[n] * edge
    image[...] = acc
    norm = jnp.sum(here * here, axis=0, keepdims=True)
    sums[...] = two_rows(norm, jnp.sum(here * half, axis=0, keepdims=True))


def rest_kernel(first, send, rows, takes, part, border, *refs):
    *pays, image, coup = refs
    width = part.shape[0]
    acc = part[...]
    for n, pay in enumerate(pays):
        build_edge(coup, takes[first + n], send, rows, border, pay)
        acc += dot(coup[...], pay[pl.ds(0, width), :])
    image[...] = acc


def near_kernel(first, field, image, mate, mate_w, own, coup, sums):
    a = first[0:1, :] / first[1:2, :]
    res = field[...] - a * image[...]
    acc = dot(own[...], res) + dot(coup[0], mate[...] - a * mate_w[...])
    sums[...] = two_rows(jnp.sum(res * res, axis=0, keepdims=True), jnp.sum(res * acc, axis=0, keepdims=True))


def far_kernel(weights, first, near, field, image, coup, *refs):
    count = len(weights)
    pays, images, sums = refs[:count], refs[count : 2 * count], refs[2 * count]
    width = field.shape[0]
    a = first[0:1, :] / first[1:2, :]
    res = field[...] - a * image[...]
    acc = jnp.zeros(res.shape, F32)
    for n, weight in enumerate(weights):
        acc += dot(coup[1 + n], weight * (pays[n][pl.ds(0, width), :] - a * images[n][...]))
    sums[...] = near[...] + two_rows(jnp.zeros(a.shape, F32), jnp.sum(res * acc, axis=0, keepdims=True))


def shards(right_side, node_diag, local_coup, block_cols, border_coup, border_send, border_rows):
    width, ncols = right_side.shape
    nblocks, _, bs, _ = local_coup.shape
    n_gx, n_gy, n_nd = (lax.axis_size(a) for a in AXES)
    assert n_nd == 2 and border_coup.shape[1] == 4 * SIDE
    gyi = lax.axis_index("gy")
    swap = [(0, 1), (1, 0)]
    right = [(i, (i + 1) % n_gx) for i in range(n_gx)]
    left = [(j, i) for i, j in right]
    up = [(i, i + 1) for i in range(n_gy - 1)]
    down = [(j, i) for i, j in up]
    facing = jnp.where(gyi == 0, 3, 2)
    slots = [("gx", right, 0), ("gx", left, 1)]
    weights = [2.0]
    if n_gy == 2:
        slots.insert(0, ("gy", swap, facing))
        weights.insert(0, 1.0)
    elif n_gy > 2:
        slots.insert(0, ("gy", up, 2))
        slots.append(("gy", down, 3))
        weights.insert(0, 2.0)
    early = len(weights)
    takes = jnp.stack([jnp.asarray(t, jnp.int32) for _, _, t in slots])
    gives = jnp.stack([jnp.asarray(facing if t is facing else t ^ 1, jnp.int32) for _, _, t in slots])
    ndi = lax.axis_index("nd").astype(jnp.int32)
    border = border_coup[0]

    packed = pl.pallas_call(
        pack_kernel,
        name="pack",
        in_specs=[smem()] * 3 + [pl.BlockSpec(memory_space=pl.ANY)] * 2,
        out_specs=[vmem()] * len(slots),
        out_shape=[pltpu.VMEM((width + bs + TAIL, ncols), F32)] * len(slots),
        scratch_shapes=[pltpu.SemaphoreType.DMA((len(slots), SIDE + 1))],
        compiler_params=pltpu.CompilerParams(vmem_limit_bytes=LIMIT),
    )(border_send, border_rows, gives, *[pltpu.with_memory_space_constraint(a, pltpu.HBM) for a in (right_side, border)])
    pays = [lax.ppermute(pay, axis, perm) for pay, (axis, perm, _) in zip(packed, slots)]
    mate = lax.ppermute(right_side, "nd", swap)
    own, pair = call(prep_kernel, "prep", 2, [(width, width)] * 2, flops=1 << 24)(
        block_cols, ndi[None], packed[0], node_diag.reshape(1, width), local_coup
    )
    mate_pair = lax.ppermute(pair, "nd", swap)

    part, coup, first = call(partial(half_kernel, weights), "half", 3, [(width, ncols), (1 + early, width, width), (TAIL, ncols)])(
        border_send, border_rows, takes, right_side, own, pair, mate, mate_pair, border, *pays[:early]
    )
    first = axis_sum(first, AXES)
    (image,) = call(partial(rest_kernel, early), "rest", 3, [(width, ncols)], scratch=[pltpu.VMEM((width, width), F32)])(
        border_send, border_rows, takes, part, border, *pays[early:]
    )
    images = [lax.ppermute(image, axis, perm) for axis, perm, _ in slots[:early]]
    mate_w = lax.ppermute(image, "nd", swap)
    (near,) = call(near_kernel, "near", 0, [(TAIL, ncols)])(first, right_side, image, mate, mate_w, own, coup)
    (second,) = call(partial(far_kernel, weights), "far", 0, [(TAIL, ncols)])(
        first, near, right_side, image, coup, *pays[:early], *images
    )
    second = axis_sum(second, AXES)
    norm, curve = first[0:1], first[1:2]
    step = norm / curve
    ratio = second[0:1] / norm
    last = second[0:1] / (second[1:2] - ratio * ratio * curve)
    return (step + last * (1.0 + ratio)) * right_side - (last * step) * image


def solution(mesh):
    blocks = P(("var", "gx", "gy", "nd"))
    tables = P(AXES)
    in_specs = (blocks, blocks, blocks, tables, blocks, tables, tables)
    return jax.shard_map(shards, mesh=mesh, in_specs=in_specs, out_specs=blocks, check_vma=False)
```

time: 60.2 us -> 55.4 us (0.920)
  waiting for transfers between devices: 26.6 us -> 19.6 us
  starting transfers between devices: 20.7 us -> 24.6 us
  Pallas kernels: 8.76 us -> 7.39 us
  local copies, waits for them, and re-layouts: 3.56 us -> 2.53 us
  other arithmetic: 0.17 us -> 0.94 us
    ppermute x3, waiting for transfers between devices: 13.1 us -> 7.65 us  [shards(): lax.ppermute(pay, axis, perm)]
    ppermute x10 -> x12, starting transfers between devices: 11.2 us -> 15.2 us  [axis_sum(): lax.ppermute(part, axes, [(i, i ^ m) for i in range(count)])]
    ppermute x10 -> x12, waiting for transfers between devices: 12.4 us -> 10.8 us  [axis_sum(): lax.ppermute(part, axes, [(i, i ^ m) for i in range(count)])]
    pallas_call x4 -> x5, Pallas kernels: 7.06 us -> 5.53 us  [run(): pl.pallas_call(kernel, name=name, in_specs=[smem()] * tables + [vmem()] *...]
    unnamed x14, local copies, waits for them, and re-layouts: 3.56 us -> 2.53 us
    sub x0 -> x1, other arithmetic: none -> 0.74 us  [shards(): return (step + last * (1.0 + ratio)) * right_side - last * step * image]
  transfers between devices with their start and end apart: 18 -> 20, of which waited for: 10 -> 9; matrix products, arithmetic and copies ran while one was open for 0% -> 0% of each run, Pallas kernels for 2% -> 9%
where the time goes in v3:
time: 55.4 us; the launch traced here: 55.2 us
  starting transfers between devices  24.6 us (44%)
  waiting for transfers between devices  19.6 us (35%)
  Pallas kernels  7.39 us (13%)
  local copies, waits for them, and re-layouts  2.53 us (5%)
  other arithmetic  0.94 us (2%)
    ppermute x12, starting transfers between devices, axis_sum(): lax.ppermute(part, axes, [(i, i ^ m) for i in range(count)])  15.2 us
    ppermute x12, waiting for transfers between devices, axis_sum(): lax.ppermute(part, axes, [(i, i ^ m) for i in range(count)])  10.8 us
    ppermute x3, waiting for transfers between devices, shards(): lax.ppermute(pay, axis, perm)  7.65 us
    ppermute x3, starting transfers between devices, shards(): lax.ppermute(pay, axis, perm)  6.8 us
    pallas_call x5, Pallas kernels, run(): pl.pallas_call(kernel, name=name, in_specs=[smem()] * tables + [vmem()] *...  5.53 us
    unnamed x14, local copies, waits for them, and re-layouts  2.53 us
    ppermute x2, starting transfers between devices, shards(): lax.ppermute(image, axis, perm)  2.08 us
    pallas_call x1, Pallas kernels, shards(): pl.pallas_call(pack_kernel, name='pack', in_specs=[smem()] * 3 + [pl.Bloc...  1.86 us
  transfers between devices with their start and end apart: 20, of which 9 were waited for; matrix products, arithmetic and copies ran while one was open for 0% of the time, Pallas kernels for 9%

profile of v3, /device:TPU:0, one launch (start us, length us, event | category | flops | bytes accessed | tf_op | source)
XLA Modules:
  0.0 55.2 jit_solution(7348697370854209406)
XLA Ops:
  0.8 1.9 %pack.1 = (f32[392,256]{1,0:T(8,128)S(1)}, f32[392,256]{1,0:T(8,128)S(1)}, f32[392,256]{1,0:T(8,128)S(1)}) custom-call(s32[1,8]{1,0:T(1,128)S(1)} %copy-done.3, s32[1,8]{1,0:T(1,128)S(1)} %copy-done.4, s32[3]{0:T(128)S(1)} %pad_add_fusion.1.gives, f32[256,256]{1,0:T(8,128)} %field.7, f32[8,128,128]{2,1,0:T(8,128)} %bitcast.6), custom_call_target="tpu_custom_call" | custom-call | tf_op jit(solution)/shard_map/pack/pallas_call | solution.py:207
  2.6 3.1 %collective-permute-start.3 = (f32[392,256]{1,0:T(8,128)S(1)}, f32[392,256]{1,0:T(8,128)S(1)}, u32[]{:S(2)}, u32[]{:S(2)}) collective-permute-start(f32[392,256]{1,0:T(8,128)S(1)} %get-tuple-element.16), channel_id=1, source_target_pairs={{0,4},{4,8},{8,12},{12,0},{1,5},{5,9},{9,13},{13,1},{2,6},{6,10},{... | collective-permute-start | bytes 1204232 | tf_op jit(solution)/shard_map/ppermute | solution.py:216
  5.7 1.5 %collective-permute-start.2 = (f32[392,256]{1,0:T(8,128)S(1)}, f32[392,256]{1,0:T(8,128)S(1)}, u32[]{:S(2)}, u32[]{:S(2)}) collective-permute-start(f32[392,256]{1,0:T(8,128)S(1)} %get-tuple-element.13.packed), channel_id=1, source_target_pairs={{0,2},{2,0},{1,3},{3,1},{4,6},{6,4},{5,7},{7,5},{8,10},{10,8},{9,1... | collective-permute-start | bytes 1204232 | tf_op jit(solution)/shard_map/ppermute | solution.py:216
  7.2 2.2 %collective-permute-start.10 = (f32[392,256]{1,0:T(8,128)S(1)}, f32[392,256]{1,0:T(8,128)S(1)}, u32[]{:S(2)}, u32[]{:S(2)}) collective-permute-start(f32[392,256]{1,0:T(8,128)S(1)} %get-tuple-element.19), channel_id=1, source_target_pairs={{4,0},{8,4},{12,8},{0,12},{5,1},{9,5},{13,9},{1,13},{6,2},{10,6},{... | collective-permute-start | bytes 1204232 | tf_op jit(solution)/shard_map/ppermute | solution.py:216
  10.1 1.2 %copy-done.2 = f32[2,7,128,128]{3,2,1,0:T(8,128)S(1)} copy-done((f32[2,7,128,128]{3,2,1,0:T(8,128)S(1)}, f32[2,7,128,128]{3,2,1,0:T(8,128)}, u32[]{:S(2)}) %copy-start.2) | copy-done | bytes 917528
  11.3 1.1 %prep.1 = (f32[256,256]{1,0:T(8,128)S(1)}, f32[256,256]{1,0:T(8,128)S(1)}) custom-call(s32[2,7]{1,0:T(2,128)S(1)} %copy-done.5, s32[1]{0:T(128)} %bitcast.1.sides, f32[392,256]{1,0:T(8,128)S(1)} %get-tuple-element.13.packed, f32[1,256]{1,0:T(1,128)S(1)} %bitcast.9, f32[2,7,128,128]{3,2,1,0:T(8,128)S(1)} %copy-done.2), custom_call_target="tpu_custom_call" | custom-call | flops 16777216 | bytes 1048576 | tf_op jit(solution)/shard_map/prep/pallas_call | solution.py:29
  13.0 1.1 %collective-permute-done.1.mate_pair = f32[256,256]{1,0:T(8,128)S(1)} collective-permute-done((f32[256,256]{1,0:T(8,128)S(1)}, f32[256,256]{1,0:T(8,128)S(1)}, u32[]{:S(2)}, u32[]{:S(2)}) %collective-permute-start.1) | collective-permute-done | bytes 262176 | tf_op jit(solution)/shard_map/ppermute | solution.py:221
  14.1 3.8 %collective-permute-done.3.refs_1_ = f32[392,256]{1,0:T(8,128)S(1)} collective-permute-done((f32[392,256]{1,0:T(8,128)S(1)}, f32[392,256]{1,0:T(8,128)S(1)}, u32[]{:S(2)}, u32[]{:S(2)}) %collective-permute-start.3) | collective-permute-done | bytes 401440 | tf_op jit(solution)/shard_map/ppermute | solution.py:216
  17.9 1.9 %half.1 = (f32[256,256]{1,0:T(8,128)S(1)}, f32[3,256,256]{2,1,0:T(8,128)S(1)}, f32[8,256]{1,0:T(8,128)S(1)}) custom-call(s32[1,8]{1,0:T(1,128)S(1)} %copy-done.3, s32[1,8]{1,0:T(1,128)S(1)} %copy-done.4, s32[3]{0:T(128)S(1)} %pad_add_fusion.takes, f32[256,256]{1,0:T(8,128)S(1)} %copy-done, f32[256,256]{1,0:T(8,128)S(1)} %get-tuple-element.14.own, ...), custom_call_target="tpu_custom_call" | custom-call | tf_op jit(solution)/shard_map/half/pallas_call | solution.py:29
  19.9 1.8 %collective-permute-start.5 = (f32[8,256]{1,0:T(8,128)S(1)}, f32[8,256]{1,0:T(8,128)S(1)}, u32[]{:S(2)}, u32[]{:S(2)}) collective-permute-start(f32[8,256]{1,0:T(8,128)S(1)} %get-tuple-element.17), channel_id=1, source_target_pairs={{0,2},{1,3},{2,0},{3,1},{4,6},{5,7},{6,4},{7,5},{8,10},{9,11},{10,... | collective-permute-start | bytes 24584 | tf_op jit(solution)/shard_map/ppermute | solution.py:50
  21.7 3.9 %collective-permute-done.10.refs_0_ = f32[392,256]{1,0:T(8,128)S(1)} collective-permute-done((f32[392,256]{1,0:T(8,128)S(1)}, f32[392,256]{1,0:T(8,128)S(1)}, u32[]{:S(2)}, u32[]{:S(2)}) %collective-permute-start.10) | collective-permute-done | bytes 401440 | tf_op jit(solution)/shard_map/ppermute | solution.py:216
  25.6 1.1 %rest.1.image = f32[256,256]{1,0:T(8,128)S(1)} custom-call(s32[1,8]{1,0:T(1,128)S(1)} %copy-done.3, s32[1,8]{1,0:T(1,128)S(1)} %copy-done.4, s32[3]{0:T(128)S(1)} %pad_add_fusion.takes, f32[256,256]{1,0:T(8,128)S(1)} %get-tuple-element.18.part, f32[8,128,128]{2,1,0:T(8,128)S(1)} %bitcast.8, f32[392,256]{1,0:T(8,128)S(1)} %collective-permute-done.10.refs_0_), custom_call_target="tpu_custom_call" | custom-call | tf_op jit(solution)/shard_map/rest/pallas_call | solution.py:29
  27.3 1.5 %collective-permute-start.12 = (f32[256,256]{1,0:T(8,128)S(1)}, f32[256,256]{1,0:T(8,128)S(1)}, u32[]{:S(2)}, u32[]{:S(2)}) collective-permute-start(f32[256,256]{1,0:T(8,128)S(1)} %rest.1.image), channel_id=1, source_target_pairs={{0,2},{2,0},{1,3},{3,1},{4,6},{6,4},{5,7},{7,5},{8,10},{10,8},{9,1... | collective-permute-start | bytes 786440 | tf_op jit(solution)/shard_map/ppermute | solution.py:230
  28.8 5.2 %collective-permute-start.9 = (f32[8,256]{1,0:T(8,128)S(1)}, f32[8,256]{1,0:T(8,128)S(1)}, u32[]{:S(2)}, u32[]{:S(2)}) collective-permute-start(f32[8,256]{1,0:T(8,128)S(1)} %add_add_fusion.3), channel_id=1, source_target_pairs={{0,12},{1,13},{2,14},{3,15},{4,8},{5,9},{6,10},{7,11},{8,4},{9,5},... | collective-permute-start | bytes 24584 | tf_op jit(solution)/shard_map/ppermute | solution.py:50
  34.0 1.0 %collective-permute-start.8 = (f32[8,256]{1,0:T(8,128)S(1)}, f32[8,256]{1,0:T(8,128)S(1)}, u32[]{:S(2)}, u32[]{:S(2)}) collective-permute-start(f32[8,256]{1,0:T(8,128)S(1)} %add_add_fusion.3), channel_id=1, source_target_pairs={{0,8},{1,9},{2,10},{3,11},{4,12},{5,13},{6,14},{7,15},{8,0},{9,1},... | collective-permute-start | bytes 24584 | tf_op jit(solution)/shard_map/ppermute | solution.py:50
  34.9 4.4 %collective-permute-done.9 = f32[8,256]{1,0:T(8,128)S(1)} collective-permute-done((f32[8,256]{1,0:T(8,128)S(1)}, f32[8,256]{1,0:T(8,128)S(1)}, u32[]{:S(2)}, u32[]{:S(2)}) %collective-permute-start.9) | collective-permute-done | bytes 8224 | tf_op jit(solution)/shard_map/ppermute | solution.py:50
  39.4 0.8 %collective-permute-start.7 = (f32[8,256]{1,0:T(8,128)S(1)}, f32[8,256]{1,0:T(8,128)S(1)}, u32[]{:S(2)}, u32[]{:S(2)}) collective-permute-start(f32[8,256]{1,0:T(8,128)S(1)} %add_add_fusion.3), channel_id=1, source_target_pairs={{0,4},{1,5},{2,6},{3,7},{4,0},{5,1},{6,2},{7,3},{8,12},{9,13},{10,... | collective-permute-start | bytes 24584 | tf_op jit(solution)/shard_map/ppermute | solution.py:50
  40.1 2.9 %collective-permute-done.7 = f32[8,256]{1,0:T(8,128)S(1)} collective-permute-done((f32[8,256]{1,0:T(8,128)S(1)}, f32[8,256]{1,0:T(8,128)S(1)}, u32[]{:S(2)}, u32[]{:S(2)}) %collective-permute-start.7) | collective-permute-done | bytes 8224 | tf_op jit(solution)/shard_map/ppermute | solution.py:50
  44.6 1.3 %collective-permute-start.15 = (f32[8,256]{1,0:T(8,128)S(1)}, f32[8,256]{1,0:T(8,128)S(1)}, u32[]{:S(2)}, u32[]{:S(2)}) collective-permute-start(f32[8,256]{1,0:T(8,128)S(1)} %far.1), channel_id=1, source_target_pairs={{0,2},{1,3},{2,0},{3,1},{4,6},{5,7},{6,4},{7,5},{8,10},{9,11},{10,... | collective-permute-start | bytes 24584 | tf_op jit(solution)/shard_map/ppermute | solution.py:50
  46.5 1.2 %collective-permute-done.16 = f32[8,256]{1,0:T(8,128)S(1)} collective-permute-done((f32[8,256]{1,0:T(8,128)S(1)}, f32[8,256]{1,0:T(8,128)S(1)}, u32[]{:S(2)}, u32[]{:S(2)}) %collective-permute-start.16) | collective-permute-done | bytes 8224 | tf_op jit(solution)/shard_map/ppermute | solution.py:50
  48.8 1.8 %collective-permute-start.18 = (f32[8,256]{1,0:T(8,128)S(1)}, f32[8,256]{1,0:T(8,128)S(1)}, u32[]{:S(2)}, u32[]{:S(2)}) collective-permute-start(f32[8,256]{1,0:T(8,128)S(1)} %add_add_fusion.1), channel_id=1, source_target_pairs={{0,8},{1,9},{2,10},{3,11},{4,12},{5,13},{6,14},{7,15},{8,0},{9,1},... | collective-permute-start | bytes 24584 | tf_op jit(solution)/shard_map/ppermute | solution.py:50
  50.6 2.2 %collective-permute-start.17 = (f32[8,256]{1,0:T(8,128)S(1)}, f32[8,256]{1,0:T(8,128)S(1)}, u32[]{:S(2)}, u32[]{:S(2)}) collective-permute-start(f32[8,256]{1,0:T(8,128)S(1)} %add_add_fusion.1), channel_id=1, source_target_pairs={{0,4},{1,5},{2,6},{3,7},{4,0},{5,1},{6,2},{7,3},{8,12},{9,13},{10,... | collective-permute-start | bytes 24584 | tf_op jit(solution)/shard_map/ppermute | solution.py:50
  52.8 1.1 %collective-permute-done.19 = f32[8,256]{1,0:T(8,128)S(1)} collective-permute-done((f32[8,256]{1,0:T(8,128)S(1)}, f32[8,256]{1,0:T(8,128)S(1)}, u32[]{:S(2)}, u32[]{:S(2)}) %collective-permute-start.19) | collective-permute-done | bytes 8224 | tf_op jit(solution)/shard_map/ppermute | solution.py:50
  54.5 0.7 %multiply_subtract_fusion = f32[256,256]{1,0:T(8,128)} fusion(f32[256,256]{1,0:T(8,128)S(1)} %rest.1.image, f32[256,256]{1,0:T(8,128)S(1)} %copy-done, f32[256]{0:T(256)S(1)} %bitcast.11, f32[256]{0:T(256)S(1)} %bitcast.10), kind=kLoop, calls=%fused_computation | loop fusion | flops 196608 | bytes 788480 | tf_op jit(solution)/shard_map/sub | solution.py:241
  (45 shorter events, 6.7 us)
Async XLA Ops:
  0.7 8.7 %copy-start = (f32[256,256]{1,0:T(8,128)S(1)}, f32[256,256]{1,0:T(8,128)}, u32[]{:S(2)}) copy-start(f32[256,256]{1,0:T(8,128)} %field.7) | copy-start | bytes 786436
  2.6 15.3 %collective-permute-start.3 = (f32[392,256]{1,0:T(8,128)S(1)}, f32[392,256]{1,0:T(8,128)S(1)}, u32[]{:S(2)}, u32[]{:S(2)}) collective-permute-start(f32[392,256]{1,0:T(8,128)S(1)} %get-tuple-element.16), channel_id=1, source_target_pairs={{0,4},{4,8},{8,12},{12,0},{1,5},{5,9},{9,13},{13,1},{2,6},{6,10},{... | collective-permute-start | bytes 1204232 | tf_op jit(solution)/shard_map/ppermute | solution.py:216
  5.7 3.7 %copy-start.6 = (f32[256]{0:T(256)S(1)}, f32[256]{0:T(256)}, u32[]{:S(2)}) copy-start(f32[256]{0:T(256)} %param.8) | copy-start | bytes 3076
  5.7 12.2 %collective-permute-start.2 = (f32[392,256]{1,0:T(8,128)S(1)}, f32[392,256]{1,0:T(8,128)S(1)}, u32[]{:S(2)}, u32[]{:S(2)}) collective-permute-start(f32[392,256]{1,0:T(8,128)S(1)} %get-tuple-element.13.packed), channel_id=1, source_target_pairs={{0,2},{2,0},{1,3},{3,1},{4,6},{6,4},{5,7},{7,5},{8,10},{10,8},{9,1... | collective-permute-start | bytes 1204232 | tf_op jit(solution)/shard_map/ppermute | solution.py:216
  7.2 18.4 %collective-permute-start.10 = (f32[392,256]{1,0:T(8,128)S(1)}, f32[392,256]{1,0:T(8,128)S(1)}, u32[]{:S(2)}, u32[]{:S(2)}) collective-permute-start(f32[392,256]{1,0:T(8,128)S(1)} %get-tuple-element.19), channel_id=1, source_target_pairs={{4,0},{8,4},{12,8},{0,12},{5,1},{9,5},{13,9},{1,13},{6,2},{10,6},{... | collective-permute-start | bytes 1204232 | tf_op jit(solution)/shard_map/ppermute | solution.py:216
  9.4 3.6 %collective-permute-start = (f32[256,256]{1,0:T(8,128)S(1)}, f32[256,256]{1,0:T(8,128)S(1)}, u32[]{:S(2)}, u32[]{:S(2)}) collective-permute-start(f32[256,256]{1,0:T(8,128)S(1)} %copy-done), channel_id=1, source_target_pairs={{0,1},{1,0},{2,3},{3,2},{4,5},{5,4},{6,7},{7,6},{8,9},{9,8},{10,11... | collective-permute-start | bytes 786440 | tf_op jit(solution)/shard_map/ppermute | solution.py:217
  10.1 1.2 %copy-start.2 = (f32[2,7,128,128]{3,2,1,0:T(8,128)S(1)}, f32[2,7,128,128]{3,2,1,0:T(8,128)}, u32[]{:S(2)}) copy-start(f32[2,7,128,128]{3,2,1,0:T(8,128)} %local.1) | copy-start | bytes 2752516
  11.3 6.6 %copy-start.1 = (f32[1,8,128,128]{3,2,1,0:T(8,128)S(1)}, f32[1,8,128,128]{3,2,1,0:T(8,128)}, u32[]{:S(2)}) copy-start(f32[1,8,128,128]{3,2,1,0:T(8,128)} %param.11) | copy-start | bytes 1572868
  12.4 1.7 %collective-permute-start.1 = (f32[256,256]{1,0:T(8,128)S(1)}, f32[256,256]{1,0:T(8,128)S(1)}, u32[]{:S(2)}, u32[]{:S(2)}) collective-permute-start(f32[256,256]{1,0:T(8,128)S(1)} %get-tuple-element.15.pair), channel_id=1, source_target_pairs={{0,1},{1,0},{2,3},{3,2},{4,5},{5,4},{6,7},{7,6},{8,9},{9,8},{10,11... | collective-permute-start | bytes 786440 | tf_op jit(solution)/shard_map/ppermute | solution.py:221
  19.8 9.0 %collective-permute-start.6 = (f32[8,256]{1,0:T(8,128)S(1)}, f32[8,256]{1,0:T(8,128)S(1)}, u32[]{:S(2)}, u32[]{:S(2)}) collective-permute-start(f32[8,256]{1,0:T(8,128)S(1)} %get-tuple-element.17), channel_id=1, source_target_pairs={{0,3},{1,2},{2,1},{3,0},{4,7},{5,6},{6,5},{7,4},{8,11},{9,10},{10,... | collective-permute-start | bytes 24584 | tf_op jit(solution)/shard_map/ppermute | solution.py:50
  19.9 8.9 %collective-permute-start.5 = (f32[8,256]{1,0:T(8,128)S(1)}, f32[8,256]{1,0:T(8,128)S(1)}, u32[]{:S(2)}, u32[]{:S(2)}) collective-permute-start(f32[8,256]{1,0:T(8,128)S(1)} %get-tuple-element.17), channel_id=1, source_target_pairs={{0,2},{1,3},{2,0},{3,1},{4,6},{5,7},{6,4},{7,5},{8,10},{9,11},{10,... | collective-permute-start | bytes 24584 | tf_op jit(solution)/shard_map/ppermute | solution.py:50
  21.7 7.2 %collective-permute-start.4 = (f32[8,256]{1,0:T(8,128)S(1)}, f32[8,256]{1,0:T(8,128)S(1)}, u32[]{:S(2)}, u32[]{:S(2)}) collective-permute-start(f32[8,256]{1,0:T(8,128)S(1)} %get-tuple-element.17), channel_id=1, source_target_pairs={{0,1},{1,0},{2,3},{3,2},{4,5},{5,4},{6,7},{7,6},{8,9},{9,8},{10,11... | collective-permute-start | bytes 24584 | tf_op jit(solution)/shard_map/ppermute | solution.py:50
  26.7 17.1 %collective-permute-start.13 = (f32[256,256]{1,0:T(8,128)S(1)}, f32[256,256]{1,0:T(8,128)S(1)}, u32[]{:S(2)}, u32[]{:S(2)}) collective-permute-start(f32[256,256]{1,0:T(8,128)S(1)} %rest.1.image), channel_id=1, source_target_pairs={{0,4},{4,8},{8,12},{12,0},{1,5},{5,9},{9,13},{13,1},{2,6},{6,10},{... | collective-permute-start | bytes 786440 | tf_op jit(solution)/shard_map/ppermute | solution.py:230
  27.3 16.5 %collective-permute-start.12 = (f32[256,256]{1,0:T(8,128)S(1)}, f32[256,256]{1,0:T(8,128)S(1)}, u32[]{:S(2)}, u32[]{:S(2)}) collective-permute-start(f32[256,256]{1,0:T(8,128)S(1)} %rest.1.image), channel_id=1, source_target_pairs={{0,2},{2,0},{1,3},{3,1},{4,6},{6,4},{5,7},{7,5},{8,10},{10,8},{9,1... | collective-permute-start | bytes 786440 | tf_op jit(solution)/shard_map/ppermute | solution.py:230
  28.8 14.2 %collective-permute-start.11 = (f32[256,256]{1,0:T(8,128)S(1)}, f32[256,256]{1,0:T(8,128)S(1)}, u32[]{:S(2)}, u32[]{:S(2)}) collective-permute-start(f32[256,256]{1,0:T(8,128)S(1)} %rest.1.image), channel_id=1, source_target_pairs={{0,1},{1,0},{2,3},{3,2},{4,5},{5,4},{6,7},{7,6},{8,9},{9,8},{10,11... | collective-permute-start | bytes 786440 | tf_op jit(solution)/shard_map/ppermute | solution.py:231
  28.8 10.5 %collective-permute-start.9 = (f32[8,256]{1,0:T(8,128)S(1)}, f32[8,256]{1,0:T(8,128)S(1)}, u32[]{:S(2)}, u32[]{:S(2)}) collective-permute-start(f32[8,256]{1,0:T(8,128)S(1)} %add_add_fusion.3), channel_id=1, source_target_pairs={{0,12},{1,13},{2,14},{3,15},{4,8},{5,9},{6,10},{7,11},{8,4},{9,5},... | collective-permute-start | bytes 24584 | tf_op jit(solution)/shard_map/ppermute | solution.py:50
  34.0 6.2 %collective-permute-start.8 = (f32[8,256]{1,0:T(8,128)S(1)}, f32[8,256]{1,0:T(8,128)S(1)}, u32[]{:S(2)}, u32[]{:S(2)}) collective-permute-start(f32[8,256]{1,0:T(8,128)S(1)} %add_add_fusion.3), channel_id=1, source_target_pairs={{0,8},{1,9},{2,10},{3,11},{4,12},{5,13},{6,14},{7,15},{8,0},{9,1},... | collective-permute-start | bytes 24584 | tf_op jit(solution)/shard_map/ppermute | solution.py:50
  39.4 3.7 %collective-permute-start.7 = (f32[8,256]{1,0:T(8,128)S(1)}, f32[8,256]{1,0:T(8,128)S(1)}, u32[]{:S(2)}, u32[]{:S(2)}) collective-permute-start(f32[8,256]{1,0:T(8,128)S(1)} %add_add_fusion.3), channel_id=1, source_target_pairs={{0,4},{1,5},{2,6},{3,7},{4,0},{5,1},{6,2},{7,3},{8,12},{9,13},{10,... | collective-permute-start | bytes 24584 | tf_op jit(solution)/shard_map/ppermute | solution.py:50
  44.5 3.1 %collective-permute-start.16 = (f32[8,256]{1,0:T(8,128)S(1)}, f32[8,256]{1,0:T(8,128)S(1)}, u32[]{:S(2)}, u32[]{:S(2)}) collective-permute-start(f32[8,256]{1,0:T(8,128)S(1)} %far.1), channel_id=1, source_target_pairs={{0,3},{1,2},{2,1},{3,0},{4,7},{5,6},{6,5},{7,4},{8,11},{9,10},{10,... | collective-permute-start | bytes 24584 | tf_op jit(solution)/shard_map/ppermute | solution.py:50
  44.6 3.7 %collective-permute-start.15 = (f32[8,256]{1,0:T(8,128)S(1)}, f32[8,256]{1,0:T(8,128)S(1)}, u32[]{:S(2)}, u32[]{:S(2)}) collective-permute-start(f32[8,256]{1,0:T(8,128)S(1)} %far.1), channel_id=1, source_target_pairs={{0,2},{1,3},{2,0},{3,1},{4,6},{5,7},{6,4},{7,5},{8,10},{9,11},{10,... | collective-permute-start | bytes 24584 | tf_op jit(solution)/shard_map/ppermute | solution.py:50
  45.9 2.4 %collective-permute-start.14 = (f32[8,256]{1,0:T(8,128)S(1)}, f32[8,256]{1,0:T(8,128)S(1)}, u32[]{:S(2)}, u32[]{:S(2)}) collective-permute-start(f32[8,256]{1,0:T(8,128)S(1)} %far.1), channel_id=1, source_target_pairs={{0,1},{1,0},{2,3},{3,2},{4,5},{5,4},{6,7},{7,6},{8,9},{9,8},{10,11... | collective-permute-start | bytes 24584 | tf_op jit(solution)/shard_map/ppermute | solution.py:50
  48.3 5.5 %collective-permute-start.19 = (f32[8,256]{1,0:T(8,128)S(1)}, f32[8,256]{1,0:T(8,128)S(1)}, u32[]{:S(2)}, u32[]{:S(2)}) collective-permute-start(f32[8,256]{1,0:T(8,128)S(1)} %add_add_fusion.1), channel_id=1, source_target_pairs={{0,12},{1,13},{2,14},{3,15},{4,8},{5,9},{6,10},{7,11},{8,4},{9,5},... | collective-permute-start | bytes 24584 | tf_op jit(solution)/shard_map/ppermute | solution.py:50
  48.8 5.0 %collective-permute-start.18 = (f32[8,256]{1,0:T(8,128)S(1)}, f32[8,256]{1,0:T(8,128)S(1)}, u32[]{:S(2)}, u32[]{:S(2)}) collective-permute-start(f32[8,256]{1,0:T(8,128)S(1)} %add_add_fusion.1), channel_id=1, source_target_pairs={{0,8},{1,9},{2,10},{3,11},{4,12},{5,13},{6,14},{7,15},{8,0},{9,1},... | collective-permute-start | bytes 24584 | tf_op jit(solution)/shard_map/ppermute | solution.py:50
  50.6 3.8 %collective-permute-start.17 = (f32[8,256]{1,0:T(8,128)S(1)}, f32[8,256]{1,0:T(8,128)S(1)}, u32[]{:S(2)}, u32[]{:S(2)}) collective-permute-start(f32[8,256]{1,0:T(8,128)S(1)} %add_add_fusion.1), channel_id=1, source_target_pairs={{0,4},{1,5},{2,6},{3,7},{4,0},{5,1},{6,2},{7,3},{8,12},{9,13},{10,... | collective-permute-start | bytes 24584 | tf_op jit(solution)/shard_map/ppermute | solution.py:50
  (3 other events, 2.0 us)

commit v4 on v3

--- a/solution.py
+++ b/solution.py
@@ -52,7 +52,35 @@
     return part
 
 
-def prep_kernel(cols, sides, packed, diag, local, own, pair):
+def write_tail(pay, give, send, rows, width, bs):
+    lane = lax.broadcasted_iota(jnp.int32, (TAIL, SIDE * bs), 1)
+    tail = jnp.zeros(lane.shape, F32)
+    for s in range(SIDE):
+        tail = jnp.where(lane == s, rows[0, give * SIDE + s].astype(F32), tail)
+        sent = send[0, (give ^ 1) * SIDE + s].astype(F32)
+        tail = jnp.where(lane == SIDE + s, sent, tail)
+    pay[pl.ds(width + bs, TAIL), :] = tail
+
+
+def pack_kernel(send, rows, gives, field, border, *refs):
+    *pays, sems = refs
+    width = field.shape[0]
+    bs = border.shape[1]
+    copies = []
+    for n, pay in enumerate(pays):
+        copies.append(pltpu.make_async_copy(field, pay.at[pl.ds(0, width), :], sems.at[n, SIDE]))
+        for s in range(SIDE):
+            block = pay.at[pl.ds(width, bs), pl.ds(s * bs, bs)]
+            copies.append(pltpu.make_async_copy(border.at[gives[n] * SIDE + s], block, sems.at[n, s]))
+    for copy in copies:
+        copy.start()
+    for n, pay in enumerate(pays):
+        write_tail(pay, gives[n], send, rows, width, bs)
+    for copy in copies:
+        copy.wait()
+
+
+def prep_kernel(first, cols, sides, send, rows, gives, packed, diag, local, border, own, pair, *pays):
     nblocks, nonzeros, bs, _ = local.shape
     width = nblocks * bs
     patch_len = 2 * nblocks
@@ -77,31 +105,12 @@
     here = lax.broadcasted_iota(jnp.int32, (width, width), 0)
     there = lax.broadcasted_iota(jnp.int32, (width, width), 1)
     own[...] = lower + lower.T + jnp.where(here == there, diag[...], 0.0)
-
-
-def pack_kernel(send, rows, gives, field, border, *refs):
-    *pays, sems = refs
-    width = field.shape[0]
-    bs = border.shape[1]
-    copies = []
-    for n, pay in enumerate(pays):
-        copies.append(pltpu.make_async_copy(field, pay.at[pl.ds(0, width), :], sems.at[n, SIDE]))
+    for n, pay in enumerate(pays):
+        give = gives[first + n]
+        pay[pl.ds(0, width), :] = packed[pl.ds(0, width), :]
         for s in range(SIDE):
-            block = pay.at[pl.ds(width, bs), pl.ds(s * bs, bs)]
-            copies.append(pltpu.make_async_copy(border.at[gives[n] * SIDE + s], block, sems.at[n, s]))
-    for copy in copies:
-        copy.start()
-    lane = lax.broadcasted_iota(jnp.int32, (TAIL, SIDE * bs), 1)
-    for n, pay in enumerate(pays):
-        give = gives[n]
-        tail = jnp.zeros(lane.shape, F32)
-        for s in range(SIDE):
-            tail = jnp.where(lane == s, rows[0, give * SIDE + s].astype(F32), tail)
-            sent = send[0, (give ^ 1) * SIDE + s].astype(F32)
-            tail = jnp.where(lane == SIDE + s, sent, tail)
-        pay[pl.ds(width + bs, TAIL), :] = tail
-    for copy in copies:
-        copy.wait()
+            pay[pl.ds(width, bs), pl.ds(s * bs, bs)] = border[give * SIDE + s]
+        write_tail(pay, give, send, rows, width, bs)
 
 
 def build_edge(coup, take, send, rows, border, pay):
@@ -148,33 +157,33 @@
     sums[...] = two_rows(norm, jnp.sum(here * half, axis=0, keepdims=True))
 
 
-def rest_kernel(first, send, rows, takes, part, border, *refs):
+def rest_kernel(skip, send, rows, takes, part, border, *refs):
     *pays, image, coup = refs
     width = part.shape[0]
     acc = part[...]
     for n, pay in enumerate(pays):
-        build_edge(coup, takes[first + n], send, rows, border, pay)
+        build_edge(coup, takes[skip + n], send, rows, border, pay)
         acc += dot(coup[...], pay[pl.ds(0, width), :])
     image[...] = acc
 
 
-def near_kernel(first, field, image, mate, mate_w, own, coup, sums):
-    a = first[0:1, :] / first[1:2, :]
-    res = field[...] - a * image[...]
-    acc = dot(own[...], res) + dot(coup[0], mate[...] - a * mate_w[...])
-    sums[...] = two_rows(jnp.sum(res * res, axis=0, keepdims=True), jnp.sum(res * acc, axis=0, keepdims=True))
-
-
-def far_kernel(weights, first, near, field, image, coup, *refs):
-    count = len(weights)
-    pays, images, sums = refs[:count], refs[count : 2 * count], refs[2 * count]
-    width = field.shape[0]
-    a = first[0:1, :] / first[1:2, :]
-    res = field[...] - a * image[...]
+def step_kernel(first, field, image, res):
+    res[...] = field[...] - first[0:1, :] / first[1:2, :] * image[...]
+
+
+def near_kernel(res, mate_r, own, coup, sums):
+    here = res[...]
+    acc = dot(own[...], here) + dot(coup[0], mate_r[...])
+    sums[...] = two_rows(jnp.sum(here * here, axis=0, keepdims=True), jnp.sum(here * acc, axis=0, keepdims=True))
+
+
+def far_kernel(weights, near, res, coup, *refs):
+    *far, sums = refs
     acc = jnp.zeros(res.shape, F32)
     for n, weight in enumerate(weights):
-        acc += dot(coup[1 + n], weight * (pays[n][pl.ds(0, width), :] - a * images[n][...]))
-    sums[...] = near[...] + two_rows(jnp.zeros(a.shape, F32), jnp.sum(res * acc, axis=0, keepdims=True))
+        acc += weight * dot(coup[1 + n], far[n][...])
+    edges = jnp.sum(res[...] * acc, axis=0, keepdims=True)
+    sums[...] = near[...] + two_rows(jnp.zeros(edges.shape, F32), edges)
 
 
 def shards(right_side, node_diag, local_coup, block_cols, border_coup, border_send, border_rows):
@@ -204,20 +213,22 @@
     ndi = lax.axis_index("nd").astype(jnp.int32)
     border = border_coup[0]
 
+    pay_shape = (width + bs + TAIL, ncols)
     packed = pl.pallas_call(
         pack_kernel,
         name="pack",
         in_specs=[smem()] * 3 + [pl.BlockSpec(memory_space=pl.ANY)] * 2,
-        out_specs=[vmem()] * len(slots),
-        out_shape=[pltpu.VMEM((width + bs + TAIL, ncols), F32)] * len(slots),
-        scratch_shapes=[pltpu.SemaphoreType.DMA((len(slots), SIDE + 1))],
+        out_specs=[vmem()] * early,
+        out_shape=[pltpu.VMEM(pay_shape, F32)] * early,
+        scratch_shapes=[pltpu.SemaphoreType.DMA((early, SIDE + 1))],
         compiler_params=pltpu.CompilerParams(vmem_limit_bytes=LIMIT),
     )(border_send, border_rows, gives, *[pltpu.with_memory_space_constraint(a, pltpu.HBM) for a in (right_side, border)])
-    pays = [lax.ppermute(pay, axis, perm) for pay, (axis, perm, _) in zip(packed, slots)]
     mate = lax.ppermute(right_side, "nd", swap)
-    own, pair = call(prep_kernel, "prep", 2, [(width, width)] * 2, flops=1 << 24)(
-        block_cols, ndi[None], packed[0], node_diag.reshape(1, width), local_coup
+    late = len(slots) - early
+    own, pair, *rest = call(partial(prep_kernel, early), "prep", 5, [(width, width)] * 2 + [pay_shape] * late, flops=1 << 24)(
+        block_cols, ndi[None], border_send, border_rows, gives, packed[0], node_diag.reshape(1, width), local_coup, border
     )
+    pays = [lax.ppermute(pay, axis, perm) for pay, (axis, perm, _) in zip([*packed, *rest], slots)]
     mate_pair = lax.ppermute(pair, "nd", swap)
 
     part, coup, first = call(partial(half_kernel, weights), "half", 3, [(width, ncols), (1 + early, width, width), (TAIL, ncols)])(
@@ -227,18 +238,16 @@
     (image,) = call(partial(rest_kernel, early), "rest", 3, [(width, ncols)], scratch=[pltpu.VMEM((width, width), F32)])(
         border_send, border_rows, takes, part, border, *pays[early:]
     )
-    images = [lax.ppermute(image, axis, perm) for axis, perm, _ in slots[:early]]
-    mate_w = lax.ppermute(image, "nd", swap)
-    (near,) = call(near_kernel, "near", 0, [(TAIL, ncols)])(first, right_side, image, mate, mate_w, own, coup)
-    (second,) = call(partial(far_kernel, weights), "far", 0, [(TAIL, ncols)])(
-        first, near, right_side, image, coup, *pays[:early], *images
-    )
+    (res,) = call(step_kernel, "step", 0, [(width, ncols)])(first, right_side, image)
+    far = [lax.ppermute(res, axis, perm) for axis, perm, _ in slots[:early]]
+    mate_r = lax.ppermute(res, "nd", swap)
+    (near,) = call(near_kernel, "near", 0, [(TAIL, ncols)])(res, mate_r, own, coup)
+    (second,) = call(partial(far_kernel, weights), "far", 0, [(TAIL, ncols)])(near, res, coup, *far)
     second = axis_sum(second, AXES)
     norm, curve = first[0:1], first[1:2]
-    step = norm / curve
     ratio = second[0:1] / norm
     last = second[0:1] / (second[1:2] - ratio * ratio * curve)
-    return (step + last * (1.0 + ratio)) * right_side - (last * step) * image
+    return (norm / curve + last * ratio) * right_side + last * res
 
 
 def solution(mesh):

time: 55.4 us -> 61.1 us (1.10)
  starting transfers between devices: 24.6 us -> 27.6 us
  waiting for transfers between devices: 19.6 us -> 21.9 us
  local copies, waits for them, and re-layouts: 2.53 us -> 3.19 us
    ppermute x3, waiting for transfers between devices: 0.01 us -> 8.2 us  [the longest x2 8.2 us: shards(): far = [lax.ppermute(res, axis, perm) for axis, perm, _ in slots[:early]]]
    ppermute x12, starting transfers between devices: 15.2 us -> 18.5 us  [axis_sum(): lax.ppermute(part, axes, [(i, i ^ m) for i in range(count)])]
    ppermute x3, waiting for transfers between devices: 7.65 us -> 4.81 us  [shards(): lax.ppermute(pay, axis, perm)]
    ppermute x12, waiting for transfers between devices: 10.8 us -> 8.83 us  [axis_sum(): lax.ppermute(part, axes, [(i, i ^ m) for i in range(count)])]
    ppermute x1, waiting for transfers between devices: 1.08 us -> 0.01 us  [shards(): mate_pair = lax.ppermute(pair, 'nd', swap)]
    add x1 -> x2, other arithmetic: 0.02 us -> 0.76 us  [shards(): return (norm / curve + last * ratio) * right_side + last * res]
    sub x1 -> x0, other arithmetic: 0.74 us -> none  [shards(): return (step + last * (1.0 + ratio)) * right_side - last * step * image]
    unnamed x14 -> x18, local copies, waits for them, and re-layouts: 2.53 us -> 3.19 us
  transfers between devices with their start and end apart: 20 -> 20, of which waited for: 9 -> 10; matrix products, arithmetic and copies ran while one was open for 0% -> 0% of each run, Pallas kernels for 9% -> 8%
where the time goes in v4:
time: 61.1 us; the launch traced here: 60.9 us
  starting transfers between devices  27.6 us (45%)
  waiting for transfers between devices  21.9 us (36%)
  Pallas kernels  7.18 us (12%)
  local copies, waits for them, and re-layouts  3.19 us (5%)
  other arithmetic  0.93 us (2%)
    ppermute x12, starting transfers between devices, axis_sum(): lax.ppermute(part, axes, [(i, i ^ m) for i in range(count)])  18.5 us
    ppermute x12, waiting for transfers between devices, axis_sum(): lax.ppermute(part, axes, [(i, i ^ m) for i in range(count)])  8.83 us
    ppermute x2, waiting for transfers between devices, shards(): far = [lax.ppermute(res, axis, perm) for axis, perm, _ in slots[:early]]  8.2 us
    ppermute x3, starting transfers between devices, shards(): lax.ppermute(pay, axis, perm)  6.82 us
    pallas_call x6, Pallas kernels, run(): pl.pallas_call(kernel, name=name, in_specs=[smem()] * tables + [vmem()] *...  5.48 us
    ppermute x3, waiting for transfers between devices, shards(): lax.ppermute(pay, axis, perm)  4.81 us
    unnamed x18, local copies, waits for them, and re-layouts  3.19 us
    pallas_call x1, Pallas kernels, shards(): pl.pallas_call(pack_kernel, name='pack', in_specs=[smem()] * 3 + [pl.Bloc...  1.7 us
  transfers between devices with their start and end apart: 20, of which 10 were waited for; matrix products, arithmetic and copies ran while one was open for 0% of the time, Pallas kernels for 8%

profile of v4, /device:TPU:0, one launch (start us, length us, event | category | flops | bytes accessed | tf_op | source)
XLA Modules:
  0.0 60.9 jit_solution(13677581718263499958)
XLA Ops:
  0.1 0.7 %copy-done.3 = s32[1,8]{1,0:T(1,128)S(1)} copy-done((s32[1,8]{1,0:T(1,128)S(1)}, s32[1,8]{1,0:T(1,128)}, u32[]{:S(2)}) %copy-start.3) | copy-done | bytes 56
  1.4 1.7 %pack.1 = (f32[392,256]{1,0:T(8,128)S(1)}, f32[392,256]{1,0:T(8,128)S(1)}) custom-call(s32[1,8]{1,0:T(1,128)S(1)} %copy-done.3, s32[1,8]{1,0:T(1,128)S(1)} %copy-done.5, s32[3]{0:T(128)S(1)} %pad_add_fusion.1.gives, f32[256,256]{1,0:T(8,128)} %field.5, f32[8,128,128]{2,1,0:T(8,128)} %bitcast.6), custom_call_target="tpu_custom_call" | custom-call | tf_op jit(solution)/shard_map/pack/pallas_call | solution.py:217
  3.2 3.1 %collective-permute-start.3 = (f32[392,256]{1,0:T(8,128)S(1)}, f32[392,256]{1,0:T(8,128)S(1)}, u32[]{:S(2)}, u32[]{:S(2)}) collective-permute-start(f32[392,256]{1,0:T(8,128)S(1)} %get-tuple-element.16), channel_id=1, source_target_pairs={{0,4},{4,8},{8,12},{12,0},{1,5},{5,9},{9,13},{13,1},{2,6},{6,10},{... | collective-permute-start | bytes 1204232 | tf_op jit(solution)/shard_map/ppermute | solution.py:231
  6.2 1.5 %collective-permute-start.2 = (f32[392,256]{1,0:T(8,128)S(1)}, f32[392,256]{1,0:T(8,128)S(1)}, u32[]{:S(2)}, u32[]{:S(2)}) collective-permute-start(f32[392,256]{1,0:T(8,128)S(1)} %get-tuple-element.13.packed), channel_id=1, source_target_pairs={{0,2},{2,0},{1,3},{3,1},{4,6},{6,4},{5,7},{7,5},{8,10},{10,8},{9,1... | collective-permute-start | bytes 1204232 | tf_op jit(solution)/shard_map/ppermute | solution.py:231
  8.4 1.2 %copy-done.2 = f32[2,7,128,128]{3,2,1,0:T(8,128)S(1)} copy-done((f32[2,7,128,128]{3,2,1,0:T(8,128)S(1)}, f32[2,7,128,128]{3,2,1,0:T(8,128)}, u32[]{:S(2)}) %copy-start.2) | copy-done | bytes 917528
  9.6 1.1 %prep.1 = (f32[256,256]{1,0:T(8,128)S(1)}, f32[256,256]{1,0:T(8,128)S(1)}, f32[392,256]{1,0:T(8,128)S(1)}) custom-call(s32[2,7]{1,0:T(2,128)S(1)} %copy-done.7, s32[1]{0:T(128)} %bitcast.1.sides, s32[1,8]{1,0:T(1,128)S(1)} %copy-done.4, s32[1,8]{1,0:T(1,128)S(1)} %copy-done.6, s32[3]{0:T(128)S(1)} %pad_add_fusion.1.gives, ...), custom_call_target="tpu_custom_call" | custom-call | flops 16777216 | bytes 1048576 | tf_op jit(solution)/shard_map/prep/pallas_call | solution.py:29
  11.3 2.2 %collective-permute-start.10 = (f32[392,256]{1,0:T(8,128)S(1)}, f32[392,256]{1,0:T(8,128)S(1)}, u32[]{:S(2)}, u32[]{:S(2)}) collective-permute-start(f32[392,256]{1,0:T(8,128)S(1)} %get-tuple-element.19), channel_id=1, source_target_pairs={{4,0},{8,4},{12,8},{0,12},{5,1},{9,5},{13,9},{1,13},{6,2},{10,6},{... | collective-permute-start | bytes 1204232 | tf_op jit(solution)/shard_map/ppermute | solution.py:231
  13.6 4.8 %collective-permute-done.3.refs_1_ = f32[392,256]{1,0:T(8,128)S(1)} collective-permute-done((f32[392,256]{1,0:T(8,128)S(1)}, f32[392,256]{1,0:T(8,128)S(1)}, u32[]{:S(2)}, u32[]{:S(2)}) %collective-permute-start.3) | collective-permute-done | bytes 401440 | tf_op jit(solution)/shard_map/ppermute | solution.py:231
  18.4 1.9 %half.1 = (f32[256,256]{1,0:T(8,128)S(1)}, f32[3,256,256]{2,1,0:T(8,128)S(1)}, f32[8,256]{1,0:T(8,128)S(1)}) custom-call(s32[1,8]{1,0:T(1,128)S(1)} %copy-done.4, s32[1,8]{1,0:T(1,128)S(1)} %copy-done.6, s32[3]{0:T(128)S(1)} %pad_add_fusion.takes, f32[256,256]{1,0:T(8,128)S(1)} %copy-done.1, f32[256,256]{1,0:T(8,128)S(1)} %get-tuple-element.14.own, ...), custom_call_target="tpu_custom_call" | custom-call | tf_op jit(solution)/shard_map/half/pallas_call | solution.py:29
  20.4 1.8 %collective-permute-start.5 = (f32[8,256]{1,0:T(8,128)S(1)}, f32[8,256]{1,0:T(8,128)S(1)}, u32[]{:S(2)}, u32[]{:S(2)}) collective-permute-start(f32[8,256]{1,0:T(8,128)S(1)} %get-tuple-element.17), channel_id=1, source_target_pairs={{0,2},{1,3},{2,0},{3,1},{4,6},{5,7},{6,4},{7,5},{8,10},{9,11},{10,... | collective-permute-start | bytes 24584 | tf_op jit(solution)/shard_map/ppermute | solution.py:50
  22.3 1.2 %collective-permute-done.6 = f32[8,256]{1,0:T(8,128)S(1)} collective-permute-done((f32[8,256]{1,0:T(8,128)S(1)}, f32[8,256]{1,0:T(8,128)S(1)}, u32[]{:S(2)}, u32[]{:S(2)}) %collective-permute-start.6) | collective-permute-done | bytes 8224 | tf_op jit(solution)/shard_map/ppermute | solution.py:50
  24.1 9.6 %collective-permute-start.9 = (f32[8,256]{1,0:T(8,128)S(1)}, f32[8,256]{1,0:T(8,128)S(1)}, u32[]{:S(2)}, u32[]{:S(2)}) collective-permute-start(f32[8,256]{1,0:T(8,128)S(1)} %add_add_fusion.3), channel_id=1, source_target_pairs={{0,12},{1,13},{2,14},{3,15},{4,8},{5,9},{6,10},{7,11},{8,4},{9,5},... | collective-permute-start | bytes 24584 | tf_op jit(solution)/shard_map/ppermute | solution.py:50
  34.3 1.1 %rest.1.image = f32[256,256]{1,0:T(8,128)S(1)} custom-call(s32[1,8]{1,0:T(1,128)S(1)} %copy-done.4, s32[1,8]{1,0:T(1,128)S(1)} %copy-done.6, s32[3]{0:T(128)S(1)} %pad_add_fusion.takes, f32[256,256]{1,0:T(8,128)S(1)} %get-tuple-element.18.part, f32[8,128,128]{2,1,0:T(8,128)S(1)} %bitcast.9, f32[392,256]{1,0:T(8,128)S(1)} %collective-permute-done.10.refs_0_), custom_call_target="tpu_custom_call" | custom-call | tf_op jit(solution)/shard_map/rest/pallas_call | solution.py:29
  35.4 2.8 %collective-permute-done.8 = f32[8,256]{1,0:T(8,128)S(1)} collective-permute-done((f32[8,256]{1,0:T(8,128)S(1)}, f32[8,256]{1,0:T(8,128)S(1)}, u32[]{:S(2)}, u32[]{:S(2)}) %collective-permute-start.8) | collective-permute-done | bytes 8224 | tf_op jit(solution)/shard_map/ppermute | solution.py:50
  38.4 1.6 %collective-permute-start.12 = (f32[256,256]{1,0:T(8,128)S(1)}, f32[256,256]{1,0:T(8,128)S(1)}, u32[]{:S(2)}, u32[]{:S(2)}) collective-permute-start(f32[256,256]{1,0:T(8,128)S(1)} %step.1.res), channel_id=1, source_target_pairs={{0,2},{2,0},{1,3},{3,1},{4,6},{6,4},{5,7},{7,5},{8,10},{10,8},{9,1... | collective-permute-start | bytes 786440 | tf_op jit(solution)/shard_map/ppermute | solution.py:242
  40.7 8.2 %collective-permute-done.13.refs_1_ = f32[256,256]{1,0:T(8,128)S(1)} collective-permute-done((f32[256,256]{1,0:T(8,128)S(1)}, f32[256,256]{1,0:T(8,128)S(1)}, u32[]{:S(2)}, u32[]{:S(2)}) %collective-permute-start.13) | collective-permute-done | bytes 262176 | tf_op jit(solution)/shard_map/ppermute | solution.py:242
  49.6 0.8 %collective-permute-start.16 = (f32[8,256]{1,0:T(8,128)S(1)}, f32[8,256]{1,0:T(8,128)S(1)}, u32[]{:S(2)}, u32[]{:S(2)}) collective-permute-start(f32[8,256]{1,0:T(8,128)S(1)} %far.1), channel_id=1, source_target_pairs={{0,3},{1,2},{2,1},{3,0},{4,7},{5,6},{6,5},{7,4},{8,11},{9,10},{10,... | collective-permute-start | bytes 24584 | tf_op jit(solution)/shard_map/ppermute | solution.py:50
  50.4 0.8 %collective-permute-start.15 = (f32[8,256]{1,0:T(8,128)S(1)}, f32[8,256]{1,0:T(8,128)S(1)}, u32[]{:S(2)}, u32[]{:S(2)}) collective-permute-start(f32[8,256]{1,0:T(8,128)S(1)} %far.1), channel_id=1, source_target_pairs={{0,2},{1,3},{2,0},{3,1},{4,6},{5,7},{6,4},{7,5},{8,10},{9,11},{10,... | collective-permute-start | bytes 24584 | tf_op jit(solution)/shard_map/ppermute | solution.py:50
  51.5 1.3 %collective-permute-done.16 = f32[8,256]{1,0:T(8,128)S(1)} collective-permute-done((f32[8,256]{1,0:T(8,128)S(1)}, f32[8,256]{1,0:T(8,128)S(1)}, u32[]{:S(2)}, u32[]{:S(2)}) %collective-permute-start.16) | collective-permute-done | bytes 8224 | tf_op jit(solution)/shard_map/ppermute | solution.py:50
  52.8 1.3 %collective-permute-done.15 = f32[8,256]{1,0:T(8,128)S(1)} collective-permute-done((f32[8,256]{1,0:T(8,128)S(1)}, f32[8,256]{1,0:T(8,128)S(1)}, u32[]{:S(2)}, u32[]{:S(2)}) %collective-permute-start.15) | collective-permute-done | bytes 8224 | tf_op jit(solution)/shard_map/ppermute | solution.py:50
  54.0 1.5 %collective-permute-start.19 = (f32[8,256]{1,0:T(8,128)S(1)}, f32[8,256]{1,0:T(8,128)S(1)}, u32[]{:S(2)}, u32[]{:S(2)}) collective-permute-start(f32[8,256]{1,0:T(8,128)S(1)} %add_add_fusion.1), channel_id=1, source_target_pairs={{0,12},{1,13},{2,14},{3,15},{4,8},{5,9},{6,10},{7,11},{8,4},{9,5},... | collective-permute-start | bytes 24584 | tf_op jit(solution)/shard_map/ppermute | solution.py:50
  55.7 2.7 %collective-permute-start.17 = (f32[8,256]{1,0:T(8,128)S(1)}, f32[8,256]{1,0:T(8,128)S(1)}, u32[]{:S(2)}, u32[]{:S(2)}) collective-permute-start(f32[8,256]{1,0:T(8,128)S(1)} %add_add_fusion.1), channel_id=1, source_target_pairs={{0,4},{1,5},{2,6},{3,7},{4,0},{5,1},{6,2},{7,3},{8,12},{9,13},{10,... | collective-permute-start | bytes 24584 | tf_op jit(solution)/shard_map/ppermute | solution.py:50
  58.5 1.1 %collective-permute-done.19 = f32[8,256]{1,0:T(8,128)S(1)} collective-permute-done((f32[8,256]{1,0:T(8,128)S(1)}, f32[8,256]{1,0:T(8,128)S(1)}, u32[]{:S(2)}, u32[]{:S(2)}) %collective-permute-start.19) | collective-permute-done | bytes 8224 | tf_op jit(solution)/shard_map/ppermute | solution.py:50
  60.2 0.7 %multiply_add_fusion = f32[256,256]{1,0:T(8,128)} fusion(f32[256,256]{1,0:T(8,128)S(1)} %step.1.res, f32[256,256]{1,0:T(8,128)S(1)} %copy-done.1, f32[256]{0:T(256)S(1)} %bitcast.12, f32[256]{0:T(256)S(1)} %bitcast.11), kind=kLoop, calls=%fused_computation | loop fusion | flops 196608 | bytes 788480 | tf_op jit(solution)/shard_map/add | solution.py:250
  (49 shorter events, 6.2 us)
Async XLA Ops:
  0.0 7.8 %copy-start = (f32[1,8,128,128]{3,2,1,0:T(8,128)S(1)}, f32[1,8,128,128]{3,2,1,0:T(8,128)}, u32[]{:S(2)}) copy-start(f32[1,8,128,128]{3,2,1,0:T(8,128)} %param.11) | copy-start | bytes 1572868
  1.4 6.3 %copy-start.1 = (f32[256,256]{1,0:T(8,128)S(1)}, f32[256,256]{1,0:T(8,128)}, u32[]{:S(2)}) copy-start(f32[256,256]{1,0:T(8,128)} %field.5) | copy-start | bytes 786436
  3.1 4.6 %copy-start.7 = (s32[2,7]{1,0:T(2,128)S(1)}, s32[2,7]{1,0:T(2,128)}, u32[]{:S(2)}) copy-start(s32[2,7]{1,0:T(2,128)} %cols.1) | copy-start | bytes 172
  3.2 4.6 %copy-start.8 = (f32[256]{0:T(256)S(1)}, f32[256]{0:T(256)}, u32[]{:S(2)}) copy-start(f32[256]{0:T(256)} %param.8) | copy-start | bytes 3076
  3.2 15.3 %collective-permute-start.3 = (f32[392,256]{1,0:T(8,128)S(1)}, f32[392,256]{1,0:T(8,128)S(1)}, u32[]{:S(2)}, u32[]{:S(2)}) collective-permute-start(f32[392,256]{1,0:T(8,128)S(1)} %get-tuple-element.16), channel_id=1, source_target_pairs={{0,4},{4,8},{8,12},{12,0},{1,5},{5,9},{9,13},{13,1},{2,6},{6,10},{... | collective-permute-start | bytes 1204232 | tf_op jit(solution)/shard_map/ppermute | solution.py:231
  6.2 12.2 %collective-permute-start.2 = (f32[392,256]{1,0:T(8,128)S(1)}, f32[392,256]{1,0:T(8,128)S(1)}, u32[]{:S(2)}, u32[]{:S(2)}) collective-permute-start(f32[392,256]{1,0:T(8,128)S(1)} %get-tuple-element.13.packed), channel_id=1, source_target_pairs={{0,2},{2,0},{1,3},{3,1},{4,6},{6,4},{5,7},{7,5},{8,10},{10,8},{9,1... | collective-permute-start | bytes 1204232 | tf_op jit(solution)/shard_map/ppermute | solution.py:231
  7.7 5.9 %collective-permute-start = (f32[256,256]{1,0:T(8,128)S(1)}, f32[256,256]{1,0:T(8,128)S(1)}, u32[]{:S(2)}, u32[]{:S(2)}) collective-permute-start(f32[256,256]{1,0:T(8,128)S(1)} %copy-done.1), channel_id=1, source_target_pairs={{0,1},{1,0},{2,3},{3,2},{4,5},{5,4},{6,7},{7,6},{8,9},{9,8},{10,11... | collective-permute-start | bytes 786440 | tf_op jit(solution)/shard_map/ppermute | solution.py:226
  10.7 2.9 %collective-permute-start.1 = (f32[256,256]{1,0:T(8,128)S(1)}, f32[256,256]{1,0:T(8,128)S(1)}, u32[]{:S(2)}, u32[]{:S(2)}) collective-permute-start(f32[256,256]{1,0:T(8,128)S(1)} %get-tuple-element.15.pair), channel_id=1, source_target_pairs={{0,1},{1,0},{2,3},{3,2},{4,5},{5,4},{6,7},{7,6},{8,9},{9,8},{10,11... | collective-permute-start | bytes 786440 | tf_op jit(solution)/shard_map/ppermute | solution.py:232
  11.3 23.1 %collective-permute-start.10 = (f32[392,256]{1,0:T(8,128)S(1)}, f32[392,256]{1,0:T(8,128)S(1)}, u32[]{:S(2)}, u32[]{:S(2)}) collective-permute-start(f32[392,256]{1,0:T(8,128)S(1)} %get-tuple-element.19), channel_id=1, source_target_pairs={{4,0},{8,4},{12,8},{0,12},{5,1},{9,5},{13,9},{1,13},{6,2},{10,6},{... | collective-permute-start | bytes 1204232 | tf_op jit(solution)/shard_map/ppermute | solution.py:231
  20.3 3.1 %collective-permute-start.6 = (f32[8,256]{1,0:T(8,128)S(1)}, f32[8,256]{1,0:T(8,128)S(1)}, u32[]{:S(2)}, u32[]{:S(2)}) collective-permute-start(f32[8,256]{1,0:T(8,128)S(1)} %get-tuple-element.17), channel_id=1, source_target_pairs={{0,3},{1,2},{2,1},{3,0},{4,7},{5,6},{6,5},{7,4},{8,11},{9,10},{10,... | collective-permute-start | bytes 24584 | tf_op jit(solution)/shard_map/ppermute | solution.py:50
  20.4 3.7 %collective-permute-start.5 = (f32[8,256]{1,0:T(8,128)S(1)}, f32[8,256]{1,0:T(8,128)S(1)}, u32[]{:S(2)}, u32[]{:S(2)}) collective-permute-start(f32[8,256]{1,0:T(8,128)S(1)} %get-tuple-element.17), channel_id=1, source_target_pairs={{0,2},{1,3},{2,0},{3,1},{4,6},{5,7},{6,4},{7,5},{8,10},{9,11},{10,... | collective-permute-start | bytes 24584 | tf_op jit(solution)/shard_map/ppermute | solution.py:50
  22.2 1.9 %collective-permute-start.4 = (f32[8,256]{1,0:T(8,128)S(1)}, f32[8,256]{1,0:T(8,128)S(1)}, u32[]{:S(2)}, u32[]{:S(2)}) collective-permute-start(f32[8,256]{1,0:T(8,128)S(1)} %get-tuple-element.17), channel_id=1, source_target_pairs={{0,1},{1,0},{2,3},{3,2},{4,5},{5,4},{6,7},{7,6},{8,9},{9,8},{10,11... | collective-permute-start | bytes 24584 | tf_op jit(solution)/shard_map/ppermute | solution.py:50
  24.1 11.3 %collective-permute-start.9 = (f32[8,256]{1,0:T(8,128)S(1)}, f32[8,256]{1,0:T(8,128)S(1)}, u32[]{:S(2)}, u32[]{:S(2)}) collective-permute-start(f32[8,256]{1,0:T(8,128)S(1)} %add_add_fusion.3), channel_id=1, source_target_pairs={{0,12},{1,13},{2,14},{3,15},{4,8},{5,9},{6,10},{7,11},{8,4},{9,5},... | collective-permute-start | bytes 24584 | tf_op jit(solution)/shard_map/ppermute | solution.py:50
  33.7 4.5 %collective-permute-start.8 = (f32[8,256]{1,0:T(8,128)S(1)}, f32[8,256]{1,0:T(8,128)S(1)}, u32[]{:S(2)}, u32[]{:S(2)}) collective-permute-start(f32[8,256]{1,0:T(8,128)S(1)} %add_add_fusion.3), channel_id=1, source_target_pairs={{0,8},{1,9},{2,10},{3,11},{4,12},{5,13},{6,14},{7,15},{8,0},{9,1},... | collective-permute-start | bytes 24584 | tf_op jit(solution)/shard_map/ppermute | solution.py:50
  33.7 4.5 %collective-permute-start.7 = (f32[8,256]{1,0:T(8,128)S(1)}, f32[8,256]{1,0:T(8,128)S(1)}, u32[]{:S(2)}, u32[]{:S(2)}) collective-permute-start(f32[8,256]{1,0:T(8,128)S(1)} %add_add_fusion.3), channel_id=1, source_target_pairs={{0,4},{1,5},{2,6},{3,7},{4,0},{5,1},{6,2},{7,3},{8,12},{9,13},{10,... | collective-permute-start | bytes 24584 | tf_op jit(solution)/shard_map/ppermute | solution.py:50
  38.3 1.7 %collective-permute-start.11 = (f32[256,256]{1,0:T(8,128)S(1)}, f32[256,256]{1,0:T(8,128)S(1)}, u32[]{:S(2)}, u32[]{:S(2)}) collective-permute-start(f32[256,256]{1,0:T(8,128)S(1)} %step.1.res), channel_id=1, source_target_pairs={{0,1},{1,0},{2,3},{3,2},{4,5},{5,4},{6,7},{7,6},{8,9},{9,8},{10,11... | collective-permute-start | bytes 786440 | tf_op jit(solution)/shard_map/ppermute | solution.py:243
  38.4 10.5 %collective-permute-start.13 = (f32[256,256]{1,0:T(8,128)S(1)}, f32[256,256]{1,0:T(8,128)S(1)}, u32[]{:S(2)}, u32[]{:S(2)}) collective-permute-start(f32[256,256]{1,0:T(8,128)S(1)} %step.1.res), channel_id=1, source_target_pairs={{0,4},{4,8},{8,12},{12,0},{1,5},{5,9},{9,13},{13,1},{2,6},{6,10},{... | collective-permute-start | bytes 786440 | tf_op jit(solution)/shard_map/ppermute | solution.py:242
  38.4 10.4 %collective-permute-start.12 = (f32[256,256]{1,0:T(8,128)S(1)}, f32[256,256]{1,0:T(8,128)S(1)}, u32[]{:S(2)}, u32[]{:S(2)}) collective-permute-start(f32[256,256]{1,0:T(8,128)S(1)} %step.1.res), channel_id=1, source_target_pairs={{0,2},{2,0},{1,3},{3,1},{4,6},{6,4},{5,7},{7,5},{8,10},{10,8},{9,1... | collective-permute-start | bytes 786440 | tf_op jit(solution)/shard_map/ppermute | solution.py:242
  49.6 3.2 %collective-permute-start.16 = (f32[8,256]{1,0:T(8,128)S(1)}, f32[8,256]{1,0:T(8,128)S(1)}, u32[]{:S(2)}, u32[]{:S(2)}) collective-permute-start(f32[8,256]{1,0:T(8,128)S(1)} %far.1), channel_id=1, source_target_pairs={{0,3},{1,2},{2,1},{3,0},{4,7},{5,6},{6,5},{7,4},{8,11},{9,10},{10,... | collective-permute-start | bytes 24584 | tf_op jit(solution)/shard_map/ppermute | solution.py:50
  50.4 3.7 %collective-permute-start.15 = (f32[8,256]{1,0:T(8,128)S(1)}, f32[8,256]{1,0:T(8,128)S(1)}, u32[]{:S(2)}, u32[]{:S(2)}) collective-permute-start(f32[8,256]{1,0:T(8,128)S(1)} %far.1), channel_id=1, source_target_pairs={{0,2},{1,3},{2,0},{3,1},{4,6},{5,7},{6,4},{7,5},{8,10},{9,11},{10,... | collective-permute-start | bytes 24584 | tf_op jit(solution)/shard_map/ppermute | solution.py:50
  51.2 2.8 %collective-permute-start.14 = (f32[8,256]{1,0:T(8,128)S(1)}, f32[8,256]{1,0:T(8,128)S(1)}, u32[]{:S(2)}, u32[]{:S(2)}) collective-permute-start(f32[8,256]{1,0:T(8,128)S(1)} %far.1), channel_id=1, source_target_pairs={{0,1},{1,0},{2,3},{3,2},{4,5},{5,4},{6,7},{7,6},{8,9},{9,8},{10,11... | collective-permute-start | bytes 24584 | tf_op jit(solution)/shard_map/ppermute | solution.py:50
  54.0 5.5 %collective-permute-start.19 = (f32[8,256]{1,0:T(8,128)S(1)}, f32[8,256]{1,0:T(8,128)S(1)}, u32[]{:S(2)}, u32[]{:S(2)}) collective-permute-start(f32[8,256]{1,0:T(8,128)S(1)} %add_add_fusion.1), channel_id=1, source_target_pairs={{0,12},{1,13},{2,14},{3,15},{4,8},{5,9},{6,10},{7,11},{8,4},{9,5},... | collective-permute-start | bytes 24584 | tf_op jit(solution)/shard_map/ppermute | solution.py:50
  55.5 4.5 %collective-permute-start.18 = (f32[8,256]{1,0:T(8,128)S(1)}, f32[8,256]{1,0:T(8,128)S(1)}, u32[]{:S(2)}, u32[]{:S(2)}) collective-permute-start(f32[8,256]{1,0:T(8,128)S(1)} %add_add_fusion.1), channel_id=1, source_target_pairs={{0,8},{1,9},{2,10},{3,11},{4,12},{5,13},{6,14},{7,15},{8,0},{9,1},... | collective-permute-start | bytes 24584 | tf_op jit(solution)/shard_map/ppermute | solution.py:50
  55.7 4.4 %collective-permute-start.17 = (f32[8,256]{1,0:T(8,128)S(1)}, f32[8,256]{1,0:T(8,128)S(1)}, u32[]{:S(2)}, u32[]{:S(2)}) collective-permute-start(f32[8,256]{1,0:T(8,128)S(1)} %add_add_fusion.1), channel_id=1, source_target_pairs={{0,4},{1,5},{2,6},{3,7},{4,0},{5,1},{6,2},{7,3},{8,12},{9,13},{10,... | collective-permute-start | bytes 24584 | tf_op jit(solution)/shard_map/ppermute | solution.py:50
  (5 other events, 3.9 us)

commit v5 on v3

--- a/solution.py
+++ b/solution.py
@@ -40,16 +40,16 @@
     return run
 
 
-def axis_sum(part, axes):
-    count = lax.axis_size(axes)
-    if count & (count - 1):
-        return lax.psum(part, axes)
+def join(state):
+    count = lax.axis_size(AXES)
+    assert count & (count - 1) == 0
     step = 1
     while step < count:
         masks = [m * step for m in (1, 2, 3) if m * step < count]
-        part = part + sum(lax.ppermute(part, axes, [(i, i ^ m) for i in range(count)]) for m in masks)
+        others = [lax.ppermute(state, AXES, [(i, i ^ m) for i in range(count)]) for m in masks]
+        (state,) = call(merge_kernel, "merge", 0, [state.shape])(state, *others)
         step *= 4
-    return part
+    return state
 
 
 def prep_kernel(cols, sides, packed, diag, local, own, pair):
@@ -126,55 +126,77 @@
     return jnp.dot(a, b, precision=HP, preferred_element_type=F32)
 
 
-def two_rows(first, second):
-    line = lax.broadcasted_iota(jnp.int32, (TAIL, first.shape[1]), 0)
-    return jnp.where(line == 0, first, jnp.where(line == 1, second, 0.0))
-
-
 def half_kernel(weights, send, rows, takes, field, own, pair, mate, mate_pair, border, *refs):
-    *pays, image, coup, sums = refs
+    *pays, image, once, coup = refs
     width = field.shape[0]
-    here = field[...]
     coup[0] = pair[...] + mate_pair[...].T
-    acc = dot(own[...], here) + dot(coup[0], mate[...])
-    half = acc
+    acc = dot(own[...], field[...]) + dot(coup[0], mate[...])
+    single = acc
     for n, pay in enumerate(pays):
         build_edge(coup.at[1 + n], takes[n], send, rows, border, pay)
         edge = dot(coup[1 + n], pay[pl.ds(0, width), :])
         acc += edge
-        half += weights[n] * edge
+        single += weights[n] * edge
     image[...] = acc
-    norm = jnp.sum(here * here, axis=0, keepdims=True)
-    sums[...] = two_rows(norm, jnp.sum(here * half, axis=0, keepdims=True))
-
-
-def rest_kernel(first, send, rows, takes, part, border, *refs):
+    once[...] = single
+
+
+def rest_kernel(skip, send, rows, takes, part, border, *refs):
     *pays, image, coup = refs
     width = part.shape[0]
     acc = part[...]
     for n, pay in enumerate(pays):
-        build_edge(coup, takes[first + n], send, rows, border, pay)
+        build_edge(coup, takes[skip + n], send, rows, border, pay)
         acc += dot(coup[...], pay[pl.ds(0, width), :])
     image[...] = acc
 
 
-def near_kernel(first, field, image, mate, mate_w, own, coup, sums):
-    a = first[0:1, :] / first[1:2, :]
-    res = field[...] - a * image[...]
-    acc = dot(own[...], res) + dot(coup[0], mate[...] - a * mate_w[...])
-    sums[...] = two_rows(jnp.sum(res * res, axis=0, keepdims=True), jnp.sum(res * acc, axis=0, keepdims=True))
-
-
-def far_kernel(weights, first, near, field, image, coup, *refs):
+def col_sum(a, b):
+    return jnp.sum(a * b, axis=0, keepdims=True)
+
+
+def near_kernel(field, image, once, mate, mate_w, own, coup, part, state):
+    b = field[...]
+    norm = col_sum(b, b)
+    c = jnp.where(norm > 0.0, col_sum(b, image[...]) / jnp.where(norm > 0.0, norm, 1.0), 0.0)
+    g = image[...] - c * b
+    part[...] = dot(own[...], g) + dot(coup[0], mate_w[...] - c * mate[...])
+    rows = [norm, c, col_sum(g, g), jnp.zeros_like(c), -col_sum(g, once[...]), col_sum(b, once[...])]
+    line = lax.broadcasted_iota(jnp.int32, state.shape, 0)
+    state[...] = sum(jnp.where(line == n, row, 0.0) for n, row in enumerate(rows))
+
+
+def far_kernel(weights, field, image, part, near, coup, *refs):
     count = len(weights)
-    pays, images, sums = refs[:count], refs[count : 2 * count], refs[2 * count]
+    pays, images, state = refs[:count], refs[count : 2 * count], refs[2 * count]
     width = field.shape[0]
-    a = first[0:1, :] / first[1:2, :]
-    res = field[...] - a * image[...]
-    acc = jnp.zeros(res.shape, F32)
+    b = field[...]
+    c = near[1:2, :]
+    acc = part[...]
     for n, weight in enumerate(weights):
-        acc += dot(coup[1 + n], weight * (pays[n][pl.ds(0, width), :] - a * images[n][...]))
-    sums[...] = near[...] + two_rows(jnp.zeros(a.shape, F32), jnp.sum(res * acc, axis=0, keepdims=True))
+        acc += weight * dot(coup[1 + n], images[n][...] - c * pays[n][pl.ds(0, width), :])
+    line = lax.broadcasted_iota(jnp.int32, state.shape, 0)
+    flat = col_sum(image[...] - c * b, acc)
+    slope = -col_sum(b, acc)
+    state[...] = near[...] + jnp.where(line == 3, flat, jnp.where(line == 4, slope, 0.0))
+
+
+def merge_kernel(*refs):
+    *states, out = refs
+    norm = sum(s[0:1, :] for s in states)
+    base = states[0][1:2, :]
+    shift = sum(s[0:1, :] * (s[1:2, :] - base) for s in states)
+    c = base + jnp.where(norm > 0.0, shift / jnp.where(norm > 0.0, norm, 1.0), 0.0)
+    rows = [norm, c] + [jnp.zeros_like(c)] * 4
+    for s in states:
+        d = c - s[1:2, :]
+        flat, slope, bend = s[3:4, :], s[4:5, :], s[5:6, :]
+        rows[2] += s[2:3, :] + s[0:1, :] * d * d
+        rows[3] += flat + (slope + bend * d) * d
+        rows[4] += slope + 2.0 * bend * d
+        rows[5] += bend
+    line = lax.broadcasted_iota(jnp.int32, out.shape, 0)
+    out[...] = sum(jnp.where(line == n, row, 0.0) for n, row in enumerate(rows))
 
 
 def shards(right_side, node_diag, local_coup, block_cols, border_coup, border_send, border_rows):
@@ -192,12 +214,12 @@
     slots = [("gx", right, 0), ("gx", left, 1)]
     weights = [2.0]
     if n_gy == 2:
-        slots.insert(0, ("gy", swap, facing))
-        weights.insert(0, 1.0)
+        slots.insert(1, ("gy", swap, facing))
+        weights.append(1.0)
     elif n_gy > 2:
-        slots.insert(0, ("gy", up, 2))
+        slots.insert(1, ("gy", up, 2))
         slots.append(("gy", down, 3))
-        weights.insert(0, 2.0)
+        weights.append(2.0)
     early = len(weights)
     takes = jnp.stack([jnp.asarray(t, jnp.int32) for _, _, t in slots])
     gives = jnp.stack([jnp.asarray(facing if t is facing else t ^ 1, jnp.int32) for _, _, t in slots])
@@ -220,25 +242,24 @@
     )
     mate_pair = lax.ppermute(pair, "nd", swap)
 
-    part, coup, first = call(partial(half_kernel, weights), "half", 3, [(width, ncols), (1 + early, width, width), (TAIL, ncols)])(
+    part, once, coup = call(partial(half_kernel, weights), "half", 3, [(width, ncols)] * 2 + [(1 + early, width, width)])(
         border_send, border_rows, takes, right_side, own, pair, mate, mate_pair, border, *pays[:early]
     )
-    first = axis_sum(first, AXES)
     (image,) = call(partial(rest_kernel, early), "rest", 3, [(width, ncols)], scratch=[pltpu.VMEM((width, width), F32)])(
         border_send, border_rows, takes, part, border, *pays[early:]
     )
     images = [lax.ppermute(image, axis, perm) for axis, perm, _ in slots[:early]]
     mate_w = lax.ppermute(image, "nd", swap)
-    (near,) = call(near_kernel, "near", 0, [(TAIL, ncols)])(first, right_side, image, mate, mate_w, own, coup)
-    (second,) = call(partial(far_kernel, weights), "far", 0, [(TAIL, ncols)])(
-        first, near, right_side, image, coup, *pays[:early], *images
-    )
-    second = axis_sum(second, AXES)
-    norm, curve = first[0:1], first[1:2]
-    step = norm / curve
-    ratio = second[0:1] / norm
-    last = second[0:1] / (second[1:2] - ratio * ratio * curve)
-    return (step + last * (1.0 + ratio)) * right_side - (last * step) * image
+    part, state = call(near_kernel, "near", 0, [(width, ncols), (TAIL, ncols)])(
+        right_side, image, once, mate, mate_w, own, coup
+    )
+    (state,) = call(partial(far_kernel, weights), "far", 0, [(TAIL, ncols)])(
+        right_side, image, part, state, coup, *pays[:early], *images
+    )
+    norm, c, size, form = (row[None] for row in join(state)[:4])
+    ratio = size / (c * c * norm)
+    last = size / (form - ratio * ratio * c * c * c * norm)
+    return ((1.0 + last * c * (1.0 + ratio)) / c) * right_side - (last / c) * image
 
 
 def solution(mesh):

time: 55.4 us -> 52.4 us (0.946)
  starting transfers between devices: 24.6 us -> 16.2 us
  waiting for transfers between devices: 19.6 us -> 24.9 us
    ppermute x12 -> x6, starting transfers between devices: 15.2 us -> 6.66 us  [join(): lax.ppermute(state, AXES, [(i, i ^ m) for i in range(count)])]
    ppermute x2, waiting for transfers between devices: 0.01 us -> 7.78 us  [shards(): lax.ppermute(image, axis, perm)]
    ppermute x12 -> x6, waiting for transfers between devices: 10.8 us -> 6.47 us  [join(): lax.ppermute(state, AXES, [(i, i ^ m) for i in range(count)])]
    ppermute x3, waiting for transfers between devices: 7.65 us -> 9.29 us  [shards(): lax.ppermute(pay, axis, perm)]
    pallas_call x5 -> x7, Pallas kernels: 5.53 us -> 5.72 us  [run(): pl.pallas_call(kernel, name=name, in_specs=[smem()] * tables + [vmem()] *...]
  transfers between devices with their start and end apart: 20 -> 14, of which waited for: 9 -> 9; matrix products, arithmetic and copies ran while one was open for 0% -> 0% of each run, Pallas kernels for 9% -> 7%
where the time goes in v5:
time: 52.4 us; the launch traced here: 52.2 us
  waiting for transfers between devices  24.9 us (48%)
  starting transfers between devices  16.2 us (31%)
  Pallas kernels  7.58 us (14%)
  local copies, waits for them, and re-layouts  2.54 us (5%)
  other arithmetic  0.92 us (2%)
    ppermute x3, waiting for transfers between devices, shards(): lax.ppermute(pay, axis, perm)  9.29 us
    ppermute x2, waiting for transfers between devices, shards(): lax.ppermute(image, axis, perm)  7.78 us
    ppermute x3, starting transfers between devices, shards(): lax.ppermute(pay, axis, perm)  6.8 us
    ppermute x6, starting transfers between devices, join(): lax.ppermute(state, AXES, [(i, i ^ m) for i in range(count)])  6.66 us
    ppermute x6, waiting for transfers between devices, join(): lax.ppermute(state, AXES, [(i, i ^ m) for i in range(count)])  6.47 us
    pallas_call x7, Pallas kernels, run(): pl.pallas_call(kernel, name=name, in_specs=[smem()] * tables + [vmem()] *...  5.72 us
    unnamed x14, local copies, waits for them, and re-layouts  2.54 us
    ppermute x2, starting transfers between devices, shards(): lax.ppermute(image, axis, perm)  2.1 us
  transfers between devices with their start and end apart: 14, of which 9 were waited for; matrix products, arithmetic and copies ran while one was open for 0% of the time, Pallas kernels for 7%

profile of v5, /device:TPU:0, one launch (start us, length us, event | category | flops | bytes accessed | tf_op | source)
XLA Modules:
  0.0 52.2 jit_solution(12479525200074648766)
XLA Ops:
  0.7 1.9 %pack.1 = (f32[392,256]{1,0:T(8,128)S(1)}, f32[392,256]{1,0:T(8,128)S(1)}, f32[392,256]{1,0:T(8,128)S(1)}) custom-call(s32[1,8]{1,0:T(1,128)S(1)} %copy-done.3, s32[1,8]{1,0:T(1,128)S(1)} %copy-done.4, s32[3]{0:T(128)S(1)} %pad_add_fusion.1.gives, f32[256,256]{1,0:T(8,128)} %field.7, f32[8,128,128]{2,1,0:T(8,128)} %bitcast.6), custom_call_target="tpu_custom_call" | custom-call | tf_op jit(solution)/shard_map/pack/pallas_call | solution.py:229
  2.6 3.1 %collective-permute-start.2 = (f32[392,256]{1,0:T(8,128)S(1)}, f32[392,256]{1,0:T(8,128)S(1)}, u32[]{:S(2)}, u32[]{:S(2)}) collective-permute-start(f32[392,256]{1,0:T(8,128)S(1)} %get-tuple-element.15.packed), channel_id=1, source_target_pairs={{0,4},{4,8},{8,12},{12,0},{1,5},{5,9},{9,13},{13,1},{2,6},{6,10},{... | collective-permute-start | bytes 1204232 | tf_op jit(solution)/shard_map/ppermute | solution.py:238
  5.7 1.5 %collective-permute-start.3 = (f32[392,256]{1,0:T(8,128)S(1)}, f32[392,256]{1,0:T(8,128)S(1)}, u32[]{:S(2)}, u32[]{:S(2)}) collective-permute-start(f32[392,256]{1,0:T(8,128)S(1)} %get-tuple-element.18), channel_id=1, source_target_pairs={{0,2},{2,0},{1,3},{3,1},{4,6},{6,4},{5,7},{7,5},{8,10},{10,8},{9,1... | collective-permute-start | bytes 1204232 | tf_op jit(solution)/shard_map/ppermute | solution.py:238
  7.2 2.2 %collective-permute-start.4 = (f32[392,256]{1,0:T(8,128)S(1)}, f32[392,256]{1,0:T(8,128)S(1)}, u32[]{:S(2)}, u32[]{:S(2)}) collective-permute-start(f32[392,256]{1,0:T(8,128)S(1)} %get-tuple-element.20), channel_id=1, source_target_pairs={{4,0},{8,4},{12,8},{0,12},{5,1},{9,5},{13,9},{1,13},{6,2},{10,6},{... | collective-permute-start | bytes 1204232 | tf_op jit(solution)/shard_map/ppermute | solution.py:238
  10.1 1.2 %copy-done.2 = f32[2,7,128,128]{3,2,1,0:T(8,128)S(1)} copy-done((f32[2,7,128,128]{3,2,1,0:T(8,128)S(1)}, f32[2,7,128,128]{3,2,1,0:T(8,128)}, u32[]{:S(2)}) %copy-start.2) | copy-done | bytes 917528
  11.3 1.1 %prep.1 = (f32[256,256]{1,0:T(8,128)S(1)}, f32[256,256]{1,0:T(8,128)S(1)}) custom-call(s32[2,7]{1,0:T(2,128)S(1)} %copy-done.5, s32[1]{0:T(128)} %bitcast.1.sides, f32[392,256]{1,0:T(8,128)S(1)} %get-tuple-element.15.packed, f32[1,256]{1,0:T(1,128)S(1)} %bitcast.9, f32[2,7,128,128]{3,2,1,0:T(8,128)S(1)} %copy-done.2), custom_call_target="tpu_custom_call" | custom-call | flops 16777216 | bytes 1048576 | tf_op jit(solution)/shard_map/prep/pallas_call | solution.py:29
  13.0 0.9 %collective-permute-done.1.mate_pair = f32[256,256]{1,0:T(8,128)S(1)} collective-permute-done((f32[256,256]{1,0:T(8,128)S(1)}, f32[256,256]{1,0:T(8,128)S(1)}, u32[]{:S(2)}, u32[]{:S(2)}) %collective-permute-start.1) | collective-permute-done | bytes 262176 | tf_op jit(solution)/shard_map/ppermute | solution.py:243
  14.3 3.5 %collective-permute-done.2.refs_0_ = f32[392,256]{1,0:T(8,128)S(1)} collective-permute-done((f32[392,256]{1,0:T(8,128)S(1)}, f32[392,256]{1,0:T(8,128)S(1)}, u32[]{:S(2)}, u32[]{:S(2)}) %collective-permute-start.2) | collective-permute-done | bytes 401440 | tf_op jit(solution)/shard_map/ppermute | solution.py:238
  17.9 2.0 %half.1 = (f32[256,256]{1,0:T(8,128)S(1)}, f32[256,256]{1,0:T(8,128)S(1)}, f32[3,256,256]{2,1,0:T(8,128)S(1)}) custom-call(s32[1,8]{1,0:T(1,128)S(1)} %copy-done.3, s32[1,8]{1,0:T(1,128)S(1)} %copy-done.4, s32[3]{0:T(128)S(1)} %pad_add_fusion.takes, f32[256,256]{1,0:T(8,128)S(1)} %copy-done, f32[256,256]{1,0:T(8,128)S(1)} %get-tuple-element.16.own, ...), custom_call_target="tpu_custom_call" | custom-call | tf_op jit(solution)/shard_map/half/pallas_call | solution.py:29
  19.9 5.8 %collective-permute-done.4.refs_0_ = f32[392,256]{1,0:T(8,128)S(1)} collective-permute-done((f32[392,256]{1,0:T(8,128)S(1)}, f32[392,256]{1,0:T(8,128)S(1)}, u32[]{:S(2)}, u32[]{:S(2)}) %collective-permute-start.4) | collective-permute-done | bytes 401440 | tf_op jit(solution)/shard_map/ppermute | solution.py:238
  25.6 1.1 %rest.1.image = f32[256,256]{1,0:T(8,128)S(1)} custom-call(s32[1,8]{1,0:T(1,128)S(1)} %copy-done.3, s32[1,8]{1,0:T(1,128)S(1)} %copy-done.4, s32[3]{0:T(128)S(1)} %pad_add_fusion.takes, f32[256,256]{1,0:T(8,128)S(1)} %get-tuple-element.19.part, f32[8,128,128]{2,1,0:T(8,128)S(1)} %bitcast.8, f32[392,256]{1,0:T(8,128)S(1)} %collective-permute-done.4.refs_0_), custom_call_target="tpu_custom_call" | custom-call | tf_op jit(solution)/shard_map/rest/pallas_call | solution.py:29
  27.4 1.5 %collective-permute-start.7 = (f32[256,256]{1,0:T(8,128)S(1)}, f32[256,256]{1,0:T(8,128)S(1)}, u32[]{:S(2)}, u32[]{:S(2)}) collective-permute-start(f32[256,256]{1,0:T(8,128)S(1)} %rest.1.image), channel_id=1, source_target_pairs={{0,2},{2,0},{1,3},{3,1},{4,6},{6,4},{5,7},{7,5},{8,10},{10,8},{9,1... | collective-permute-start | bytes 786440 | tf_op jit(solution)/shard_map/ppermute | solution.py:251
  28.9 0.8 %near.1 = (f32[256,256]{1,0:T(8,128)S(1)}, f32[8,256]{1,0:T(8,128)S(1)}) custom-call(f32[256,256]{1,0:T(8,128)S(1)} %copy-done, f32[256,256]{1,0:T(8,128)S(1)} %rest.1.image, f32[256,256]{1,0:T(8,128)S(1)} %get-tuple-element.21.once, f32[256,256]{1,0:T(8,128)S(1)} %collective-permute-done.mate, f32[256,256]{1,0:T(8,128)S(1)} %collective-permute-done.5.mate_w, ...), custom_call_target="tpu_custom_call" | custom-call | tf_op jit(solution)/shard_map/near/pallas_call | solution.py:29
  29.7 7.8 %collective-permute-done.6.refs_2_ = f32[256,256]{1,0:T(8,128)S(1)} collective-permute-done((f32[256,256]{1,0:T(8,128)S(1)}, f32[256,256]{1,0:T(8,128)S(1)}, u32[]{:S(2)}, u32[]{:S(2)}) %collective-permute-start.6) | collective-permute-done | bytes 262176 | tf_op jit(solution)/shard_map/ppermute | solution.py:251
  37.5 0.7 %far.1.refs_0_ = f32[8,256]{1,0:T(8,128)S(1)} custom-call(f32[256,256]{1,0:T(8,128)S(1)} %copy-done, f32[256,256]{1,0:T(8,128)S(1)} %rest.1.image, f32[256,256]{1,0:T(8,128)S(1)} %get-tuple-element.23.part, f32[8,256]{1,0:T(8,128)S(1)} %get-tuple-element.24.near, f32[3,256,256]{2,1,0:T(8,128)S(1)} %get-tuple-element.22.coup, ...), custom_call_target="tpu_custom_call" | custom-call | tf_op jit(solution)/shard_map/far/pallas_call | solution.py:29
  38.2 1.0 %collective-permute-start.10 = (f32[8,256]{1,0:T(8,128)S(1)}, f32[8,256]{1,0:T(8,128)S(1)}, u32[]{:S(2)}, u32[]{:S(2)}) collective-permute-start(f32[8,256]{1,0:T(8,128)S(1)} %far.1.refs_0_), channel_id=1, source_target_pairs={{0,3},{1,2},{2,1},{3,0},{4,7},{5,6},{6,5},{7,4},{8,11},{9,10},{10,... | collective-permute-start | bytes 24584 | tf_op jit(solution)/shard_map/ppermute | solution.py:49
  40.4 1.0 %collective-permute-done.10.refs_3_ = f32[8,256]{1,0:T(8,128)S(1)} collective-permute-done((f32[8,256]{1,0:T(8,128)S(1)}, f32[8,256]{1,0:T(8,128)S(1)}, u32[]{:S(2)}, u32[]{:S(2)}) %collective-permute-start.10) | collective-permute-done | bytes 8224 | tf_op jit(solution)/shard_map/ppermute | solution.py:49
  41.4 2.1 %collective-permute-done.9.refs_2_ = f32[8,256]{1,0:T(8,128)S(1)} collective-permute-done((f32[8,256]{1,0:T(8,128)S(1)}, f32[8,256]{1,0:T(8,128)S(1)}, u32[]{:S(2)}, u32[]{:S(2)}) %collective-permute-start.9) | collective-permute-done | bytes 8224 | tf_op jit(solution)/shard_map/ppermute | solution.py:49
  43.6 1.1 %collective-permute-start.11 = (f32[8,256]{1,0:T(8,128)S(1)}, f32[8,256]{1,0:T(8,128)S(1)}, u32[]{:S(2)}, u32[]{:S(2)}) collective-permute-start(f32[8,256]{1,0:T(8,128)S(1)} %merge.2.refs_0_), channel_id=1, source_target_pairs={{0,4},{1,5},{2,6},{3,7},{4,0},{5,1},{6,2},{7,3},{8,12},{9,13},{10,... | collective-permute-start | bytes 24584 | tf_op jit(solution)/shard_map/ppermute | solution.py:49
  44.6 1.3 %collective-permute-start.12 = (f32[8,256]{1,0:T(8,128)S(1)}, f32[8,256]{1,0:T(8,128)S(1)}, u32[]{:S(2)}, u32[]{:S(2)}) collective-permute-start(f32[8,256]{1,0:T(8,128)S(1)} %merge.2.refs_0_), channel_id=1, source_target_pairs={{0,8},{1,9},{2,10},{3,11},{4,12},{5,13},{6,14},{7,15},{8,0},{9,1},... | collective-permute-start | bytes 24584 | tf_op jit(solution)/shard_map/ppermute | solution.py:49
  45.9 2.1 %collective-permute-start.13 = (f32[8,256]{1,0:T(8,128)S(1)}, f32[8,256]{1,0:T(8,128)S(1)}, u32[]{:S(2)}, u32[]{:S(2)}) collective-permute-start(f32[8,256]{1,0:T(8,128)S(1)} %merge.2.refs_0_), channel_id=1, source_target_pairs={{0,12},{1,13},{2,14},{3,15},{4,8},{5,9},{6,10},{7,11},{8,4},{9,5},... | collective-permute-start | bytes 24584 | tf_op jit(solution)/shard_map/ppermute | solution.py:49
  48.0 1.2 %collective-permute-done.12.refs_2_ = f32[8,256]{1,0:T(8,128)S(1)} collective-permute-done((f32[8,256]{1,0:T(8,128)S(1)}, f32[8,256]{1,0:T(8,128)S(1)}, u32[]{:S(2)}, u32[]{:S(2)}) %collective-permute-start.12) | collective-permute-done | bytes 8224 | tf_op jit(solution)/shard_map/ppermute | solution.py:49
  49.2 2.2 %collective-permute-done.13.refs_3_ = f32[8,256]{1,0:T(8,128)S(1)} collective-permute-done((f32[8,256]{1,0:T(8,128)S(1)}, f32[8,256]{1,0:T(8,128)S(1)}, u32[]{:S(2)}, u32[]{:S(2)}) %collective-permute-start.13) | collective-permute-done | bytes 8224 | tf_op jit(solution)/shard_map/ppermute | solution.py:49
  51.5 0.7 %multiply_subtract_fusion = f32[256,256]{1,0:T(8,128)} fusion(f32[256,256]{1,0:T(8,128)S(1)} %rest.1.image, f32[256,256]{1,0:T(8,128)S(1)} %copy-done, f32[256]{0:T(256)S(1)} %bitcast.11, f32[256]{0:T(256)S(1)} %bitcast.10), kind=kLoop, calls=%fused_computation | loop fusion | flops 196608 | bytes 788480 | tf_op jit(solution)/shard_map/sub | solution.py:262
  (31 shorter events, 4.4 us)
Async XLA Ops:
  0.1 0.7 %copy-start.3 = (s32[1,8]{1,0:T(1,128)S(1)}, s32[1,8]{1,0:T(1,128)}, u32[]{:S(2)}) copy-start(s32[1,8]{1,0:T(1,128)} %send.5) | copy-start | bytes 100
  0.1 0.7 %copy-start.4 = (s32[1,8]{1,0:T(1,128)S(1)}, s32[1,8]{1,0:T(1,128)}, u32[]{:S(2)}) copy-start(s32[1,8]{1,0:T(1,128)} %rows.5) | copy-start | bytes 100
  2.6 15.3 %collective-permute-start.2 = (f32[392,256]{1,0:T(8,128)S(1)}, f32[392,256]{1,0:T(8,128)S(1)}, u32[]{:S(2)}, u32[]{:S(2)}) collective-permute-start(f32[392,256]{1,0:T(8,128)S(1)} %get-tuple-element.15.packed), channel_id=1, source_target_pairs={{0,4},{4,8},{8,12},{12,0},{1,5},{5,9},{9,13},{13,1},{2,6},{6,10},{... | collective-permute-start | bytes 1204232 | tf_op jit(solution)/shard_map/ppermute | solution.py:238
  5.7 3.7 %copy-start.6 = (f32[256]{0:T(256)S(1)}, f32[256]{0:T(256)}, u32[]{:S(2)}) copy-start(f32[256]{0:T(256)} %param.8) | copy-start | bytes 3076
  5.7 12.2 %collective-permute-start.3 = (f32[392,256]{1,0:T(8,128)S(1)}, f32[392,256]{1,0:T(8,128)S(1)}, u32[]{:S(2)}, u32[]{:S(2)}) collective-permute-start(f32[392,256]{1,0:T(8,128)S(1)} %get-tuple-element.18), channel_id=1, source_target_pairs={{0,2},{2,0},{1,3},{3,1},{4,6},{6,4},{5,7},{7,5},{8,10},{10,8},{9,1... | collective-permute-start | bytes 1204232 | tf_op jit(solution)/shard_map/ppermute | solution.py:238
  7.2 18.4 %collective-permute-start.4 = (f32[392,256]{1,0:T(8,128)S(1)}, f32[392,256]{1,0:T(8,128)S(1)}, u32[]{:S(2)}, u32[]{:S(2)}) collective-permute-start(f32[392,256]{1,0:T(8,128)S(1)} %get-tuple-element.20), channel_id=1, source_target_pairs={{4,0},{8,4},{12,8},{0,12},{5,1},{9,5},{13,9},{1,13},{6,2},{10,6},{... | collective-permute-start | bytes 1204232 | tf_op jit(solution)/shard_map/ppermute | solution.py:238
  9.4 0.7 %copy-start.5 = (s32[2,7]{1,0:T(2,128)S(1)}, s32[2,7]{1,0:T(2,128)}, u32[]{:S(2)}) copy-start(s32[2,7]{1,0:T(2,128)} %cols.1) | copy-start | bytes 172
  10.1 1.2 %copy-start.2 = (f32[2,7,128,128]{3,2,1,0:T(8,128)S(1)}, f32[2,7,128,128]{3,2,1,0:T(8,128)}, u32[]{:S(2)}) copy-start(f32[2,7,128,128]{3,2,1,0:T(8,128)} %local.1) | copy-start | bytes 2752516
  11.3 1.2 %copy-start = (f32[256,256]{1,0:T(8,128)S(1)}, f32[256,256]{1,0:T(8,128)}, u32[]{:S(2)}) copy-start(f32[256,256]{1,0:T(8,128)} %field.7) | copy-start | bytes 786436
  11.3 6.6 %copy-start.1 = (f32[1,8,128,128]{3,2,1,0:T(8,128)S(1)}, f32[1,8,128,128]{3,2,1,0:T(8,128)}, u32[]{:S(2)}) copy-start(f32[1,8,128,128]{3,2,1,0:T(8,128)} %param.11) | copy-start | bytes 1572868
  12.4 1.6 %collective-permute-start.1 = (f32[256,256]{1,0:T(8,128)S(1)}, f32[256,256]{1,0:T(8,128)S(1)}, u32[]{:S(2)}, u32[]{:S(2)}) collective-permute-start(f32[256,256]{1,0:T(8,128)S(1)} %get-tuple-element.17.pair), channel_id=1, source_target_pairs={{0,1},{1,0},{2,3},{3,2},{4,5},{5,4},{6,7},{7,6},{8,9},{9,8},{10,11... | collective-permute-start | bytes 786440 | tf_op jit(solution)/shard_map/ppermute | solution.py:243
  12.5 1.9 %collective-permute-start = (f32[256,256]{1,0:T(8,128)S(1)}, f32[256,256]{1,0:T(8,128)S(1)}, u32[]{:S(2)}, u32[]{:S(2)}) collective-permute-start(f32[256,256]{1,0:T(8,128)S(1)} %copy-done), channel_id=1, source_target_pairs={{0,1},{1,0},{2,3},{3,2},{4,5},{5,4},{6,7},{7,6},{8,9},{9,8},{10,11... | collective-permute-start | bytes 786440 | tf_op jit(solution)/shard_map/ppermute | solution.py:239
  26.7 2.2 %collective-permute-start.5 = (f32[256,256]{1,0:T(8,128)S(1)}, f32[256,256]{1,0:T(8,128)S(1)}, u32[]{:S(2)}, u32[]{:S(2)}) collective-permute-start(f32[256,256]{1,0:T(8,128)S(1)} %rest.1.image), channel_id=1, source_target_pairs={{0,1},{1,0},{2,3},{3,2},{4,5},{5,4},{6,7},{7,6},{8,9},{9,8},{10,11... | collective-permute-start | bytes 786440 | tf_op jit(solution)/shard_map/ppermute | solution.py:252
  26.8 10.7 %collective-permute-start.6 = (f32[256,256]{1,0:T(8,128)S(1)}, f32[256,256]{1,0:T(8,128)S(1)}, u32[]{:S(2)}, u32[]{:S(2)}) collective-permute-start(f32[256,256]{1,0:T(8,128)S(1)} %rest.1.image), channel_id=1, source_target_pairs={{0,4},{4,8},{8,12},{12,0},{1,5},{5,9},{9,13},{13,1},{2,6},{6,10},{... | collective-permute-start | bytes 786440 | tf_op jit(solution)/shard_map/ppermute | solution.py:251
  27.4 10.1 %collective-permute-start.7 = (f32[256,256]{1,0:T(8,128)S(1)}, f32[256,256]{1,0:T(8,128)S(1)}, u32[]{:S(2)}, u32[]{:S(2)}) collective-permute-start(f32[256,256]{1,0:T(8,128)S(1)} %rest.1.image), channel_id=1, source_target_pairs={{0,2},{2,0},{1,3},{3,1},{4,6},{6,4},{5,7},{7,5},{8,10},{10,8},{9,1... | collective-permute-start | bytes 786440 | tf_op jit(solution)/shard_map/ppermute | solution.py:251
  38.2 3.2 %collective-permute-start.10 = (f32[8,256]{1,0:T(8,128)S(1)}, f32[8,256]{1,0:T(8,128)S(1)}, u32[]{:S(2)}, u32[]{:S(2)}) collective-permute-start(f32[8,256]{1,0:T(8,128)S(1)} %far.1.refs_0_), channel_id=1, source_target_pairs={{0,3},{1,2},{2,1},{3,0},{4,7},{5,6},{6,5},{7,4},{8,11},{9,10},{10,... | collective-permute-start | bytes 24584 | tf_op jit(solution)/shard_map/ppermute | solution.py:49
  39.2 2.2 %collective-permute-start.8 = (f32[8,256]{1,0:T(8,128)S(1)}, f32[8,256]{1,0:T(8,128)S(1)}, u32[]{:S(2)}, u32[]{:S(2)}) collective-permute-start(f32[8,256]{1,0:T(8,128)S(1)} %far.1.refs_0_), channel_id=1, source_target_pairs={{0,1},{1,0},{2,3},{3,2},{4,5},{5,4},{6,7},{7,6},{8,9},{9,8},{10,11... | collective-permute-start | bytes 24584 | tf_op jit(solution)/shard_map/ppermute | solution.py:49
  39.9 3.7 %collective-permute-start.9 = (f32[8,256]{1,0:T(8,128)S(1)}, f32[8,256]{1,0:T(8,128)S(1)}, u32[]{:S(2)}, u32[]{:S(2)}) collective-permute-start(f32[8,256]{1,0:T(8,128)S(1)} %far.1.refs_0_), channel_id=1, source_target_pairs={{0,2},{1,3},{2,0},{3,1},{4,6},{5,7},{6,4},{7,5},{8,10},{9,11},{10,... | collective-permute-start | bytes 24584 | tf_op jit(solution)/shard_map/ppermute | solution.py:49
  43.6 4.5 %collective-permute-start.11 = (f32[8,256]{1,0:T(8,128)S(1)}, f32[8,256]{1,0:T(8,128)S(1)}, u32[]{:S(2)}, u32[]{:S(2)}) collective-permute-start(f32[8,256]{1,0:T(8,128)S(1)} %merge.2.refs_0_), channel_id=1, source_target_pairs={{0,4},{1,5},{2,6},{3,7},{4,0},{5,1},{6,2},{7,3},{8,12},{9,13},{10,... | collective-permute-start | bytes 24584 | tf_op jit(solution)/shard_map/ppermute | solution.py:49
  44.6 4.5 %collective-permute-start.12 = (f32[8,256]{1,0:T(8,128)S(1)}, f32[8,256]{1,0:T(8,128)S(1)}, u32[]{:S(2)}, u32[]{:S(2)}) collective-permute-start(f32[8,256]{1,0:T(8,128)S(1)} %merge.2.refs_0_), channel_id=1, source_target_pairs={{0,8},{1,9},{2,10},{3,11},{4,12},{5,13},{6,14},{7,15},{8,0},{9,1},... | collective-permute-start | bytes 24584 | tf_op jit(solution)/shard_map/ppermute | solution.py:49
  45.9 5.4 %collective-permute-start.13 = (f32[8,256]{1,0:T(8,128)S(1)}, f32[8,256]{1,0:T(8,128)S(1)}, u32[]{:S(2)}, u32[]{:S(2)}) collective-permute-start(f32[8,256]{1,0:T(8,128)S(1)} %merge.2.refs_0_), channel_id=1, source_target_pairs={{0,12},{1,13},{2,14},{3,15},{4,8},{5,9},{6,10},{7,11},{8,4},{9,5},... | collective-permute-start | bytes 24584 | tf_op jit(solution)/shard_map/ppermute | solution.py:49

commit v6 on v5

v6 whole, which is shorter than its diff:
```python
from functools import partial

import jax
import jax.numpy as jnp
from jax import lax
from jax.experimental import pallas as pl
from jax.experimental.pallas import tpu as pltpu
from jax.sharding import PartitionSpec as P

F32 = jnp.float32
BF16 = jnp.bfloat16
AXES = ("gx", "gy", "nd")
SIDE = 2
LIMIT = 8 << 20
TAIL = 8


def vmem():
    return pl.BlockSpec(memory_space=pltpu.VMEM)


def call(kernel, name, shapes, scratch=(), flops=None):
    def run(*args):
        args = [pltpu.with_memory_space_constraint(a, pltpu.VMEM) for a in args]
        return pl.pallas_call(
            kernel,
            name=name,
            in_specs=[vmem()] * len(args),
            out_specs=[vmem()] * len(shapes),
            out_shape=[pltpu.VMEM(shape, F32) for shape in shapes],
            scratch_shapes=scratch,
            compiler_params=pltpu.CompilerParams(vmem_limit_bytes=LIMIT),
            cost_estimate=flops and pl.CostEstimate(flops=flops, bytes_accessed=1 << 20, transcendentals=0),
        )(*args)

    return run


def join(state):
    count = lax.axis_size(AXES)
    assert count & (count - 1) == 0
    step = 1
    while step < count:
        masks = [m * step for m in (1, 2, 3) if m * step < count]
        others = [lax.ppermute(state, AXES, [(i, i ^ m) for i in range(count)]) for m in masks]
        (state,) = call(merge_kernel, "merge", [state.shape])(state, *others)
        step *= 4
    return state


def split(a):
    high = a.astype(BF16)
    return high, (a - high.astype(F32)).astype(BF16)


def dot(a, b):
    (ah, al), (bh, bl) = split(a), split(b)
    mul = partial(jnp.dot, preferred_element_type=F32)
    return mul(ah, bh) + (mul(ah, bl) + mul(al, bh))


def col_sum(a, b):
    return jnp.sum(a * b, axis=0, keepdims=True)


def stack_rows(rows, shape):
    line = lax.broadcasted_iota(jnp.int32, shape, 0)
    return sum(jnp.where(line == n, row, 0.0) for n, row in rows)


def pack_kernel(gives, marks, field, border, send, rows, *refs):
    *pays, sems, table, table_sems = refs
    width = field.shape[0]
    bs = border.shape[1]
    tables = [pltpu.make_async_copy(ref, table.at[n], table_sems.at[n]) for n, ref in enumerate((rows, send))]
    copies = []
    for n, pay in enumerate(pays):
        give = marks[0] if gives[n] is None else gives[n]
        copies.append(pltpu.make_async_copy(field, pay.at[pl.ds(0, width), :], sems.at[n, SIDE]))
        for s in range(SIDE):
            block = pay.at[pl.ds(width, bs), pl.ds(s * bs, bs)]
            copies.append(pltpu.make_async_copy(border.at[give * SIDE + s], block, sems.at[n, s]))
    for copy in tables + copies:
        copy.start()
    for copy in tables:
        copy.wait()
    count = table.shape[2]
    for pay in pays:
        for n in range(2):
            pay[pl.ds(width + bs + n, 1), pl.ds(0, count)] = table[n].astype(F32)
    for copy in copies:
        copy.wait()


def prep_kernel(cols, marks, diag, local, packed, own, pair):
    nblocks, nonzeros, bs, _ = local.shape
    width = nblocks * bs
    patch_len = 2 * nblocks
    base = marks[1] * nblocks
    own[...] = jnp.zeros((width, width), F32)
    pair[...] = jnp.zeros((width, width), F32)
    for b in range(nblocks):
        for k in range(nonzeros):
            spot = lax.rem(cols[b, k] - base + patch_len, patch_len)
            block = local[b, k]
            for c in range(nblocks):

                @pl.when(spot == c)
                def _():
                    own[pl.ds(b * bs, bs), pl.ds(c * bs, bs)] += block

                @pl.when(spot == c + nblocks)
                def _():
                    pair[pl.ds(b * bs, bs), pl.ds(c * bs, bs)] += block

    lower = own[...]
    here = lax.broadcasted_iota(jnp.int32, (width, width), 0)
    there = lax.broadcasted_iota(jnp.int32, (width, width), 1)
    own[...] = lower + lower.T + jnp.where(here == there, diag[...], 0.0)


def edge(take, mine, pay, border):
    bs = border.shape[1]
    width = pay.shape[0] - bs - TAIL
    options = [take] if isinstance(take, int) else [2, 3]

    def number(ref, line, flip, s):
        at = [(t ^ flip) * SIDE + s for t in options]
        found = [ref[pl.ds(width + bs + line, 1), pl.ds(i, 1)] for i in at]
        return found[0] if len(found) == 1 else jnp.where(take == options[0], found[0], found[1])

    blocks = [[0.0] * (width // bs) for _ in range(width // bs)]
    for s in range(SIDE):
        pairs = [
            (border[take * SIDE + s], number(mine, 0, 0, s), number(pay, 1, 0, s)),
            (pay[pl.ds(width, bs), pl.ds(s * bs, bs)].T, number(mine, 1, 1, s), number(pay, 0, 1, s)),
        ]
        for block, to, at in pairs:
            for i, line in enumerate(blocks):
                for j in range(len(line)):
                    line[j] = line[j] + jnp.where((to == i) & (at == j), block, 0.0)
    return jnp.concatenate([jnp.concatenate(line, axis=1) for line in blocks], axis=0)


def base_kernel(mine, own, pair, mate, mate_pair, image, coup):
    width = mate.shape[0]
    coup[...] = pair[...] + mate_pair[...].T
    image[...] = dot(own[...], mine[pl.ds(0, width), :]) + dot(coup[...], mate[...])


def left_kernel(mine, part, border, pay, image, once, coup):
    width = part.shape[0]
    coup[...] = edge(0, mine, pay, border)
    term = dot(coup[...], pay[pl.ds(0, width), :])
    image[...] = part[...] + term
    once[...] = part[...] + 2.0 * term


def gy_kernel(take, weight, marks, mine, part, single, border, pay, image, once, coup):
    width = part.shape[0]
    coup[...] = edge(marks[0] if take is None else take, mine, pay, border)
    term = dot(coup[...], pay[pl.ds(0, width), :])
    image[...] = part[...] + term
    once[...] = single[...] + weight * term


def right_kernel(mine, part, border, pay, image):
    width = part.shape[0]
    image[...] = part[...] + dot(edge(1, mine, pay, border), pay[pl.ds(0, width), :])


def near_kernel(field, image, once, mate, mate_w, own, coup, part, state):
    b = field[...]
    norm = col_sum(b, b)
    c = jnp.where(norm > 0.0, col_sum(b, image[...]) / jnp.where(norm > 0.0, norm, 1.0), 0.0)
    g = image[...] - c * b
    part[...] = dot(own[...], g) + dot(coup[...], mate_w[...] - c * mate[...])
    rows = [(0, norm), (1, c), (2, col_sum(g, g)), (4, -col_sum(g, once[...])), (5, col_sum(b, once[...]))]
    state[...] = stack_rows(rows, state.shape)


def far_kernel(weights, field, image, part, near, *refs):
    count = len(weights)
    coups, pays, fars, state = refs[:count], refs[count : 2 * count], refs[2 * count : -1], refs[-1]
    width = field.shape[0]
    b = field[...]
    c = near[1:2, :]
    acc = part[...]
    for weight, coup, pay, far in zip(weights, coups, pays, fars):
        acc += weight * dot(coup[...], far[...] - c * pay[pl.ds(0, width), :])
    state[...] = near[...] + stack_rows([(3, col_sum(image[...] - c * b, acc)), (4, -col_sum(b, acc))], state.shape)


def merge_kernel(*refs):
    *states, out = refs
    norm = sum(s[0:1, :] for s in states)
    base = states[0][1:2, :]
    shift = sum(s[0:1, :] * (s[1:2, :] - base) for s in states)
    c = base + jnp.where(norm > 0.0, shift / jnp.where(norm > 0.0, norm, 1.0), 0.0)
    size, flat, slope, bend = (jnp.zeros_like(c) for _ in range(4))
    for s in states:
        d = c - s[1:2, :]
        size += s[2:3, :] + s[0:1, :] * d * d
        flat += s[3:4, :] + (s[4:5, :] + s[5:6, :] * d) * d
        slope += s[4:5, :] + 2.0 * s[5:6, :] * d
        bend += s[5:6, :]
    out[...] = stack_rows(list(enumerate([norm, c, size, flat, slope, bend])), out.shape)


def shards(right_side, node_diag, local_coup, block_cols, border_coup, border_send, border_rows):
    width, ncols = right_side.shape
    nblocks, _, bs, _ = local_coup.shape
    n_gx, n_gy, n_nd = (lax.axis_size(a) for a in AXES)
    assert n_nd == 2 and border_coup.shape[1] == 4 * SIDE
    swap = [(0, 1), (1, 0)]
    right = [(i, (i + 1) % n_gx) for i in range(n_gx)]
    left = [(j, i) for i, j in right]
    up = [(i, i + 1) for i in range(n_gy - 1)]
    down = [(j, i) for i, j in up]
    facing = jnp.where(lax.axis_index("gy") == 0, 3, 2).astype(jnp.int32)
    if n_gy == 2:
        sides = [(swap, None, 1.0)]
    elif n_gy > 2:
        sides = [(up, 2, 2.0), (down, 3, 0.0)]
    else:
        sides = []
    sends = [("gx", right), ("gx", left)] + [("gy", perm) for perm, _, _ in sides]
    gives = [1, 0] + [None if t is None else t ^ 1 for _, t, _ in sides]
    marks = jnp.stack([facing, lax.axis_index("nd").astype(jnp.int32)])
    border = border_coup[0]

    def smem(n):
        return [pl.BlockSpec(memory_space=pltpu.SMEM)] * n

    pay_shape = (width + bs + TAIL, ncols)
    nsends = len(sends)
    packed = pl.pallas_call(
        partial(pack_kernel, gives),
        name="pack",
        in_specs=smem(1) + [pl.BlockSpec(memory_space=pl.ANY)] * 4,
        out_specs=[vmem()] * nsends,
        out_shape=[pltpu.VMEM(pay_shape, F32)] * nsends,
        scratch_shapes=[
            pltpu.SemaphoreType.DMA((nsends, SIDE + 1)),
            pltpu.VMEM((2, 1, 4 * SIDE), jnp.int32),
            pltpu.SemaphoreType.DMA((2,)),
        ],
        compiler_params=pltpu.CompilerParams(vmem_limit_bytes=LIMIT),
    )(marks, *[pltpu.with_memory_space_constraint(a, pltpu.HBM) for a in (right_side, border, border_send, border_rows)])
    pays = [lax.ppermute(pay, axis, perm) for pay, (axis, perm) in zip(packed, sends)]
    mine = packed[0]
    mate = lax.ppermute(right_side, "nd", swap)

    def tabled(kernel, name, tables, shapes, flops=None):
        def run(*args):
            args = list(args[:tables]) + [pltpu.with_memory_space_constraint(a, pltpu.VMEM) for a in args[tables:]]
            return pl.pallas_call(
                kernel,
                name=name,
                in_specs=smem(tables) + [vmem()] * (len(args) - tables),
                out_specs=[vmem()] * len(shapes),
                out_shape=[pltpu.VMEM(shape, F32) for shape in shapes],
                compiler_params=pltpu.CompilerParams(vmem_limit_bytes=LIMIT),
                cost_estimate=flops and pl.CostEstimate(flops=flops, bytes_accessed=1 << 20, transcendentals=0),
            )(*args)

        return run

    field, square = (width, ncols), (width, width)
    own, pair = tabled(prep_kernel, "prep", 2, [square] * 2, 1 << 24)(
        block_cols, marks, node_diag.reshape(1, width), local_coup, mine
    )
    mate_pair = lax.ppermute(pair, "nd", swap)

    part, coup = call(base_kernel, "base", [field, square])(mine, own, pair, mate, mate_pair)
    part, once, left_coup = call(left_kernel, "left", [field, field, square])(mine, part, border, pays[0])
    side_coup = []
    for (_, take, weight), pay in zip(sides, pays[2:]):
        part, once, block = tabled(partial(gy_kernel, take, weight), "gy", 1, [field, field, square])(
            marks, mine, part, once, border, pay
        )
        side_coup.append(block)
    (image,) = call(right_kernel, "right", [field])(mine, part, border, pays[1])

    used = [(2.0, left_coup, pays[0], ("gx", right))]
    if sides:
        used.append((sides[0][2], side_coup[0], pays[2], ("gy", sides[0][0])))
    weights, coups, near_b, perms = zip(*used)
    fars = [lax.ppermute(image, axis, perm) for axis, perm in perms]
    mate_w = lax.ppermute(image, "nd", swap)
    part, state = call(near_kernel, "near", [field, (TAIL, ncols)])(right_side, image, once, mate, mate_w, own, coup)
    (state,) = call(partial(far_kernel, weights), "far", [(TAIL, ncols)])(
        right_side, image, part, state, *coups, *near_b, *fars
    )
    norm, c, size, form = (row[None] for row in join(state)[:4])
    ratio = size / (c * c * norm)
    last = size / (form - ratio * ratio * c * c * c * norm)
    return ((1.0 + last * c * (1.0 + ratio)) / c) * right_side - (last / c) * image


def solution(mesh):
    blocks = P(("var", "gx", "gy", "nd"))
    tables = P(AXES)
    in_specs = (blocks, blocks, blocks, tables, blocks, tables, tables)
    return jax.shard_map(shards, mesh=mesh, in_specs=in_specs, out_specs=blocks, check_vma=False)
```

time: 52.4 us -> 48.4 us (0.924)
  Pallas kernels: 7.58 us -> 6.17 us
  local copies, waits for them, and re-layouts: 2.54 us -> 1.19 us
  waiting for transfers between devices: 24.9 us -> 23.9 us
    ppermute x6, waiting for transfers between devices: 6.47 us -> 3.68 us  [join(): lax.ppermute(state, AXES, [(i, i ^ m) for i in range(count)])]
    pallas_call x8 -> x10, Pallas kernels: 7.58 us -> 6.17 us  [the longest x7 2.23 us: run(): pl.pallas_call(kernel, name=name, in_specs=[vmem()] * len(args), out_spec...]
    unnamed x14 -> x10, local copies, waits for them, and re-layouts: 2.54 us -> 1.19 us
    ppermute x3, waiting for transfers between devices: 9.29 us -> 10.3 us  [shards(): lax.ppermute(pay, axis, perm)]
    ppermute x2, waiting for transfers between devices: 7.78 us -> 8.75 us  [shards(): fars = [lax.ppermute(image, axis, perm) for axis, perm in perms]]
where the time goes in v6:
time: 48.4 us; the launch traced here: 48.2 us
  waiting for transfers between devices  23.9 us (49%)
  starting transfers between devices  15.9 us (33%)
  Pallas kernels  6.17 us (13%)
  local copies, waits for them, and re-layouts  1.19 us (2%)
  other arithmetic  0.85 us (2%)
    ppermute x3, waiting for transfers between devices, shards(): lax.ppermute(pay, axis, perm)  10.3 us
    ppermute x2, waiting for transfers between devices, shards(): fars = [lax.ppermute(image, axis, perm) for axis, perm in perms]  8.75 us
    ppermute x3, starting transfers between devices, shards(): lax.ppermute(pay, axis, perm)  6.81 us
    ppermute x6, starting transfers between devices, join(): lax.ppermute(state, AXES, [(i, i ^ m) for i in range(count)])  6.37 us
    ppermute x6, waiting for transfers between devices, join(): lax.ppermute(state, AXES, [(i, i ^ m) for i in range(count)])  3.68 us
    pallas_call x7, Pallas kernels, run(): pl.pallas_call(kernel, name=name, in_specs=[vmem()] * len(args), out_spec...  2.23 us
    ppermute x2, starting transfers between devices, shards(): fars = [lax.ppermute(image, axis, perm) for axis, perm in perms]  2.12 us
    pallas_call x2, Pallas kernels, run(): pl.pallas_call(kernel, name=name, in_specs=smem(tables) + [vmem()] * (len...  2.08 us
  transfers between devices with their start and end apart: 14, of which 9 were waited for; matrix products, arithmetic and copies ran while one was open for 0% of the time, Pallas kernels for 7%

profile of v6, /device:TPU:0, one launch (start us, length us, event | category | flops | bytes accessed | tf_op | source)
XLA Modules:
  0.0 48.2 jit_solution(405499165781837590)
XLA Ops:
  0.1 1.9 %pack.1 = (f32[392,256]{1,0:T(8,128)S(1)}, f32[392,256]{1,0:T(8,128)S(1)}, f32[392,256]{1,0:T(8,128)S(1)}) custom-call(s32[2]{0:T(128)S(1)} %pad_add_fusion.marks, f32[256,256]{1,0:T(8,128)} %field.5, f32[8,128,128]{2,1,0:T(8,128)} %bitcast.6, s32[1,8]{1,0:T(1,128)} %send.1, s32[1,8]{1,0:T(1,128)} %rows.1), custom_call_target="tpu_custom_call" | custom-call | tf_op jit(solution)/shard_map/pack/pallas_call | solution.py:237
  1.9 3.1 %collective-permute-start.2 = (f32[392,256]{1,0:T(8,128)S(1)}, f32[392,256]{1,0:T(8,128)S(1)}, u32[]{:S(2)}, u32[]{:S(2)}) collective-permute-start(f32[392,256]{1,0:T(8,128)S(1)} %get-tuple-element.20.packed.mine), channel_id=1, source_target_pairs={{0,4},{4,8},{8,12},{12,0},{1,5},{5,9},{9,13},{13,1},{2,6},{6,10},{... | collective-permute-start | bytes 1204232 | tf_op jit(solution)/shard_map/ppermute | solution.py:250
  5.0 1.5 %collective-permute-start.3 = (f32[392,256]{1,0:T(8,128)S(1)}, f32[392,256]{1,0:T(8,128)S(1)}, u32[]{:S(2)}, u32[]{:S(2)}) collective-permute-start(f32[392,256]{1,0:T(8,128)S(1)} %get-tuple-element.26), channel_id=1, source_target_pairs={{0,2},{2,0},{1,3},{3,1},{4,6},{6,4},{5,7},{7,5},{8,10},{10,8},{9,1... | collective-permute-start | bytes 1204232 | tf_op jit(solution)/shard_map/ppermute | solution.py:250
  6.5 2.2 %collective-permute-start.4 = (f32[392,256]{1,0:T(8,128)S(1)}, f32[392,256]{1,0:T(8,128)S(1)}, u32[]{:S(2)}, u32[]{:S(2)}) collective-permute-start(f32[392,256]{1,0:T(8,128)S(1)} %get-tuple-element.28), channel_id=1, source_target_pairs={{4,0},{8,4},{12,8},{0,12},{5,1},{9,5},{13,9},{1,13},{6,2},{10,6},{... | collective-permute-start | bytes 1204232 | tf_op jit(solution)/shard_map/ppermute | solution.py:250
  8.8 1.2 %copy-done.2 = f32[2,7,128,128]{3,2,1,0:T(8,128)S(1)} copy-done((f32[2,7,128,128]{3,2,1,0:T(8,128)S(1)}, f32[2,7,128,128]{3,2,1,0:T(8,128)}, u32[]{:S(2)}) %copy-start.2) | copy-done | bytes 917528
  10.0 1.1 %prep.1 = (f32[256,256]{1,0:T(8,128)S(1)}, f32[256,256]{1,0:T(8,128)S(1)}) custom-call(s32[2,7]{1,0:T(2,128)S(1)} %copy-done.3, s32[2]{0:T(128)S(1)} %pad_add_fusion.marks, f32[1,256]{1,0:T(1,128)S(1)} %bitcast.10, f32[2,7,128,128]{3,2,1,0:T(8,128)S(1)} %copy-done.2, f32[392,256]{1,0:T(8,128)S(1)} %get-tuple-element.20.packed.mine), custom_call_target="tpu_custom_call" | custom-call | flops 16777216 | bytes 1048576 | tf_op jit(solution)/shard_map/prep/pallas_call | solution.py:257
  11.1 0.6 %collective-permute-start.1 = (f32[256,256]{1,0:T(8,128)S(1)}, f32[256,256]{1,0:T(8,128)S(1)}, u32[]{:S(2)}, u32[]{:S(2)}) collective-permute-start(f32[256,256]{1,0:T(8,128)S(1)} %get-tuple-element.22.pair), channel_id=1, source_target_pairs={{0,1},{1,0},{2,3},{3,2},{4,5},{5,4},{6,7},{7,6},{8,9},{9,8},{10,11... | collective-permute-start | bytes 786440 | tf_op jit(solution)/shard_map/ppermute | solution.py:273
  11.6 1.2 %collective-permute-done.1.mate_pair = f32[256,256]{1,0:T(8,128)S(1)} collective-permute-done((f32[256,256]{1,0:T(8,128)S(1)}, f32[256,256]{1,0:T(8,128)S(1)}, u32[]{:S(2)}, u32[]{:S(2)}) %collective-permute-start.1) | collective-permute-done | bytes 262176 | tf_op jit(solution)/shard_map/ppermute | solution.py:273
  13.2 4.0 %collective-permute-done.2.pay.refs_2_ = f32[392,256]{1,0:T(8,128)S(1)} collective-permute-done((f32[392,256]{1,0:T(8,128)S(1)}, f32[392,256]{1,0:T(8,128)S(1)}, u32[]{:S(2)}, u32[]{:S(2)}) %collective-permute-start.2) | collective-permute-done | bytes 401440 | tf_op jit(solution)/shard_map/ppermute | solution.py:250
  17.6 1.0 %gy.1 = (f32[256,256]{1,0:T(8,128)S(1)}, f32[256,256]{1,0:T(8,128)S(1)}, f32[256,256]{1,0:T(8,128)S(1)}) custom-call(s32[2]{0:T(128)S(1)} %pad_add_fusion.marks, f32[392,256]{1,0:T(8,128)S(1)} %get-tuple-element.20.packed.mine, f32[256,256]{1,0:T(8,128)S(1)} %get-tuple-element.24.part, f32[256,256]{1,0:T(8,128)S(1)} %get-tuple-element.25.single, ...), custom_call_target="tpu_custom_call" | custom-call | tf_op jit(solution)/shard_map/gy/pallas_call | solution.py:257
  18.6 6.3 %collective-permute-done.4.pay = f32[392,256]{1,0:T(8,128)S(1)} collective-permute-done((f32[392,256]{1,0:T(8,128)S(1)}, f32[392,256]{1,0:T(8,128)S(1)}, u32[]{:S(2)}, u32[]{:S(2)}) %collective-permute-start.4) | collective-permute-done | bytes 401440 | tf_op jit(solution)/shard_map/ppermute | solution.py:250
  25.4 1.3 %collective-permute-start.7 = (f32[256,256]{1,0:T(8,128)S(1)}, f32[256,256]{1,0:T(8,128)S(1)}, u32[]{:S(2)}, u32[]{:S(2)}) collective-permute-start(f32[256,256]{1,0:T(8,128)S(1)} %right.1.image), channel_id=1, source_target_pairs={{0,2},{2,0},{1,3},{3,1},{4,6},{6,4},{5,7},{7,5},{8,10},{10,8},{9,1... | collective-permute-start | bytes 786440 | tf_op jit(solution)/shard_map/ppermute | solution.py:289
  26.6 0.9 %collective-permute-start.6 = (f32[256,256]{1,0:T(8,128)S(1)}, f32[256,256]{1,0:T(8,128)S(1)}, u32[]{:S(2)}, u32[]{:S(2)}) collective-permute-start(f32[256,256]{1,0:T(8,128)S(1)} %right.1.image), channel_id=1, source_target_pairs={{0,4},{4,8},{8,12},{12,0},{1,5},{5,9},{9,13},{13,1},{2,6},{6,10},{... | collective-permute-start | bytes 786440 | tf_op jit(solution)/shard_map/ppermute | solution.py:289
  28.1 6.0 %collective-permute-done.7.refs_5_ = f32[256,256]{1,0:T(8,128)S(1)} collective-permute-done((f32[256,256]{1,0:T(8,128)S(1)}, f32[256,256]{1,0:T(8,128)S(1)}, u32[]{:S(2)}, u32[]{:S(2)}) %collective-permute-start.7) | collective-permute-done | bytes 262176 | tf_op jit(solution)/shard_map/ppermute | solution.py:289
  34.1 2.7 %collective-permute-done.6.refs_4_ = f32[256,256]{1,0:T(8,128)S(1)} collective-permute-done((f32[256,256]{1,0:T(8,128)S(1)}, f32[256,256]{1,0:T(8,128)S(1)}, u32[]{:S(2)}, u32[]{:S(2)}) %collective-permute-start.6) | collective-permute-done | bytes 262176 | tf_op jit(solution)/shard_map/ppermute | solution.py:289
  37.4 1.0 %collective-permute-start.9 = (f32[8,256]{1,0:T(8,128)S(1)}, f32[8,256]{1,0:T(8,128)S(1)}, u32[]{:S(2)}, u32[]{:S(2)}) collective-permute-start(f32[8,256]{1,0:T(8,128)S(1)} %far.1.refs_0_), channel_id=1, source_target_pairs={{0,2},{1,3},{2,0},{3,1},{4,6},{5,7},{6,4},{7,5},{8,10},{9,11},{10,... | collective-permute-start | bytes 24584 | tf_op jit(solution)/shard_map/ppermute | solution.py:45
  38.3 0.9 %collective-permute-start.8 = (f32[8,256]{1,0:T(8,128)S(1)}, f32[8,256]{1,0:T(8,128)S(1)}, u32[]{:S(2)}, u32[]{:S(2)}) collective-permute-start(f32[8,256]{1,0:T(8,128)S(1)} %far.1.refs_0_), channel_id=1, source_target_pairs={{0,1},{1,0},{2,3},{3,2},{4,5},{5,4},{6,7},{7,6},{8,9},{9,8},{10,11... | collective-permute-start | bytes 24584 | tf_op jit(solution)/shard_map/ppermute | solution.py:45
  39.2 1.2 %collective-permute-done.10.refs_3_ = f32[8,256]{1,0:T(8,128)S(1)} collective-permute-done((f32[8,256]{1,0:T(8,128)S(1)}, f32[8,256]{1,0:T(8,128)S(1)}, u32[]{:S(2)}, u32[]{:S(2)}) %collective-permute-start.10) | collective-permute-done | bytes 8224 | tf_op jit(solution)/shard_map/ppermute | solution.py:45
  40.4 0.7 %collective-permute-done.9.refs_2_ = f32[8,256]{1,0:T(8,128)S(1)} collective-permute-done((f32[8,256]{1,0:T(8,128)S(1)}, f32[8,256]{1,0:T(8,128)S(1)}, u32[]{:S(2)}, u32[]{:S(2)}) %collective-permute-start.9) | collective-permute-done | bytes 8224 | tf_op jit(solution)/shard_map/ppermute | solution.py:45
  41.1 1.7 %collective-permute-start.13 = (f32[8,256]{1,0:T(8,128)S(1)}, f32[8,256]{1,0:T(8,128)S(1)}, u32[]{:S(2)}, u32[]{:S(2)}) collective-permute-start(f32[8,256]{1,0:T(8,128)S(1)} %merge.2.refs_0_), channel_id=1, source_target_pairs={{0,12},{1,13},{2,14},{3,15},{4,8},{5,9},{6,10},{7,11},{8,4},{9,5},... | collective-permute-start | bytes 24584 | tf_op jit(solution)/shard_map/ppermute | solution.py:45
  42.8 2.7 %collective-permute-start.11 = (f32[8,256]{1,0:T(8,128)S(1)}, f32[8,256]{1,0:T(8,128)S(1)}, u32[]{:S(2)}, u32[]{:S(2)}) collective-permute-start(f32[8,256]{1,0:T(8,128)S(1)} %merge.2.refs_0_), channel_id=1, source_target_pairs={{0,4},{1,5},{2,6},{3,7},{4,0},{5,1},{6,2},{7,3},{8,12},{9,13},{10,... | collective-permute-start | bytes 24584 | tf_op jit(solution)/shard_map/ppermute | solution.py:45
  45.6 1.1 %collective-permute-done.13.refs_3_ = f32[8,256]{1,0:T(8,128)S(1)} collective-permute-done((f32[8,256]{1,0:T(8,128)S(1)}, f32[8,256]{1,0:T(8,128)S(1)}, u32[]{:S(2)}, u32[]{:S(2)}) %collective-permute-start.13) | collective-permute-done | bytes 8224 | tf_op jit(solution)/shard_map/ppermute | solution.py:45
  46.6 0.8 %collective-permute-done.12.refs_2_ = f32[8,256]{1,0:T(8,128)S(1)} collective-permute-done((f32[8,256]{1,0:T(8,128)S(1)}, f32[8,256]{1,0:T(8,128)S(1)}, u32[]{:S(2)}, u32[]{:S(2)}) %collective-permute-start.12) | collective-permute-done | bytes 8224 | tf_op jit(solution)/shard_map/ppermute | solution.py:45
  47.5 0.7 %multiply_subtract_fusion = f32[256,256]{1,0:T(8,128)} fusion(f32[256,256]{1,0:T(8,128)S(1)} %right.1.image, f32[256,256]{1,0:T(8,128)S(1)} %copy-done.1, f32[256]{0:T(256)S(1)} %bitcast.12, f32[256]{0:T(256)S(1)} %bitcast.11), kind=kLoop, calls=%fused_computation | loop fusion | flops 196608 | bytes 788480 | tf_op jit(solution)/shard_map/sub | solution.py:298
  (28 shorter events, 2.5 us)
Async XLA Ops:
  0.1 8.7 %copy-start.1 = (f32[256,256]{1,0:T(8,128)S(1)}, f32[256,256]{1,0:T(8,128)}, u32[]{:S(2)}) copy-start(f32[256,256]{1,0:T(8,128)} %field.5) | copy-start | bytes 786436
  1.9 15.3 %collective-permute-start.2 = (f32[392,256]{1,0:T(8,128)S(1)}, f32[392,256]{1,0:T(8,128)S(1)}, u32[]{:S(2)}, u32[]{:S(2)}) collective-permute-start(f32[392,256]{1,0:T(8,128)S(1)} %get-tuple-element.20.packed.mine), channel_id=1, source_target_pairs={{0,4},{4,8},{8,12},{12,0},{1,5},{5,9},{9,13},{13,1},{2,6},{6,10},{... | collective-permute-start | bytes 1204232 | tf_op jit(solution)/shard_map/ppermute | solution.py:250
  5.0 12.6 %collective-permute-start.3 = (f32[392,256]{1,0:T(8,128)S(1)}, f32[392,256]{1,0:T(8,128)S(1)}, u32[]{:S(2)}, u32[]{:S(2)}) collective-permute-start(f32[392,256]{1,0:T(8,128)S(1)} %get-tuple-element.26), channel_id=1, source_target_pairs={{0,2},{2,0},{1,3},{3,1},{4,6},{6,4},{5,7},{7,5},{8,10},{10,8},{9,1... | collective-permute-start | bytes 1204232 | tf_op jit(solution)/shard_map/ppermute | solution.py:250
  6.5 2.3 %copy-start.4 = (f32[256]{0:T(256)S(1)}, f32[256]{0:T(256)}, u32[]{:S(2)}) copy-start(f32[256]{0:T(256)} %param.8) | copy-start | bytes 3076
  6.5 2.3 %copy-start.3 = (s32[2,7]{1,0:T(2,128)S(1)}, s32[2,7]{1,0:T(2,128)}, u32[]{:S(2)}) copy-start(s32[2,7]{1,0:T(2,128)} %cols.1) | copy-start | bytes 172
  6.5 18.4 %collective-permute-start.4 = (f32[392,256]{1,0:T(8,128)S(1)}, f32[392,256]{1,0:T(8,128)S(1)}, u32[]{:S(2)}, u32[]{:S(2)}) collective-permute-start(f32[392,256]{1,0:T(8,128)S(1)} %get-tuple-element.28), channel_id=1, source_target_pairs={{4,0},{8,4},{12,8},{0,12},{5,1},{9,5},{13,9},{1,13},{6,2},{10,6},{... | collective-permute-start | bytes 1204232 | tf_op jit(solution)/shard_map/ppermute | solution.py:250
  8.8 2.9 %collective-permute-start = (f32[256,256]{1,0:T(8,128)S(1)}, f32[256,256]{1,0:T(8,128)S(1)}, u32[]{:S(2)}, u32[]{:S(2)}) collective-permute-start(f32[256,256]{1,0:T(8,128)S(1)} %copy-done.1), channel_id=1, source_target_pairs={{0,1},{1,0},{2,3},{3,2},{4,5},{5,4},{6,7},{7,6},{8,9},{9,8},{10,11... | collective-permute-start | bytes 786440 | tf_op jit(solution)/shard_map/ppermute | solution.py:252
  8.8 1.2 %copy-start.2 = (f32[2,7,128,128]{3,2,1,0:T(8,128)S(1)}, f32[2,7,128,128]{3,2,1,0:T(8,128)}, u32[]{:S(2)}) copy-start(f32[2,7,128,128]{3,2,1,0:T(8,128)} %local.1) | copy-start | bytes 2752516
  11.1 1.7 %collective-permute-start.1 = (f32[256,256]{1,0:T(8,128)S(1)}, f32[256,256]{1,0:T(8,128)S(1)}, u32[]{:S(2)}, u32[]{:S(2)}) collective-permute-start(f32[256,256]{1,0:T(8,128)S(1)} %get-tuple-element.22.pair), channel_id=1, source_target_pairs={{0,1},{1,0},{2,3},{3,2},{4,5},{5,4},{6,7},{7,6},{8,9},{9,8},{10,11... | collective-permute-start | bytes 786440 | tf_op jit(solution)/shard_map/ppermute | solution.py:273
  12.8 4.4 %copy-start = (f32[1,8,128,128]{3,2,1,0:T(8,128)S(1)}, f32[1,8,128,128]{3,2,1,0:T(8,128)}, u32[]{:S(2)}) copy-start(f32[1,8,128,128]{3,2,1,0:T(8,128)} %param.11) | copy-start | bytes 1572868
  25.3 2.2 %collective-permute-start.5 = (f32[256,256]{1,0:T(8,128)S(1)}, f32[256,256]{1,0:T(8,128)S(1)}, u32[]{:S(2)}, u32[]{:S(2)}) collective-permute-start(f32[256,256]{1,0:T(8,128)S(1)} %right.1.image), channel_id=1, source_target_pairs={{0,1},{1,0},{2,3},{3,2},{4,5},{5,4},{6,7},{7,6},{8,9},{9,8},{10,11... | collective-permute-start | bytes 786440 | tf_op jit(solution)/shard_map/ppermute | solution.py:290
  25.4 8.7 %collective-permute-start.7 = (f32[256,256]{1,0:T(8,128)S(1)}, f32[256,256]{1,0:T(8,128)S(1)}, u32[]{:S(2)}, u32[]{:S(2)}) collective-permute-start(f32[256,256]{1,0:T(8,128)S(1)} %right.1.image), channel_id=1, source_target_pairs={{0,2},{2,0},{1,3},{3,1},{4,6},{6,4},{5,7},{7,5},{8,10},{10,8},{9,1... | collective-permute-start | bytes 786440 | tf_op jit(solution)/shard_map/ppermute | solution.py:289
  26.6 10.2 %collective-permute-start.6 = (f32[256,256]{1,0:T(8,128)S(1)}, f32[256,256]{1,0:T(8,128)S(1)}, u32[]{:S(2)}, u32[]{:S(2)}) collective-permute-start(f32[256,256]{1,0:T(8,128)S(1)} %right.1.image), channel_id=1, source_target_pairs={{0,4},{4,8},{8,12},{12,0},{1,5},{5,9},{9,13},{13,1},{2,6},{6,10},{... | collective-permute-start | bytes 786440 | tf_op jit(solution)/shard_map/ppermute | solution.py:289
  37.3 3.1 %collective-permute-start.10 = (f32[8,256]{1,0:T(8,128)S(1)}, f32[8,256]{1,0:T(8,128)S(1)}, u32[]{:S(2)}, u32[]{:S(2)}) collective-permute-start(f32[8,256]{1,0:T(8,128)S(1)} %far.1.refs_0_), channel_id=1, source_target_pairs={{0,3},{1,2},{2,1},{3,0},{4,7},{5,6},{6,5},{7,4},{8,11},{9,10},{10,... | collective-permute-start | bytes 24584 | tf_op jit(solution)/shard_map/ppermute | solution.py:45
  37.4 3.7 %collective-permute-start.9 = (f32[8,256]{1,0:T(8,128)S(1)}, f32[8,256]{1,0:T(8,128)S(1)}, u32[]{:S(2)}, u32[]{:S(2)}) collective-permute-start(f32[8,256]{1,0:T(8,128)S(1)} %far.1.refs_0_), channel_id=1, source_target_pairs={{0,2},{1,3},{2,0},{3,1},{4,6},{5,7},{6,4},{7,5},{8,10},{9,11},{10,... | collective-permute-start | bytes 24584 | tf_op jit(solution)/shard_map/ppermute | solution.py:45
  38.3 2.8 %collective-permute-start.8 = (f32[8,256]{1,0:T(8,128)S(1)}, f32[8,256]{1,0:T(8,128)S(1)}, u32[]{:S(2)}, u32[]{:S(2)}) collective-permute-start(f32[8,256]{1,0:T(8,128)S(1)} %far.1.refs_0_), channel_id=1, source_target_pairs={{0,1},{1,0},{2,3},{3,2},{4,5},{5,4},{6,7},{7,6},{8,9},{9,8},{10,11... | collective-permute-start | bytes 24584 | tf_op jit(solution)/shard_map/ppermute | solution.py:45
  41.1 5.5 %collective-permute-start.13 = (f32[8,256]{1,0:T(8,128)S(1)}, f32[8,256]{1,0:T(8,128)S(1)}, u32[]{:S(2)}, u32[]{:S(2)}) collective-permute-start(f32[8,256]{1,0:T(8,128)S(1)} %merge.2.refs_0_), channel_id=1, source_target_pairs={{0,12},{1,13},{2,14},{3,15},{4,8},{5,9},{6,10},{7,11},{8,4},{9,5},... | collective-permute-start | bytes 24584 | tf_op jit(solution)/shard_map/ppermute | solution.py:45
  42.8 4.5 %collective-permute-start.12 = (f32[8,256]{1,0:T(8,128)S(1)}, f32[8,256]{1,0:T(8,128)S(1)}, u32[]{:S(2)}, u32[]{:S(2)}) collective-permute-start(f32[8,256]{1,0:T(8,128)S(1)} %merge.2.refs_0_), channel_id=1, source_target_pairs={{0,8},{1,9},{2,10},{3,11},{4,12},{5,13},{6,14},{7,15},{8,0},{9,1},... | collective-permute-start | bytes 24584 | tf_op jit(solution)/shard_map/ppermute | solution.py:45
  42.8 4.5 %collective-permute-start.11 = (f32[8,256]{1,0:T(8,128)S(1)}, f32[8,256]{1,0:T(8,128)S(1)}, u32[]{:S(2)}, u32[]{:S(2)}) collective-permute-start(f32[8,256]{1,0:T(8,128)S(1)} %merge.2.refs_0_), channel_id=1, source_target_pairs={{0,4},{1,5},{2,6},{3,7},{4,0},{5,1},{6,2},{7,3},{8,12},{9,13},{10,... | collective-permute-start | bytes 24584 | tf_op jit(solution)/shard_map/ppermute | solution.py:45

commit v7 on v6

--- a/solution.py
+++ b/solution.py
@@ -88,6 +88,7 @@
     for pay in pays:
         for n in range(2):
             pay[pl.ds(width + bs + n, 1), pl.ds(0, count)] = table[n].astype(F32)
+        pay[pl.ds(width + bs + 2, 1), :] = jnp.full((1, pay.shape[1]), marks[0].astype(F32))
     for copy in copies:
         copy.wait()
 
@@ -122,18 +123,20 @@
 def edge(take, mine, pay, border):
     bs = border.shape[1]
     width = pay.shape[0] - bs - TAIL
-    options = [take] if isinstance(take, int) else [2, 3]
-
-    def number(ref, line, flip, s):
-        at = [(t ^ flip) * SIDE + s for t in options]
-        found = [ref[pl.ds(width + bs + line, 1), pl.ds(i, 1)] for i in at]
-        return found[0] if len(found) == 1 else jnp.where(take == options[0], found[0], found[1])
+    known = isinstance(take, int)
+
+    def pick(of):
+        return of(take) if known else jnp.where(take == 2.0, of(2), of(3))
+
+    def number(ref, line, t):
+        return ref[pl.ds(width + bs + line, 1), pl.ds(t * SIDE + s, 1)]
 
     blocks = [[0.0] * (width // bs) for _ in range(width // bs)]
     for s in range(SIDE):
+        turned = pay[pl.ds(width, bs), pl.ds(s * bs, bs)].T
         pairs = [
-            (border[take * SIDE + s], number(mine, 0, 0, s), number(pay, 1, 0, s)),
-            (pay[pl.ds(width, bs), pl.ds(s * bs, bs)].T, number(mine, 1, 1, s), number(pay, 0, 1, s)),
+            (pick(lambda t: border[t * SIDE + s]), pick(lambda t: number(mine, 0, t)), pick(lambda t: number(pay, 1, t))),
+            (turned, pick(lambda t: number(mine, 1, t ^ 1)), pick(lambda t: number(pay, 0, t ^ 1))),
         ]
         for block, to, at in pairs:
             for i, line in enumerate(blocks):
@@ -148,46 +151,68 @@
     image[...] = dot(own[...], mine[pl.ds(0, width), :]) + dot(coup[...], mate[...])
 
 
-def left_kernel(mine, part, border, pay, image, once, coup):
+def left_kernel(mine, part, border, pay, image, once, coup, back):
     width = part.shape[0]
     coup[...] = edge(0, mine, pay, border)
     term = dot(coup[...], pay[pl.ds(0, width), :])
     image[...] = part[...] + term
     once[...] = part[...] + 2.0 * term
-
-
-def gy_kernel(take, weight, marks, mine, part, single, border, pay, image, once, coup):
-    width = part.shape[0]
-    coup[...] = edge(marks[0] if take is None else take, mine, pay, border)
+    back[...] = dot(coup[...].T, mine[pl.ds(0, width), :])
+
+
+def turn(mine, width):
+    toward = mine[pl.ds(mine.shape[0] - TAIL + 2, 1), :]
+    column = lax.broadcasted_iota(jnp.int32, toward.shape, 1)
+    return jnp.where((toward == 3.0) == (column < toward.shape[1] // 2), 1.0, 0.0)
+
+
+def gy_kernel(take, weight, mine, part, single, border, pay, image, once, coup):
+    width = coup.shape[0]
+    toward = mine[pl.ds(mine.shape[0] - TAIL + 2, 1), pl.ds(0, 1)]
+    coup[...] = edge(toward if take is None else take, mine, pay, border)
     term = dot(coup[...], pay[pl.ds(0, width), :])
-    image[...] = part[...] + term
-    once[...] = single[...] + weight * term
-
-
-def right_kernel(mine, part, border, pay, image):
-    width = part.shape[0]
-    image[...] = part[...] + dot(edge(1, mine, pay, border), pay[pl.ds(0, width), :])
-
-
-def near_kernel(field, image, once, mate, mate_w, own, coup, part, state):
+    image[pl.ds(0, width), :] = part[pl.ds(0, width), :] + term
+    image[pl.ds(width, TAIL), :] = jnp.zeros((TAIL, term.shape[1]), F32)
+    scale = weight * turn(mine, width) if take is None else weight
+    once[...] = single[...] + scale * term
+
+
+def right_kernel(mine, part, border, pay, image, half):
+    width = image.shape[0]
+    full = part[pl.ds(0, width), :] + dot(edge(1, mine, pay, border), pay[pl.ds(0, width), :])
+    image[...] = full
+    middle = full.shape[1] // 2
+    toward = mine[pl.ds(mine.shape[0] - TAIL + 2, 1), pl.ds(0, 1)]
+    half[...] = jnp.where(toward == 3.0, full[:, middle:], full[:, :middle])
+
+
+def near_kernel(field, image, once, mate, mate_w, own, coup, pay, back, part, lift, state):
     b = field[...]
     norm = col_sum(b, b)
     c = jnp.where(norm > 0.0, col_sum(b, image[...]) / jnp.where(norm > 0.0, norm, 1.0), 0.0)
     g = image[...] - c * b
     part[...] = dot(own[...], g) + dot(coup[...], mate_w[...] - c * mate[...])
+    lift[...] = back[...] - c * pay[pl.ds(0, b.shape[0]), :]
     rows = [(0, norm), (1, c), (2, col_sum(g, g)), (4, -col_sum(g, once[...])), (5, col_sum(b, once[...]))]
     state[...] = stack_rows(rows, state.shape)
 
 
-def far_kernel(weights, field, image, part, near, *refs):
-    count = len(weights)
-    coups, pays, fars, state = refs[:count], refs[count : 2 * count], refs[2 * count : -1], refs[-1]
+def far_kernel(take, field, image, part, near, lift, coup, left, *refs):
+    *sides, state = refs
     width = field.shape[0]
     b = field[...]
     c = near[1:2, :]
-    acc = part[...]
-    for weight, coup, pay, far in zip(weights, coups, pays, fars):
-        acc += weight * dot(coup[...], far[...] - c * pay[pl.ds(0, width), :])
+    acc = part[...] + 2.0 * dot(coup[...], left[pl.ds(0, width), :] + lift[...])
+    if sides:
+        mine, coup_gy, pay, side = sides
+        if take is None:
+            toward = mine[pl.ds(mine.shape[0] - TAIL + 2, 1), pl.ds(0, 1)]
+            middle = b.shape[1] // 2
+            shift = c * pay[pl.ds(0, width), :]
+            term = dot(coup_gy[...], side[...] - jnp.where(toward == 3.0, shift[:, :middle], shift[:, middle:]))
+            acc += 2.0 * turn(mine, width) * jnp.concatenate([term, term], axis=1)
+        else:
+            acc += 2.0 * dot(coup_gy[...], side[...] - c * pay[pl.ds(0, width), :])
     state[...] = near[...] + stack_rows([(3, col_sum(image[...] - c * b, acc)), (4, -col_sum(b, acc))], state.shape)
 
 
@@ -219,7 +244,7 @@
     down = [(j, i) for i, j in up]
     facing = jnp.where(lax.axis_index("gy") == 0, 3, 2).astype(jnp.int32)
     if n_gy == 2:
-        sides = [(swap, None, 1.0)]
+        sides = [(swap, None, 2.0)]
     elif n_gy > 2:
         sides = [(up, 2, 2.0), (down, 3, 0.0)]
     else:
@@ -233,20 +258,24 @@
         return [pl.BlockSpec(memory_space=pltpu.SMEM)] * n
 
     pay_shape = (width + bs + TAIL, ncols)
-    nsends = len(sends)
-    packed = pl.pallas_call(
-        partial(pack_kernel, gives),
-        name="pack",
-        in_specs=smem(1) + [pl.BlockSpec(memory_space=pl.ANY)] * 4,
-        out_specs=[vmem()] * nsends,
-        out_shape=[pltpu.VMEM(pay_shape, F32)] * nsends,
-        scratch_shapes=[
-            pltpu.SemaphoreType.DMA((nsends, SIDE + 1)),
-            pltpu.VMEM((2, 1, 4 * SIDE), jnp.int32),
-            pltpu.SemaphoreType.DMA((2,)),
-        ],
-        compiler_params=pltpu.CompilerParams(vmem_limit_bytes=LIMIT),
-    )(marks, *[pltpu.with_memory_space_constraint(a, pltpu.HBM) for a in (right_side, border, border_send, border_rows)])
+
+    def pack(gives):
+        count = len(gives)
+        return pl.pallas_call(
+            partial(pack_kernel, gives),
+            name="pack",
+            in_specs=smem(1) + [pl.BlockSpec(memory_space=pl.ANY)] * 4,
+            out_specs=[vmem()] * count,
+            out_shape=[pltpu.VMEM(pay_shape, F32)] * count,
+            scratch_shapes=[
+                pltpu.SemaphoreType.DMA((count, SIDE + 1)),
+                pltpu.VMEM((2, 1, 4 * SIDE), jnp.int32),
+                pltpu.SemaphoreType.DMA((2,)),
+            ],
+            compiler_params=pltpu.CompilerParams(vmem_limit_bytes=LIMIT),
+        )(marks, *[pltpu.with_memory_space_constraint(a, pltpu.HBM) for a in (right_side, border, border_send, border_rows)])
+
+    packed = [*pack(gives[:1]), *pack(gives[1:])]
     pays = [lax.ppermute(pay, axis, perm) for pay, (axis, perm) in zip(packed, sends)]
     mine = packed[0]
     mate = lax.ppermute(right_side, "nd", swap)
@@ -273,26 +302,27 @@
     mate_pair = lax.ppermute(pair, "nd", swap)
 
     part, coup = call(base_kernel, "base", [field, square])(mine, own, pair, mate, mate_pair)
-    part, once, left_coup = call(left_kernel, "left", [field, field, square])(mine, part, border, pays[0])
+    part, once, left_coup, back = call(left_kernel, "left", [field, field, square, field])(mine, part, border, pays[0])
     side_coup = []
     for (_, take, weight), pay in zip(sides, pays[2:]):
-        part, once, block = tabled(partial(gy_kernel, take, weight), "gy", 1, [field, field, square])(
-            marks, mine, part, once, border, pay
-        )
+        part, once, block = call(partial(gy_kernel, take, weight), "gy", [(width + TAIL, ncols), field, square])(mine, part, once, border, pay)
         side_coup.append(block)
-    (image,) = call(right_kernel, "right", [field])(mine, part, border, pays[1])
-
-    used = [(2.0, left_coup, pays[0], ("gx", right))]
+    left_w = lax.ppermute(part, "gx", right)
+    image, half = call(right_kernel, "right", [field, (width, ncols // 2)])(mine, part, border, pays[1])
+    mate_w = lax.ppermute(image, "nd", swap)
+    part, lift, state = call(near_kernel, "near", [field, field, (TAIL, ncols)])(
+        right_side, image, once, mate, mate_w, own, coup, pays[0], back
+    )
+    far = []
+    take = None
     if sides:
-        used.append((sides[0][2], side_coup[0], pays[2], ("gy", sides[0][0])))
-    weights, coups, near_b, perms = zip(*used)
-    fars = [lax.ppermute(image, axis, perm) for axis, perm in perms]
-    mate_w = lax.ppermute(image, "nd", swap)
-    part, state = call(near_kernel, "near", [field, (TAIL, ncols)])(right_side, image, once, mate, mate_w, own, coup)
-    (state,) = call(partial(far_kernel, weights), "far", [(TAIL, ncols)])(
-        right_side, image, part, state, *coups, *near_b, *fars
+        perm, take, _ = sides[0]
+        far = [mine, side_coup[0], pays[2], lax.ppermute(half if take is None else image, "gy", perm)]
+    (state,) = call(partial(far_kernel, take), "far", [(TAIL, ncols)])(
+        right_side, image, part, state, lift, left_coup, left_w, *far
     )
-    norm, c, size, form = (row[None] for row in join(state)[:4])
+    state = join(state)
+    norm, c, size, form = (row[None] for row in state[:4])
     ratio = size / (c * c * norm)
     last = size / (form - ratio * ratio * c * c * c * norm)
     return ((1.0 + last * c * (1.0 + ratio)) / c) * right_side - (last / c) * image

time: 48.4 us -> 44.3 us (0.915)
  waiting for transfers between devices: 23.9 us -> 18.8 us
  starting transfers between devices: 15.9 us -> 17.1 us
  local copies, waits for them, and re-layouts: 1.19 us -> 0.02 us
  Pallas kernels: 6.17 us -> 7.25 us
    ppermute x2, waiting for transfers between devices: 8.75 us -> 3.55 us  [the longest x1 3.54 us: shards(): lax.ppermute(half if take is None else image, 'gy', perm)]
    pallas_call x1 -> x2, Pallas kernels: 1.85 us -> 3.28 us  [pack(): pl.pallas_call(partial(pack_kernel, gives), name='pack', in_specs=smem(1)...]
    unnamed x10, local copies, waits for them, and re-layouts: 1.19 us -> 0.02 us
    ppermute x2, starting transfers between devices: 2.12 us -> 3.2 us  [the longest x1 1.8 us: shards(): lax.ppermute(half if take is None else image, 'gy', perm)]
    pallas_call x2 -> x1, Pallas kernels: 2.08 us -> 1.09 us  [run(): pl.pallas_call(kernel, name=name, in_specs=smem(tables) + [vmem()] * (len...]
    ppermute x6, waiting for transfers between devices: 3.68 us -> 4.61 us  [join(): lax.ppermute(state, AXES, [(i, i ^ m) for i in range(count)])]
    ppermute x3, waiting for transfers between devices: 10.3 us -> 9.5 us  [shards(): lax.ppermute(pay, axis, perm)]
    pallas_call x7 -> x8, Pallas kernels: 2.23 us -> 2.87 us  [run(): pl.pallas_call(kernel, name=name, in_specs=[vmem()] * len(args), out_spec...]
  transfers between devices with their start and end apart: 14 -> 14, of which waited for: 9 -> 8; matrix products, arithmetic and copies ran while one was open for 0% -> 0% of each run, Pallas kernels for 7% -> 12%
where the time goes in v7:
time: 44.3 us; the launch traced here: 44.2 us
  waiting for transfers between devices  18.8 us (42%)
  starting transfers between devices  17.1 us (39%)
  Pallas kernels  7.25 us (16%)
  other arithmetic  0.85 us (2%)
    ppermute x3, waiting for transfers between devices, shards(): lax.ppermute(pay, axis, perm)  9.5 us
    ppermute x3, starting transfers between devices, shards(): lax.ppermute(pay, axis, perm)  6.88 us
    ppermute x6, starting transfers between devices, join(): lax.ppermute(state, AXES, [(i, i ^ m) for i in range(count)])  6.4 us
    ppermute x6, waiting for transfers between devices, join(): lax.ppermute(state, AXES, [(i, i ^ m) for i in range(count)])  4.61 us
    ppermute x1, waiting for transfers between devices, shards(): lax.ppermute(half if take is None else image, 'gy', perm)  3.54 us
    pallas_call x2, Pallas kernels, pack(): pl.pallas_call(partial(pack_kernel, gives), name='pack', in_specs=smem(1)...  3.28 us
    pallas_call x8, Pallas kernels, run(): pl.pallas_call(kernel, name=name, in_specs=[vmem()] * len(args), out_spec...  2.87 us
    ppermute x1, starting transfers between devices, shards(): lax.ppermute(half if take is None else image, 'gy', perm)  1.8 us
  transfers between devices with their start and end apart: 14, of which 8 were waited for; matrix products, arithmetic and copies ran while one was open for 0% of the time, Pallas kernels for 12%

profile of v7, /device:TPU:0, one launch (start us, length us, event | category | flops | bytes accessed | tf_op | source)
XLA Modules:
  0.0 44.2 jit_solution(16333192887148890787)
XLA Ops:
  0.1 1.6 %pack.2.packed.mine.refs_0_ = f32[392,256]{1,0:T(8,128)S(1)} custom-call(s32[2]{0:T(128)S(1)} %pad_add_fusion.marks, f32[256,256]{1,0:T(8,128)} %field.7, f32[8,128,128]{2,1,0:T(8,128)} %bitcast.6, s32[1,8]{1,0:T(1,128)} %send.3, s32[1,8]{1,0:T(1,128)} %rows.3), custom_call_target="tpu_custom_call" | custom-call | tf_op jit(solution)/shard_map/pack/pallas_call | solution.py:264
  1.7 3.1 %collective-permute-start.2 = (f32[392,256]{1,0:T(8,128)S(1)}, f32[392,256]{1,0:T(8,128)S(1)}, u32[]{:S(2)}, u32[]{:S(2)}) collective-permute-start(f32[392,256]{1,0:T(8,128)S(1)} %pack.2.packed.mine.refs_0_), channel_id=1, source_target_pairs={{0,4},{4,8},{8,12},{12,0},{1,5},{5,9},{9,13},{13,1},{2,6},{6,10},{... | collective-permute-start | bytes 1204232 | tf_op jit(solution)/shard_map/ppermute | solution.py:279
  4.7 1.7 %pack.3 = (f32[392,256]{1,0:T(8,128)S(1)}, f32[392,256]{1,0:T(8,128)S(1)}) custom-call(s32[2]{0:T(128)S(1)} %pad_add_fusion.marks, f32[256,256]{1,0:T(8,128)} %field.7, f32[8,128,128]{2,1,0:T(8,128)} %bitcast.7, s32[1,8]{1,0:T(1,128)} %send.3, s32[1,8]{1,0:T(1,128)} %rows.3), custom_call_target="tpu_custom_call" | custom-call | tf_op jit(solution)/shard_map/pack/pallas_call | solution.py:264
  6.5 1.6 %collective-permute-start.3 = (f32[392,256]{1,0:T(8,128)S(1)}, f32[392,256]{1,0:T(8,128)S(1)}, u32[]{:S(2)}, u32[]{:S(2)}) collective-permute-start(f32[392,256]{1,0:T(8,128)S(1)} %get-tuple-element.28), channel_id=1, source_target_pairs={{0,2},{2,0},{1,3},{3,1},{4,6},{6,4},{5,7},{7,5},{8,10},{10,8},{9,1... | collective-permute-start | bytes 1204232 | tf_op jit(solution)/shard_map/ppermute | solution.py:279
  8.0 2.2 %collective-permute-start.4 = (f32[392,256]{1,0:T(8,128)S(1)}, f32[392,256]{1,0:T(8,128)S(1)}, u32[]{:S(2)}, u32[]{:S(2)}) collective-permute-start(f32[392,256]{1,0:T(8,128)S(1)} %get-tuple-element.30), channel_id=1, source_target_pairs={{4,0},{8,4},{12,8},{0,12},{5,1},{9,5},{13,9},{1,13},{6,2},{10,6},{... | collective-permute-start | bytes 1204232 | tf_op jit(solution)/shard_map/ppermute | solution.py:279
  10.3 1.1 %prep.1 = (f32[256,256]{1,0:T(8,128)S(1)}, f32[256,256]{1,0:T(8,128)S(1)}) custom-call(s32[2,7]{1,0:T(2,128)S(1)} %copy-done.3, s32[2]{0:T(128)S(1)} %pad_add_fusion.marks, f32[1,256]{1,0:T(1,128)S(1)} %bitcast.11, f32[2,7,128,128]{3,2,1,0:T(8,128)S(1)} %copy-done.2, f32[392,256]{1,0:T(8,128)S(1)} %pack.2.packed.mine.refs_0_), custom_call_target="tpu_custom_call" | custom-call | flops 16777216 | bytes 1048576 | tf_op jit(solution)/shard_map/prep/pallas_call | solution.py:286
  11.4 0.6 %collective-permute-start.1 = (f32[256,256]{1,0:T(8,128)S(1)}, f32[256,256]{1,0:T(8,128)S(1)}, u32[]{:S(2)}, u32[]{:S(2)}) collective-permute-start(f32[256,256]{1,0:T(8,128)S(1)} %get-tuple-element.24.pair), channel_id=1, source_target_pairs={{0,1},{1,0},{2,3},{3,2},{4,5},{5,4},{6,7},{7,6},{8,9},{9,8},{10,11... | collective-permute-start | bytes 786440 | tf_op jit(solution)/shard_map/ppermute | solution.py:302
  12.0 1.2 %collective-permute-done.1.mate_pair = f32[256,256]{1,0:T(8,128)S(1)} collective-permute-done((f32[256,256]{1,0:T(8,128)S(1)}, f32[256,256]{1,0:T(8,128)S(1)}, u32[]{:S(2)}, u32[]{:S(2)}) %collective-permute-start.1) | collective-permute-done | bytes 262176 | tf_op jit(solution)/shard_map/ppermute | solution.py:302
  13.6 3.4 %collective-permute-done.2.pay = f32[392,256]{1,0:T(8,128)S(1)} collective-permute-done((f32[392,256]{1,0:T(8,128)S(1)}, f32[392,256]{1,0:T(8,128)S(1)}, u32[]{:S(2)}, u32[]{:S(2)}) %collective-permute-start.2) | collective-permute-done | bytes 401440 | tf_op jit(solution)/shard_map/ppermute | solution.py:279
  16.9 0.6 %left.1 = (f32[256,256]{1,0:T(8,128)S(1)}, f32[256,256]{1,0:T(8,128)S(1)}, f32[256,256]{1,0:T(8,128)S(1)}, f32[256,256]{1,0:T(8,128)S(1)}) custom-call(f32[392,256]{1,0:T(8,128)S(1)} %pack.2.packed.mine.refs_0_, f32[256,256]{1,0:T(8,128)S(1)} %get-tuple-element.25.part, f32[8,128,128]{2,1,0:T(8,128)S(1)} %bitcast.8, f32[392,256]{1,0:T(8,128)S(1)} %collective-permute-done.2.pay), custom_call_target="tpu_custom_call" | custom-call | tf_op jit(solution)/shard_map/left/pallas_call | solution.py:25
  17.9 1.4 %collective-permute-start.6 = (f32[264,256]{1,0:T(8,128)S(1)}, f32[264,256]{1,0:T(8,128)S(1)}, u32[]{:S(2)}, u32[]{:S(2)}) collective-permute-start(f32[264,256]{1,0:T(8,128)S(1)} %get-tuple-element.29.part), channel_id=1, source_target_pairs={{0,4},{4,8},{8,12},{12,0},{1,5},{5,9},{9,13},{13,1},{2,6},{6,10},{... | collective-permute-start | bytes 811016 | tf_op jit(solution)/shard_map/ppermute | solution.py:310
  19.3 6.1 %collective-permute-done.4.pay = f32[392,256]{1,0:T(8,128)S(1)} collective-permute-done((f32[392,256]{1,0:T(8,128)S(1)}, f32[392,256]{1,0:T(8,128)S(1)}, u32[]{:S(2)}, u32[]{:S(2)}) %collective-permute-start.4) | collective-permute-done | bytes 401440 | tf_op jit(solution)/shard_map/ppermute | solution.py:279
  25.9 1.8 %collective-permute-start.7 = (f32[256,128]{1,0:T(8,128)S(1)}, f32[256,128]{1,0:T(8,128)S(1)}, u32[]{:S(2)}, u32[]{:S(2)}) collective-permute-start(f32[256,128]{1,0:T(8,128)S(1)} %get-tuple-element.40), channel_id=1, source_target_pairs={{0,2},{2,0},{1,3},{3,1},{4,6},{6,4},{5,7},{7,5},{8,10},{10,8},{9,1... | collective-permute-start | bytes 393224 | tf_op jit(solution)/shard_map/ppermute | solution.py:320
  27.7 0.6 %near.1 = (f32[256,256]{1,0:T(8,128)S(1)}, f32[256,256]{1,0:T(8,128)S(1)}, f32[8,256]{1,0:T(8,128)S(1)}) custom-call(f32[256,256]{1,0:T(8,128)S(1)} %copy-done.1, f32[256,256]{1,0:T(8,128)S(1)} %get-tuple-element.31.image, f32[256,256]{1,0:T(8,128)S(1)} %get-tuple-element.32.once, f32[256,256]{1,0:T(8,128)S(1)} %collective-permute-done.mate, ...), custom_call_target="tpu_custom_call" | custom-call | tf_op jit(solution)/shard_map/near/pallas_call | solution.py:25
  28.3 3.5 %collective-permute-done.7.refs_3_ = f32[256,128]{1,0:T(8,128)S(1)} collective-permute-done((f32[256,128]{1,0:T(8,128)S(1)}, f32[256,128]{1,0:T(8,128)S(1)}, u32[]{:S(2)}, u32[]{:S(2)}) %collective-permute-start.7) | collective-permute-done | bytes 131104 | tf_op jit(solution)/shard_map/ppermute | solution.py:320
  32.3 1.1 %collective-permute-start.10 = (f32[8,256]{1,0:T(8,128)S(1)}, f32[8,256]{1,0:T(8,128)S(1)}, u32[]{:S(2)}, u32[]{:S(2)}) collective-permute-start(f32[8,256]{1,0:T(8,128)S(1)} %far.1.refs_0_), channel_id=1, source_target_pairs={{0,3},{1,2},{2,1},{3,0},{4,7},{5,6},{6,5},{7,4},{8,11},{9,10},{10,... | collective-permute-start | bytes 24584 | tf_op jit(solution)/shard_map/ppermute | solution.py:45
  33.4 0.8 %collective-permute-start.9 = (f32[8,256]{1,0:T(8,128)S(1)}, f32[8,256]{1,0:T(8,128)S(1)}, u32[]{:S(2)}, u32[]{:S(2)}) collective-permute-start(f32[8,256]{1,0:T(8,128)S(1)} %far.1.refs_0_), channel_id=1, source_target_pairs={{0,2},{1,3},{2,0},{3,1},{4,6},{5,7},{6,4},{7,5},{8,10},{9,11},{10,... | collective-permute-start | bytes 24584 | tf_op jit(solution)/shard_map/ppermute | solution.py:45
  34.3 1.2 %collective-permute-done.10.refs_3_ = f32[8,256]{1,0:T(8,128)S(1)} collective-permute-done((f32[8,256]{1,0:T(8,128)S(1)}, f32[8,256]{1,0:T(8,128)S(1)}, u32[]{:S(2)}, u32[]{:S(2)}) %collective-permute-start.10) | collective-permute-done | bytes 8224 | tf_op jit(solution)/shard_map/ppermute | solution.py:45
  35.5 1.6 %collective-permute-done.9.refs_2_ = f32[8,256]{1,0:T(8,128)S(1)} collective-permute-done((f32[8,256]{1,0:T(8,128)S(1)}, f32[8,256]{1,0:T(8,128)S(1)}, u32[]{:S(2)}, u32[]{:S(2)}) %collective-permute-start.9) | collective-permute-done | bytes 8224 | tf_op jit(solution)/shard_map/ppermute | solution.py:45
  37.1 1.7 %collective-permute-start.13 = (f32[8,256]{1,0:T(8,128)S(1)}, f32[8,256]{1,0:T(8,128)S(1)}, u32[]{:S(2)}, u32[]{:S(2)}) collective-permute-start(f32[8,256]{1,0:T(8,128)S(1)} %merge.2.refs_0_), channel_id=1, source_target_pairs={{0,12},{1,13},{2,14},{3,15},{4,8},{5,9},{6,10},{7,11},{8,4},{9,5},... | collective-permute-start | bytes 24584 | tf_op jit(solution)/shard_map/ppermute | solution.py:45
  39.2 2.4 %collective-permute-start.11 = (f32[8,256]{1,0:T(8,128)S(1)}, f32[8,256]{1,0:T(8,128)S(1)}, u32[]{:S(2)}, u32[]{:S(2)}) collective-permute-start(f32[8,256]{1,0:T(8,128)S(1)} %merge.2.refs_0_), channel_id=1, source_target_pairs={{0,4},{1,5},{2,6},{3,7},{4,0},{5,1},{6,2},{7,3},{8,12},{9,13},{10,... | collective-permute-start | bytes 24584 | tf_op jit(solution)/shard_map/ppermute | solution.py:45
  41.5 1.1 %collective-permute-done.13.refs_3_ = f32[8,256]{1,0:T(8,128)S(1)} collective-permute-done((f32[8,256]{1,0:T(8,128)S(1)}, f32[8,256]{1,0:T(8,128)S(1)}, u32[]{:S(2)}, u32[]{:S(2)}) %collective-permute-start.13) | collective-permute-done | bytes 8224 | tf_op jit(solution)/shard_map/ppermute | solution.py:45
  42.6 0.8 %collective-permute-done.12.refs_2_ = f32[8,256]{1,0:T(8,128)S(1)} collective-permute-done((f32[8,256]{1,0:T(8,128)S(1)}, f32[8,256]{1,0:T(8,128)S(1)}, u32[]{:S(2)}, u32[]{:S(2)}) %collective-permute-start.12) | collective-permute-done | bytes 8224 | tf_op jit(solution)/shard_map/ppermute | solution.py:45
  43.5 0.7 %multiply_subtract_fusion = f32[256,256]{1,0:T(8,128)} fusion(f32[256,256]{1,0:T(8,128)S(1)} %get-tuple-element.31.image, f32[256,256]{1,0:T(8,128)S(1)} %copy-done.1, f32[256]{0:T(256)S(1)} %bitcast.13, f32[256]{0:T(256)S(1)} %bitcast.12), kind=kLoop, calls=%fused_computation | loop fusion | flops 196608 | bytes 788480 | tf_op jit(solution)/shard_map/sub | solution.py:328
  (29 shorter events, 2.4 us)
Async XLA Ops:
  0.1 10.2 %copy-start.2 = (f32[2,7,128,128]{3,2,1,0:T(8,128)S(1)}, f32[2,7,128,128]{3,2,1,0:T(8,128)}, u32[]{:S(2)}) copy-start(f32[2,7,128,128]{3,2,1,0:T(8,128)} %local.1) | copy-start | bytes 2752516
  1.6 8.6 %copy-start.1 = (f32[256,256]{1,0:T(8,128)S(1)}, f32[256,256]{1,0:T(8,128)}, u32[]{:S(2)}) copy-start(f32[256,256]{1,0:T(8,128)} %field.7) | copy-start | bytes 786436
  1.7 15.3 %collective-permute-start.2 = (f32[392,256]{1,0:T(8,128)S(1)}, f32[392,256]{1,0:T(8,128)S(1)}, u32[]{:S(2)}, u32[]{:S(2)}) collective-permute-start(f32[392,256]{1,0:T(8,128)S(1)} %pack.2.packed.mine.refs_0_), channel_id=1, source_target_pairs={{0,4},{4,8},{8,12},{12,0},{1,5},{5,9},{9,13},{13,1},{2,6},{6,10},{... | collective-permute-start | bytes 1204232 | tf_op jit(solution)/shard_map/ppermute | solution.py:279
  6.5 11.0 %collective-permute-start.3 = (f32[392,256]{1,0:T(8,128)S(1)}, f32[392,256]{1,0:T(8,128)S(1)}, u32[]{:S(2)}, u32[]{:S(2)}) collective-permute-start(f32[392,256]{1,0:T(8,128)S(1)} %get-tuple-element.28), channel_id=1, source_target_pairs={{0,2},{2,0},{1,3},{3,1},{4,6},{6,4},{5,7},{7,5},{8,10},{10,8},{9,1... | collective-permute-start | bytes 1204232 | tf_op jit(solution)/shard_map/ppermute | solution.py:279
  8.0 2.3 %copy-start.4 = (f32[256]{0:T(256)S(1)}, f32[256]{0:T(256)}, u32[]{:S(2)}) copy-start(f32[256]{0:T(256)} %param.8) | copy-start | bytes 3076
  8.0 2.3 %copy-start.3 = (s32[2,7]{1,0:T(2,128)S(1)}, s32[2,7]{1,0:T(2,128)}, u32[]{:S(2)}) copy-start(s32[2,7]{1,0:T(2,128)} %cols.1) | copy-start | bytes 172
  8.0 17.4 %collective-permute-start.4 = (f32[392,256]{1,0:T(8,128)S(1)}, f32[392,256]{1,0:T(8,128)S(1)}, u32[]{:S(2)}, u32[]{:S(2)}) collective-permute-start(f32[392,256]{1,0:T(8,128)S(1)} %get-tuple-element.30), channel_id=1, source_target_pairs={{4,0},{8,4},{12,8},{0,12},{5,1},{9,5},{13,9},{1,13},{6,2},{10,6},{... | collective-permute-start | bytes 1204232 | tf_op jit(solution)/shard_map/ppermute | solution.py:279
  10.3 1.7 %collective-permute-start = (f32[256,256]{1,0:T(8,128)S(1)}, f32[256,256]{1,0:T(8,128)S(1)}, u32[]{:S(2)}, u32[]{:S(2)}) collective-permute-start(f32[256,256]{1,0:T(8,128)S(1)} %copy-done.1), channel_id=1, source_target_pairs={{0,1},{1,0},{2,3},{3,2},{4,5},{5,4},{6,7},{7,6},{8,9},{9,8},{10,11... | collective-permute-start | bytes 786440 | tf_op jit(solution)/shard_map/ppermute | solution.py:281
  11.4 1.7 %collective-permute-start.1 = (f32[256,256]{1,0:T(8,128)S(1)}, f32[256,256]{1,0:T(8,128)S(1)}, u32[]{:S(2)}, u32[]{:S(2)}) collective-permute-start(f32[256,256]{1,0:T(8,128)S(1)} %get-tuple-element.24.pair), channel_id=1, source_target_pairs={{0,1},{1,0},{2,3},{3,2},{4,5},{5,4},{6,7},{7,6},{8,9},{9,8},{10,11... | collective-permute-start | bytes 786440 | tf_op jit(solution)/shard_map/ppermute | solution.py:302
  13.1 3.8 %copy-start = (f32[1,8,128,128]{3,2,1,0:T(8,128)S(1)}, f32[1,8,128,128]{3,2,1,0:T(8,128)}, u32[]{:S(2)}) copy-start(f32[1,8,128,128]{3,2,1,0:T(8,128)} %param.11) | copy-start | bytes 1572868
  17.9 13.9 %collective-permute-start.6 = (f32[264,256]{1,0:T(8,128)S(1)}, f32[264,256]{1,0:T(8,128)S(1)}, u32[]{:S(2)}, u32[]{:S(2)}) collective-permute-start(f32[264,256]{1,0:T(8,128)S(1)} %get-tuple-element.29.part), channel_id=1, source_target_pairs={{0,4},{4,8},{8,12},{12,0},{1,5},{5,9},{9,13},{13,1},{2,6},{6,10},{... | collective-permute-start | bytes 811016 | tf_op jit(solution)/shard_map/ppermute | solution.py:310
  25.8 1.9 %collective-permute-start.5 = (f32[256,256]{1,0:T(8,128)S(1)}, f32[256,256]{1,0:T(8,128)S(1)}, u32[]{:S(2)}, u32[]{:S(2)}) collective-permute-start(f32[256,256]{1,0:T(8,128)S(1)} %get-tuple-element.31.image), channel_id=1, source_target_pairs={{0,1},{1,0},{2,3},{3,2},{4,5},{5,4},{6,7},{7,6},{8,9},{9,8},{10,11... | collective-permute-start | bytes 786440 | tf_op jit(solution)/shard_map/ppermute | solution.py:312
  25.9 5.9 %collective-permute-start.7 = (f32[256,128]{1,0:T(8,128)S(1)}, f32[256,128]{1,0:T(8,128)S(1)}, u32[]{:S(2)}, u32[]{:S(2)}) collective-permute-start(f32[256,128]{1,0:T(8,128)S(1)} %get-tuple-element.40), channel_id=1, source_target_pairs={{0,2},{2,0},{1,3},{3,1},{4,6},{6,4},{5,7},{7,5},{8,10},{10,8},{9,1... | collective-permute-start | bytes 393224 | tf_op jit(solution)/shard_map/ppermute | solution.py:320
  32.3 3.1 %collective-permute-start.10 = (f32[8,256]{1,0:T(8,128)S(1)}, f32[8,256]{1,0:T(8,128)S(1)}, u32[]{:S(2)}, u32[]{:S(2)}) collective-permute-start(f32[8,256]{1,0:T(8,128)S(1)} %far.1.refs_0_), channel_id=1, source_target_pairs={{0,3},{1,2},{2,1},{3,0},{4,7},{5,6},{6,5},{7,4},{8,11},{9,10},{10,... | collective-permute-start | bytes 24584 | tf_op jit(solution)/shard_map/ppermute | solution.py:45
  33.4 3.7 %collective-permute-start.9 = (f32[8,256]{1,0:T(8,128)S(1)}, f32[8,256]{1,0:T(8,128)S(1)}, u32[]{:S(2)}, u32[]{:S(2)}) collective-permute-start(f32[8,256]{1,0:T(8,128)S(1)} %far.1.refs_0_), channel_id=1, source_target_pairs={{0,2},{1,3},{2,0},{3,1},{4,6},{5,7},{6,4},{7,5},{8,10},{9,11},{10,... | collective-permute-start | bytes 24584 | tf_op jit(solution)/shard_map/ppermute | solution.py:45
  34.2 2.8 %collective-permute-start.8 = (f32[8,256]{1,0:T(8,128)S(1)}, f32[8,256]{1,0:T(8,128)S(1)}, u32[]{:S(2)}, u32[]{:S(2)}) collective-permute-start(f32[8,256]{1,0:T(8,128)S(1)} %far.1.refs_0_), channel_id=1, source_target_pairs={{0,1},{1,0},{2,3},{3,2},{4,5},{5,4},{6,7},{7,6},{8,9},{9,8},{10,11... | collective-permute-start | bytes 24584 | tf_op jit(solution)/shard_map/ppermute | solution.py:45
  37.1 5.5 %collective-permute-start.13 = (f32[8,256]{1,0:T(8,128)S(1)}, f32[8,256]{1,0:T(8,128)S(1)}, u32[]{:S(2)}, u32[]{:S(2)}) collective-permute-start(f32[8,256]{1,0:T(8,128)S(1)} %merge.2.refs_0_), channel_id=1, source_target_pairs={{0,12},{1,13},{2,14},{3,15},{4,8},{5,9},{6,10},{7,11},{8,4},{9,5},... | collective-permute-start | bytes 24584 | tf_op jit(solution)/shard_map/ppermute | solution.py:45
  38.8 4.5 %collective-permute-start.12 = (f32[8,256]{1,0:T(8,128)S(1)}, f32[8,256]{1,0:T(8,128)S(1)}, u32[]{:S(2)}, u32[]{:S(2)}) collective-permute-start(f32[8,256]{1,0:T(8,128)S(1)} %merge.2.refs_0_), channel_id=1, source_target_pairs={{0,8},{1,9},{2,10},{3,11},{4,12},{5,13},{6,14},{7,15},{8,0},{9,1},... | collective-permute-start | bytes 24584 | tf_op jit(solution)/shard_map/ppermute | solution.py:45
  39.2 4.2 %collective-permute-start.11 = (f32[8,256]{1,0:T(8,128)S(1)}, f32[8,256]{1,0:T(8,128)S(1)}, u32[]{:S(2)}, u32[]{:S(2)}) collective-permute-start(f32[8,256]{1,0:T(8,128)S(1)} %merge.2.refs_0_), channel_id=1, source_target_pairs={{0,4},{1,5},{2,6},{3,7},{4,0},{5,1},{6,2},{7,3},{8,12},{9,13},{10,... | collective-permute-start | bytes 24584 | tf_op jit(solution)/shard_map/ppermute | solution.py:45

commit v8 on v7

--- a/solution.py
+++ b/solution.py
@@ -12,6 +12,7 @@
 AXES = ("gx", "gy", "nd")
 SIDE = 2
 LIMIT = 8 << 20
+EXTRA = 8
 TAIL = 8
 
 
@@ -57,6 +58,10 @@
     (ah, al), (bh, bl) = split(a), split(b)
     mul = partial(jnp.dot, preferred_element_type=F32)
     return mul(ah, bh) + (mul(ah, bl) + mul(al, bh))
+
+
+def mark_line(mine):
+    return mine.shape[0] - EXTRA - TAIL + 2
 
 
 def col_sum(a, b):
@@ -122,7 +127,7 @@
 
 def edge(take, mine, pay, border):
     bs = border.shape[1]
-    width = pay.shape[0] - bs - TAIL
+    width = bs * (pay.shape[0] // bs - 1)
     known = isinstance(take, int)
 
     def pick(of):
@@ -151,38 +156,37 @@
     image[...] = dot(own[...], mine[pl.ds(0, width), :]) + dot(coup[...], mate[...])
 
 
-def left_kernel(mine, part, border, pay, image, once, coup, back):
-    width = part.shape[0]
-    coup[...] = edge(0, mine, pay, border)
+def turn(mine):
+    toward = mine[pl.ds(mark_line(mine), 1), :]
+    column = lax.broadcasted_iota(jnp.int32, toward.shape, 1)
+    return jnp.where((toward == 3.0) == (column < toward.shape[1] // 2), 1.0, 0.0)
+
+
+def gy_kernel(take, weight, mine, part, single, border, pay, image, once, coup):
+    width = coup.shape[0]
+    toward = mine[pl.ds(mark_line(mine), 1), pl.ds(0, 1)]
+    coup[...] = edge(toward if take is None else take, mine, pay, border)
     term = dot(coup[...], pay[pl.ds(0, width), :])
     image[...] = part[...] + term
-    once[...] = part[...] + 2.0 * term
+    once[...] = single[...] + (weight * turn(mine) if take is None else weight) * term
+
+
+def left_kernel(mine, part, single, border, pay, image, once, coup, back):
+    width = coup.shape[0]
+    coup[...] = edge(0, mine, pay, border)
     back[...] = dot(coup[...].T, mine[pl.ds(0, width), :])
-
-
-def turn(mine, width):
-    toward = mine[pl.ds(mine.shape[0] - TAIL + 2, 1), :]
-    column = lax.broadcasted_iota(jnp.int32, toward.shape, 1)
-    return jnp.where((toward == 3.0) == (column < toward.shape[1] // 2), 1.0, 0.0)
-
-
-def gy_kernel(take, weight, mine, part, single, border, pay, image, once, coup):
-    width = coup.shape[0]
-    toward = mine[pl.ds(mine.shape[0] - TAIL + 2, 1), pl.ds(0, 1)]
-    coup[...] = edge(toward if take is None else take, mine, pay, border)
     term = dot(coup[...], pay[pl.ds(0, width), :])
-    image[pl.ds(0, width), :] = part[pl.ds(0, width), :] + term
-    image[pl.ds(width, TAIL), :] = jnp.zeros((TAIL, term.shape[1]), F32)
-    scale = weight * turn(mine, width) if take is None else weight
-    once[...] = single[...] + scale * term
-
-
-def right_kernel(mine, part, border, pay, image, half):
+    image[pl.ds(0, width), :] = part[...] + term
+    image[pl.ds(width, EXTRA), :] = jnp.zeros((EXTRA, term.shape[1]), F32)
+    once[...] = single[...] + 2.0 * term
+
+
+def right_kernel(mine, part, back, image, half):
     width = image.shape[0]
-    full = part[pl.ds(0, width), :] + dot(edge(1, mine, pay, border), pay[pl.ds(0, width), :])
+    full = part[pl.ds(0, width), :] + back[...]
     image[...] = full
     middle = full.shape[1] // 2
-    toward = mine[pl.ds(mine.shape[0] - TAIL + 2, 1), pl.ds(0, 1)]
+    toward = mine[pl.ds(mark_line(mine), 1), pl.ds(0, 1)]
     half[...] = jnp.where(toward == 3.0, full[:, middle:], full[:, :middle])
 
 
@@ -206,11 +210,11 @@
     if sides:
         mine, coup_gy, pay, side = sides
         if take is None:
-            toward = mine[pl.ds(mine.shape[0] - TAIL + 2, 1), pl.ds(0, 1)]
+            toward = mine[pl.ds(mark_line(mine), 1), pl.ds(0, 1)]
             middle = b.shape[1] // 2
             shift = c * pay[pl.ds(0, width), :]
             term = dot(coup_gy[...], side[...] - jnp.where(toward == 3.0, shift[:, :middle], shift[:, middle:]))
-            acc += 2.0 * turn(mine, width) * jnp.concatenate([term, term], axis=1)
+            acc += 2.0 * turn(mine) * jnp.concatenate([term, term], axis=1)
         else:
             acc += 2.0 * dot(coup_gy[...], side[...] - c * pay[pl.ds(0, width), :])
     state[...] = near[...] + stack_rows([(3, col_sum(image[...] - c * b, acc)), (4, -col_sum(b, acc))], state.shape)
@@ -249,24 +253,24 @@
         sides = [(up, 2, 2.0), (down, 3, 0.0)]
     else:
         sides = []
-    sends = [("gx", right), ("gx", left)] + [("gy", perm) for perm, _, _ in sides]
-    gives = [1, 0] + [None if t is None else t ^ 1 for _, t, _ in sides]
+    sends = [("gx", right)] + [("gy", perm) for perm, _, _ in sides]
+    gives = [1] + [None if t is None else t ^ 1 for _, t, _ in sides]
     marks = jnp.stack([facing, lax.axis_index("nd").astype(jnp.int32)])
     border = border_coup[0]
 
     def smem(n):
         return [pl.BlockSpec(memory_space=pltpu.SMEM)] * n
 
-    pay_shape = (width + bs + TAIL, ncols)
-
-    def pack(gives):
+    rows = width + bs + TAIL
+
+    def pack(gives, extra):
         count = len(gives)
         return pl.pallas_call(
             partial(pack_kernel, gives),
             name="pack",
             in_specs=smem(1) + [pl.BlockSpec(memory_space=pl.ANY)] * 4,
             out_specs=[vmem()] * count,
-            out_shape=[pltpu.VMEM(pay_shape, F32)] * count,
+            out_shape=[pltpu.VMEM((rows + extra, ncols), F32)] * count,
             scratch_shapes=[
                 pltpu.SemaphoreType.DMA((count, SIDE + 1)),
                 pltpu.VMEM((2, 1, 4 * SIDE), jnp.int32),
@@ -275,7 +279,7 @@
             compiler_params=pltpu.CompilerParams(vmem_limit_bytes=LIMIT),
         )(marks, *[pltpu.with_memory_space_constraint(a, pltpu.HBM) for a in (right_side, border, border_send, border_rows)])
 
-    packed = [*pack(gives[:1]), *pack(gives[1:])]
+    packed = pack(gives[:1], EXTRA) + (pack(gives[1:], 0) if sides else [])
     pays = [lax.ppermute(pay, axis, perm) for pay, (axis, perm) in zip(packed, sends)]
     mine = packed[0]
     mate = lax.ppermute(right_side, "nd", swap)
@@ -302,13 +306,17 @@
     mate_pair = lax.ppermute(pair, "nd", swap)
 
     part, coup = call(base_kernel, "base", [field, square])(mine, own, pair, mate, mate_pair)
-    part, once, left_coup, back = call(left_kernel, "left", [field, field, square, field])(mine, part, border, pays[0])
+    once = part
     side_coup = []
-    for (_, take, weight), pay in zip(sides, pays[2:]):
-        part, once, block = call(partial(gy_kernel, take, weight), "gy", [(width + TAIL, ncols), field, square])(mine, part, once, border, pay)
+    for (_, take, weight), pay in zip(sides, pays[1:]):
+        part, once, block = call(partial(gy_kernel, take, weight), "gy", [field, field, square])(mine, part, once, border, pay)
         side_coup.append(block)
+    part, once, left_coup, back = call(left_kernel, "left", [(width + EXTRA, ncols), field, square, field])(
+        mine, part, once, border, pays[0]
+    )
+    right_part = lax.ppermute(back, "gx", left)
     left_w = lax.ppermute(part, "gx", right)
-    image, half = call(right_kernel, "right", [field, (width, ncols // 2)])(mine, part, border, pays[1])
+    image, half = call(right_kernel, "right", [field, (width, ncols // 2)])(mine, part, right_part)
     mate_w = lax.ppermute(image, "nd", swap)
     part, lift, state = call(near_kernel, "near", [field, field, (TAIL, ncols)])(
         right_side, image, once, mate, mate_w, own, coup, pays[0], back
@@ -317,7 +325,7 @@
     take = None
     if sides:
         perm, take, _ = sides[0]
-        far = [mine, side_coup[0], pays[2], lax.ppermute(half if take is None else image, "gy", perm)]
+        far = [mine, side_coup[0], pays[1], lax.ppermute(half if take is None else image, "gy", perm)]
     (state,) = call(partial(far_kernel, take), "far", [(TAIL, ncols)])(
         right_side, image, part, state, lift, left_coup, left_w, *far
     )

time: 44.3 us -> 48.2 us (1.088)
  waiting for transfers between devices: 18.8 us -> 24.2 us
  starting transfers between devices: 17.1 us -> 16.1 us
    ppermute x0 -> x1, waiting for transfers between devices: none -> 6.76 us  [shards(): right_part = lax.ppermute(back, 'gx', left)]
    ppermute x3 -> x2, waiting for transfers between devices: 9.5 us -> 5.98 us  [shards(): lax.ppermute(pay, axis, perm)]
    ppermute x1, waiting for transfers between devices: 0.01 us -> 3.3 us  [shards(): left_w = lax.ppermute(part, 'gx', right)]
    ppermute x1, waiting for transfers between devices: 3.54 us -> 0.49 us  [shards(): lax.ppermute(half if take is None else image, 'gy', perm)]
    ppermute x0 -> x1, starting transfers between devices: none -> 2.38 us  [shards(): right_part = lax.ppermute(back, 'gx', left)]
    ppermute x3 -> x2, starting transfers between devices: 6.88 us -> 4.63 us  [shards(): lax.ppermute(pay, axis, perm)]
    ppermute x6, waiting for transfers between devices: 4.61 us -> 6.45 us  [join(): lax.ppermute(state, AXES, [(i, i ^ m) for i in range(count)])]
    ppermute x1, starting transfers between devices: 1.4 us -> 0.01 us  [shards(): left_w = lax.ppermute(part, 'gx', right)]
  transfers between devices with their start and end apart: 14 -> 14, of which waited for: 8 -> 9; matrix products, arithmetic and copies ran while one was open for 0% -> 0% of each run, Pallas kernels for 12% -> 9%
where the time goes in v8:
time: 48.2 us; the launch traced here: 48.1 us
  waiting for transfers between devices  24.2 us (50%)
  starting transfers between devices  16.1 us (33%)
  Pallas kernels  6.77 us (14%)
  other arithmetic  0.85 us (2%)
    ppermute x6, starting transfers between devices, join(): lax.ppermute(state, AXES, [(i, i ^ m) for i in range(count)])  6.92 us
    ppermute x1, waiting for transfers between devices, shards(): right_part = lax.ppermute(back, 'gx', left)  6.76 us
    ppermute x6, waiting for transfers between devices, join(): lax.ppermute(state, AXES, [(i, i ^ m) for i in range(count)])  6.45 us
    ppermute x2, waiting for transfers between devices, shards(): lax.ppermute(pay, axis, perm)  5.98 us
    ppermute x2, starting transfers between devices, shards(): lax.ppermute(pay, axis, perm)  4.63 us
    ppermute x1, waiting for transfers between devices, shards(): left_w = lax.ppermute(part, 'gx', right)  3.3 us
    pallas_call x2, Pallas kernels, pack(): pl.pallas_call(partial(pack_kernel, gives), name='pack', in_specs=smem(1)...  3.13 us
    pallas_call x8, Pallas kernels, run(): pl.pallas_call(kernel, name=name, in_specs=[vmem()] * len(args), out_spec...  2.55 us
  transfers between devices with their start and end apart: 14, of which 9 were waited for; matrix products, arithmetic and copies ran while one was open for 0% of the time, Pallas kernels for 9%

profile of v8, /device:TPU:0, one launch (start us, length us, event | category | flops | bytes accessed | tf_op | source)
XLA Modules:
  0.0 48.1 jit_solution(10815328453479134517)
XLA Ops:
  0.1 1.6 %pack.2.packed.mine.refs_0_ = f32[400,256]{1,0:T(8,128)S(1)} custom-call(s32[2]{0:T(128)S(1)} %pad_add_fusion.marks, f32[256,256]{1,0:T(8,128)} %field.7, f32[8,128,128]{2,1,0:T(8,128)} %bitcast.6, s32[1,8]{1,0:T(1,128)} %send.3, s32[1,8]{1,0:T(1,128)} %rows.3), custom_call_target="tpu_custom_call" | custom-call | tf_op jit(solution)/shard_map/pack/pallas_call | solution.py:268
  1.7 3.1 %collective-permute-start.3 = (f32[400,256]{1,0:T(8,128)S(1)}, f32[400,256]{1,0:T(8,128)S(1)}, u32[]{:S(2)}, u32[]{:S(2)}) collective-permute-start(f32[400,256]{1,0:T(8,128)S(1)} %pack.2.packed.mine.refs_0_), channel_id=1, source_target_pairs={{0,4},{4,8},{8,12},{12,0},{1,5},{5,9},{9,13},{13,1},{2,6},{6,10},{... | collective-permute-start | bytes 1228808 | tf_op jit(solution)/shard_map/ppermute | solution.py:283
  4.7 1.6 %pack.3 = f32[392,256]{1,0:T(8,128)S(1)} custom-call(s32[2]{0:T(128)S(1)} %pad_add_fusion.marks, f32[256,256]{1,0:T(8,128)} %field.7, f32[8,128,128]{2,1,0:T(8,128)} %bitcast.7, s32[1,8]{1,0:T(1,128)} %send.3, s32[1,8]{1,0:T(1,128)} %rows.3), custom_call_target="tpu_custom_call" | custom-call | tf_op jit(solution)/shard_map/pack/pallas_call | solution.py:268
  6.3 1.6 %collective-permute-start.2 = (f32[392,256]{1,0:T(8,128)S(1)}, f32[392,256]{1,0:T(8,128)S(1)}, u32[]{:S(2)}, u32[]{:S(2)}) collective-permute-start(f32[392,256]{1,0:T(8,128)S(1)} %pack.3), channel_id=1, source_target_pairs={{0,2},{2,0},{1,3},{3,1},{4,6},{6,4},{5,7},{7,5},{8,10},{10,8},{9,1... | collective-permute-start | bytes 1204232 | tf_op jit(solution)/shard_map/ppermute | solution.py:283
  7.9 1.1 %prep.1 = (f32[256,256]{1,0:T(8,128)S(1)}, f32[256,256]{1,0:T(8,128)S(1)}) custom-call(s32[2,7]{1,0:T(2,128)S(1)} %copy-done.3, s32[2]{0:T(128)S(1)} %pad_add_fusion.marks, f32[1,256]{1,0:T(1,128)S(1)} %bitcast.10, f32[2,7,128,128]{3,2,1,0:T(8,128)S(1)} %copy-done.2, f32[400,256]{1,0:T(8,128)S(1)} %pack.2.packed.mine.refs_0_), custom_call_target="tpu_custom_call" | custom-call | flops 16777216 | bytes 1048576 | tf_op jit(solution)/shard_map/prep/pallas_call | solution.py:290
  9.0 0.6 %collective-permute-start.1 = (f32[256,256]{1,0:T(8,128)S(1)}, f32[256,256]{1,0:T(8,128)S(1)}, u32[]{:S(2)}, u32[]{:S(2)}) collective-permute-start(f32[256,256]{1,0:T(8,128)S(1)} %get-tuple-element.22.pair), channel_id=1, source_target_pairs={{0,1},{1,0},{2,3},{3,2},{4,5},{5,4},{6,7},{7,6},{8,9},{9,8},{10,11... | collective-permute-start | bytes 786440 | tf_op jit(solution)/shard_map/ppermute | solution.py:306
  9.6 1.2 %collective-permute-done.1.mate_pair = f32[256,256]{1,0:T(8,128)S(1)} collective-permute-done((f32[256,256]{1,0:T(8,128)S(1)}, f32[256,256]{1,0:T(8,128)S(1)}, u32[]{:S(2)}, u32[]{:S(2)}) %collective-permute-start.1) | collective-permute-done | bytes 262176 | tf_op jit(solution)/shard_map/ppermute | solution.py:306
  11.2 6.0 %collective-permute-done.2.pay.refs_2_ = f32[392,256]{1,0:T(8,128)S(1)} collective-permute-done((f32[392,256]{1,0:T(8,128)S(1)}, f32[392,256]{1,0:T(8,128)S(1)}, u32[]{:S(2)}, u32[]{:S(2)}) %collective-permute-start.2) | collective-permute-done | bytes 401440 | tf_op jit(solution)/shard_map/ppermute | solution.py:283
  17.5 0.6 %left.1 = (f32[264,256]{1,0:T(8,128)S(1)}, f32[256,256]{1,0:T(8,128)S(1)}, f32[256,256]{1,0:T(8,128)S(1)}, f32[256,256]{1,0:T(8,128)S(1)}) custom-call(f32[400,256]{1,0:T(8,128)S(1)} %pack.2.packed.mine.refs_0_, f32[256,256]{1,0:T(8,128)S(1)} %get-tuple-element.24.part, f32[256,256]{1,0:T(8,128)S(1)} %get-tuple-element.25.single, ...), custom_call_target="tpu_custom_call" | custom-call | tf_op jit(solution)/shard_map/left/pallas_call | solution.py:26
  18.1 2.4 %collective-permute-start.4 = (f32[256,256]{1,0:T(8,128)S(1)}, f32[256,256]{1,0:T(8,128)S(1)}, u32[]{:S(2)}, u32[]{:S(2)}) collective-permute-start(f32[256,256]{1,0:T(8,128)S(1)} %get-tuple-element.27.back), channel_id=1, source_target_pairs={{4,0},{8,4},{12,8},{0,12},{5,1},{9,5},{13,9},{1,13},{6,2},{10,6},{... | collective-permute-start | bytes 786440 | tf_op jit(solution)/shard_map/ppermute | solution.py:317
  20.5 6.8 %collective-permute-done.4.back = f32[256,256]{1,0:T(8,128)S(1)} collective-permute-done((f32[256,256]{1,0:T(8,128)S(1)}, f32[256,256]{1,0:T(8,128)S(1)}, u32[]{:S(2)}, u32[]{:S(2)}) %collective-permute-start.4) | collective-permute-done | bytes 262176 | tf_op jit(solution)/shard_map/ppermute | solution.py:317
  27.4 1.6 %collective-permute-start.7 = (f32[256,128]{1,0:T(8,128)S(1)}, f32[256,128]{1,0:T(8,128)S(1)}, u32[]{:S(2)}, u32[]{:S(2)}) collective-permute-start(f32[256,128]{1,0:T(8,128)S(1)} %get-tuple-element.36), channel_id=1, source_target_pairs={{0,2},{2,0},{1,3},{3,1},{4,6},{6,4},{5,7},{7,5},{8,10},{10,8},{9,1... | collective-permute-start | bytes 393224 | tf_op jit(solution)/shard_map/ppermute | solution.py:328
  29.0 0.6 %near.1 = (f32[256,256]{1,0:T(8,128)S(1)}, f32[256,256]{1,0:T(8,128)S(1)}, f32[8,256]{1,0:T(8,128)S(1)}) custom-call(f32[256,256]{1,0:T(8,128)S(1)} %copy-done.1, f32[256,256]{1,0:T(8,128)S(1)} %get-tuple-element.28.image, f32[256,256]{1,0:T(8,128)S(1)} %get-tuple-element.29.once, f32[256,256]{1,0:T(8,128)S(1)} %collective-permute-done.mate, ...), custom_call_target="tpu_custom_call" | custom-call | tf_op jit(solution)/shard_map/near/pallas_call | solution.py:26
  29.6 3.3 %collective-permute-done.6.left = f32[264,256]{1,0:T(8,128)S(1)} collective-permute-done((f32[264,256]{1,0:T(8,128)S(1)}, f32[264,256]{1,0:T(8,128)S(1)}, u32[]{:S(2)}, u32[]{:S(2)}) %collective-permute-start.6) | collective-permute-done | bytes 270368 | tf_op jit(solution)/shard_map/ppermute | solution.py:318
  32.8 0.5 %collective-permute-done.7.refs_3_ = f32[256,128]{1,0:T(8,128)S(1)} collective-permute-done((f32[256,128]{1,0:T(8,128)S(1)}, f32[256,128]{1,0:T(8,128)S(1)}, u32[]{:S(2)}, u32[]{:S(2)}) %collective-permute-start.7) | collective-permute-done | bytes 131104 | tf_op jit(solution)/shard_map/ppermute | solution.py:328
  33.8 0.8 %collective-permute-start.10 = (f32[8,256]{1,0:T(8,128)S(1)}, f32[8,256]{1,0:T(8,128)S(1)}, u32[]{:S(2)}, u32[]{:S(2)}) collective-permute-start(f32[8,256]{1,0:T(8,128)S(1)} %far.1.refs_0_), channel_id=1, source_target_pairs={{0,3},{1,2},{2,1},{3,0},{4,7},{5,6},{6,5},{7,4},{8,11},{9,10},{10,... | collective-permute-start | bytes 24584 | tf_op jit(solution)/shard_map/ppermute | solution.py:46
  34.6 0.8 %collective-permute-start.9 = (f32[8,256]{1,0:T(8,128)S(1)}, f32[8,256]{1,0:T(8,128)S(1)}, u32[]{:S(2)}, u32[]{:S(2)}) collective-permute-start(f32[8,256]{1,0:T(8,128)S(1)} %far.1.refs_0_), channel_id=1, source_target_pairs={{0,2},{1,3},{2,0},{3,1},{4,6},{5,7},{6,4},{7,5},{8,10},{9,11},{10,... | collective-permute-start | bytes 24584 | tf_op jit(solution)/shard_map/ppermute | solution.py:46
  35.8 1.3 %collective-permute-done.10.refs_3_ = f32[8,256]{1,0:T(8,128)S(1)} collective-permute-done((f32[8,256]{1,0:T(8,128)S(1)}, f32[8,256]{1,0:T(8,128)S(1)}, u32[]{:S(2)}, u32[]{:S(2)}) %collective-permute-start.10) | collective-permute-done | bytes 8224 | tf_op jit(solution)/shard_map/ppermute | solution.py:46
  37.0 1.3 %collective-permute-done.9.refs_2_ = f32[8,256]{1,0:T(8,128)S(1)} collective-permute-done((f32[8,256]{1,0:T(8,128)S(1)}, f32[8,256]{1,0:T(8,128)S(1)}, u32[]{:S(2)}, u32[]{:S(2)}) %collective-permute-start.9) | collective-permute-done | bytes 8224 | tf_op jit(solution)/shard_map/ppermute | solution.py:46
  38.3 4.3 %collective-permute-start.13 = (f32[8,256]{1,0:T(8,128)S(1)}, f32[8,256]{1,0:T(8,128)S(1)}, u32[]{:S(2)}, u32[]{:S(2)}) collective-permute-start(f32[8,256]{1,0:T(8,128)S(1)} %merge.2.refs_0_), channel_id=1, source_target_pairs={{0,12},{1,13},{2,14},{3,15},{4,8},{5,9},{6,10},{7,11},{8,4},{9,5},... | collective-permute-start | bytes 24584 | tf_op jit(solution)/shard_map/ppermute | solution.py:46
  42.7 0.6 %collective-permute-start.11 = (f32[8,256]{1,0:T(8,128)S(1)}, f32[8,256]{1,0:T(8,128)S(1)}, u32[]{:S(2)}, u32[]{:S(2)}) collective-permute-start(f32[8,256]{1,0:T(8,128)S(1)} %merge.2.refs_0_), channel_id=1, source_target_pairs={{0,4},{1,5},{2,6},{3,7},{4,0},{5,1},{6,2},{7,3},{8,12},{9,13},{10,... | collective-permute-start | bytes 24584 | tf_op jit(solution)/shard_map/ppermute | solution.py:46
  43.3 1.0 %collective-permute-done.13.refs_3_ = f32[8,256]{1,0:T(8,128)S(1)} collective-permute-done((f32[8,256]{1,0:T(8,128)S(1)}, f32[8,256]{1,0:T(8,128)S(1)}, u32[]{:S(2)}, u32[]{:S(2)}) %collective-permute-start.13) | collective-permute-done | bytes 8224 | tf_op jit(solution)/shard_map/ppermute | solution.py:46
  44.3 2.9 %collective-permute-done.12.refs_2_ = f32[8,256]{1,0:T(8,128)S(1)} collective-permute-done((f32[8,256]{1,0:T(8,128)S(1)}, f32[8,256]{1,0:T(8,128)S(1)}, u32[]{:S(2)}, u32[]{:S(2)}) %collective-permute-start.12) | collective-permute-done | bytes 8224 | tf_op jit(solution)/shard_map/ppermute | solution.py:46
  47.3 0.7 %multiply_subtract_fusion = f32[256,256]{1,0:T(8,128)} fusion(f32[256,256]{1,0:T(8,128)S(1)} %get-tuple-element.28.image, f32[256,256]{1,0:T(8,128)S(1)} %copy-done.1, f32[256]{0:T(256)S(1)} %bitcast.12, f32[256]{0:T(256)S(1)} %bitcast.11), kind=kLoop, calls=%fused_computation | loop fusion | flops 196608 | bytes 788480 | tf_op jit(solution)/shard_map/sub | solution.py:336
  (29 shorter events, 1.9 us)
Async XLA Ops:
  0.1 7.8 %copy-start.2 = (f32[2,7,128,128]{3,2,1,0:T(8,128)S(1)}, f32[2,7,128,128]{3,2,1,0:T(8,128)}, u32[]{:S(2)}) copy-start(f32[2,7,128,128]{3,2,1,0:T(8,128)} %local.1) | copy-start | bytes 2752516
  1.6 6.2 %copy-start.1 = (f32[256,256]{1,0:T(8,128)S(1)}, f32[256,256]{1,0:T(8,128)}, u32[]{:S(2)}) copy-start(f32[256,256]{1,0:T(8,128)} %field.7) | copy-start | bytes 786436
  1.7 15.9 %collective-permute-start.3 = (f32[400,256]{1,0:T(8,128)S(1)}, f32[400,256]{1,0:T(8,128)S(1)}, u32[]{:S(2)}, u32[]{:S(2)}) collective-permute-start(f32[400,256]{1,0:T(8,128)S(1)} %pack.2.packed.mine.refs_0_), channel_id=1, source_target_pairs={{0,4},{4,8},{8,12},{12,0},{1,5},{5,9},{9,13},{13,1},{2,6},{6,10},{... | collective-permute-start | bytes 1228808 | tf_op jit(solution)/shard_map/ppermute | solution.py:283
  4.7 3.2 %copy-start.4 = (f32[256]{0:T(256)S(1)}, f32[256]{0:T(256)}, u32[]{:S(2)}) copy-start(f32[256]{0:T(256)} %param.8) | copy-start | bytes 3076
  6.3 1.6 %copy-start.3 = (s32[2,7]{1,0:T(2,128)S(1)}, s32[2,7]{1,0:T(2,128)}, u32[]{:S(2)}) copy-start(s32[2,7]{1,0:T(2,128)} %cols.1) | copy-start | bytes 172
  6.3 10.8 %collective-permute-start.2 = (f32[392,256]{1,0:T(8,128)S(1)}, f32[392,256]{1,0:T(8,128)S(1)}, u32[]{:S(2)}, u32[]{:S(2)}) collective-permute-start(f32[392,256]{1,0:T(8,128)S(1)} %pack.3), channel_id=1, source_target_pairs={{0,2},{2,0},{1,3},{3,1},{4,6},{6,4},{5,7},{7,5},{8,10},{10,8},{9,1... | collective-permute-start | bytes 1204232 | tf_op jit(solution)/shard_map/ppermute | solution.py:283
  7.9 1.7 %collective-permute-start = (f32[256,256]{1,0:T(8,128)S(1)}, f32[256,256]{1,0:T(8,128)S(1)}, u32[]{:S(2)}, u32[]{:S(2)}) collective-permute-start(f32[256,256]{1,0:T(8,128)S(1)} %copy-done.1), channel_id=1, source_target_pairs={{0,1},{1,0},{2,3},{3,2},{4,5},{5,4},{6,7},{7,6},{8,9},{9,8},{10,11... | collective-permute-start | bytes 786440 | tf_op jit(solution)/shard_map/ppermute | solution.py:285
  9.0 1.7 %collective-permute-start.1 = (f32[256,256]{1,0:T(8,128)S(1)}, f32[256,256]{1,0:T(8,128)S(1)}, u32[]{:S(2)}, u32[]{:S(2)}) collective-permute-start(f32[256,256]{1,0:T(8,128)S(1)} %get-tuple-element.22.pair), channel_id=1, source_target_pairs={{0,1},{1,0},{2,3},{3,2},{4,5},{5,4},{6,7},{7,6},{8,9},{9,8},{10,11... | collective-permute-start | bytes 786440 | tf_op jit(solution)/shard_map/ppermute | solution.py:306
  10.7 6.4 %copy-start = (f32[1,8,128,128]{3,2,1,0:T(8,128)S(1)}, f32[1,8,128,128]{3,2,1,0:T(8,128)}, u32[]{:S(2)}) copy-start(f32[1,8,128,128]{3,2,1,0:T(8,128)} %param.11) | copy-start | bytes 1572868
  18.1 9.1 %collective-permute-start.4 = (f32[256,256]{1,0:T(8,128)S(1)}, f32[256,256]{1,0:T(8,128)S(1)}, u32[]{:S(2)}, u32[]{:S(2)}) collective-permute-start(f32[256,256]{1,0:T(8,128)S(1)} %get-tuple-element.27.back), channel_id=1, source_target_pairs={{4,0},{8,4},{12,8},{0,12},{5,1},{9,5},{13,9},{1,13},{6,2},{10,6},{... | collective-permute-start | bytes 786440 | tf_op jit(solution)/shard_map/ppermute | solution.py:317
  20.5 12.3 %collective-permute-start.6 = (f32[264,256]{1,0:T(8,128)S(1)}, f32[264,256]{1,0:T(8,128)S(1)}, u32[]{:S(2)}, u32[]{:S(2)}) collective-permute-start(f32[264,256]{1,0:T(8,128)S(1)} %get-tuple-element.26.part), channel_id=1, source_target_pairs={{0,4},{4,8},{8,12},{12,0},{1,5},{5,9},{9,13},{13,1},{2,6},{6,10},{... | collective-permute-start | bytes 811016 | tf_op jit(solution)/shard_map/ppermute | solution.py:318
  27.4 1.6 %collective-permute-start.5 = (f32[256,256]{1,0:T(8,128)S(1)}, f32[256,256]{1,0:T(8,128)S(1)}, u32[]{:S(2)}, u32[]{:S(2)}) collective-permute-start(f32[256,256]{1,0:T(8,128)S(1)} %get-tuple-element.28.image), channel_id=1, source_target_pairs={{0,1},{1,0},{2,3},{3,2},{4,5},{5,4},{6,7},{7,6},{8,9},{9,8},{10,11... | collective-permute-start | bytes 786440 | tf_op jit(solution)/shard_map/ppermute | solution.py:320
  27.4 5.9 %collective-permute-start.7 = (f32[256,128]{1,0:T(8,128)S(1)}, f32[256,128]{1,0:T(8,128)S(1)}, u32[]{:S(2)}, u32[]{:S(2)}) collective-permute-start(f32[256,128]{1,0:T(8,128)S(1)} %get-tuple-element.36), channel_id=1, source_target_pairs={{0,2},{2,0},{1,3},{3,1},{4,6},{6,4},{5,7},{7,5},{8,10},{10,8},{9,1... | collective-permute-start | bytes 393224 | tf_op jit(solution)/shard_map/ppermute | solution.py:328
  33.8 3.2 %collective-permute-start.10 = (f32[8,256]{1,0:T(8,128)S(1)}, f32[8,256]{1,0:T(8,128)S(1)}, u32[]{:S(2)}, u32[]{:S(2)}) collective-permute-start(f32[8,256]{1,0:T(8,128)S(1)} %far.1.refs_0_), channel_id=1, source_target_pairs={{0,3},{1,2},{2,1},{3,0},{4,7},{5,6},{6,5},{7,4},{8,11},{9,10},{10,... | collective-permute-start | bytes 24584 | tf_op jit(solution)/shard_map/ppermute | solution.py:46
  34.6 3.7 %collective-permute-start.9 = (f32[8,256]{1,0:T(8,128)S(1)}, f32[8,256]{1,0:T(8,128)S(1)}, u32[]{:S(2)}, u32[]{:S(2)}) collective-permute-start(f32[8,256]{1,0:T(8,128)S(1)} %far.1.refs_0_), channel_id=1, source_target_pairs={{0,2},{1,3},{2,0},{3,1},{4,6},{5,7},{6,4},{7,5},{8,10},{9,11},{10,... | collective-permute-start | bytes 24584 | tf_op jit(solution)/shard_map/ppermute | solution.py:46
  35.5 2.8 %collective-permute-start.8 = (f32[8,256]{1,0:T(8,128)S(1)}, f32[8,256]{1,0:T(8,128)S(1)}, u32[]{:S(2)}, u32[]{:S(2)}) collective-permute-start(f32[8,256]{1,0:T(8,128)S(1)} %far.1.refs_0_), channel_id=1, source_target_pairs={{0,1},{1,0},{2,3},{3,2},{4,5},{5,4},{6,7},{7,6},{8,9},{9,8},{10,11... | collective-permute-start | bytes 24584 | tf_op jit(solution)/shard_map/ppermute | solution.py:46
  38.3 6.0 %collective-permute-start.13 = (f32[8,256]{1,0:T(8,128)S(1)}, f32[8,256]{1,0:T(8,128)S(1)}, u32[]{:S(2)}, u32[]{:S(2)}) collective-permute-start(f32[8,256]{1,0:T(8,128)S(1)} %merge.2.refs_0_), channel_id=1, source_target_pairs={{0,12},{1,13},{2,14},{3,15},{4,8},{5,9},{6,10},{7,11},{8,4},{9,5},... | collective-permute-start | bytes 24584 | tf_op jit(solution)/shard_map/ppermute | solution.py:46
  42.7 4.5 %collective-permute-start.12 = (f32[8,256]{1,0:T(8,128)S(1)}, f32[8,256]{1,0:T(8,128)S(1)}, u32[]{:S(2)}, u32[]{:S(2)}) collective-permute-start(f32[8,256]{1,0:T(8,128)S(1)} %merge.2.refs_0_), channel_id=1, source_target_pairs={{0,8},{1,9},{2,10},{3,11},{4,12},{5,13},{6,14},{7,15},{8,0},{9,1},... | collective-permute-start | bytes 24584 | tf_op jit(solution)/shard_map/ppermute | solution.py:46
  42.7 4.5 %collective-permute-start.11 = (f32[8,256]{1,0:T(8,128)S(1)}, f32[8,256]{1,0:T(8,128)S(1)}, u32[]{:S(2)}, u32[]{:S(2)}) collective-permute-start(f32[8,256]{1,0:T(8,128)S(1)} %merge.2.refs_0_), channel_id=1, source_target_pairs={{0,4},{1,5},{2,6},{3,7},{4,0},{5,1},{6,2},{7,3},{8,12},{9,13},{10,... | collective-permute-start | bytes 24584 | tf_op jit(solution)/shard_map/ppermute | solution.py:46

commit v9 on v8

--- a/solution.py
+++ b/solution.py
@@ -167,18 +167,19 @@
     toward = mine[pl.ds(mark_line(mine), 1), pl.ds(0, 1)]
     coup[...] = edge(toward if take is None else take, mine, pay, border)
     term = dot(coup[...], pay[pl.ds(0, width), :])
-    image[...] = part[...] + term
+    image[pl.ds(0, width), :] = part[...] + term
+    if image.shape[0] > width:
+        image[pl.ds(width, EXTRA), :] = jnp.zeros((EXTRA, term.shape[1]), F32)
     once[...] = single[...] + (weight * turn(mine) if take is None else weight) * term
 
 
-def left_kernel(mine, part, single, border, pay, image, once, coup, back):
+def left_kernel(mine, part, border, pay, image, once, coup, back):
     width = coup.shape[0]
     coup[...] = edge(0, mine, pay, border)
     back[...] = dot(coup[...].T, mine[pl.ds(0, width), :])
     term = dot(coup[...], pay[pl.ds(0, width), :])
-    image[pl.ds(0, width), :] = part[...] + term
-    image[pl.ds(width, EXTRA), :] = jnp.zeros((EXTRA, term.shape[1]), F32)
-    once[...] = single[...] + 2.0 * term
+    image[...] = part[...] + term
+    once[...] = part[...] + 2.0 * term
 
 
 def right_kernel(mine, part, back, image, half):
@@ -262,24 +263,20 @@
         return [pl.BlockSpec(memory_space=pltpu.SMEM)] * n
 
     rows = width + bs + TAIL
-
-    def pack(gives, extra):
-        count = len(gives)
-        return pl.pallas_call(
-            partial(pack_kernel, gives),
-            name="pack",
-            in_specs=smem(1) + [pl.BlockSpec(memory_space=pl.ANY)] * 4,
-            out_specs=[vmem()] * count,
-            out_shape=[pltpu.VMEM((rows + extra, ncols), F32)] * count,
-            scratch_shapes=[
-                pltpu.SemaphoreType.DMA((count, SIDE + 1)),
-                pltpu.VMEM((2, 1, 4 * SIDE), jnp.int32),
-                pltpu.SemaphoreType.DMA((2,)),
-            ],
-            compiler_params=pltpu.CompilerParams(vmem_limit_bytes=LIMIT),
-        )(marks, *[pltpu.with_memory_space_constraint(a, pltpu.HBM) for a in (right_side, border, border_send, border_rows)])
-
-    packed = pack(gives[:1], EXTRA) + (pack(gives[1:], 0) if sides else [])
+    count = len(gives)
+    packed = pl.pallas_call(
+        partial(pack_kernel, gives),
+        name="pack",
+        in_specs=smem(1) + [pl.BlockSpec(memory_space=pl.ANY)] * 4,
+        out_specs=[vmem()] * count,
+        out_shape=[pltpu.VMEM((rows + (0 if n else EXTRA), ncols), F32) for n in range(count)],
+        scratch_shapes=[
+            pltpu.SemaphoreType.DMA((count, SIDE + 1)),
+            pltpu.VMEM((2, 1, 4 * SIDE), jnp.int32),
+            pltpu.SemaphoreType.DMA((2,)),
+        ],
+        compiler_params=pltpu.CompilerParams(vmem_limit_bytes=LIMIT),
+    )(marks, *[pltpu.with_memory_space_constraint(a, pltpu.HBM) for a in (right_side, border, border_send, border_rows)])
     pays = [lax.ppermute(pay, axis, perm) for pay, (axis, perm) in zip(packed, sends)]
     mine = packed[0]
     mate = lax.ppermute(right_side, "nd", swap)
@@ -306,15 +303,15 @@
     mate_pair = lax.ppermute(pair, "nd", swap)
 
     part, coup = call(base_kernel, "base", [field, square])(mine, own, pair, mate, mate_pair)
-    once = part
+    part, once, left_coup, back = call(left_kernel, "left", [field, field, square, field])(mine, part, border, pays[0])
+    right_part = lax.ppermute(back, "gx", left)
     side_coup = []
-    for (_, take, weight), pay in zip(sides, pays[1:]):
-        part, once, block = call(partial(gy_kernel, take, weight), "gy", [field, field, square])(mine, part, once, border, pay)
+    for n, ((_, take, weight), pay) in enumerate(zip(sides, pays[1:])):
+        extra = EXTRA if n == len(sides) - 1 else 0
+        part, once, block = call(partial(gy_kernel, take, weight), "gy", [(width + extra, ncols), field, square])(
+            mine, part, once, border, pay
+        )
         side_coup.append(block)
-    part, once, left_coup, back = call(left_kernel, "left", [(width + EXTRA, ncols), field, square, field])(
-        mine, part, once, border, pays[0]
-    )
-    right_part = lax.ppermute(back, "gx", left)
     left_w = lax.ppermute(part, "gx", right)
     image, half = call(right_kernel, "right", [field, (width, ncols // 2)])(mine, part, right_part)
     mate_w = lax.ppermute(image, "nd", swap)

time: 48.2 us -> 47.8 us (level)
  Pallas kernels: 6.77 us -> 5.38 us
  local copies, waits for them, and re-layouts: 0.02 us -> 1.19 us
  starting transfers between devices: 16.1 us -> 15.1 us
  waiting for transfers between devices: 24.2 us -> 25 us
    ppermute x1, waiting for transfers between devices: 0.49 us -> 3.82 us  [shards(): lax.ppermute(half if take is None else image, 'gy', perm)]
    ppermute x1, waiting for transfers between devices: 3.3 us -> 0.01 us  [shards(): left_w = lax.ppermute(part, 'gx', right)]
    ppermute x6, waiting for transfers between devices: 6.45 us -> 3.47 us  [join(): lax.ppermute(state, AXES, [(i, i ^ m) for i in range(count)])]
    ppermute x1, waiting for transfers between devices: 6.76 us -> 9.25 us  [shards(): right_part = lax.ppermute(back, 'gx', left)]
    ppermute x1, starting transfers between devices: 0.01 us -> 1.63 us  [shards(): left_w = lax.ppermute(part, 'gx', right)]
    ppermute x1, starting transfers between devices: 1.56 us -> 0.07 us  [shards(): lax.ppermute(half if take is None else image, 'gy', perm)]
    ppermute x1, waiting for transfers between devices: 0.01 us -> 1.44 us  [shards(): mate_w = lax.ppermute(image, 'nd', swap)]
    pallas_call x2 -> x1, Pallas kernels: 3.13 us -> 1.72 us  [shards(): pl.pallas_call(partial(pack_kernel, gives), name='pack', in_specs=smem(1)...]
  transfers between devices with their start and end apart: 14 -> 14, of which waited for: 9 -> 9; matrix products, arithmetic and copies ran while one was open for 0% -> 0% of each run, Pallas kernels for 9% -> 7%
where the time goes in v9:
time: 47.8 us; the launch traced here: 47.6 us
  waiting for transfers between devices  25 us (52%)
  starting transfers between devices  15.1 us (32%)
  Pallas kernels  5.38 us (11%)
  local copies, waits for them, and re-layouts  1.19 us (2%)
  other arithmetic  0.85 us (2%)
    ppermute x1, waiting for transfers between devices, shards(): right_part = lax.ppermute(back, 'gx', left)  9.25 us
    ppermute x2, waiting for transfers between devices, shards(): lax.ppermute(pay, axis, perm)  6.97 us
    ppermute x6, starting transfers between devices, join(): lax.ppermute(state, AXES, [(i, i ^ m) for i in range(count)])  6.39 us
    ppermute x2, starting transfers between devices, shards(): lax.ppermute(pay, axis, perm)  4.57 us
    ppermute x1, waiting for transfers between devices, shards(): lax.ppermute(half if take is None else image, 'gy', perm)  3.82 us
    ppermute x6, waiting for transfers between devices, join(): lax.ppermute(state, AXES, [(i, i ^ m) for i in range(count)])  3.47 us
    pallas_call x8, Pallas kernels, run(): pl.pallas_call(kernel, name=name, in_specs=[vmem()] * len(args), out_spec...  2.57 us
    ppermute x1, starting transfers between devices, shards(): right_part = lax.ppermute(back, 'gx', left)  1.79 us
  transfers between devices with their start and end apart: 14, of which 9 were waited for; matrix products, arithmetic and copies ran while one was open for 0% of the time, Pallas kernels for 7%

profile of v9, /device:TPU:0, one launch (start us, length us, event | category | flops | bytes accessed | tf_op | source)
XLA Modules:
  0.0 47.6 jit_solution(16987060046491971784)
XLA Ops:
  0.1 1.7 %pack.1 = (f32[400,256]{1,0:T(8,128)S(1)}, f32[392,256]{1,0:T(8,128)S(1)}) custom-call(s32[2]{0:T(128)S(1)} %pad_add_fusion.marks, f32[256,256]{1,0:T(8,128)} %field.5, f32[8,128,128]{2,1,0:T(8,128)} %bitcast.6, s32[1,8]{1,0:T(1,128)} %send.1, s32[1,8]{1,0:T(1,128)} %rows.1), custom_call_target="tpu_custom_call" | custom-call | tf_op jit(solution)/shard_map/pack/pallas_call | solution.py:267
  1.8 3.1 %collective-permute-start.2 = (f32[400,256]{1,0:T(8,128)S(1)}, f32[400,256]{1,0:T(8,128)S(1)}, u32[]{:S(2)}, u32[]{:S(2)}) collective-permute-start(f32[400,256]{1,0:T(8,128)S(1)} %get-tuple-element.23.packed.mine.refs_0_), channel_id=1, source_target_pairs={{0,4},{4,8},{8,12},{12,0},{1,5},{5,9},{9,13},{13,1},{2,6},{6,10},{... | collective-permute-start | bytes 1228808 | tf_op jit(solution)/shard_map/ppermute | solution.py:280
  4.9 1.2 %copy-done.2 = f32[2,7,128,128]{3,2,1,0:T(8,128)S(1)} copy-done((f32[2,7,128,128]{3,2,1,0:T(8,128)S(1)}, f32[2,7,128,128]{3,2,1,0:T(8,128)}, u32[]{:S(2)}) %copy-start.2) | copy-done | bytes 917528
  6.1 1.1 %prep.1 = (f32[256,256]{1,0:T(8,128)S(1)}, f32[256,256]{1,0:T(8,128)S(1)}) custom-call(s32[2,7]{1,0:T(2,128)S(1)} %copy-done.3, s32[2]{0:T(128)S(1)} %pad_add_fusion.marks, f32[1,256]{1,0:T(1,128)S(1)} %bitcast.9, f32[2,7,128,128]{3,2,1,0:T(8,128)S(1)} %copy-done.2, f32[400,256]{1,0:T(8,128)S(1)} %get-tuple-element.23.packed.mine.refs_0_), custom_call_target="tpu_custom_call" | custom-call | flops 16777216 | bytes 1048576 | tf_op jit(solution)/shard_map/prep/pallas_call | solution.py:287
  7.2 0.6 %collective-permute-start.1 = (f32[256,256]{1,0:T(8,128)S(1)}, f32[256,256]{1,0:T(8,128)S(1)}, u32[]{:S(2)}, u32[]{:S(2)}) collective-permute-start(f32[256,256]{1,0:T(8,128)S(1)} %get-tuple-element.25.pair), channel_id=1, source_target_pairs={{0,1},{1,0},{2,3},{3,2},{4,5},{5,4},{6,7},{7,6},{8,9},{9,8},{10,11... | collective-permute-start | bytes 786440 | tf_op jit(solution)/shard_map/ppermute | solution.py:303
  7.8 1.5 %collective-permute-start.3 = (f32[392,256]{1,0:T(8,128)S(1)}, f32[392,256]{1,0:T(8,128)S(1)}, u32[]{:S(2)}, u32[]{:S(2)}) collective-permute-start(f32[392,256]{1,0:T(8,128)S(1)} %get-tuple-element.29), channel_id=1, source_target_pairs={{0,2},{2,0},{1,3},{3,1},{4,6},{6,4},{5,7},{7,5},{8,10},{10,8},{9,1... | collective-permute-start | bytes 1204232 | tf_op jit(solution)/shard_map/ppermute | solution.py:280
  9.3 0.4 base.1
  9.7 6.7 %collective-permute-done.2.pay = f32[400,256]{1,0:T(8,128)S(1)} collective-permute-done((f32[400,256]{1,0:T(8,128)S(1)}, f32[400,256]{1,0:T(8,128)S(1)}, u32[]{:S(2)}, u32[]{:S(2)}) %collective-permute-start.2) | collective-permute-done | bytes 409632 | tf_op jit(solution)/shard_map/ppermute | solution.py:280
  16.4 0.6 %left.1 = (f32[256,256]{1,0:T(8,128)S(1)}, f32[256,256]{1,0:T(8,128)S(1)}, f32[256,256]{1,0:T(8,128)S(1)}, f32[256,256]{1,0:T(8,128)S(1)}) custom-call(f32[400,256]{1,0:T(8,128)S(1)} %get-tuple-element.23.packed.mine.refs_0_, f32[256,256]{1,0:T(8,128)S(1)} %get-tuple-element.26.part, f32[8,128,128]{2,1,0:T(8,128)S(1)} %bitcast.7, ...), custom_call_target="tpu_custom_call" | custom-call | tf_op jit(solution)/shard_map/left/pallas_call | solution.py:26
  17.0 1.8 %collective-permute-start.4 = (f32[256,256]{1,0:T(8,128)S(1)}, f32[256,256]{1,0:T(8,128)S(1)}, u32[]{:S(2)}, u32[]{:S(2)}) collective-permute-start(f32[256,256]{1,0:T(8,128)S(1)} %get-tuple-element.31.back), channel_id=1, source_target_pairs={{4,0},{8,4},{12,8},{0,12},{5,1},{9,5},{13,9},{1,13},{6,2},{10,6},{... | collective-permute-start | bytes 786440 | tf_op jit(solution)/shard_map/ppermute | solution.py:307
  19.4 1.6 %collective-permute-start.6 = (f32[264,256]{1,0:T(8,128)S(1)}, f32[264,256]{1,0:T(8,128)S(1)}, u32[]{:S(2)}, u32[]{:S(2)}) collective-permute-start(f32[264,256]{1,0:T(8,128)S(1)} %get-tuple-element.30.part), channel_id=1, source_target_pairs={{0,4},{4,8},{8,12},{12,0},{1,5},{5,9},{9,13},{13,1},{2,6},{6,10},{... | collective-permute-start | bytes 811016 | tf_op jit(solution)/shard_map/ppermute | solution.py:315
  21.1 9.2 %collective-permute-done.4.back = f32[256,256]{1,0:T(8,128)S(1)} collective-permute-done((f32[256,256]{1,0:T(8,128)S(1)}, f32[256,256]{1,0:T(8,128)S(1)}, u32[]{:S(2)}, u32[]{:S(2)}) %collective-permute-start.4) | collective-permute-done | bytes 262176 | tf_op jit(solution)/shard_map/ppermute | solution.py:307
  30.6 1.4 %collective-permute-done.5.mate_w = f32[256,256]{1,0:T(8,128)S(1)} collective-permute-done((f32[256,256]{1,0:T(8,128)S(1)}, f32[256,256]{1,0:T(8,128)S(1)}, u32[]{:S(2)}, u32[]{:S(2)}) %collective-permute-start.5) | collective-permute-done | bytes 262176 | tf_op jit(solution)/shard_map/ppermute | solution.py:317
  32.0 0.6 %near.1 = (f32[256,256]{1,0:T(8,128)S(1)}, f32[256,256]{1,0:T(8,128)S(1)}, f32[8,256]{1,0:T(8,128)S(1)}) custom-call(f32[256,256]{1,0:T(8,128)S(1)} %copy-done.1, f32[256,256]{1,0:T(8,128)S(1)} %get-tuple-element.32.image, f32[256,256]{1,0:T(8,128)S(1)} %get-tuple-element.33.once, f32[256,256]{1,0:T(8,128)S(1)} %collective-permute-done.mate, ...), custom_call_target="tpu_custom_call" | custom-call | tf_op jit(solution)/shard_map/near/pallas_call | solution.py:26
  32.6 3.8 %collective-permute-done.7.refs_3_ = f32[256,128]{1,0:T(8,128)S(1)} collective-permute-done((f32[256,128]{1,0:T(8,128)S(1)}, f32[256,128]{1,0:T(8,128)S(1)}, u32[]{:S(2)}, u32[]{:S(2)}) %collective-permute-start.7) | collective-permute-done | bytes 131104 | tf_op jit(solution)/shard_map/ppermute | solution.py:325
  36.4 0.5 %far.1.refs_0_ = f32[8,256]{1,0:T(8,128)S(1)} custom-call(f32[256,256]{1,0:T(8,128)S(1)} %copy-done.1, f32[256,256]{1,0:T(8,128)S(1)} %get-tuple-element.32.image, f32[256,256]{1,0:T(8,128)S(1)} %get-tuple-element.35.part, f32[8,256]{1,0:T(8,128)S(1)} %get-tuple-element.36.near, f32[256,256]{1,0:T(8,128)S(1)} %get-tuple-element.37.lift, ...), custom_call_target="tpu_custom_call" | custom-call | tf_op jit(solution)/shard_map/far/pallas_call | solution.py:26
  37.0 1.3 %collective-permute-start.9 = (f32[8,256]{1,0:T(8,128)S(1)}, f32[8,256]{1,0:T(8,128)S(1)}, u32[]{:S(2)}, u32[]{:S(2)}) collective-permute-start(f32[8,256]{1,0:T(8,128)S(1)} %far.1.refs_0_), channel_id=1, source_target_pairs={{0,2},{1,3},{2,0},{3,1},{4,6},{5,7},{6,4},{7,5},{8,10},{9,11},{10,... | collective-permute-start | bytes 24584 | tf_op jit(solution)/shard_map/ppermute | solution.py:46
  38.2 0.6 %collective-permute-start.8 = (f32[8,256]{1,0:T(8,128)S(1)}, f32[8,256]{1,0:T(8,128)S(1)}, u32[]{:S(2)}, u32[]{:S(2)}) collective-permute-start(f32[8,256]{1,0:T(8,128)S(1)} %far.1.refs_0_), channel_id=1, source_target_pairs={{0,1},{1,0},{2,3},{3,2},{4,5},{5,4},{6,7},{7,6},{8,9},{9,8},{10,11... | collective-permute-start | bytes 24584 | tf_op jit(solution)/shard_map/ppermute | solution.py:46
  38.8 1.2 %collective-permute-done.10.refs_3_ = f32[8,256]{1,0:T(8,128)S(1)} collective-permute-done((f32[8,256]{1,0:T(8,128)S(1)}, f32[8,256]{1,0:T(8,128)S(1)}, u32[]{:S(2)}, u32[]{:S(2)}) %collective-permute-start.10) | collective-permute-done | bytes 8224 | tf_op jit(solution)/shard_map/ppermute | solution.py:46
  40.0 0.6 %collective-permute-done.9.refs_2_ = f32[8,256]{1,0:T(8,128)S(1)} collective-permute-done((f32[8,256]{1,0:T(8,128)S(1)}, f32[8,256]{1,0:T(8,128)S(1)}, u32[]{:S(2)}, u32[]{:S(2)}) %collective-permute-start.9) | collective-permute-done | bytes 8224 | tf_op jit(solution)/shard_map/ppermute | solution.py:46
  41.0 4.2 %collective-permute-start.11 = (f32[8,256]{1,0:T(8,128)S(1)}, f32[8,256]{1,0:T(8,128)S(1)}, u32[]{:S(2)}, u32[]{:S(2)}) collective-permute-start(f32[8,256]{1,0:T(8,128)S(1)} %merge.2.refs_0_), channel_id=1, source_target_pairs={{0,4},{1,5},{2,6},{3,7},{4,0},{5,1},{6,2},{7,3},{8,12},{9,13},{10,... | collective-permute-start | bytes 24584 | tf_op jit(solution)/shard_map/ppermute | solution.py:46
  45.2 1.1 %collective-permute-done.13.refs_3_ = f32[8,256]{1,0:T(8,128)S(1)} collective-permute-done((f32[8,256]{1,0:T(8,128)S(1)}, f32[8,256]{1,0:T(8,128)S(1)}, u32[]{:S(2)}, u32[]{:S(2)}) %collective-permute-start.13) | collective-permute-done | bytes 8224 | tf_op jit(solution)/shard_map/ppermute | solution.py:46
  46.2 0.6 %collective-permute-done.11.refs_1_ = f32[8,256]{1,0:T(8,128)S(1)} collective-permute-done((f32[8,256]{1,0:T(8,128)S(1)}, f32[8,256]{1,0:T(8,128)S(1)}, u32[]{:S(2)}, u32[]{:S(2)}) %collective-permute-start.11) | collective-permute-done | bytes 8224 | tf_op jit(solution)/shard_map/ppermute | solution.py:46
  46.9 0.7 %multiply_subtract_fusion = f32[256,256]{1,0:T(8,128)} fusion(f32[256,256]{1,0:T(8,128)S(1)} %get-tuple-element.32.image, f32[256,256]{1,0:T(8,128)S(1)} %copy-done.1, f32[256]{0:T(256)S(1)} %bitcast.11, f32[256]{0:T(256)S(1)} %bitcast.10), kind=kLoop, calls=%fused_computation | loop fusion | flops 196608 | bytes 788480 | tf_op jit(solution)/shard_map/sub | solution.py:333
  (28 shorter events, 1.4 us)
Async XLA Ops:
  0.1 4.8 %copy-start.1 = (f32[256,256]{1,0:T(8,128)S(1)}, f32[256,256]{1,0:T(8,128)}, u32[]{:S(2)}) copy-start(f32[256,256]{1,0:T(8,128)} %field.5) | copy-start | bytes 786436
  1.8 3.1 %copy-start.4 = (f32[256]{0:T(256)S(1)}, f32[256]{0:T(256)}, u32[]{:S(2)}) copy-start(f32[256]{0:T(256)} %param.8) | copy-start | bytes 3076
  1.8 3.1 %copy-start.3 = (s32[2,7]{1,0:T(2,128)S(1)}, s32[2,7]{1,0:T(2,128)}, u32[]{:S(2)}) copy-start(s32[2,7]{1,0:T(2,128)} %cols.1) | copy-start | bytes 172
  1.8 14.6 %collective-permute-start.2 = (f32[400,256]{1,0:T(8,128)S(1)}, f32[400,256]{1,0:T(8,128)S(1)}, u32[]{:S(2)}, u32[]{:S(2)}) collective-permute-start(f32[400,256]{1,0:T(8,128)S(1)} %get-tuple-element.23.packed.mine.refs_0_), channel_id=1, source_target_pairs={{0,4},{4,8},{8,12},{12,0},{1,5},{5,9},{9,13},{13,1},{2,6},{6,10},{... | collective-permute-start | bytes 1228808 | tf_op jit(solution)/shard_map/ppermute | solution.py:280
  4.9 4.3 %collective-permute-start = (f32[256,256]{1,0:T(8,128)S(1)}, f32[256,256]{1,0:T(8,128)S(1)}, u32[]{:S(2)}, u32[]{:S(2)}) collective-permute-start(f32[256,256]{1,0:T(8,128)S(1)} %copy-done.1), channel_id=1, source_target_pairs={{0,1},{1,0},{2,3},{3,2},{4,5},{5,4},{6,7},{7,6},{8,9},{9,8},{10,11... | collective-permute-start | bytes 786440 | tf_op jit(solution)/shard_map/ppermute | solution.py:282
  4.9 1.2 %copy-start.2 = (f32[2,7,128,128]{3,2,1,0:T(8,128)S(1)}, f32[2,7,128,128]{3,2,1,0:T(8,128)}, u32[]{:S(2)}) copy-start(f32[2,7,128,128]{3,2,1,0:T(8,128)} %local.1) | copy-start | bytes 2752516
  7.2 2.1 %collective-permute-start.1 = (f32[256,256]{1,0:T(8,128)S(1)}, f32[256,256]{1,0:T(8,128)S(1)}, u32[]{:S(2)}, u32[]{:S(2)}) collective-permute-start(f32[256,256]{1,0:T(8,128)S(1)} %get-tuple-element.25.pair), channel_id=1, source_target_pairs={{0,1},{1,0},{2,3},{3,2},{4,5},{5,4},{6,7},{7,6},{8,9},{9,8},{10,11... | collective-permute-start | bytes 786440 | tf_op jit(solution)/shard_map/ppermute | solution.py:303
  7.8 11.3 %collective-permute-start.3 = (f32[392,256]{1,0:T(8,128)S(1)}, f32[392,256]{1,0:T(8,128)S(1)}, u32[]{:S(2)}, u32[]{:S(2)}) collective-permute-start(f32[392,256]{1,0:T(8,128)S(1)} %get-tuple-element.29), channel_id=1, source_target_pairs={{0,2},{2,0},{1,3},{3,1},{4,6},{6,4},{5,7},{7,5},{8,10},{10,8},{9,1... | collective-permute-start | bytes 1204232 | tf_op jit(solution)/shard_map/ppermute | solution.py:280
  9.3 7.1 %copy-start = (f32[1,8,128,128]{3,2,1,0:T(8,128)S(1)}, f32[1,8,128,128]{3,2,1,0:T(8,128)}, u32[]{:S(2)}) copy-start(f32[1,8,128,128]{3,2,1,0:T(8,128)} %param.11) | copy-start | bytes 1572868
  17.0 13.3 %collective-permute-start.4 = (f32[256,256]{1,0:T(8,128)S(1)}, f32[256,256]{1,0:T(8,128)S(1)}, u32[]{:S(2)}, u32[]{:S(2)}) collective-permute-start(f32[256,256]{1,0:T(8,128)S(1)} %get-tuple-element.31.back), channel_id=1, source_target_pairs={{4,0},{8,4},{12,8},{0,12},{5,1},{9,5},{13,9},{1,13},{6,2},{10,6},{... | collective-permute-start | bytes 786440 | tf_op jit(solution)/shard_map/ppermute | solution.py:307
  19.4 13.1 %collective-permute-start.6 = (f32[264,256]{1,0:T(8,128)S(1)}, f32[264,256]{1,0:T(8,128)S(1)}, u32[]{:S(2)}, u32[]{:S(2)}) collective-permute-start(f32[264,256]{1,0:T(8,128)S(1)} %get-tuple-element.30.part), channel_id=1, source_target_pairs={{0,4},{4,8},{8,12},{12,0},{1,5},{5,9},{9,13},{13,1},{2,6},{6,10},{... | collective-permute-start | bytes 811016 | tf_op jit(solution)/shard_map/ppermute | solution.py:315
  30.4 1.6 %collective-permute-start.5 = (f32[256,256]{1,0:T(8,128)S(1)}, f32[256,256]{1,0:T(8,128)S(1)}, u32[]{:S(2)}, u32[]{:S(2)}) collective-permute-start(f32[256,256]{1,0:T(8,128)S(1)} %get-tuple-element.32.image), channel_id=1, source_target_pairs={{0,1},{1,0},{2,3},{3,2},{4,5},{5,4},{6,7},{7,6},{8,9},{9,8},{10,11... | collective-permute-start | bytes 786440 | tf_op jit(solution)/shard_map/ppermute | solution.py:317
  30.5 5.9 %collective-permute-start.7 = (f32[256,128]{1,0:T(8,128)S(1)}, f32[256,128]{1,0:T(8,128)S(1)}, u32[]{:S(2)}, u32[]{:S(2)}) collective-permute-start(f32[256,128]{1,0:T(8,128)S(1)} %get-tuple-element.40), channel_id=1, source_target_pairs={{0,2},{2,0},{1,3},{3,1},{4,6},{6,4},{5,7},{7,5},{8,10},{10,8},{9,1... | collective-permute-start | bytes 393224 | tf_op jit(solution)/shard_map/ppermute | solution.py:325
  36.9 3.2 %collective-permute-start.10 = (f32[8,256]{1,0:T(8,128)S(1)}, f32[8,256]{1,0:T(8,128)S(1)}, u32[]{:S(2)}, u32[]{:S(2)}) collective-permute-start(f32[8,256]{1,0:T(8,128)S(1)} %far.1.refs_0_), channel_id=1, source_target_pairs={{0,3},{1,2},{2,1},{3,0},{4,7},{5,6},{6,5},{7,4},{8,11},{9,10},{10,... | collective-permute-start | bytes 24584 | tf_op jit(solution)/shard_map/ppermute | solution.py:46
  37.0 3.7 %collective-permute-start.9 = (f32[8,256]{1,0:T(8,128)S(1)}, f32[8,256]{1,0:T(8,128)S(1)}, u32[]{:S(2)}, u32[]{:S(2)}) collective-permute-start(f32[8,256]{1,0:T(8,128)S(1)} %far.1.refs_0_), channel_id=1, source_target_pairs={{0,2},{1,3},{2,0},{3,1},{4,6},{5,7},{6,4},{7,5},{8,10},{9,11},{10,... | collective-permute-start | bytes 24584 | tf_op jit(solution)/shard_map/ppermute | solution.py:46
  38.2 2.4 %collective-permute-start.8 = (f32[8,256]{1,0:T(8,128)S(1)}, f32[8,256]{1,0:T(8,128)S(1)}, u32[]{:S(2)}, u32[]{:S(2)}) collective-permute-start(f32[8,256]{1,0:T(8,128)S(1)} %far.1.refs_0_), channel_id=1, source_target_pairs={{0,1},{1,0},{2,3},{3,2},{4,5},{5,4},{6,7},{7,6},{8,9},{9,8},{10,11... | collective-permute-start | bytes 24584 | tf_op jit(solution)/shard_map/ppermute | solution.py:46
  40.7 5.5 %collective-permute-start.13 = (f32[8,256]{1,0:T(8,128)S(1)}, f32[8,256]{1,0:T(8,128)S(1)}, u32[]{:S(2)}, u32[]{:S(2)}) collective-permute-start(f32[8,256]{1,0:T(8,128)S(1)} %merge.2.refs_0_), channel_id=1, source_target_pairs={{0,12},{1,13},{2,14},{3,15},{4,8},{5,9},{6,10},{7,11},{8,4},{9,5},... | collective-permute-start | bytes 24584 | tf_op jit(solution)/shard_map/ppermute | solution.py:46
  41.0 5.3 %collective-permute-start.12 = (f32[8,256]{1,0:T(8,128)S(1)}, f32[8,256]{1,0:T(8,128)S(1)}, u32[]{:S(2)}, u32[]{:S(2)}) collective-permute-start(f32[8,256]{1,0:T(8,128)S(1)} %merge.2.refs_0_), channel_id=1, source_target_pairs={{0,8},{1,9},{2,10},{3,11},{4,12},{5,13},{6,14},{7,15},{8,0},{9,1},... | collective-permute-start | bytes 24584 | tf_op jit(solution)/shard_map/ppermute | solution.py:46
  41.0 5.8 %collective-permute-start.11 = (f32[8,256]{1,0:T(8,128)S(1)}, f32[8,256]{1,0:T(8,128)S(1)}, u32[]{:S(2)}, u32[]{:S(2)}) collective-permute-start(f32[8,256]{1,0:T(8,128)S(1)} %merge.2.refs_0_), channel_id=1, source_target_pairs={{0,4},{1,5},{2,6},{3,7},{4,0},{5,1},{6,2},{7,3},{8,12},{9,13},{10,... | collective-permute-start | bytes 24584 | tf_op jit(solution)/shard_map/ppermute | solution.py:46

commit v10 on v7

--- a/solution.py
+++ b/solution.py
@@ -68,11 +68,12 @@
     return sum(jnp.where(line == n, row, 0.0) for n, row in rows)
 
 
-def pack_kernel(gives, marks, field, border, send, rows, *refs):
-    *pays, sems, table, table_sems = refs
+def pack_kernel(gives, *refs):
+    marks, refs = (refs[0], refs[1:]) if None in gives else (None, refs)
+    field, border, send, rows, toward, *pays, sems, table, table_sems = refs
     width = field.shape[0]
     bs = border.shape[1]
-    tables = [pltpu.make_async_copy(ref, table.at[n], table_sems.at[n]) for n, ref in enumerate((rows, send))]
+    tables = [pltpu.make_async_copy(ref, table.at[n], table_sems.at[n]) for n, ref in enumerate((rows, send, toward))]
     copies = []
     for n, pay in enumerate(pays):
         give = marks[0] if gives[n] is None else gives[n]
@@ -86,9 +87,8 @@
         copy.wait()
     count = table.shape[2]
     for pay in pays:
-        for n in range(2):
+        for n in range(3):
             pay[pl.ds(width + bs + n, 1), pl.ds(0, count)] = table[n].astype(F32)
-        pay[pl.ds(width + bs + 2, 1), :] = jnp.full((1, pay.shape[1]), marks[0].astype(F32))
     for copy in copies:
         copy.wait()
 
@@ -161,9 +161,10 @@
 
 
 def turn(mine, width):
-    toward = mine[pl.ds(mine.shape[0] - TAIL + 2, 1), :]
-    column = lax.broadcasted_iota(jnp.int32, toward.shape, 1)
-    return jnp.where((toward == 3.0) == (column < toward.shape[1] // 2), 1.0, 0.0)
+    toward = mine[pl.ds(mine.shape[0] - TAIL + 2, 1), pl.ds(0, 1)]
+    count = mine.shape[1]
+    first = jnp.where(lax.broadcasted_iota(jnp.int32, (1, count), 1) < count // 2, 1.0, 0.0)
+    return jnp.where(toward == 3.0, first, 1.0 - first)
 
 
 def gy_kernel(take, weight, mine, part, single, border, pay, image, once, coup):
@@ -171,15 +172,14 @@
     toward = mine[pl.ds(mine.shape[0] - TAIL + 2, 1), pl.ds(0, 1)]
     coup[...] = edge(toward if take is None else take, mine, pay, border)
     term = dot(coup[...], pay[pl.ds(0, width), :])
-    image[pl.ds(0, width), :] = part[pl.ds(0, width), :] + term
-    image[pl.ds(width, TAIL), :] = jnp.zeros((TAIL, term.shape[1]), F32)
+    image[...] = part[...] + term
     scale = weight * turn(mine, width) if take is None else weight
     once[...] = single[...] + scale * term
 
 
 def right_kernel(mine, part, border, pay, image, half):
     width = image.shape[0]
-    full = part[pl.ds(0, width), :] + dot(edge(1, mine, pay, border), pay[pl.ds(0, width), :])
+    full = part[...] + dot(edge(1, mine, pay, border), pay[pl.ds(0, width), :])
     image[...] = full
     middle = full.shape[1] // 2
     toward = mine[pl.ds(mine.shape[0] - TAIL + 2, 1), pl.ds(0, 1)]
@@ -202,7 +202,7 @@
     width = field.shape[0]
     b = field[...]
     c = near[1:2, :]
-    acc = part[...] + 2.0 * dot(coup[...], left[pl.ds(0, width), :] + lift[...])
+    acc = part[...] + 2.0 * dot(coup[...], left[...] + lift[...])
     if sides:
         mine, coup_gy, pay, side = sides
         if take is None:
@@ -251,6 +251,7 @@
         sides = []
     sends = [("gx", right), ("gx", left)] + [("gy", perm) for perm, _, _ in sides]
     gives = [1, 0] + [None if t is None else t ^ 1 for _, t, _ in sides]
+    toward = jnp.full((1, 4 * SIDE), facing)
     marks = jnp.stack([facing, lax.axis_index("nd").astype(jnp.int32)])
     border = border_coup[0]
 
@@ -261,19 +262,20 @@
 
     def pack(gives):
         count = len(gives)
+        tables = [marks] if None in gives else []
         return pl.pallas_call(
             partial(pack_kernel, gives),
             name="pack",
-            in_specs=smem(1) + [pl.BlockSpec(memory_space=pl.ANY)] * 4,
+            in_specs=smem(len(tables)) + [pl.BlockSpec(memory_space=pl.ANY)] * 5,
             out_specs=[vmem()] * count,
             out_shape=[pltpu.VMEM(pay_shape, F32)] * count,
             scratch_shapes=[
                 pltpu.SemaphoreType.DMA((count, SIDE + 1)),
-                pltpu.VMEM((2, 1, 4 * SIDE), jnp.int32),
-                pltpu.SemaphoreType.DMA((2,)),
+                pltpu.VMEM((3, 1, 4 * SIDE), jnp.int32),
+                pltpu.SemaphoreType.DMA((3,)),
             ],
             compiler_params=pltpu.CompilerParams(vmem_limit_bytes=LIMIT),
-        )(marks, *[pltpu.with_memory_space_constraint(a, pltpu.HBM) for a in (right_side, border, border_send, border_rows)])
+        )(*tables, *[pltpu.with_memory_space_constraint(a, pltpu.HBM) for a in (right_side, border, border_send, border_rows)], toward)
 
     packed = [*pack(gives[:1]), *pack(gives[1:])]
     pays = [lax.ppermute(pay, axis, perm) for pay, (axis, perm) in zip(packed, sends)]
@@ -305,7 +307,7 @@
     part, once, left_coup, back = call(left_kernel, "left", [field, field, square, field])(mine, part, border, pays[0])
     side_coup = []
     for (_, take, weight), pay in zip(sides, pays[2:]):
-        part, once, block = call(partial(gy_kernel, take, weight), "gy", [(width + TAIL, ncols), field, square])(mine, part, once, border, pay)
+        part, once, block = call(partial(gy_kernel, take, weight), "gy", [field, field, square])(mine, part, once, border, pay)
         side_coup.append(block)
     left_w = lax.ppermute(part, "gx", right)
     image, half = call(right_kernel, "right", [field, (width, ncols // 2)])(mine, part, border, pays[1])

time: 44.3 us -> 47.2 us (1.065)
  waiting for transfers between devices: 18.8 us -> 23.2 us
  starting transfers between devices: 17.1 us -> 16 us
    ppermute x1, waiting for transfers between devices: 0.01 us -> 4.32 us  [shards(): left_w = lax.ppermute(part, 'gx', right)]
    ppermute x1, starting transfers between devices: 1.4 us -> 0.62 us  [shards(): left_w = lax.ppermute(part, 'gx', right)]
    ppermute x3, waiting for transfers between devices: 9.5 us -> 10 us  [shards(): lax.ppermute(pay, axis, perm)]
  transfers between devices with their start and end apart: 14 -> 14, of which waited for: 8 -> 10; matrix products, arithmetic and copies ran while one was open for 0% -> 0% of each run, Pallas kernels for 12% -> 10%
where the time goes in v10:
time: 47.2 us; the launch traced here: 47 us
  waiting for transfers between devices  23.2 us (49%)
  starting transfers between devices  16 us (34%)
  Pallas kernels  6.81 us (14%)
  other arithmetic  0.85 us (2%)
    ppermute x3, waiting for transfers between devices, shards(): lax.ppermute(pay, axis, perm)  10 us
    ppermute x3, starting transfers between devices, shards(): lax.ppermute(pay, axis, perm)  6.88 us
    ppermute x6, starting transfers between devices, join(): lax.ppermute(state, AXES, [(i, i ^ m) for i in range(count)])  6.38 us
    ppermute x1, waiting for transfers between devices, shards(): left_w = lax.ppermute(part, 'gx', right)  4.32 us
    ppermute x6, waiting for transfers between devices, join(): lax.ppermute(state, AXES, [(i, i ^ m) for i in range(count)])  4.18 us
    ppermute x1, waiting for transfers between devices, shards(): lax.ppermute(half if take is None else image, 'gy', perm)  3.51 us
    pallas_call x2, Pallas kernels, pack(): pl.pallas_call(partial(pack_kernel, gives), name='pack', in_specs=smem(le...  2.87 us
    pallas_call x8, Pallas kernels, run(): pl.pallas_call(kernel, name=name, in_specs=[vmem()] * len(args), out_spec...  2.86 us
  transfers between devices with their start and end apart: 14, of which 10 were waited for; matrix products, arithmetic and copies ran while one was open for 0% of the time, Pallas kernels for 10%

profile of v10, /device:TPU:0, one launch (start us, length us, event | category | flops | bytes accessed | tf_op | source)
XLA Modules:
  0.0 47.0 jit_solution(18314726878819484617)
XLA Ops:
  0.0 1.1 %pack.2.packed.mine.refs_0_ = f32[392,256]{1,0:T(8,128)S(1)} custom-call(f32[256,256]{1,0:T(8,128)} %field.3, f32[8,128,128]{2,1,0:T(8,128)} %bitcast.6, s32[1,8]{1,0:T(1,128)} %refs_3_.3, s32[1,8]{1,0:T(1,128)} %refs_4_.1, s32[1,8]{1,0:T(1,128)S(1)} %broadcast_in_dim.3.refs_4_.refs_5_), custom_call_target="tpu_custom_call" | custom-call | tf_op jit(solution)/shard_map/pack/pallas_call | solution.py:266
  1.1 3.1 %collective-permute-start.2 = (f32[392,256]{1,0:T(8,128)S(1)}, f32[392,256]{1,0:T(8,128)S(1)}, u32[]{:S(2)}, u32[]{:S(2)}) collective-permute-start(f32[392,256]{1,0:T(8,128)S(1)} %pack.2.packed.mine.refs_0_), channel_id=1, source_target_pairs={{0,4},{4,8},{8,12},{12,0},{1,5},{5,9},{9,13},{13,1},{2,6},{6,10},{... | collective-permute-start | bytes 1204232 | tf_op jit(solution)/shard_map/ppermute | solution.py:281
  4.3 1.7 %pack.3 = (f32[392,256]{1,0:T(8,128)S(1)}, f32[392,256]{1,0:T(8,128)S(1)}) custom-call(s32[2]{0:T(128)S(1)} %pad_add_fusion.marks.refs_0_, f32[256,256]{1,0:T(8,128)} %field.3, f32[8,128,128]{2,1,0:T(8,128)} %bitcast.7, s32[1,8]{1,0:T(1,128)} %refs_3_.3, s32[1,8]{1,0:T(1,128)} %refs_4_.1, s32[1,8]{1,0:T(1,128)S(1)} %broadcast_in_dim.3.refs_4_.refs_5_), custom_call_target="tpu_custom_call" | custom-call | tf_op jit(solution)/shard_map/pack/pallas_call | solution.py:266
  6.0 1.6 %collective-permute-start.3 = (f32[392,256]{1,0:T(8,128)S(1)}, f32[392,256]{1,0:T(8,128)S(1)}, u32[]{:S(2)}, u32[]{:S(2)}) collective-permute-start(f32[392,256]{1,0:T(8,128)S(1)} %get-tuple-element.28), channel_id=1, source_target_pairs={{0,2},{2,0},{1,3},{3,1},{4,6},{6,4},{5,7},{7,5},{8,10},{10,8},{9,1... | collective-permute-start | bytes 1204232 | tf_op jit(solution)/shard_map/ppermute | solution.py:281
  7.6 2.2 %collective-permute-start.4 = (f32[392,256]{1,0:T(8,128)S(1)}, f32[392,256]{1,0:T(8,128)S(1)}, u32[]{:S(2)}, u32[]{:S(2)}) collective-permute-start(f32[392,256]{1,0:T(8,128)S(1)} %get-tuple-element.30), channel_id=1, source_target_pairs={{4,0},{8,4},{12,8},{0,12},{5,1},{9,5},{13,9},{1,13},{6,2},{10,6},{... | collective-permute-start | bytes 1204232 | tf_op jit(solution)/shard_map/ppermute | solution.py:281
  9.9 1.1 %prep.1 = (f32[256,256]{1,0:T(8,128)S(1)}, f32[256,256]{1,0:T(8,128)S(1)}) custom-call(s32[2,7]{1,0:T(2,128)S(1)} %copy-done.3, s32[2]{0:T(128)S(1)} %pad_add_fusion.marks.refs_0_, f32[1,256]{1,0:T(1,128)S(1)} %bitcast.11, f32[2,7,128,128]{3,2,1,0:T(8,128)S(1)} %copy-done.2, f32[392,256]{1,0:T(8,128)S(1)} %pack.2.packed.mine.refs_0_), custom_call_target="tpu_custom_call" | custom-call | flops 16777216 | bytes 1048576 | tf_op jit(solution)/shard_map/prep/pallas_call | solution.py:288
  11.0 0.6 %collective-permute-start.1 = (f32[256,256]{1,0:T(8,128)S(1)}, f32[256,256]{1,0:T(8,128)S(1)}, u32[]{:S(2)}, u32[]{:S(2)}) collective-permute-start(f32[256,256]{1,0:T(8,128)S(1)} %get-tuple-element.24.pair), channel_id=1, source_target_pairs={{0,1},{1,0},{2,3},{3,2},{4,5},{5,4},{6,7},{7,6},{8,9},{9,8},{10,11... | collective-permute-start | bytes 786440 | tf_op jit(solution)/shard_map/ppermute | solution.py:304
  11.5 1.2 %collective-permute-done.1.mate_pair = f32[256,256]{1,0:T(8,128)S(1)} collective-permute-done((f32[256,256]{1,0:T(8,128)S(1)}, f32[256,256]{1,0:T(8,128)S(1)}, u32[]{:S(2)}, u32[]{:S(2)}) %collective-permute-start.1) | collective-permute-done | bytes 262176 | tf_op jit(solution)/shard_map/ppermute | solution.py:304
  13.1 3.3 %collective-permute-done.2.pay = f32[392,256]{1,0:T(8,128)S(1)} collective-permute-done((f32[392,256]{1,0:T(8,128)S(1)}, f32[392,256]{1,0:T(8,128)S(1)}, u32[]{:S(2)}, u32[]{:S(2)}) %collective-permute-start.2) | collective-permute-done | bytes 401440 | tf_op jit(solution)/shard_map/ppermute | solution.py:281
  16.4 0.6 %left.1 = (f32[256,256]{1,0:T(8,128)S(1)}, f32[256,256]{1,0:T(8,128)S(1)}, f32[256,256]{1,0:T(8,128)S(1)}, f32[256,256]{1,0:T(8,128)S(1)}) custom-call(f32[392,256]{1,0:T(8,128)S(1)} %pack.2.packed.mine.refs_0_, f32[256,256]{1,0:T(8,128)S(1)} %get-tuple-element.25.part, f32[8,128,128]{2,1,0:T(8,128)S(1)} %bitcast.8, f32[392,256]{1,0:T(8,128)S(1)} %collective-permute-done.2.pay), custom_call_target="tpu_custom_call" | custom-call | tf_op jit(solution)/shard_map/left/pallas_call | solution.py:25
  17.4 6.7 %collective-permute-done.4.pay = f32[392,256]{1,0:T(8,128)S(1)} collective-permute-done((f32[392,256]{1,0:T(8,128)S(1)}, f32[392,256]{1,0:T(8,128)S(1)}, u32[]{:S(2)}, u32[]{:S(2)}) %collective-permute-start.4) | collective-permute-done | bytes 401440 | tf_op jit(solution)/shard_map/ppermute | solution.py:281
  24.6 0.6 %collective-permute-start.6 = (f32[256,256]{1,0:T(8,128)S(1)}, f32[256,256]{1,0:T(8,128)S(1)}, u32[]{:S(2)}, u32[]{:S(2)}) collective-permute-start(f32[256,256]{1,0:T(8,128)S(1)} %get-tuple-element.29.part), channel_id=1, source_target_pairs={{0,4},{4,8},{8,12},{12,0},{1,5},{5,9},{9,13},{13,1},{2,6},{6,10},{... | collective-permute-start | bytes 786440 | tf_op jit(solution)/shard_map/ppermute | solution.py:312
  25.2 1.5 %collective-permute-start.7 = (f32[256,128]{1,0:T(8,128)S(1)}, f32[256,128]{1,0:T(8,128)S(1)}, u32[]{:S(2)}, u32[]{:S(2)}) collective-permute-start(f32[256,128]{1,0:T(8,128)S(1)} %get-tuple-element.40), channel_id=1, source_target_pairs={{0,2},{2,0},{1,3},{3,1},{4,6},{6,4},{5,7},{7,5},{8,10},{10,8},{9,1... | collective-permute-start | bytes 393224 | tf_op jit(solution)/shard_map/ppermute | solution.py:322
  26.7 0.6 %near.1 = (f32[256,256]{1,0:T(8,128)S(1)}, f32[256,256]{1,0:T(8,128)S(1)}, f32[8,256]{1,0:T(8,128)S(1)}) custom-call(f32[256,256]{1,0:T(8,128)S(1)} %copy-done.1, f32[256,256]{1,0:T(8,128)S(1)} %get-tuple-element.31.image, f32[256,256]{1,0:T(8,128)S(1)} %get-tuple-element.32.once, f32[256,256]{1,0:T(8,128)S(1)} %collective-permute-done.mate, ...), custom_call_target="tpu_custom_call" | custom-call | tf_op jit(solution)/shard_map/near/pallas_call | solution.py:25
  27.3 3.5 %collective-permute-done.7.refs_3_ = f32[256,128]{1,0:T(8,128)S(1)} collective-permute-done((f32[256,128]{1,0:T(8,128)S(1)}, f32[256,128]{1,0:T(8,128)S(1)}, u32[]{:S(2)}, u32[]{:S(2)}) %collective-permute-start.7) | collective-permute-done | bytes 131104 | tf_op jit(solution)/shard_map/ppermute | solution.py:322
  30.8 4.3 %collective-permute-done.6.left = f32[256,256]{1,0:T(8,128)S(1)} collective-permute-done((f32[256,256]{1,0:T(8,128)S(1)}, f32[256,256]{1,0:T(8,128)S(1)}, u32[]{:S(2)}, u32[]{:S(2)}) %collective-permute-start.6) | collective-permute-done | bytes 262176 | tf_op jit(solution)/shard_map/ppermute | solution.py:312
  35.6 0.8 %collective-permute-start.10 = (f32[8,256]{1,0:T(8,128)S(1)}, f32[8,256]{1,0:T(8,128)S(1)}, u32[]{:S(2)}, u32[]{:S(2)}) collective-permute-start(f32[8,256]{1,0:T(8,128)S(1)} %far.1.refs_0_), channel_id=1, source_target_pairs={{0,3},{1,2},{2,1},{3,0},{4,7},{5,6},{6,5},{7,4},{8,11},{9,10},{10,... | collective-permute-start | bytes 24584 | tf_op jit(solution)/shard_map/ppermute | solution.py:45
  36.4 0.8 %collective-permute-start.9 = (f32[8,256]{1,0:T(8,128)S(1)}, f32[8,256]{1,0:T(8,128)S(1)}, u32[]{:S(2)}, u32[]{:S(2)}) collective-permute-start(f32[8,256]{1,0:T(8,128)S(1)} %far.1.refs_0_), channel_id=1, source_target_pairs={{0,2},{1,3},{2,0},{3,1},{4,6},{5,7},{6,4},{7,5},{8,10},{9,11},{10,... | collective-permute-start | bytes 24584 | tf_op jit(solution)/shard_map/ppermute | solution.py:45
  37.5 1.2 %collective-permute-done.10.refs_3_ = f32[8,256]{1,0:T(8,128)S(1)} collective-permute-done((f32[8,256]{1,0:T(8,128)S(1)}, f32[8,256]{1,0:T(8,128)S(1)}, u32[]{:S(2)}, u32[]{:S(2)}) %collective-permute-start.10) | collective-permute-done | bytes 8224 | tf_op jit(solution)/shard_map/ppermute | solution.py:45
  38.8 1.3 %collective-permute-done.9.refs_2_ = f32[8,256]{1,0:T(8,128)S(1)} collective-permute-done((f32[8,256]{1,0:T(8,128)S(1)}, f32[8,256]{1,0:T(8,128)S(1)}, u32[]{:S(2)}, u32[]{:S(2)}) %collective-permute-start.9) | collective-permute-done | bytes 8224 | tf_op jit(solution)/shard_map/ppermute | solution.py:45
  40.1 1.0 %collective-permute-start.13 = (f32[8,256]{1,0:T(8,128)S(1)}, f32[8,256]{1,0:T(8,128)S(1)}, u32[]{:S(2)}, u32[]{:S(2)}) collective-permute-start(f32[8,256]{1,0:T(8,128)S(1)} %merge.2.refs_0_), channel_id=1, source_target_pairs={{0,12},{1,13},{2,14},{3,15},{4,8},{5,9},{6,10},{7,11},{8,4},{9,5},... | collective-permute-start | bytes 24584 | tf_op jit(solution)/shard_map/ppermute | solution.py:45
  41.1 3.4 %collective-permute-start.11 = (f32[8,256]{1,0:T(8,128)S(1)}, f32[8,256]{1,0:T(8,128)S(1)}, u32[]{:S(2)}, u32[]{:S(2)}) collective-permute-start(f32[8,256]{1,0:T(8,128)S(1)} %merge.2.refs_0_), channel_id=1, source_target_pairs={{0,4},{1,5},{2,6},{3,7},{4,0},{5,1},{6,2},{7,3},{8,12},{9,13},{10,... | collective-permute-start | bytes 24584 | tf_op jit(solution)/shard_map/ppermute | solution.py:45
  44.6 1.1 %collective-permute-done.13.refs_3_ = f32[8,256]{1,0:T(8,128)S(1)} collective-permute-done((f32[8,256]{1,0:T(8,128)S(1)}, f32[8,256]{1,0:T(8,128)S(1)}, u32[]{:S(2)}, u32[]{:S(2)}) %collective-permute-start.13) | collective-permute-done | bytes 8224 | tf_op jit(solution)/shard_map/ppermute | solution.py:45
  46.3 0.7 %multiply_subtract_fusion = f32[256,256]{1,0:T(8,128)} fusion(f32[256,256]{1,0:T(8,128)S(1)} %get-tuple-element.31.image, f32[256,256]{1,0:T(8,128)S(1)} %copy-done.1, f32[256]{0:T(256)S(1)} %bitcast.13, f32[256]{0:T(256)S(1)} %bitcast.12), kind=kLoop, calls=%fused_computation | loop fusion | flops 196608 | bytes 788480 | tf_op jit(solution)/shard_map/sub | solution.py:330
  (30 shorter events, 2.8 us)
Async XLA Ops:
  0.0 9.9 %copy-start.2 = (f32[2,7,128,128]{3,2,1,0:T(8,128)S(1)}, f32[2,7,128,128]{3,2,1,0:T(8,128)}, u32[]{:S(2)}) copy-start(f32[2,7,128,128]{3,2,1,0:T(8,128)} %local.1) | copy-start | bytes 2752516
  1.1 15.3 %collective-permute-start.2 = (f32[392,256]{1,0:T(8,128)S(1)}, f32[392,256]{1,0:T(8,128)S(1)}, u32[]{:S(2)}, u32[]{:S(2)}) collective-permute-start(f32[392,256]{1,0:T(8,128)S(1)} %pack.2.packed.mine.refs_0_), channel_id=1, source_target_pairs={{0,4},{4,8},{8,12},{12,0},{1,5},{5,9},{9,13},{13,1},{2,6},{6,10},{... | collective-permute-start | bytes 1204232 | tf_op jit(solution)/shard_map/ppermute | solution.py:281
  4.3 5.6 %copy-start.1 = (f32[256,256]{1,0:T(8,128)S(1)}, f32[256,256]{1,0:T(8,128)}, u32[]{:S(2)}) copy-start(f32[256,256]{1,0:T(8,128)} %field.3) | copy-start | bytes 786436
  6.0 10.9 %collective-permute-start.3 = (f32[392,256]{1,0:T(8,128)S(1)}, f32[392,256]{1,0:T(8,128)S(1)}, u32[]{:S(2)}, u32[]{:S(2)}) collective-permute-start(f32[392,256]{1,0:T(8,128)S(1)} %get-tuple-element.28), channel_id=1, source_target_pairs={{0,2},{2,0},{1,3},{3,1},{4,6},{6,4},{5,7},{7,5},{8,10},{10,8},{9,1... | collective-permute-start | bytes 1204232 | tf_op jit(solution)/shard_map/ppermute | solution.py:281
  7.6 2.3 %copy-start.4 = (f32[256]{0:T(256)S(1)}, f32[256]{0:T(256)}, u32[]{:S(2)}) copy-start(f32[256]{0:T(256)} %param.8) | copy-start | bytes 3076
  7.6 2.3 %copy-start.3 = (s32[2,7]{1,0:T(2,128)S(1)}, s32[2,7]{1,0:T(2,128)}, u32[]{:S(2)}) copy-start(s32[2,7]{1,0:T(2,128)} %cols.1) | copy-start | bytes 172
  7.6 16.5 %collective-permute-start.4 = (f32[392,256]{1,0:T(8,128)S(1)}, f32[392,256]{1,0:T(8,128)S(1)}, u32[]{:S(2)}, u32[]{:S(2)}) collective-permute-start(f32[392,256]{1,0:T(8,128)S(1)} %get-tuple-element.30), channel_id=1, source_target_pairs={{4,0},{8,4},{12,8},{0,12},{5,1},{9,5},{13,9},{1,13},{6,2},{10,6},{... | collective-permute-start | bytes 1204232 | tf_op jit(solution)/shard_map/ppermute | solution.py:281
  9.9 1.7 %collective-permute-start = (f32[256,256]{1,0:T(8,128)S(1)}, f32[256,256]{1,0:T(8,128)S(1)}, u32[]{:S(2)}, u32[]{:S(2)}) collective-permute-start(f32[256,256]{1,0:T(8,128)S(1)} %copy-done.1), channel_id=1, source_target_pairs={{0,1},{1,0},{2,3},{3,2},{4,5},{5,4},{6,7},{7,6},{8,9},{9,8},{10,11... | collective-permute-start | bytes 786440 | tf_op jit(solution)/shard_map/ppermute | solution.py:283
  11.0 1.7 %collective-permute-start.1 = (f32[256,256]{1,0:T(8,128)S(1)}, f32[256,256]{1,0:T(8,128)S(1)}, u32[]{:S(2)}, u32[]{:S(2)}) collective-permute-start(f32[256,256]{1,0:T(8,128)S(1)} %get-tuple-element.24.pair), channel_id=1, source_target_pairs={{0,1},{1,0},{2,3},{3,2},{4,5},{5,4},{6,7},{7,6},{8,9},{9,8},{10,11... | collective-permute-start | bytes 786440 | tf_op jit(solution)/shard_map/ppermute | solution.py:304
  12.7 3.7 %copy-start = (f32[1,8,128,128]{3,2,1,0:T(8,128)S(1)}, f32[1,8,128,128]{3,2,1,0:T(8,128)}, u32[]{:S(2)}) copy-start(f32[1,8,128,128]{3,2,1,0:T(8,128)} %param.11) | copy-start | bytes 1572868
  24.5 2.2 %collective-permute-start.5 = (f32[256,256]{1,0:T(8,128)S(1)}, f32[256,256]{1,0:T(8,128)S(1)}, u32[]{:S(2)}, u32[]{:S(2)}) collective-permute-start(f32[256,256]{1,0:T(8,128)S(1)} %get-tuple-element.31.image), channel_id=1, source_target_pairs={{0,1},{1,0},{2,3},{3,2},{4,5},{5,4},{6,7},{7,6},{8,9},{9,8},{10,11... | collective-permute-start | bytes 786440 | tf_op jit(solution)/shard_map/ppermute | solution.py:314
  24.6 10.5 %collective-permute-start.6 = (f32[256,256]{1,0:T(8,128)S(1)}, f32[256,256]{1,0:T(8,128)S(1)}, u32[]{:S(2)}, u32[]{:S(2)}) collective-permute-start(f32[256,256]{1,0:T(8,128)S(1)} %get-tuple-element.29.part), channel_id=1, source_target_pairs={{0,4},{4,8},{8,12},{12,0},{1,5},{5,9},{9,13},{13,1},{2,6},{6,10},{... | collective-permute-start | bytes 786440 | tf_op jit(solution)/shard_map/ppermute | solution.py:312
  25.2 5.6 %collective-permute-start.7 = (f32[256,128]{1,0:T(8,128)S(1)}, f32[256,128]{1,0:T(8,128)S(1)}, u32[]{:S(2)}, u32[]{:S(2)}) collective-permute-start(f32[256,128]{1,0:T(8,128)S(1)} %get-tuple-element.40), channel_id=1, source_target_pairs={{0,2},{2,0},{1,3},{3,1},{4,6},{6,4},{5,7},{7,5},{8,10},{10,8},{9,1... | collective-permute-start | bytes 393224 | tf_op jit(solution)/shard_map/ppermute | solution.py:322
  35.6 3.2 %collective-permute-start.10 = (f32[8,256]{1,0:T(8,128)S(1)}, f32[8,256]{1,0:T(8,128)S(1)}, u32[]{:S(2)}, u32[]{:S(2)}) collective-permute-start(f32[8,256]{1,0:T(8,128)S(1)} %far.1.refs_0_), channel_id=1, source_target_pairs={{0,3},{1,2},{2,1},{3,0},{4,7},{5,6},{6,5},{7,4},{8,11},{9,10},{10,... | collective-permute-start | bytes 24584 | tf_op jit(solution)/shard_map/ppermute | solution.py:45
  36.4 3.7 %collective-permute-start.9 = (f32[8,256]{1,0:T(8,128)S(1)}, f32[8,256]{1,0:T(8,128)S(1)}, u32[]{:S(2)}, u32[]{:S(2)}) collective-permute-start(f32[8,256]{1,0:T(8,128)S(1)} %far.1.refs_0_), channel_id=1, source_target_pairs={{0,2},{1,3},{2,0},{3,1},{4,6},{5,7},{6,4},{7,5},{8,10},{9,11},{10,... | collective-permute-start | bytes 24584 | tf_op jit(solution)/shard_map/ppermute | solution.py:45
  37.2 2.8 %collective-permute-start.8 = (f32[8,256]{1,0:T(8,128)S(1)}, f32[8,256]{1,0:T(8,128)S(1)}, u32[]{:S(2)}, u32[]{:S(2)}) collective-permute-start(f32[8,256]{1,0:T(8,128)S(1)} %far.1.refs_0_), channel_id=1, source_target_pairs={{0,1},{1,0},{2,3},{3,2},{4,5},{5,4},{6,7},{7,6},{8,9},{9,8},{10,11... | collective-permute-start | bytes 24584 | tf_op jit(solution)/shard_map/ppermute | solution.py:45
  40.1 5.5 %collective-permute-start.13 = (f32[8,256]{1,0:T(8,128)S(1)}, f32[8,256]{1,0:T(8,128)S(1)}, u32[]{:S(2)}, u32[]{:S(2)}) collective-permute-start(f32[8,256]{1,0:T(8,128)S(1)} %merge.2.refs_0_), channel_id=1, source_target_pairs={{0,12},{1,13},{2,14},{3,15},{4,8},{5,9},{6,10},{7,11},{8,4},{9,5},... | collective-permute-start | bytes 24584 | tf_op jit(solution)/shard_map/ppermute | solution.py:45
  41.1 4.7 %collective-permute-start.12 = (f32[8,256]{1,0:T(8,128)S(1)}, f32[8,256]{1,0:T(8,128)S(1)}, u32[]{:S(2)}, u32[]{:S(2)}) collective-permute-start(f32[8,256]{1,0:T(8,128)S(1)} %merge.2.refs_0_), channel_id=1, source_target_pairs={{0,8},{1,9},{2,10},{3,11},{4,12},{5,13},{6,14},{7,15},{8,0},{9,1},... | collective-permute-start | bytes 24584 | tf_op jit(solution)/shard_map/ppermute | solution.py:45
  41.1 5.1 %collective-permute-start.11 = (f32[8,256]{1,0:T(8,128)S(1)}, f32[8,256]{1,0:T(8,128)S(1)}, u32[]{:S(2)}, u32[]{:S(2)}) collective-permute-start(f32[8,256]{1,0:T(8,128)S(1)} %merge.2.refs_0_), channel_id=1, source_target_pairs={{0,4},{1,5},{2,6},{3,7},{4,0},{5,1},{6,2},{7,3},{8,12},{9,13},{10,... | collective-permute-start | bytes 24584 | tf_op jit(solution)/shard_map/ppermute | solution.py:45

commit v11 on v10

--- a/solution.py
+++ b/solution.py
@@ -12,6 +12,7 @@
 AXES = ("gx", "gy", "nd")
 SIDE = 2
 LIMIT = 8 << 20
+EXTRA = 8
 TAIL = 8
 
 
@@ -172,14 +173,16 @@
     toward = mine[pl.ds(mine.shape[0] - TAIL + 2, 1), pl.ds(0, 1)]
     coup[...] = edge(toward if take is None else take, mine, pay, border)
     term = dot(coup[...], pay[pl.ds(0, width), :])
-    image[...] = part[...] + term
+    image[pl.ds(0, width), :] = part[pl.ds(0, width), :] + term
+    if image.shape[0] > width:
+        image[pl.ds(width, EXTRA), :] = jnp.zeros((EXTRA, term.shape[1]), F32)
     scale = weight * turn(mine, width) if take is None else weight
     once[...] = single[...] + scale * term
 
 
 def right_kernel(mine, part, border, pay, image, half):
     width = image.shape[0]
-    full = part[...] + dot(edge(1, mine, pay, border), pay[pl.ds(0, width), :])
+    full = part[pl.ds(0, width), :] + dot(edge(1, mine, pay, border), pay[pl.ds(0, width), :])
     image[...] = full
     middle = full.shape[1] // 2
     toward = mine[pl.ds(mine.shape[0] - TAIL + 2, 1), pl.ds(0, 1)]
@@ -202,7 +205,7 @@
     width = field.shape[0]
     b = field[...]
     c = near[1:2, :]
-    acc = part[...] + 2.0 * dot(coup[...], left[...] + lift[...])
+    acc = part[...] + 2.0 * dot(coup[...], left[pl.ds(0, width), :] + lift[...])
     if sides:
         mine, coup_gy, pay, side = sides
         if take is None:
@@ -307,7 +310,7 @@
     part, once, left_coup, back = call(left_kernel, "left", [field, field, square, field])(mine, part, border, pays[0])
     side_coup = []
     for (_, take, weight), pay in zip(sides, pays[2:]):
-        part, once, block = call(partial(gy_kernel, take, weight), "gy", [field, field, square])(mine, part, once, border, pay)
+        part, once, block = call(partial(gy_kernel, take, weight), "gy", [(width + EXTRA, ncols), field, square])(mine, part, once, border, pay)
         side_coup.append(block)
     left_w = lax.ppermute(part, "gx", right)
     image, half = call(right_kernel, "right", [field, (width, ncols // 2)])(mine, part, border, pays[1])

time: 47.2 us -> 43.8 us (0.928)
  waiting for transfers between devices: 23.2 us -> 18.6 us
  starting transfers between devices: 16 us -> 17.2 us
    ppermute x1, waiting for transfers between devices: 4.32 us -> 0.01 us  [shards(): left_w = lax.ppermute(part, 'gx', right)]
    ppermute x1, starting transfers between devices: 0.62 us -> 1.5 us  [shards(): left_w = lax.ppermute(part, 'gx', right)]
    ppermute x3, waiting for transfers between devices: 10 us -> 9.32 us  [shards(): lax.ppermute(pay, axis, perm)]
  transfers between devices with their start and end apart: 14 -> 14, of which waited for: 10 -> 8; matrix products, arithmetic and copies ran while one was open for 0% -> 0% of each run, Pallas kernels for 10% -> 12%
where the time goes in v11:
time: 43.8 us; the launch traced here: 43.7 us
  waiting for transfers between devices  18.6 us (42%)
  starting transfers between devices  17.2 us (39%)
  Pallas kernels  6.82 us (16%)
  other arithmetic  0.85 us (2%)
    ppermute x3, waiting for transfers between devices, shards(): lax.ppermute(pay, axis, perm)  9.32 us
    ppermute x3, starting transfers between devices, shards(): lax.ppermute(pay, axis, perm)  6.88 us
    ppermute x6, starting transfers between devices, join(): lax.ppermute(state, AXES, [(i, i ^ m) for i in range(count)])  6.4 us
    ppermute x6, waiting for transfers between devices, join(): lax.ppermute(state, AXES, [(i, i ^ m) for i in range(count)])  4.61 us
    ppermute x1, waiting for transfers between devices, shards(): lax.ppermute(half if take is None else image, 'gy', perm)  3.55 us
    pallas_call x2, Pallas kernels, pack(): pl.pallas_call(partial(pack_kernel, gives), name='pack', in_specs=smem(le...  2.87 us
    pallas_call x8, Pallas kernels, run(): pl.pallas_call(kernel, name=name, in_specs=[vmem()] * len(args), out_spec...  2.86 us
    ppermute x1, starting transfers between devices, shards(): lax.ppermute(half if take is None else image, 'gy', perm)  1.8 us
  transfers between devices with their start and end apart: 14, of which 8 were waited for; matrix products, arithmetic and copies ran while one was open for 0% of the time, Pallas kernels for 12%

profile of v11, /device:TPU:0, one launch (start us, length us, event | category | flops | bytes accessed | tf_op | source)
XLA Modules:
  0.0 43.7 jit_solution(11135186909385346191)
XLA Ops:
  0.0 1.1 %pack.2.packed.mine.refs_0_ = f32[392,256]{1,0:T(8,128)S(1)} custom-call(f32[256,256]{1,0:T(8,128)} %field.3, f32[8,128,128]{2,1,0:T(8,128)} %bitcast.6, s32[1,8]{1,0:T(1,128)} %refs_3_.3, s32[1,8]{1,0:T(1,128)} %refs_4_.1, s32[1,8]{1,0:T(1,128)S(1)} %broadcast_in_dim.3.refs_4_.refs_5_), custom_call_target="tpu_custom_call" | custom-call | tf_op jit(solution)/shard_map/pack/pallas_call | solution.py:269
  1.1 3.1 %collective-permute-start.2 = (f32[392,256]{1,0:T(8,128)S(1)}, f32[392,256]{1,0:T(8,128)S(1)}, u32[]{:S(2)}, u32[]{:S(2)}) collective-permute-start(f32[392,256]{1,0:T(8,128)S(1)} %pack.2.packed.mine.refs_0_), channel_id=1, source_target_pairs={{0,4},{4,8},{8,12},{12,0},{1,5},{5,9},{9,13},{13,1},{2,6},{6,10},{... | collective-permute-start | bytes 1204232 | tf_op jit(solution)/shard_map/ppermute | solution.py:284
  4.3 1.7 %pack.3 = (f32[392,256]{1,0:T(8,128)S(1)}, f32[392,256]{1,0:T(8,128)S(1)}) custom-call(s32[2]{0:T(128)S(1)} %pad_add_fusion.marks.refs_0_, f32[256,256]{1,0:T(8,128)} %field.3, f32[8,128,128]{2,1,0:T(8,128)} %bitcast.7, s32[1,8]{1,0:T(1,128)} %refs_3_.3, s32[1,8]{1,0:T(1,128)} %refs_4_.1, s32[1,8]{1,0:T(1,128)S(1)} %broadcast_in_dim.3.refs_4_.refs_5_), custom_call_target="tpu_custom_call" | custom-call | tf_op jit(solution)/shard_map/pack/pallas_call | solution.py:269
  6.0 1.6 %collective-permute-start.3 = (f32[392,256]{1,0:T(8,128)S(1)}, f32[392,256]{1,0:T(8,128)S(1)}, u32[]{:S(2)}, u32[]{:S(2)}) collective-permute-start(f32[392,256]{1,0:T(8,128)S(1)} %get-tuple-element.28), channel_id=1, source_target_pairs={{0,2},{2,0},{1,3},{3,1},{4,6},{6,4},{5,7},{7,5},{8,10},{10,8},{9,1... | collective-permute-start | bytes 1204232 | tf_op jit(solution)/shard_map/ppermute | solution.py:284
  7.6 2.2 %collective-permute-start.4 = (f32[392,256]{1,0:T(8,128)S(1)}, f32[392,256]{1,0:T(8,128)S(1)}, u32[]{:S(2)}, u32[]{:S(2)}) collective-permute-start(f32[392,256]{1,0:T(8,128)S(1)} %get-tuple-element.30), channel_id=1, source_target_pairs={{4,0},{8,4},{12,8},{0,12},{5,1},{9,5},{13,9},{1,13},{6,2},{10,6},{... | collective-permute-start | bytes 1204232 | tf_op jit(solution)/shard_map/ppermute | solution.py:284
  9.9 1.1 %prep.1 = (f32[256,256]{1,0:T(8,128)S(1)}, f32[256,256]{1,0:T(8,128)S(1)}) custom-call(s32[2,7]{1,0:T(2,128)S(1)} %copy-done.3, s32[2]{0:T(128)S(1)} %pad_add_fusion.marks.refs_0_, f32[1,256]{1,0:T(1,128)S(1)} %bitcast.11, f32[2,7,128,128]{3,2,1,0:T(8,128)S(1)} %copy-done.2, f32[392,256]{1,0:T(8,128)S(1)} %pack.2.packed.mine.refs_0_), custom_call_target="tpu_custom_call" | custom-call | flops 16777216 | bytes 1048576 | tf_op jit(solution)/shard_map/prep/pallas_call | solution.py:291
  11.0 0.6 %collective-permute-start.1 = (f32[256,256]{1,0:T(8,128)S(1)}, f32[256,256]{1,0:T(8,128)S(1)}, u32[]{:S(2)}, u32[]{:S(2)}) collective-permute-start(f32[256,256]{1,0:T(8,128)S(1)} %get-tuple-element.24.pair), channel_id=1, source_target_pairs={{0,1},{1,0},{2,3},{3,2},{4,5},{5,4},{6,7},{7,6},{8,9},{9,8},{10,11... | collective-permute-start | bytes 786440 | tf_op jit(solution)/shard_map/ppermute | solution.py:307
  11.5 1.2 %collective-permute-done.1.mate_pair = f32[256,256]{1,0:T(8,128)S(1)} collective-permute-done((f32[256,256]{1,0:T(8,128)S(1)}, f32[256,256]{1,0:T(8,128)S(1)}, u32[]{:S(2)}, u32[]{:S(2)}) %collective-permute-start.1) | collective-permute-done | bytes 262176 | tf_op jit(solution)/shard_map/ppermute | solution.py:307
  13.1 3.3 %collective-permute-done.2.pay = f32[392,256]{1,0:T(8,128)S(1)} collective-permute-done((f32[392,256]{1,0:T(8,128)S(1)}, f32[392,256]{1,0:T(8,128)S(1)}, u32[]{:S(2)}, u32[]{:S(2)}) %collective-permute-start.2) | collective-permute-done | bytes 401440 | tf_op jit(solution)/shard_map/ppermute | solution.py:284
  16.4 0.6 %left.1 = (f32[256,256]{1,0:T(8,128)S(1)}, f32[256,256]{1,0:T(8,128)S(1)}, f32[256,256]{1,0:T(8,128)S(1)}, f32[256,256]{1,0:T(8,128)S(1)}) custom-call(f32[392,256]{1,0:T(8,128)S(1)} %pack.2.packed.mine.refs_0_, f32[256,256]{1,0:T(8,128)S(1)} %get-tuple-element.25.part, f32[8,128,128]{2,1,0:T(8,128)S(1)} %bitcast.8, f32[392,256]{1,0:T(8,128)S(1)} %collective-permute-done.2.pay), custom_call_target="tpu_custom_call" | custom-call | tf_op jit(solution)/shard_map/left/pallas_call | solution.py:26
  17.4 1.5 %collective-permute-start.6 = (f32[264,256]{1,0:T(8,128)S(1)}, f32[264,256]{1,0:T(8,128)S(1)}, u32[]{:S(2)}, u32[]{:S(2)}) collective-permute-start(f32[264,256]{1,0:T(8,128)S(1)} %get-tuple-element.29.part), channel_id=1, source_target_pairs={{0,4},{4,8},{8,12},{12,0},{1,5},{5,9},{9,13},{13,1},{2,6},{6,10},{... | collective-permute-start | bytes 811016 | tf_op jit(solution)/shard_map/ppermute | solution.py:315
  18.9 6.0 %collective-permute-done.4.pay = f32[392,256]{1,0:T(8,128)S(1)} collective-permute-done((f32[392,256]{1,0:T(8,128)S(1)}, f32[392,256]{1,0:T(8,128)S(1)}, u32[]{:S(2)}, u32[]{:S(2)}) %collective-permute-start.4) | collective-permute-done | bytes 401440 | tf_op jit(solution)/shard_map/ppermute | solution.py:284
  25.4 1.8 %collective-permute-start.7 = (f32[256,128]{1,0:T(8,128)S(1)}, f32[256,128]{1,0:T(8,128)S(1)}, u32[]{:S(2)}, u32[]{:S(2)}) collective-permute-start(f32[256,128]{1,0:T(8,128)S(1)} %get-tuple-element.40), channel_id=1, source_target_pairs={{0,2},{2,0},{1,3},{3,1},{4,6},{6,4},{5,7},{7,5},{8,10},{10,8},{9,1... | collective-permute-start | bytes 393224 | tf_op jit(solution)/shard_map/ppermute | solution.py:325
  27.2 0.6 %near.1 = (f32[256,256]{1,0:T(8,128)S(1)}, f32[256,256]{1,0:T(8,128)S(1)}, f32[8,256]{1,0:T(8,128)S(1)}) custom-call(f32[256,256]{1,0:T(8,128)S(1)} %copy-done.1, f32[256,256]{1,0:T(8,128)S(1)} %get-tuple-element.31.image, f32[256,256]{1,0:T(8,128)S(1)} %get-tuple-element.32.once, f32[256,256]{1,0:T(8,128)S(1)} %collective-permute-done.mate, ...), custom_call_target="tpu_custom_call" | custom-call | tf_op jit(solution)/shard_map/near/pallas_call | solution.py:26
  27.7 3.5 %collective-permute-done.7.refs_3_ = f32[256,128]{1,0:T(8,128)S(1)} collective-permute-done((f32[256,128]{1,0:T(8,128)S(1)}, f32[256,128]{1,0:T(8,128)S(1)}, u32[]{:S(2)}, u32[]{:S(2)}) %collective-permute-start.7) | collective-permute-done | bytes 131104 | tf_op jit(solution)/shard_map/ppermute | solution.py:325
  31.8 1.1 %collective-permute-start.10 = (f32[8,256]{1,0:T(8,128)S(1)}, f32[8,256]{1,0:T(8,128)S(1)}, u32[]{:S(2)}, u32[]{:S(2)}) collective-permute-start(f32[8,256]{1,0:T(8,128)S(1)} %far.1.refs_0_), channel_id=1, source_target_pairs={{0,3},{1,2},{2,1},{3,0},{4,7},{5,6},{6,5},{7,4},{8,11},{9,10},{10,... | collective-permute-start | bytes 24584 | tf_op jit(solution)/shard_map/ppermute | solution.py:46
  32.9 0.8 %collective-permute-start.9 = (f32[8,256]{1,0:T(8,128)S(1)}, f32[8,256]{1,0:T(8,128)S(1)}, u32[]{:S(2)}, u32[]{:S(2)}) collective-permute-start(f32[8,256]{1,0:T(8,128)S(1)} %far.1.refs_0_), channel_id=1, source_target_pairs={{0,2},{1,3},{2,0},{3,1},{4,6},{5,7},{6,4},{7,5},{8,10},{9,11},{10,... | collective-permute-start | bytes 24584 | tf_op jit(solution)/shard_map/ppermute | solution.py:46
  33.8 1.2 %collective-permute-done.10.refs_3_ = f32[8,256]{1,0:T(8,128)S(1)} collective-permute-done((f32[8,256]{1,0:T(8,128)S(1)}, f32[8,256]{1,0:T(8,128)S(1)}, u32[]{:S(2)}, u32[]{:S(2)}) %collective-permute-start.10) | collective-permute-done | bytes 8224 | tf_op jit(solution)/shard_map/ppermute | solution.py:46
  34.9 1.6 %collective-permute-done.9.refs_2_ = f32[8,256]{1,0:T(8,128)S(1)} collective-permute-done((f32[8,256]{1,0:T(8,128)S(1)}, f32[8,256]{1,0:T(8,128)S(1)}, u32[]{:S(2)}, u32[]{:S(2)}) %collective-permute-start.9) | collective-permute-done | bytes 8224 | tf_op jit(solution)/shard_map/ppermute | solution.py:46
  36.6 1.7 %collective-permute-start.13 = (f32[8,256]{1,0:T(8,128)S(1)}, f32[8,256]{1,0:T(8,128)S(1)}, u32[]{:S(2)}, u32[]{:S(2)}) collective-permute-start(f32[8,256]{1,0:T(8,128)S(1)} %merge.2.refs_0_), channel_id=1, source_target_pairs={{0,12},{1,13},{2,14},{3,15},{4,8},{5,9},{6,10},{7,11},{8,4},{9,5},... | collective-permute-start | bytes 24584 | tf_op jit(solution)/shard_map/ppermute | solution.py:46
  38.7 2.4 %collective-permute-start.11 = (f32[8,256]{1,0:T(8,128)S(1)}, f32[8,256]{1,0:T(8,128)S(1)}, u32[]{:S(2)}, u32[]{:S(2)}) collective-permute-start(f32[8,256]{1,0:T(8,128)S(1)} %merge.2.refs_0_), channel_id=1, source_target_pairs={{0,4},{1,5},{2,6},{3,7},{4,0},{5,1},{6,2},{7,3},{8,12},{9,13},{10,... | collective-permute-start | bytes 24584 | tf_op jit(solution)/shard_map/ppermute | solution.py:46
  41.0 1.1 %collective-permute-done.13.refs_3_ = f32[8,256]{1,0:T(8,128)S(1)} collective-permute-done((f32[8,256]{1,0:T(8,128)S(1)}, f32[8,256]{1,0:T(8,128)S(1)}, u32[]{:S(2)}, u32[]{:S(2)}) %collective-permute-start.13) | collective-permute-done | bytes 8224 | tf_op jit(solution)/shard_map/ppermute | solution.py:46
  42.1 0.8 %collective-permute-done.12.refs_2_ = f32[8,256]{1,0:T(8,128)S(1)} collective-permute-done((f32[8,256]{1,0:T(8,128)S(1)}, f32[8,256]{1,0:T(8,128)S(1)}, u32[]{:S(2)}, u32[]{:S(2)}) %collective-permute-start.12) | collective-permute-done | bytes 8224 | tf_op jit(solution)/shard_map/ppermute | solution.py:46
  42.9 0.7 %multiply_subtract_fusion = f32[256,256]{1,0:T(8,128)} fusion(f32[256,256]{1,0:T(8,128)S(1)} %get-tuple-element.31.image, f32[256,256]{1,0:T(8,128)S(1)} %copy-done.1, f32[256]{0:T(256)S(1)} %bitcast.13, f32[256]{0:T(256)S(1)} %bitcast.12), kind=kLoop, calls=%fused_computation | loop fusion | flops 196608 | bytes 788480 | tf_op jit(solution)/shard_map/sub | solution.py:333
  (30 shorter events, 2.4 us)
Async XLA Ops:
  0.0 9.9 %copy-start.2 = (f32[2,7,128,128]{3,2,1,0:T(8,128)S(1)}, f32[2,7,128,128]{3,2,1,0:T(8,128)}, u32[]{:S(2)}) copy-start(f32[2,7,128,128]{3,2,1,0:T(8,128)} %local.1) | copy-start | bytes 2752516
  1.1 15.3 %collective-permute-start.2 = (f32[392,256]{1,0:T(8,128)S(1)}, f32[392,256]{1,0:T(8,128)S(1)}, u32[]{:S(2)}, u32[]{:S(2)}) collective-permute-start(f32[392,256]{1,0:T(8,128)S(1)} %pack.2.packed.mine.refs_0_), channel_id=1, source_target_pairs={{0,4},{4,8},{8,12},{12,0},{1,5},{5,9},{9,13},{13,1},{2,6},{6,10},{... | collective-permute-start | bytes 1204232 | tf_op jit(solution)/shard_map/ppermute | solution.py:284
  4.3 5.6 %copy-start.1 = (f32[256,256]{1,0:T(8,128)S(1)}, f32[256,256]{1,0:T(8,128)}, u32[]{:S(2)}) copy-start(f32[256,256]{1,0:T(8,128)} %field.3) | copy-start | bytes 786436
  6.0 10.9 %collective-permute-start.3 = (f32[392,256]{1,0:T(8,128)S(1)}, f32[392,256]{1,0:T(8,128)S(1)}, u32[]{:S(2)}, u32[]{:S(2)}) collective-permute-start(f32[392,256]{1,0:T(8,128)S(1)} %get-tuple-element.28), channel_id=1, source_target_pairs={{0,2},{2,0},{1,3},{3,1},{4,6},{6,4},{5,7},{7,5},{8,10},{10,8},{9,1... | collective-permute-start | bytes 1204232 | tf_op jit(solution)/shard_map/ppermute | solution.py:284
  7.6 2.3 %copy-start.4 = (f32[256]{0:T(256)S(1)}, f32[256]{0:T(256)}, u32[]{:S(2)}) copy-start(f32[256]{0:T(256)} %param.8) | copy-start | bytes 3076
  7.6 2.3 %copy-start.3 = (s32[2,7]{1,0:T(2,128)S(1)}, s32[2,7]{1,0:T(2,128)}, u32[]{:S(2)}) copy-start(s32[2,7]{1,0:T(2,128)} %cols.1) | copy-start | bytes 172
  7.6 17.3 %collective-permute-start.4 = (f32[392,256]{1,0:T(8,128)S(1)}, f32[392,256]{1,0:T(8,128)S(1)}, u32[]{:S(2)}, u32[]{:S(2)}) collective-permute-start(f32[392,256]{1,0:T(8,128)S(1)} %get-tuple-element.30), channel_id=1, source_target_pairs={{4,0},{8,4},{12,8},{0,12},{5,1},{9,5},{13,9},{1,13},{6,2},{10,6},{... | collective-permute-start | bytes 1204232 | tf_op jit(solution)/shard_map/ppermute | solution.py:284
  9.9 1.7 %collective-permute-start = (f32[256,256]{1,0:T(8,128)S(1)}, f32[256,256]{1,0:T(8,128)S(1)}, u32[]{:S(2)}, u32[]{:S(2)}) collective-permute-start(f32[256,256]{1,0:T(8,128)S(1)} %copy-done.1), channel_id=1, source_target_pairs={{0,1},{1,0},{2,3},{3,2},{4,5},{5,4},{6,7},{7,6},{8,9},{9,8},{10,11... | collective-permute-start | bytes 786440 | tf_op jit(solution)/shard_map/ppermute | solution.py:286
  11.0 1.7 %collective-permute-start.1 = (f32[256,256]{1,0:T(8,128)S(1)}, f32[256,256]{1,0:T(8,128)S(1)}, u32[]{:S(2)}, u32[]{:S(2)}) collective-permute-start(f32[256,256]{1,0:T(8,128)S(1)} %get-tuple-element.24.pair), channel_id=1, source_target_pairs={{0,1},{1,0},{2,3},{3,2},{4,5},{5,4},{6,7},{7,6},{8,9},{9,8},{10,11... | collective-permute-start | bytes 786440 | tf_op jit(solution)/shard_map/ppermute | solution.py:307
  12.7 3.7 %copy-start = (f32[1,8,128,128]{3,2,1,0:T(8,128)S(1)}, f32[1,8,128,128]{3,2,1,0:T(8,128)}, u32[]{:S(2)}) copy-start(f32[1,8,128,128]{3,2,1,0:T(8,128)} %param.11) | copy-start | bytes 1572868
  17.4 13.9 %collective-permute-start.6 = (f32[264,256]{1,0:T(8,128)S(1)}, f32[264,256]{1,0:T(8,128)S(1)}, u32[]{:S(2)}, u32[]{:S(2)}) collective-permute-start(f32[264,256]{1,0:T(8,128)S(1)} %get-tuple-element.29.part), channel_id=1, source_target_pairs={{0,4},{4,8},{8,12},{12,0},{1,5},{5,9},{9,13},{13,1},{2,6},{6,10},{... | collective-permute-start | bytes 811016 | tf_op jit(solution)/shard_map/ppermute | solution.py:315
  25.3 1.9 %collective-permute-start.5 = (f32[256,256]{1,0:T(8,128)S(1)}, f32[256,256]{1,0:T(8,128)S(1)}, u32[]{:S(2)}, u32[]{:S(2)}) collective-permute-start(f32[256,256]{1,0:T(8,128)S(1)} %get-tuple-element.31.image), channel_id=1, source_target_pairs={{0,1},{1,0},{2,3},{3,2},{4,5},{5,4},{6,7},{7,6},{8,9},{9,8},{10,11... | collective-permute-start | bytes 786440 | tf_op jit(solution)/shard_map/ppermute | solution.py:317
  25.4 5.9 %collective-permute-start.7 = (f32[256,128]{1,0:T(8,128)S(1)}, f32[256,128]{1,0:T(8,128)S(1)}, u32[]{:S(2)}, u32[]{:S(2)}) collective-permute-start(f32[256,128]{1,0:T(8,128)S(1)} %get-tuple-element.40), channel_id=1, source_target_pairs={{0,2},{2,0},{1,3},{3,1},{4,6},{6,4},{5,7},{7,5},{8,10},{10,8},{9,1... | collective-permute-start | bytes 393224 | tf_op jit(solution)/shard_map/ppermute | solution.py:325
  31.8 3.1 %collective-permute-start.10 = (f32[8,256]{1,0:T(8,128)S(1)}, f32[8,256]{1,0:T(8,128)S(1)}, u32[]{:S(2)}, u32[]{:S(2)}) collective-permute-start(f32[8,256]{1,0:T(8,128)S(1)} %far.1.refs_0_), channel_id=1, source_target_pairs={{0,3},{1,2},{2,1},{3,0},{4,7},{5,6},{6,5},{7,4},{8,11},{9,10},{10,... | collective-permute-start | bytes 24584 | tf_op jit(solution)/shard_map/ppermute | solution.py:46
  32.9 3.7 %collective-permute-start.9 = (f32[8,256]{1,0:T(8,128)S(1)}, f32[8,256]{1,0:T(8,128)S(1)}, u32[]{:S(2)}, u32[]{:S(2)}) collective-permute-start(f32[8,256]{1,0:T(8,128)S(1)} %far.1.refs_0_), channel_id=1, source_target_pairs={{0,2},{1,3},{2,0},{3,1},{4,6},{5,7},{6,4},{7,5},{8,10},{9,11},{10,... | collective-permute-start | bytes 24584 | tf_op jit(solution)/shard_map/ppermute | solution.py:46
  33.7 2.8 %collective-permute-start.8 = (f32[8,256]{1,0:T(8,128)S(1)}, f32[8,256]{1,0:T(8,128)S(1)}, u32[]{:S(2)}, u32[]{:S(2)}) collective-permute-start(f32[8,256]{1,0:T(8,128)S(1)} %far.1.refs_0_), channel_id=1, source_target_pairs={{0,1},{1,0},{2,3},{3,2},{4,5},{5,4},{6,7},{7,6},{8,9},{9,8},{10,11... | collective-permute-start | bytes 24584 | tf_op jit(solution)/shard_map/ppermute | solution.py:46
  36.6 5.5 %collective-permute-start.13 = (f32[8,256]{1,0:T(8,128)S(1)}, f32[8,256]{1,0:T(8,128)S(1)}, u32[]{:S(2)}, u32[]{:S(2)}) collective-permute-start(f32[8,256]{1,0:T(8,128)S(1)} %merge.2.refs_0_), channel_id=1, source_target_pairs={{0,12},{1,13},{2,14},{3,15},{4,8},{5,9},{6,10},{7,11},{8,4},{9,5},... | collective-permute-start | bytes 24584 | tf_op jit(solution)/shard_map/ppermute | solution.py:46
  38.3 4.5 %collective-permute-start.12 = (f32[8,256]{1,0:T(8,128)S(1)}, f32[8,256]{1,0:T(8,128)S(1)}, u32[]{:S(2)}, u32[]{:S(2)}) collective-permute-start(f32[8,256]{1,0:T(8,128)S(1)} %merge.2.refs_0_), channel_id=1, source_target_pairs={{0,8},{1,9},{2,10},{3,11},{4,12},{5,13},{6,14},{7,15},{8,0},{9,1},... | collective-permute-start | bytes 24584 | tf_op jit(solution)/shard_map/ppermute | solution.py:46
  38.7 4.2 %collective-permute-start.11 = (f32[8,256]{1,0:T(8,128)S(1)}, f32[8,256]{1,0:T(8,128)S(1)}, u32[]{:S(2)}, u32[]{:S(2)}) collective-permute-start(f32[8,256]{1,0:T(8,128)S(1)} %merge.2.refs_0_), channel_id=1, source_target_pairs={{0,4},{1,5},{2,6},{3,7},{4,0},{5,1},{6,2},{7,3},{8,12},{9,13},{10,... | collective-permute-start | bytes 24584 | tf_op jit(solution)/shard_map/ppermute | solution.py:46

commit v12 on v10

--- a/solution.py
+++ b/solution.py
@@ -12,6 +12,7 @@
 AXES = ("gx", "gy", "nd")
 SIDE = 2
 LIMIT = 8 << 20
+EXTRA = 8
 TAIL = 8
 
 
@@ -69,28 +70,41 @@
 
 
 def pack_kernel(gives, *refs):
-    marks, refs = (refs[0], refs[1:]) if None in gives else (None, refs)
-    field, border, send, rows, toward, *pays, sems, table, table_sems = refs
+    marks, refs = (refs[0], refs[1:]) if gives != [1] else (None, refs)
+    field, border, send, rows, toward, *pays, sems, table, table_sems, whole = refs
     width = field.shape[0]
     bs = border.shape[1]
     tables = [pltpu.make_async_copy(ref, table.at[n], table_sems.at[n]) for n, ref in enumerate((rows, send, toward))]
-    copies = []
-    for n, pay in enumerate(pays):
-        give = marks[0] if gives[n] is None else gives[n]
-        copies.append(pltpu.make_async_copy(field, pay.at[pl.ds(0, width), :], sems.at[n, SIDE]))
-        for s in range(SIDE):
-            block = pay.at[pl.ds(width, bs), pl.ds(s * bs, bs)]
-            copies.append(pltpu.make_async_copy(border.at[give * SIDE + s], block, sems.at[n, s]))
+    copies, tails, split = [], [], []
+    for n, give in enumerate(gives):
+        pay = pays.pop(0)
+        tails.append(pay)
+        if give == "halves":
+            other = pays.pop(0)
+            for s in range(SIDE):
+                copies.append(pltpu.make_async_copy(border.at[s], pay.at[pl.ds(width + s * bs, bs), :], sems.at[n, s]))
+            copies.append(pltpu.make_async_copy(field, whole, sems.at[n, SIDE]))
+            split.append((pay, other))
+        else:
+            give = marks[0] if give is None else give
+            copies.append(pltpu.make_async_copy(field, pay.at[pl.ds(0, width), :], sems.at[n, SIDE]))
+            for s in range(SIDE):
+                block = pay.at[pl.ds(width, bs), pl.ds(s * bs, bs)]
+                copies.append(pltpu.make_async_copy(border.at[give * SIDE + s], block, sems.at[n, s]))
     for copy in tables + copies:
         copy.start()
     for copy in tables:
         copy.wait()
     count = table.shape[2]
-    for pay in pays:
+    for pay in tails:
         for n in range(3):
-            pay[pl.ds(width + bs + n, 1), pl.ds(0, count)] = table[n].astype(F32)
+            pay[pl.ds(pay.shape[0] - TAIL + n, 1), pl.ds(0, count)] = table[n].astype(F32)
     for copy in copies:
         copy.wait()
+    for pay, other in split:
+        low, high = whole[:, : whole.shape[1] // 2], whole[:, whole.shape[1] // 2 :]
+        pay[pl.ds(0, width), :] = jnp.where(marks[0] == 3, high, low)
+        other[pl.ds(0, width), :] = jnp.where(marks[0] == 3, low, high)
 
 
 def prep_kernel(cols, marks, diag, local, packed, own, pair):
@@ -120,20 +134,20 @@
     own[...] = lower + lower.T + jnp.where(here == there, diag[...], 0.0)
 
 
-def edge(take, mine, pay, border):
+def edge(take, width, mine, pay, border):
     bs = border.shape[1]
-    width = pay.shape[0] - bs - TAIL
     known = isinstance(take, int)
 
     def pick(of):
         return of(take) if known else jnp.where(take == 2.0, of(2), of(3))
 
     def number(ref, line, t):
-        return ref[pl.ds(width + bs + line, 1), pl.ds(t * SIDE + s, 1)]
+        return ref[pl.ds(ref.shape[0] - TAIL + line, 1), pl.ds(t * SIDE + s, 1)]
 
     blocks = [[0.0] * (width // bs) for _ in range(width // bs)]
     for s in range(SIDE):
-        turned = pay[pl.ds(width, bs), pl.ds(s * bs, bs)].T
+        beside = pay.shape[1] > bs
+        turned = (pay[pl.ds(width, bs), pl.ds(s * bs, bs)] if beside else pay[pl.ds(width + s * bs, bs), :]).T
         pairs = [
             (pick(lambda t: border[t * SIDE + s]), pick(lambda t: number(mine, 0, t)), pick(lambda t: number(pay, 1, t))),
             (turned, pick(lambda t: number(mine, 1, t ^ 1)), pick(lambda t: number(pay, 0, t ^ 1))),
@@ -153,7 +167,7 @@
 
 def left_kernel(mine, part, border, pay, image, once, coup, back):
     width = part.shape[0]
-    coup[...] = edge(0, mine, pay, border)
+    coup[...] = edge(0, width, mine, pay, border)
     term = dot(coup[...], pay[pl.ds(0, width), :])
     image[...] = part[...] + term
     once[...] = part[...] + 2.0 * term
@@ -170,28 +184,48 @@
 def gy_kernel(take, weight, mine, part, single, border, pay, image, once, coup):
     width = coup.shape[0]
     toward = mine[pl.ds(mine.shape[0] - TAIL + 2, 1), pl.ds(0, 1)]
-    coup[...] = edge(toward if take is None else take, mine, pay, border)
+    coup[...] = edge(toward if take is None else take, width, mine, pay, border)
     term = dot(coup[...], pay[pl.ds(0, width), :])
     image[...] = part[...] + term
     scale = weight * turn(mine, width) if take is None else weight
     once[...] = single[...] + scale * term
 
 
-def right_kernel(mine, part, border, pay, image, half):
-    width = image.shape[0]
-    full = part[...] + dot(edge(1, mine, pay, border), pay[pl.ds(0, width), :])
-    image[...] = full
-    middle = full.shape[1] // 2
-    toward = mine[pl.ds(mine.shape[0] - TAIL + 2, 1), pl.ds(0, 1)]
-    half[...] = jnp.where(toward == 3.0, full[:, middle:], full[:, :middle])
-
-
-def near_kernel(field, image, once, mate, mate_w, own, coup, pay, back, part, lift, state):
+def columns(ref, toward, out):
+    middle = ref.shape[1] // 2
+    return jnp.where((toward == 3.0) == out, ref[:, middle:], ref[:, :middle])
+
+
+def right_kernel(mine, part, border, pay, half, across, coup, pass_on):
+    width = part.shape[0]
+    toward = mine[pl.ds(mine.shape[0] - TAIL + 2, 1), pl.ds(0, 1)]
+    coup[...] = edge(1, width, mine, pay, border)
+    half[...] = columns(part, toward, True) + dot(coup[...], pay[pl.ds(0, width), :])
+    across[pl.ds(0, width), :] = half[...]
+    across[pl.ds(width, EXTRA), :] = jnp.zeros((EXTRA, half.shape[1]), F32)
+    pass_on[...] = part[...]
+
+
+def joined(toward, out, other):
+    low = jnp.where(toward == 3.0, other, out)
+    high = jnp.where(toward == 3.0, out, other)
+    return jnp.concatenate([low, high], axis=1)
+
+
+def whole_kernel(mine, part, half, coup, pay, image, other):
+    toward = mine[pl.ds(mine.shape[0] - TAIL + 2, 1), pl.ds(0, 1)]
+    other[...] = columns(part, toward, False) + dot(coup[...], pay[pl.ds(0, part.shape[0]), :])
+    image[...] = joined(toward, half[...], other[...])
+
+
+def near_kernel(mine, field, image, once, mate, mate_out, mate_other, own, coup, pay, back, part, lift, state):
     b = field[...]
+    toward = mine[pl.ds(mine.shape[0] - TAIL + 2, 1), pl.ds(0, 1)]
+    mate_w = joined(toward, mate_out[...], mate_other[...])
     norm = col_sum(b, b)
     c = jnp.where(norm > 0.0, col_sum(b, image[...]) / jnp.where(norm > 0.0, norm, 1.0), 0.0)
     g = image[...] - c * b
-    part[...] = dot(own[...], g) + dot(coup[...], mate_w[...] - c * mate[...])
+    part[...] = dot(own[...], g) + dot(coup[...], mate_w - c * mate[...])
     lift[...] = back[...] - c * pay[pl.ds(0, b.shape[0]), :]
     rows = [(0, norm), (1, c), (2, col_sum(g, g)), (4, -col_sum(g, once[...])), (5, col_sum(b, once[...]))]
     state[...] = stack_rows(rows, state.shape)
@@ -209,7 +243,7 @@
             toward = mine[pl.ds(mine.shape[0] - TAIL + 2, 1), pl.ds(0, 1)]
             middle = b.shape[1] // 2
             shift = c * pay[pl.ds(0, width), :]
-            term = dot(coup_gy[...], side[...] - jnp.where(toward == 3.0, shift[:, :middle], shift[:, middle:]))
+            term = dot(coup_gy[...], side[pl.ds(0, width), :] - jnp.where(toward == 3.0, shift[:, :middle], shift[:, middle:]))
             acc += 2.0 * turn(mine, width) * jnp.concatenate([term, term], axis=1)
         else:
             acc += 2.0 * dot(coup_gy[...], side[...] - c * pay[pl.ds(0, width), :])
@@ -249,8 +283,8 @@
         sides = [(up, 2, 2.0), (down, 3, 0.0)]
     else:
         sides = []
-    sends = [("gx", right), ("gx", left)] + [("gy", perm) for perm, _, _ in sides]
-    gives = [1, 0] + [None if t is None else t ^ 1 for _, t, _ in sides]
+    sends = [("gx", right), ("gx", left), ("gx", left)] + [("gy", perm) for perm, _, _ in sides]
+    gives = [1, "halves"] + [None if t is None else t ^ 1 for _, t, _ in sides]
     toward = jnp.full((1, 4 * SIDE), facing)
     marks = jnp.stack([facing, lax.axis_index("nd").astype(jnp.int32)])
     border = border_coup[0]
@@ -258,21 +292,24 @@
     def smem(n):
         return [pl.BlockSpec(memory_space=pltpu.SMEM)] * n
 
-    pay_shape = (width + bs + TAIL, ncols)
+    wider = width + EXTRA
+    full, blocks, half = (width + bs + TAIL, ncols), (width + SIDE * bs + TAIL, ncols // 2), (width, ncols // 2)
 
     def pack(gives):
-        count = len(gives)
-        tables = [marks] if None in gives else []
+        shapes = sum(([blocks, (wider, ncols // 2)] if give == "halves" else [full] for give in gives), [])
+        count = len(shapes)
+        tables = [marks] if gives != [1] else []
         return pl.pallas_call(
             partial(pack_kernel, gives),
             name="pack",
             in_specs=smem(len(tables)) + [pl.BlockSpec(memory_space=pl.ANY)] * 5,
             out_specs=[vmem()] * count,
-            out_shape=[pltpu.VMEM(pay_shape, F32)] * count,
+            out_shape=[pltpu.VMEM(shape, F32) for shape in shapes],
             scratch_shapes=[
                 pltpu.SemaphoreType.DMA((count, SIDE + 1)),
                 pltpu.VMEM((3, 1, 4 * SIDE), jnp.int32),
                 pltpu.SemaphoreType.DMA((3,)),
+                pltpu.VMEM((width, ncols), F32),
             ],
             compiler_params=pltpu.CompilerParams(vmem_limit_bytes=LIMIT),
         )(*tables, *[pltpu.with_memory_space_constraint(a, pltpu.HBM) for a in (right_side, border, border_send, border_rows)], toward)
@@ -306,20 +343,23 @@
     part, coup = call(base_kernel, "base", [field, square])(mine, own, pair, mate, mate_pair)
     part, once, left_coup, back = call(left_kernel, "left", [field, field, square, field])(mine, part, border, pays[0])
     side_coup = []
-    for (_, take, weight), pay in zip(sides, pays[2:]):
+    for (_, take, weight), pay in zip(sides, pays[3:]):
         part, once, block = call(partial(gy_kernel, take, weight), "gy", [field, field, square])(mine, part, once, border, pay)
         side_coup.append(block)
-    left_w = lax.ppermute(part, "gx", right)
-    image, half = call(right_kernel, "right", [field, (width, ncols // 2)])(mine, part, border, pays[1])
-    mate_w = lax.ppermute(image, "nd", swap)
+    half_w, across, right_coup, pass_on = call(right_kernel, "right", [half, (wider, ncols // 2), square, field])(
+        mine, part, border, pays[1]
+    )
+    left_w = lax.ppermute(pass_on, "gx", right)
+    image, other_w = call(whole_kernel, "whole", [field, half])(mine, part, half_w, right_coup, pays[2])
+    mate_w = [lax.ppermute(w, "nd", swap) for w in (half_w, other_w)]
     part, lift, state = call(near_kernel, "near", [field, field, (TAIL, ncols)])(
-        right_side, image, once, mate, mate_w, own, coup, pays[0], back
+        mine, right_side, image, once, mate, *mate_w, own, coup, pays[0], back
     )
     far = []
     take = None
     if sides:
         perm, take, _ = sides[0]
-        far = [mine, side_coup[0], pays[2], lax.ppermute(half if take is None else image, "gy", perm)]
+        far = [mine, side_coup[0], pays[3], lax.ppermute(across if take is None else image, "gy", perm)]
     (state,) = call(partial(far_kernel, take), "far", [(TAIL, ncols)])(
         right_side, image, part, state, lift, left_coup, left_w, *far
     )

time: 47.2 us -> 43.6 us (0.924)
  waiting for transfers between devices: 23.2 us -> 17.3 us
  starting transfers between devices: 16 us -> 18 us
    ppermute x3 -> x4, waiting for transfers between devices: 10 us -> 7.09 us  [shards(): lax.ppermute(pay, axis, perm)]
    ppermute x3 -> x4, starting transfers between devices: 6.88 us -> 8.74 us  [shards(): lax.ppermute(pay, axis, perm)]
    ppermute x3 -> x4, waiting for transfers between devices: 7.83 us -> 6.23 us  [the longest x1 4.23 us: shards(): left_w = lax.ppermute(pass_on, 'gx', right)]
    ppermute x1, waiting for transfers between devices: 1.16 us -> 0.01 us  [shards(): mate_pair = lax.ppermute(pair, 'nd', swap)]
    ppermute x3 -> x4, starting transfers between devices: 2.18 us -> 2.68 us  [the longest x1 1.49 us: shards(): lax.ppermute(across if take is None else image, 'gy', perm)]
    pallas_call x8 -> x9, Pallas kernels: 2.86 us -> 3.13 us  [run(): pl.pallas_call(kernel, name=name, in_specs=[vmem()] * len(args), out_spec...]
  transfers between devices with their start and end apart: 14 -> 16, of which waited for: 10 -> 11; matrix products, arithmetic and copies ran while one was open for 0% -> 0% of each run, Pallas kernels for 10% -> 13%
where the time goes in v12:
time: 43.6 us; the launch traced here: 43.5 us
  starting transfers between devices  18 us (41%)
  waiting for transfers between devices  17.3 us (40%)
  Pallas kernels  7.14 us (16%)
  other arithmetic  0.85 us (2%)
    ppermute x4, starting transfers between devices, shards(): lax.ppermute(pay, axis, perm)  8.74 us
    ppermute x4, waiting for transfers between devices, shards(): lax.ppermute(pay, axis, perm)  7.09 us
    ppermute x6, starting transfers between devices, join(): lax.ppermute(state, AXES, [(i, i ^ m) for i in range(count)])  6.39 us
    ppermute x1, waiting for transfers between devices, shards(): left_w = lax.ppermute(pass_on, 'gx', right)  4.23 us
    ppermute x6, waiting for transfers between devices, join(): lax.ppermute(state, AXES, [(i, i ^ m) for i in range(count)])  3.96 us
    pallas_call x9, Pallas kernels, run(): pl.pallas_call(kernel, name=name, in_specs=[vmem()] * len(args), out_spec...  3.13 us
    pallas_call x2, Pallas kernels, pack(): pl.pallas_call(partial(pack_kernel, gives), name='pack', in_specs=smem(le...  2.92 us
    ppermute x1, starting transfers between devices, shards(): lax.ppermute(across if take is None else image, 'gy', perm)  1.49 us
  transfers between devices with their start and end apart: 16, of which 11 were waited for; matrix products, arithmetic and copies ran while one was open for 0% of the time, Pallas kernels for 13%

profile of v12, /device:TPU:0, one launch (start us, length us, event | category | flops | bytes accessed | tf_op | source)
XLA Modules:
  0.0 43.5 jit_solution(15289625329230404936)
XLA Ops:
  0.0 1.1 %pack.2.packed.mine.refs_0_ = f32[392,256]{1,0:T(8,128)S(1)} custom-call(f32[256,256]{1,0:T(8,128)} %field.3, f32[8,128,128]{2,1,0:T(8,128)} %bitcast.6, s32[1,8]{1,0:T(1,128)} %refs_3_.3, s32[1,8]{1,0:T(1,128)} %refs_4_.1, s32[1,8]{1,0:T(1,128)S(1)} %broadcast_in_dim.3.refs_4_.refs_5_), custom_call_target="tpu_custom_call" | custom-call | tf_op jit(solution)/shard_map/pack/pallas_call | solution.py:302
  1.1 3.1 %collective-permute-start.2 = (f32[392,256]{1,0:T(8,128)S(1)}, f32[392,256]{1,0:T(8,128)S(1)}, u32[]{:S(2)}, u32[]{:S(2)}) collective-permute-start(f32[392,256]{1,0:T(8,128)S(1)} %pack.2.packed.mine.refs_0_), channel_id=1, source_target_pairs={{0,4},{4,8},{8,12},{12,0},{1,5},{5,9},{9,13},{13,1},{2,6},{6,10},{... | collective-permute-start | bytes 1204232 | tf_op jit(solution)/shard_map/ppermute | solution.py:318
  4.3 1.8 %pack.3 = (f32[520,128]{1,0:T(8,128)S(1)}, f32[264,128]{1,0:T(8,128)S(1)}, f32[392,256]{1,0:T(8,128)S(1)}) custom-call(s32[2]{0:T(128)S(1)} %pad_add_fusion.marks.refs_0_, f32[256,256]{1,0:T(8,128)} %field.3, f32[8,128,128]{2,1,0:T(8,128)} %bitcast.7, s32[1,8]{1,0:T(1,128)} %refs_3_.3, s32[1,8]{1,0:T(1,128)} %refs_4_.1, ...), custom_call_target="tpu_custom_call" | custom-call | tf_op jit(solution)/shard_map/pack/pallas_call | solution.py:302
  6.1 1.6 %collective-permute-start.3 = (f32[392,256]{1,0:T(8,128)S(1)}, f32[392,256]{1,0:T(8,128)S(1)}, u32[]{:S(2)}, u32[]{:S(2)}) collective-permute-start(f32[392,256]{1,0:T(8,128)S(1)} %get-tuple-element.33), channel_id=1, source_target_pairs={{0,2},{2,0},{1,3},{3,1},{4,6},{6,4},{5,7},{7,5},{8,10},{10,8},{9,1... | collective-permute-start | bytes 1204232 | tf_op jit(solution)/shard_map/ppermute | solution.py:318
  7.7 2.3 %collective-permute-start.4 = (f32[520,128]{1,0:T(8,128)S(1)}, f32[520,128]{1,0:T(8,128)S(1)}, u32[]{:S(2)}, u32[]{:S(2)}) collective-permute-start(f32[520,128]{1,0:T(8,128)S(1)} %get-tuple-element.35), channel_id=1, source_target_pairs={{4,0},{8,4},{12,8},{0,12},{5,1},{9,5},{13,9},{1,13},{6,2},{10,6},{... | collective-permute-start | bytes 798728 | tf_op jit(solution)/shard_map/ppermute | solution.py:318
  10.0 1.1 %prep.1 = (f32[256,256]{1,0:T(8,128)S(1)}, f32[256,256]{1,0:T(8,128)S(1)}) custom-call(s32[2,7]{1,0:T(2,128)S(1)} %copy-done.3, s32[2]{0:T(128)S(1)} %pad_add_fusion.marks.refs_0_, f32[1,256]{1,0:T(1,128)S(1)} %bitcast.11, f32[2,7,128,128]{3,2,1,0:T(8,128)S(1)} %copy-done.2, f32[392,256]{1,0:T(8,128)S(1)} %pack.2.packed.mine.refs_0_), custom_call_target="tpu_custom_call" | custom-call | flops 16777216 | bytes 1048576 | tf_op jit(solution)/shard_map/prep/pallas_call | solution.py:325
  11.3 1.8 %collective-permute-start.5 = (f32[264,128]{1,0:T(8,128)S(1)}, f32[264,128]{1,0:T(8,128)S(1)}, u32[]{:S(2)}, u32[]{:S(2)}) collective-permute-start(f32[264,128]{1,0:T(8,128)S(1)} %get-tuple-element.38), channel_id=1, source_target_pairs={{4,0},{8,4},{12,8},{0,12},{5,1},{9,5},{13,9},{1,13},{6,2},{10,6},{... | collective-permute-start | bytes 405512 | tf_op jit(solution)/shard_map/ppermute | solution.py:318
  13.6 2.8 %collective-permute-done.2.pay = f32[392,256]{1,0:T(8,128)S(1)} collective-permute-done((f32[392,256]{1,0:T(8,128)S(1)}, f32[392,256]{1,0:T(8,128)S(1)}, u32[]{:S(2)}, u32[]{:S(2)}) %collective-permute-start.2) | collective-permute-done | bytes 401440 | tf_op jit(solution)/shard_map/ppermute | solution.py:318
  16.4 0.6 %left.1 = (f32[256,256]{1,0:T(8,128)S(1)}, f32[256,256]{1,0:T(8,128)S(1)}, f32[256,256]{1,0:T(8,128)S(1)}, f32[256,256]{1,0:T(8,128)S(1)}) custom-call(f32[392,256]{1,0:T(8,128)S(1)} %pack.2.packed.mine.refs_0_, f32[256,256]{1,0:T(8,128)S(1)} %get-tuple-element.30.part, f32[8,128,128]{2,1,0:T(8,128)S(1)} %bitcast.8, f32[392,256]{1,0:T(8,128)S(1)} %collective-permute-done.2.pay), custom_call_target="tpu_custom_call" | custom-call | tf_op jit(solution)/shard_map/left/pallas_call | solution.py:26
  17.4 3.9 %collective-permute-done.4.pay = f32[520,128]{1,0:T(8,128)S(1)} collective-permute-done((f32[520,128]{1,0:T(8,128)S(1)}, f32[520,128]{1,0:T(8,128)S(1)}, u32[]{:S(2)}, u32[]{:S(2)}) %collective-permute-start.4) | collective-permute-done | bytes 266272 | tf_op jit(solution)/shard_map/ppermute | solution.py:318
  21.7 0.6 %collective-permute-start.8 = (f32[256,256]{1,0:T(8,128)S(1)}, f32[256,256]{1,0:T(8,128)S(1)}, u32[]{:S(2)}, u32[]{:S(2)}) collective-permute-start(f32[256,256]{1,0:T(8,128)S(1)} %get-tuple-element.48), channel_id=1, source_target_pairs={{0,4},{4,8},{8,12},{12,0},{1,5},{5,9},{9,13},{13,1},{2,6},{6,10},{... | collective-permute-start | bytes 786440 | tf_op jit(solution)/shard_map/ppermute | solution.py:352
  22.3 1.5 %collective-permute-start.9 = (f32[264,128]{1,0:T(8,128)S(1)}, f32[264,128]{1,0:T(8,128)S(1)}, u32[]{:S(2)}, u32[]{:S(2)}) collective-permute-start(f32[264,128]{1,0:T(8,128)S(1)} %get-tuple-element.50), channel_id=1, source_target_pairs={{0,2},{2,0},{1,3},{3,1},{4,6},{6,4},{5,7},{7,5},{8,10},{10,8},{9,1... | collective-permute-start | bytes 405512 | tf_op jit(solution)/shard_map/ppermute | solution.py:362
  25.0 0.8 %collective-permute-done.7.mate_other = f32[256,128]{1,0:T(8,128)S(1)} collective-permute-done((f32[256,128]{1,0:T(8,128)S(1)}, f32[256,128]{1,0:T(8,128)S(1)}, u32[]{:S(2)}, u32[]{:S(2)}) %collective-permute-start.7) | collective-permute-done | bytes 131104 | tf_op jit(solution)/shard_map/ppermute | solution.py:354
  26.0 0.6 %near.1 = (f32[256,256]{1,0:T(8,128)S(1)}, f32[256,256]{1,0:T(8,128)S(1)}, f32[8,256]{1,0:T(8,128)S(1)}) custom-call(f32[392,256]{1,0:T(8,128)S(1)} %pack.2.packed.mine.refs_0_, f32[256,256]{1,0:T(8,128)S(1)} %copy-done.1, f32[256,256]{1,0:T(8,128)S(1)} %get-tuple-element.39.image, f32[256,256]{1,0:T(8,128)S(1)} %get-tuple-element.40.once, ...), custom_call_target="tpu_custom_call" | custom-call | tf_op jit(solution)/shard_map/near/pallas_call | solution.py:26
  26.5 1.0 %collective-permute-done.9.refs_3_ = f32[264,128]{1,0:T(8,128)S(1)} collective-permute-done((f32[264,128]{1,0:T(8,128)S(1)}, f32[264,128]{1,0:T(8,128)S(1)}, u32[]{:S(2)}, u32[]{:S(2)}) %collective-permute-start.9) | collective-permute-done | bytes 135200 | tf_op jit(solution)/shard_map/ppermute | solution.py:362
  27.5 4.2 %collective-permute-done.8.left = f32[256,256]{1,0:T(8,128)S(1)} collective-permute-done((f32[256,256]{1,0:T(8,128)S(1)}, f32[256,256]{1,0:T(8,128)S(1)}, u32[]{:S(2)}, u32[]{:S(2)}) %collective-permute-start.8) | collective-permute-done | bytes 262176 | tf_op jit(solution)/shard_map/ppermute | solution.py:352
  32.3 1.6 %collective-permute-start.11 = (f32[8,256]{1,0:T(8,128)S(1)}, f32[8,256]{1,0:T(8,128)S(1)}, u32[]{:S(2)}, u32[]{:S(2)}) collective-permute-start(f32[8,256]{1,0:T(8,128)S(1)} %far.1.refs_0_), channel_id=1, source_target_pairs={{0,2},{1,3},{2,0},{3,1},{4,6},{5,7},{6,4},{7,5},{8,10},{9,11},{10,... | collective-permute-start | bytes 24584 | tf_op jit(solution)/shard_map/ppermute | solution.py:46
  34.2 1.3 %collective-permute-done.12.refs_3_ = f32[8,256]{1,0:T(8,128)S(1)} collective-permute-done((f32[8,256]{1,0:T(8,128)S(1)}, f32[8,256]{1,0:T(8,128)S(1)}, u32[]{:S(2)}, u32[]{:S(2)}) %collective-permute-start.12) | collective-permute-done | bytes 8224 | tf_op jit(solution)/shard_map/ppermute | solution.py:46
  35.4 0.6 %collective-permute-done.11.refs_2_ = f32[8,256]{1,0:T(8,128)S(1)} collective-permute-done((f32[8,256]{1,0:T(8,128)S(1)}, f32[8,256]{1,0:T(8,128)S(1)}, u32[]{:S(2)}, u32[]{:S(2)}) %collective-permute-start.11) | collective-permute-done | bytes 8224 | tf_op jit(solution)/shard_map/ppermute | solution.py:46
  36.1 2.0 %collective-permute-start.15 = (f32[8,256]{1,0:T(8,128)S(1)}, f32[8,256]{1,0:T(8,128)S(1)}, u32[]{:S(2)}, u32[]{:S(2)}) collective-permute-start(f32[8,256]{1,0:T(8,128)S(1)} %merge.2.refs_0_), channel_id=1, source_target_pairs={{0,12},{1,13},{2,14},{3,15},{4,8},{5,9},{6,10},{7,11},{8,4},{9,5},... | collective-permute-start | bytes 24584 | tf_op jit(solution)/shard_map/ppermute | solution.py:46
  38.1 2.5 %collective-permute-start.13 = (f32[8,256]{1,0:T(8,128)S(1)}, f32[8,256]{1,0:T(8,128)S(1)}, u32[]{:S(2)}, u32[]{:S(2)}) collective-permute-start(f32[8,256]{1,0:T(8,128)S(1)} %merge.2.refs_0_), channel_id=1, source_target_pairs={{0,4},{1,5},{2,6},{3,7},{4,0},{5,1},{6,2},{7,3},{8,12},{9,13},{10,... | collective-permute-start | bytes 24584 | tf_op jit(solution)/shard_map/ppermute | solution.py:46
  40.6 1.1 %collective-permute-done.15.refs_3_ = f32[8,256]{1,0:T(8,128)S(1)} collective-permute-done((f32[8,256]{1,0:T(8,128)S(1)}, f32[8,256]{1,0:T(8,128)S(1)}, u32[]{:S(2)}, u32[]{:S(2)}) %collective-permute-start.15) | collective-permute-done | bytes 8224 | tf_op jit(solution)/shard_map/ppermute | solution.py:46
  41.6 1.0 %collective-permute-done.14.refs_2_ = f32[8,256]{1,0:T(8,128)S(1)} collective-permute-done((f32[8,256]{1,0:T(8,128)S(1)}, f32[8,256]{1,0:T(8,128)S(1)}, u32[]{:S(2)}, u32[]{:S(2)}) %collective-permute-start.14) | collective-permute-done | bytes 8224 | tf_op jit(solution)/shard_map/ppermute | solution.py:46
  42.7 0.7 %multiply_subtract_fusion = f32[256,256]{1,0:T(8,128)} fusion(f32[256,256]{1,0:T(8,128)S(1)} %get-tuple-element.39.image, f32[256,256]{1,0:T(8,128)S(1)} %copy-done.1, f32[256]{0:T(256)S(1)} %bitcast.13, f32[256]{0:T(256)S(1)} %bitcast.12), kind=kLoop, calls=%fused_computation | loop fusion | flops 196608 | bytes 788480 | tf_op jit(solution)/shard_map/sub | solution.py:370
  (35 shorter events, 3.9 us)
Async XLA Ops:
  0.0 10.0 %copy-start.2 = (f32[2,7,128,128]{3,2,1,0:T(8,128)S(1)}, f32[2,7,128,128]{3,2,1,0:T(8,128)}, u32[]{:S(2)}) copy-start(f32[2,7,128,128]{3,2,1,0:T(8,128)} %local.1) | copy-start | bytes 2752516
  1.1 15.3 %collective-permute-start.2 = (f32[392,256]{1,0:T(8,128)S(1)}, f32[392,256]{1,0:T(8,128)S(1)}, u32[]{:S(2)}, u32[]{:S(2)}) collective-permute-start(f32[392,256]{1,0:T(8,128)S(1)} %pack.2.packed.mine.refs_0_), channel_id=1, source_target_pairs={{0,4},{4,8},{8,12},{12,0},{1,5},{5,9},{9,13},{13,1},{2,6},{6,10},{... | collective-permute-start | bytes 1204232 | tf_op jit(solution)/shard_map/ppermute | solution.py:318
  4.3 3.4 %copy-start.1 = (f32[256,256]{1,0:T(8,128)S(1)}, f32[256,256]{1,0:T(8,128)}, u32[]{:S(2)}) copy-start(f32[256,256]{1,0:T(8,128)} %field.3) | copy-start | bytes 786436
  6.1 10.9 %collective-permute-start.3 = (f32[392,256]{1,0:T(8,128)S(1)}, f32[392,256]{1,0:T(8,128)S(1)}, u32[]{:S(2)}, u32[]{:S(2)}) collective-permute-start(f32[392,256]{1,0:T(8,128)S(1)} %get-tuple-element.33), channel_id=1, source_target_pairs={{0,2},{2,0},{1,3},{3,1},{4,6},{6,4},{5,7},{7,5},{8,10},{10,8},{9,1... | collective-permute-start | bytes 1204232 | tf_op jit(solution)/shard_map/ppermute | solution.py:318
  7.7 3.7 %collective-permute-start = (f32[256,256]{1,0:T(8,128)S(1)}, f32[256,256]{1,0:T(8,128)S(1)}, u32[]{:S(2)}, u32[]{:S(2)}) collective-permute-start(f32[256,256]{1,0:T(8,128)S(1)} %copy-done.1), channel_id=1, source_target_pairs={{0,1},{1,0},{2,3},{3,2},{4,5},{5,4},{6,7},{7,6},{8,9},{9,8},{10,11... | collective-permute-start | bytes 786440 | tf_op jit(solution)/shard_map/ppermute | solution.py:320
  7.7 2.3 %copy-start.4 = (f32[256]{0:T(256)S(1)}, f32[256]{0:T(256)}, u32[]{:S(2)}) copy-start(f32[256]{0:T(256)} %param.8) | copy-start | bytes 3076
  7.7 2.3 %copy-start.3 = (s32[2,7]{1,0:T(2,128)S(1)}, s32[2,7]{1,0:T(2,128)}, u32[]{:S(2)}) copy-start(s32[2,7]{1,0:T(2,128)} %cols.1) | copy-start | bytes 172
  7.7 13.6 %collective-permute-start.4 = (f32[520,128]{1,0:T(8,128)S(1)}, f32[520,128]{1,0:T(8,128)S(1)}, u32[]{:S(2)}, u32[]{:S(2)}) collective-permute-start(f32[520,128]{1,0:T(8,128)S(1)} %get-tuple-element.35), channel_id=1, source_target_pairs={{4,0},{8,4},{12,8},{0,12},{5,1},{9,5},{13,9},{1,13},{6,2},{10,6},{... | collective-permute-start | bytes 798728 | tf_op jit(solution)/shard_map/ppermute | solution.py:318
  11.1 2.0 %collective-permute-start.1 = (f32[256,256]{1,0:T(8,128)S(1)}, f32[256,256]{1,0:T(8,128)S(1)}, u32[]{:S(2)}, u32[]{:S(2)}) collective-permute-start(f32[256,256]{1,0:T(8,128)S(1)} %get-tuple-element.29.pair), channel_id=1, source_target_pairs={{0,1},{1,0},{2,3},{3,2},{4,5},{5,4},{6,7},{7,6},{8,9},{9,8},{10,11... | collective-permute-start | bytes 786440 | tf_op jit(solution)/shard_map/ppermute | solution.py:341
  11.3 12.8 %collective-permute-start.5 = (f32[264,128]{1,0:T(8,128)S(1)}, f32[264,128]{1,0:T(8,128)S(1)}, u32[]{:S(2)}, u32[]{:S(2)}) collective-permute-start(f32[264,128]{1,0:T(8,128)S(1)} %get-tuple-element.38), channel_id=1, source_target_pairs={{4,0},{8,4},{12,8},{0,12},{5,1},{9,5},{13,9},{1,13},{6,2},{10,6},{... | collective-permute-start | bytes 405512 | tf_op jit(solution)/shard_map/ppermute | solution.py:318
  13.1 3.3 %copy-start = (f32[1,8,128,128]{3,2,1,0:T(8,128)S(1)}, f32[1,8,128,128]{3,2,1,0:T(8,128)}, u32[]{:S(2)}) copy-start(f32[1,8,128,128]{3,2,1,0:T(8,128)} %param.11) | copy-start | bytes 1572868
  21.7 10.1 %collective-permute-start.8 = (f32[256,256]{1,0:T(8,128)S(1)}, f32[256,256]{1,0:T(8,128)S(1)}, u32[]{:S(2)}, u32[]{:S(2)}) collective-permute-start(f32[256,256]{1,0:T(8,128)S(1)} %get-tuple-element.48), channel_id=1, source_target_pairs={{0,4},{4,8},{8,12},{12,0},{1,5},{5,9},{9,13},{13,1},{2,6},{6,10},{... | collective-permute-start | bytes 786440 | tf_op jit(solution)/shard_map/ppermute | solution.py:352
  22.3 5.2 %collective-permute-start.9 = (f32[264,128]{1,0:T(8,128)S(1)}, f32[264,128]{1,0:T(8,128)S(1)}, u32[]{:S(2)}, u32[]{:S(2)}) collective-permute-start(f32[264,128]{1,0:T(8,128)S(1)} %get-tuple-element.50), channel_id=1, source_target_pairs={{0,2},{2,0},{1,3},{3,1},{4,6},{6,4},{5,7},{7,5},{8,10},{10,8},{9,1... | collective-permute-start | bytes 405512 | tf_op jit(solution)/shard_map/ppermute | solution.py:362
  24.4 1.4 %collective-permute-start.7 = (f32[256,128]{1,0:T(8,128)S(1)}, f32[256,128]{1,0:T(8,128)S(1)}, u32[]{:S(2)}, u32[]{:S(2)}) collective-permute-start(f32[256,128]{1,0:T(8,128)S(1)} %get-tuple-element.41), channel_id=1, source_target_pairs={{0,1},{1,0},{2,3},{3,2},{4,5},{5,4},{6,7},{7,6},{8,9},{9,8},{10,11... | collective-permute-start | bytes 393224 | tf_op jit(solution)/shard_map/ppermute | solution.py:354
  24.5 1.5 %collective-permute-start.6 = (f32[256,128]{1,0:T(8,128)S(1)}, f32[256,128]{1,0:T(8,128)S(1)}, u32[]{:S(2)}, u32[]{:S(2)}) collective-permute-start(f32[256,128]{1,0:T(8,128)S(1)} %get-tuple-element.36.half), channel_id=1, source_target_pairs={{0,1},{1,0},{2,3},{3,2},{4,5},{5,4},{6,7},{7,6},{8,9},{9,8},{10,11... | collective-permute-start | bytes 393224 | tf_op jit(solution)/shard_map/ppermute | solution.py:354
  32.3 3.2 %collective-permute-start.12 = (f32[8,256]{1,0:T(8,128)S(1)}, f32[8,256]{1,0:T(8,128)S(1)}, u32[]{:S(2)}, u32[]{:S(2)}) collective-permute-start(f32[8,256]{1,0:T(8,128)S(1)} %far.1.refs_0_), channel_id=1, source_target_pairs={{0,3},{1,2},{2,1},{3,0},{4,7},{5,6},{6,5},{7,4},{8,11},{9,10},{10,... | collective-permute-start | bytes 24584 | tf_op jit(solution)/shard_map/ppermute | solution.py:46
  32.3 3.7 %collective-permute-start.11 = (f32[8,256]{1,0:T(8,128)S(1)}, f32[8,256]{1,0:T(8,128)S(1)}, u32[]{:S(2)}, u32[]{:S(2)}) collective-permute-start(f32[8,256]{1,0:T(8,128)S(1)} %far.1.refs_0_), channel_id=1, source_target_pairs={{0,2},{1,3},{2,0},{3,1},{4,6},{5,7},{6,4},{7,5},{8,10},{9,11},{10,... | collective-permute-start | bytes 24584 | tf_op jit(solution)/shard_map/ppermute | solution.py:46
  33.9 2.2 %collective-permute-start.10 = (f32[8,256]{1,0:T(8,128)S(1)}, f32[8,256]{1,0:T(8,128)S(1)}, u32[]{:S(2)}, u32[]{:S(2)}) collective-permute-start(f32[8,256]{1,0:T(8,128)S(1)} %far.1.refs_0_), channel_id=1, source_target_pairs={{0,1},{1,0},{2,3},{3,2},{4,5},{5,4},{6,7},{7,6},{8,9},{9,8},{10,11... | collective-permute-start | bytes 24584 | tf_op jit(solution)/shard_map/ppermute | solution.py:46
  36.1 5.5 %collective-permute-start.15 = (f32[8,256]{1,0:T(8,128)S(1)}, f32[8,256]{1,0:T(8,128)S(1)}, u32[]{:S(2)}, u32[]{:S(2)}) collective-permute-start(f32[8,256]{1,0:T(8,128)S(1)} %merge.2.refs_0_), channel_id=1, source_target_pairs={{0,12},{1,13},{2,14},{3,15},{4,8},{5,9},{6,10},{7,11},{8,4},{9,5},... | collective-permute-start | bytes 24584 | tf_op jit(solution)/shard_map/ppermute | solution.py:46
  38.1 4.5 %collective-permute-start.14 = (f32[8,256]{1,0:T(8,128)S(1)}, f32[8,256]{1,0:T(8,128)S(1)}, u32[]{:S(2)}, u32[]{:S(2)}) collective-permute-start(f32[8,256]{1,0:T(8,128)S(1)} %merge.2.refs_0_), channel_id=1, source_target_pairs={{0,8},{1,9},{2,10},{3,11},{4,12},{5,13},{6,14},{7,15},{8,0},{9,1},... | collective-permute-start | bytes 24584 | tf_op jit(solution)/shard_map/ppermute | solution.py:46
  38.1 4.5 %collective-permute-start.13 = (f32[8,256]{1,0:T(8,128)S(1)}, f32[8,256]{1,0:T(8,128)S(1)}, u32[]{:S(2)}, u32[]{:S(2)}) collective-permute-start(f32[8,256]{1,0:T(8,128)S(1)} %merge.2.refs_0_), channel_id=1, source_target_pairs={{0,4},{1,5},{2,6},{3,7},{4,0},{5,1},{6,2},{7,3},{8,12},{9,13},{10,... | collective-permute-start | bytes 24584 | tf_op jit(solution)/shard_map/ppermute | solution.py:46

commit v13 on v12

--- a/solution.py
+++ b/solution.py
@@ -71,43 +71,42 @@
 
 def pack_kernel(gives, *refs):
     marks, refs = (refs[0], refs[1:]) if gives != [1] else (None, refs)
-    field, border, send, rows, toward, *pays, sems, table, table_sems, whole = refs
+    field, border, send, rows, toward, *pays, sems, table, table_sems = refs
     width = field.shape[0]
     bs = border.shape[1]
     tables = [pltpu.make_async_copy(ref, table.at[n], table_sems.at[n]) for n, ref in enumerate((rows, send, toward))]
-    copies, tails, split = [], [], []
-    for n, give in enumerate(gives):
-        pay = pays.pop(0)
-        tails.append(pay)
-        if give == "halves":
-            other = pays.pop(0)
-            for s in range(SIDE):
-                copies.append(pltpu.make_async_copy(border.at[s], pay.at[pl.ds(width + s * bs, bs), :], sems.at[n, s]))
-            copies.append(pltpu.make_async_copy(field, whole, sems.at[n, SIDE]))
-            split.append((pay, other))
-        else:
-            give = marks[0] if give is None else give
-            copies.append(pltpu.make_async_copy(field, pay.at[pl.ds(0, width), :], sems.at[n, SIDE]))
-            for s in range(SIDE):
-                block = pay.at[pl.ds(width, bs), pl.ds(s * bs, bs)]
-                copies.append(pltpu.make_async_copy(border.at[give * SIDE + s], block, sems.at[n, s]))
+    copies = []
+    for n, (give, pay) in enumerate(zip(gives, pays)):
+        give = marks[0] if give is None else give
+        copies.append(pltpu.make_async_copy(field, pay.at[pl.ds(0, width), :], sems.at[n, SIDE]))
+        for s in range(SIDE):
+            block = pay.at[pl.ds(width, bs), pl.ds(s * bs, bs)]
+            copies.append(pltpu.make_async_copy(border.at[give * SIDE + s], block, sems.at[n, s]))
     for copy in tables + copies:
         copy.start()
     for copy in tables:
         copy.wait()
     count = table.shape[2]
-    for pay in tails:
+    for pay in pays:
         for n in range(3):
             pay[pl.ds(pay.shape[0] - TAIL + n, 1), pl.ds(0, count)] = table[n].astype(F32)
     for copy in copies:
         copy.wait()
-    for pay, other in split:
-        low, high = whole[:, : whole.shape[1] // 2], whole[:, whole.shape[1] // 2 :]
-        pay[pl.ds(0, width), :] = jnp.where(marks[0] == 3, high, low)
-        other[pl.ds(0, width), :] = jnp.where(marks[0] == 3, low, high)
-
-
-def prep_kernel(cols, marks, diag, local, packed, own, pair):
+
+
+def pack_right_kernel(mine, field, border, low, high, pay, other):
+    width = field.shape[0]
+    bs = border.shape[1]
+    last = mine.shape[0] - TAIL
+    toward = mine[pl.ds(last + 2, 1), pl.ds(0, 1)]
+    pay[pl.ds(0, width), :] = columns(field, toward, True)
+    for s in range(SIDE):
+        pay[pl.ds(width + s * bs, bs), :] = border[s]
+    pay[pl.ds(width + SIDE * bs, TAIL), :] = mine[pl.ds(last, TAIL), pl.ds(0, bs)]
+    other[pl.ds(0, width), :] = columns(field, toward, False)
+
+
+def prep_kernel(cols, marks, diag, local, packed, own, pair, low, high):
     nblocks, nonzeros, bs, _ = local.shape
     width = nblocks * bs
     patch_len = 2 * nblocks
@@ -132,6 +131,8 @@
     here = lax.broadcasted_iota(jnp.int32, (width, width), 0)
     there = lax.broadcasted_iota(jnp.int32, (width, width), 1)
     own[...] = lower + lower.T + jnp.where(here == there, diag[...], 0.0)
+    low[...] = pair[:, : width // 2]
+    high[...] = pair[:, width // 2 :]
 
 
 def edge(take, width, mine, pay, border):
@@ -159,9 +160,9 @@
     return jnp.concatenate([jnp.concatenate(line, axis=1) for line in blocks], axis=0)
 
 
-def base_kernel(mine, own, pair, mate, mate_pair, image, coup):
+def base_kernel(mine, own, pair, mate, low, high, image, coup):
     width = mate.shape[0]
-    coup[...] = pair[...] + mate_pair[...].T
+    coup[...] = pair[...] + jnp.concatenate([low[...].T, high[...].T], axis=0)
     image[...] = dot(own[...], mine[pl.ds(0, width), :]) + dot(coup[...], mate[...])
 
 
@@ -283,8 +284,8 @@
         sides = [(up, 2, 2.0), (down, 3, 0.0)]
     else:
         sides = []
-    sends = [("gx", right), ("gx", left), ("gx", left)] + [("gy", perm) for perm, _, _ in sides]
-    gives = [1, "halves"] + [None if t is None else t ^ 1 for _, t, _ in sides]
+    sends = [("gx", right)] + [("gy", perm) for perm, _, _ in sides]
+    gives = [1] + [None if t is None else t ^ 1 for _, t, _ in sides]
     toward = jnp.full((1, 4 * SIDE), facing)
     marks = jnp.stack([facing, lax.axis_index("nd").astype(jnp.int32)])
     border = border_coup[0]
@@ -296,25 +297,23 @@
     full, blocks, half = (width + bs + TAIL, ncols), (width + SIDE * bs + TAIL, ncols // 2), (width, ncols // 2)
 
     def pack(gives):
-        shapes = sum(([blocks, (wider, ncols // 2)] if give == "halves" else [full] for give in gives), [])
-        count = len(shapes)
+        count = len(gives)
         tables = [marks] if gives != [1] else []
         return pl.pallas_call(
             partial(pack_kernel, gives),
             name="pack",
             in_specs=smem(len(tables)) + [pl.BlockSpec(memory_space=pl.ANY)] * 5,
             out_specs=[vmem()] * count,
-            out_shape=[pltpu.VMEM(shape, F32) for shape in shapes],
+            out_shape=[pltpu.VMEM(full, F32)] * count,
             scratch_shapes=[
                 pltpu.SemaphoreType.DMA((count, SIDE + 1)),
                 pltpu.VMEM((3, 1, 4 * SIDE), jnp.int32),
                 pltpu.SemaphoreType.DMA((3,)),
-                pltpu.VMEM((width, ncols), F32),
             ],
             compiler_params=pltpu.CompilerParams(vmem_limit_bytes=LIMIT),
         )(*tables, *[pltpu.with_memory_space_constraint(a, pltpu.HBM) for a in (right_side, border, border_send, border_rows)], toward)
 
-    packed = [*pack(gives[:1]), *pack(gives[1:])]
+    packed = [*pack(gives[:1]), *(pack(gives[1:]) if sides else [])]
     pays = [lax.ppermute(pay, axis, perm) for pay, (axis, perm) in zip(packed, sends)]
     mine = packed[0]
     mate = lax.ppermute(right_side, "nd", swap)
@@ -335,22 +334,26 @@
         return run
 
     field, square = (width, ncols), (width, width)
-    own, pair = tabled(prep_kernel, "prep", 2, [square] * 2, 1 << 24)(
+    own, pair, *pieces = tabled(prep_kernel, "prep", 2, [square] * 2 + [(width, width // 2)] * 2, 1 << 24)(
         block_cols, marks, node_diag.reshape(1, width), local_coup, mine
     )
-    mate_pair = lax.ppermute(pair, "nd", swap)
-
-    part, coup = call(base_kernel, "base", [field, square])(mine, own, pair, mate, mate_pair)
+    mate_pair = [lax.ppermute(piece, "nd", swap) for piece in pieces]
+
+    part, coup = call(base_kernel, "base", [field, square])(mine, own, pair, mate, *mate_pair)
+    to_left = call(pack_right_kernel, "pack_right", [blocks, (wider, ncols // 2)])(
+        mine, right_side, border, *mate_pair
+    )
+    from_right = [lax.ppermute(pay, "gx", left) for pay in to_left]
     part, once, left_coup, back = call(left_kernel, "left", [field, field, square, field])(mine, part, border, pays[0])
     side_coup = []
-    for (_, take, weight), pay in zip(sides, pays[3:]):
+    for (_, take, weight), pay in zip(sides, pays[1:]):
         part, once, block = call(partial(gy_kernel, take, weight), "gy", [field, field, square])(mine, part, once, border, pay)
         side_coup.append(block)
     half_w, across, right_coup, pass_on = call(right_kernel, "right", [half, (wider, ncols // 2), square, field])(
-        mine, part, border, pays[1]
+        mine, part, border, from_right[0]
     )
     left_w = lax.ppermute(pass_on, "gx", right)
-    image, other_w = call(whole_kernel, "whole", [field, half])(mine, part, half_w, right_coup, pays[2])
+    image, other_w = call(whole_kernel, "whole", [field, half])(mine, part, half_w, right_coup, from_right[1])
     mate_w = [lax.ppermute(w, "nd", swap) for w in (half_w, other_w)]
     part, lift, state = call(near_kernel, "near", [field, field, (TAIL, ncols)])(
         mine, right_side, image, once, mate, *mate_w, own, coup, pays[0], back
@@ -359,7 +362,7 @@
     take = None
     if sides:
         perm, take, _ = sides[0]
-        far = [mine, side_coup[0], pays[3], lax.ppermute(across if take is None else image, "gy", perm)]
+        far = [mine, side_coup[0], pays[1], lax.ppermute(across if take is None else image, "gy", perm)]
     (state,) = call(partial(far_kernel, take), "far", [(TAIL, ncols)])(
         right_side, image, part, state, lift, left_coup, left_w, *far
     )

time: 43.6 us -> 43.2 us (level)
  waiting for transfers between devices: 17.3 us -> 16.6 us
    ppermute x4 -> x2, waiting for transfers between devices: 7.09 us -> 1.28 us  [shards(): lax.ppermute(pay, axis, perm)]
    ppermute x1 -> x4, waiting for transfers between devices: 0.01 us -> 5.55 us  [the longest x2 4.53 us: shards(): from_right = [lax.ppermute(pay, 'gx', left) for pay in to_left]]
    ppermute x1 -> x4, starting transfers between devices: 0.23 us -> 4.67 us  [the longest x2 4.11 us: shards(): from_right = [lax.ppermute(pay, 'gx', left) for pay in to_left]]
    ppermute x4 -> x2, starting transfers between devices: 8.74 us -> 4.63 us  [shards(): lax.ppermute(pay, axis, perm)]
    ppermute x6, waiting for transfers between devices: 3.96 us -> 3.51 us  [join(): lax.ppermute(state, AXES, [(i, i ^ m) for i in range(count)])]
    pallas_call x9 -> x10, Pallas kernels: 3.13 us -> 3.23 us  [run(): pl.pallas_call(kernel, name=name, in_specs=[vmem()] * len(args), out_spec...]
  transfers between devices with their start and end apart: 16 -> 17, of which waited for: 11 -> 15; matrix products, arithmetic and copies ran while one was open for 0% -> 0% of each run, Pallas kernels for 13% -> 12%
where the time goes in v13:
time: 43.2 us; the launch traced here: 43 us
  starting transfers between devices  18.4 us (43%)
  waiting for transfers between devices  16.6 us (38%)
  Pallas kernels  7.02 us (16%)
  other arithmetic  0.85 us (2%)
    ppermute x6, starting transfers between devices, join(): lax.ppermute(state, AXES, [(i, i ^ m) for i in range(count)])  6.39 us
    ppermute x2, starting transfers between devices, shards(): lax.ppermute(pay, axis, perm)  4.63 us
    ppermute x2, waiting for transfers between devices, shards(): from_right = [lax.ppermute(pay, 'gx', left) for pay in to_left]  4.53 us
    ppermute x1, waiting for transfers between devices, shards(): left_w = lax.ppermute(pass_on, 'gx', right)  4.23 us
    ppermute x2, starting transfers between devices, shards(): from_right = [lax.ppermute(pay, 'gx', left) for pay in to_left]  4.11 us
    ppermute x6, waiting for transfers between devices, join(): lax.ppermute(state, AXES, [(i, i ^ m) for i in range(count)])  3.51 us
    pallas_call x10, Pallas kernels, run(): pl.pallas_call(kernel, name=name, in_specs=[vmem()] * len(args), out_spec...  3.23 us
    pallas_call x2, Pallas kernels, pack(): pl.pallas_call(partial(pack_kernel, gives), name='pack', in_specs=smem(le...  2.7 us
  transfers between devices with their start and end apart: 17, of which 15 were waited for; matrix products, arithmetic and copies ran while one was open for 0% of the time, Pallas kernels for 12%

profile of v13, /device:TPU:0, one launch (start us, length us, event | category | flops | bytes accessed | tf_op | source)
XLA Modules:
  0.0 43.0 jit_solution(9673145064715024467)
XLA Ops:
  0.0 1.1 %pack.2.packed.mine.refs_0_ = f32[392,256]{1,0:T(8,128)S(1)} custom-call(f32[256,256]{1,0:T(8,128)} %field.5, f32[8,128,128]{2,1,0:T(8,128)} %bitcast.6, s32[1,8]{1,0:T(1,128)} %refs_3_.3, s32[1,8]{1,0:T(1,128)} %refs_4_.1, s32[1,8]{1,0:T(1,128)S(1)} %broadcast_in_dim.3.refs_4_.refs_5_), custom_call_target="tpu_custom_call" | custom-call | tf_op jit(solution)/shard_map/pack/pallas_call | solution.py:302
  1.1 3.1 %collective-permute-start.3 = (f32[392,256]{1,0:T(8,128)S(1)}, f32[392,256]{1,0:T(8,128)S(1)}, u32[]{:S(2)}, u32[]{:S(2)}) collective-permute-start(f32[392,256]{1,0:T(8,128)S(1)} %pack.2.packed.mine.refs_0_), channel_id=1, source_target_pairs={{0,4},{4,8},{8,12},{12,0},{1,5},{5,9},{9,13},{13,1},{2,6},{6,10},{... | collective-permute-start | bytes 1204232 | tf_op jit(solution)/shard_map/ppermute | solution.py:317
  4.3 1.6 %pack.3 = f32[392,256]{1,0:T(8,128)S(1)} custom-call(s32[2]{0:T(128)S(1)} %pad_add_fusion.marks.refs_0_, f32[256,256]{1,0:T(8,128)} %field.5, f32[8,128,128]{2,1,0:T(8,128)} %bitcast.7, s32[1,8]{1,0:T(1,128)} %refs_3_.3, s32[1,8]{1,0:T(1,128)} %refs_4_.1, s32[1,8]{1,0:T(1,128)S(1)} %broadcast_in_dim.3.refs_4_.refs_5_), custom_call_target="tpu_custom_call" | custom-call | tf_op jit(solution)/shard_map/pack/pallas_call | solution.py:302
  5.9 1.6 %collective-permute-start.4 = (f32[392,256]{1,0:T(8,128)S(1)}, f32[392,256]{1,0:T(8,128)S(1)}, u32[]{:S(2)}, u32[]{:S(2)}) collective-permute-start(f32[392,256]{1,0:T(8,128)S(1)} %pack.3), channel_id=1, source_target_pairs={{0,2},{2,0},{1,3},{3,1},{4,6},{6,4},{5,7},{7,5},{8,10},{10,8},{9,1... | collective-permute-start | bytes 1204232 | tf_op jit(solution)/shard_map/ppermute | solution.py:317
  7.5 1.1 %prep.1 = (f32[256,256]{1,0:T(8,128)S(1)}, f32[256,256]{1,0:T(8,128)S(1)}, f32[256,128]{1,0:T(8,128)S(1)}, f32[256,128]{1,0:T(8,128)S(1)}) custom-call(s32[2,7]{1,0:T(2,128)S(1)} %copy-done.3, s32[2]{0:T(128)S(1)} %pad_add_fusion.marks.refs_0_, f32[1,256]{1,0:T(1,128)S(1)} %bitcast.12, f32[2,7,128,128]{3,2,1,0:T(8,128)S(1)} %copy-done.2, ...), custom_call_target="tpu_custom_call" | custom-call | flops 16777216 | bytes 1048576 | tf_op jit(solution)/shard_map/prep/pallas_call | solution.py:324
  9.1 0.8 %collective-permute-done.1.low = f32[256,128]{1,0:T(8,128)S(1)} collective-permute-done((f32[256,128]{1,0:T(8,128)S(1)}, f32[256,128]{1,0:T(8,128)S(1)}, u32[]{:S(2)}, u32[]{:S(2)}) %collective-permute-start.1) | collective-permute-done | bytes 131104 | tf_op jit(solution)/shard_map/ppermute | solution.py:340
  10.3 2.3 %collective-permute-start.5 = (f32[520,128]{1,0:T(8,128)S(1)}, f32[520,128]{1,0:T(8,128)S(1)}, u32[]{:S(2)}, u32[]{:S(2)}) collective-permute-start(f32[520,128]{1,0:T(8,128)S(1)} %get-tuple-element.37), channel_id=1, source_target_pairs={{4,0},{8,4},{12,8},{0,12},{5,1},{9,5},{13,9},{1,13},{6,2},{10,6},{... | collective-permute-start | bytes 798728 | tf_op jit(solution)/shard_map/ppermute | solution.py:346
  12.6 1.8 %collective-permute-start.6 = (f32[264,128]{1,0:T(8,128)S(1)}, f32[264,128]{1,0:T(8,128)S(1)}, u32[]{:S(2)}, u32[]{:S(2)}) collective-permute-start(f32[264,128]{1,0:T(8,128)S(1)} %get-tuple-element.40), channel_id=1, source_target_pairs={{4,0},{8,4},{12,8},{0,12},{5,1},{9,5},{13,9},{1,13},{6,2},{10,6},{... | collective-permute-start | bytes 405512 | tf_op jit(solution)/shard_map/ppermute | solution.py:346
  14.8 0.9 %collective-permute-done.3.pay = f32[392,256]{1,0:T(8,128)S(1)} collective-permute-done((f32[392,256]{1,0:T(8,128)S(1)}, f32[392,256]{1,0:T(8,128)S(1)}, u32[]{:S(2)}, u32[]{:S(2)}) %collective-permute-start.3) | collective-permute-done | bytes 401440 | tf_op jit(solution)/shard_map/ppermute | solution.py:317
  15.7 0.6 %left.1 = (f32[256,256]{1,0:T(8,128)S(1)}, f32[256,256]{1,0:T(8,128)S(1)}, f32[256,256]{1,0:T(8,128)S(1)}, f32[256,256]{1,0:T(8,128)S(1)}) custom-call(f32[392,256]{1,0:T(8,128)S(1)} %pack.2.packed.mine.refs_0_, f32[256,256]{1,0:T(8,128)S(1)} %get-tuple-element.33.part, f32[8,128,128]{2,1,0:T(8,128)S(1)} %bitcast.9, f32[392,256]{1,0:T(8,128)S(1)} %collective-permute-done.3.pay), custom_call_target="tpu_custom_call" | custom-call | tf_op jit(solution)/shard_map/left/pallas_call | solution.py:26
  17.1 4.2 %collective-permute-done.5.pay = f32[520,128]{1,0:T(8,128)S(1)} collective-permute-done((f32[520,128]{1,0:T(8,128)S(1)}, f32[520,128]{1,0:T(8,128)S(1)}, u32[]{:S(2)}, u32[]{:S(2)}) %collective-permute-start.5) | collective-permute-done | bytes 266272 | tf_op jit(solution)/shard_map/ppermute | solution.py:346
  21.7 0.6 %collective-permute-start.9 = (f32[256,256]{1,0:T(8,128)S(1)}, f32[256,256]{1,0:T(8,128)S(1)}, u32[]{:S(2)}, u32[]{:S(2)}) collective-permute-start(f32[256,256]{1,0:T(8,128)S(1)} %get-tuple-element.50), channel_id=1, source_target_pairs={{0,4},{4,8},{8,12},{12,0},{1,5},{5,9},{9,13},{13,1},{2,6},{6,10},{... | collective-permute-start | bytes 786440 | tf_op jit(solution)/shard_map/ppermute | solution.py:355
  22.3 1.5 %collective-permute-start.10 = (f32[264,128]{1,0:T(8,128)S(1)}, f32[264,128]{1,0:T(8,128)S(1)}, u32[]{:S(2)}, u32[]{:S(2)}) collective-permute-start(f32[264,128]{1,0:T(8,128)S(1)} %get-tuple-element.52), channel_id=1, source_target_pairs={{0,2},{2,0},{1,3},{3,1},{4,6},{6,4},{5,7},{7,5},{8,10},{10,8},{9,1... | collective-permute-start | bytes 405512 | tf_op jit(solution)/shard_map/ppermute | solution.py:365
  25.0 0.8 %collective-permute-done.8.mate_other = f32[256,128]{1,0:T(8,128)S(1)} collective-permute-done((f32[256,128]{1,0:T(8,128)S(1)}, f32[256,128]{1,0:T(8,128)S(1)}, u32[]{:S(2)}, u32[]{:S(2)}) %collective-permute-start.8) | collective-permute-done | bytes 131104 | tf_op jit(solution)/shard_map/ppermute | solution.py:357
  26.0 0.6 %near.1 = (f32[256,256]{1,0:T(8,128)S(1)}, f32[256,256]{1,0:T(8,128)S(1)}, f32[8,256]{1,0:T(8,128)S(1)}) custom-call(f32[392,256]{1,0:T(8,128)S(1)} %pack.2.packed.mine.refs_0_, f32[256,256]{1,0:T(8,128)S(1)} %copy-done.1, f32[256,256]{1,0:T(8,128)S(1)} %get-tuple-element.41.image, f32[256,256]{1,0:T(8,128)S(1)} %get-tuple-element.42.once, ...), custom_call_target="tpu_custom_call" | custom-call | tf_op jit(solution)/shard_map/near/pallas_call | solution.py:26
  26.5 1.0 %collective-permute-done.10.refs_3_ = f32[264,128]{1,0:T(8,128)S(1)} collective-permute-done((f32[264,128]{1,0:T(8,128)S(1)}, f32[264,128]{1,0:T(8,128)S(1)}, u32[]{:S(2)}, u32[]{:S(2)}) %collective-permute-start.10) | collective-permute-done | bytes 135200 | tf_op jit(solution)/shard_map/ppermute | solution.py:365
  27.5 4.2 %collective-permute-done.9.left = f32[256,256]{1,0:T(8,128)S(1)} collective-permute-done((f32[256,256]{1,0:T(8,128)S(1)}, f32[256,256]{1,0:T(8,128)S(1)}, u32[]{:S(2)}, u32[]{:S(2)}) %collective-permute-start.9) | collective-permute-done | bytes 262176 | tf_op jit(solution)/shard_map/ppermute | solution.py:355
  32.3 1.6 %collective-permute-start.12 = (f32[8,256]{1,0:T(8,128)S(1)}, f32[8,256]{1,0:T(8,128)S(1)}, u32[]{:S(2)}, u32[]{:S(2)}) collective-permute-start(f32[8,256]{1,0:T(8,128)S(1)} %far.1.refs_0_), channel_id=1, source_target_pairs={{0,2},{1,3},{2,0},{3,1},{4,6},{5,7},{6,4},{7,5},{8,10},{9,11},{10,... | collective-permute-start | bytes 24584 | tf_op jit(solution)/shard_map/ppermute | solution.py:46
  34.2 1.2 %collective-permute-done.13.refs_3_ = f32[8,256]{1,0:T(8,128)S(1)} collective-permute-done((f32[8,256]{1,0:T(8,128)S(1)}, f32[8,256]{1,0:T(8,128)S(1)}, u32[]{:S(2)}, u32[]{:S(2)}) %collective-permute-start.13) | collective-permute-done | bytes 8224 | tf_op jit(solution)/shard_map/ppermute | solution.py:46
  35.4 0.6 %collective-permute-done.12.refs_2_ = f32[8,256]{1,0:T(8,128)S(1)} collective-permute-done((f32[8,256]{1,0:T(8,128)S(1)}, f32[8,256]{1,0:T(8,128)S(1)}, u32[]{:S(2)}, u32[]{:S(2)}) %collective-permute-start.12) | collective-permute-done | bytes 8224 | tf_op jit(solution)/shard_map/ppermute | solution.py:46
  36.1 1.5 %collective-permute-start.16 = (f32[8,256]{1,0:T(8,128)S(1)}, f32[8,256]{1,0:T(8,128)S(1)}, u32[]{:S(2)}, u32[]{:S(2)}) collective-permute-start(f32[8,256]{1,0:T(8,128)S(1)} %merge.2.refs_0_), channel_id=1, source_target_pairs={{0,12},{1,13},{2,14},{3,15},{4,8},{5,9},{6,10},{7,11},{8,4},{9,5},... | collective-permute-start | bytes 24584 | tf_op jit(solution)/shard_map/ppermute | solution.py:46
  37.6 3.0 %collective-permute-start.14 = (f32[8,256]{1,0:T(8,128)S(1)}, f32[8,256]{1,0:T(8,128)S(1)}, u32[]{:S(2)}, u32[]{:S(2)}) collective-permute-start(f32[8,256]{1,0:T(8,128)S(1)} %merge.2.refs_0_), channel_id=1, source_target_pairs={{0,4},{1,5},{2,6},{3,7},{4,0},{5,1},{6,2},{7,3},{8,12},{9,13},{10,... | collective-permute-start | bytes 24584 | tf_op jit(solution)/shard_map/ppermute | solution.py:46
  40.6 1.1 %collective-permute-done.16.refs_3_ = f32[8,256]{1,0:T(8,128)S(1)} collective-permute-done((f32[8,256]{1,0:T(8,128)S(1)}, f32[8,256]{1,0:T(8,128)S(1)}, u32[]{:S(2)}, u32[]{:S(2)}) %collective-permute-start.16) | collective-permute-done | bytes 8224 | tf_op jit(solution)/shard_map/ppermute | solution.py:46
  42.3 0.7 %multiply_subtract_fusion = f32[256,256]{1,0:T(8,128)} fusion(f32[256,256]{1,0:T(8,128)S(1)} %get-tuple-element.41.image, f32[256,256]{1,0:T(8,128)S(1)} %copy-done.1, f32[256]{0:T(256)S(1)} %bitcast.14, f32[256]{0:T(256)S(1)} %bitcast.13), kind=kLoop, calls=%fused_computation | loop fusion | flops 196608 | bytes 788480 | tf_op jit(solution)/shard_map/sub | solution.py:373
  (38 shorter events, 5.5 us)
Async XLA Ops:
  0.0 7.4 %copy-start.2 = (f32[2,7,128,128]{3,2,1,0:T(8,128)S(1)}, f32[2,7,128,128]{3,2,1,0:T(8,128)}, u32[]{:S(2)}) copy-start(f32[2,7,128,128]{3,2,1,0:T(8,128)} %local.1) | copy-start | bytes 2752516
  1.1 14.6 %collective-permute-start.3 = (f32[392,256]{1,0:T(8,128)S(1)}, f32[392,256]{1,0:T(8,128)S(1)}, u32[]{:S(2)}, u32[]{:S(2)}) collective-permute-start(f32[392,256]{1,0:T(8,128)S(1)} %pack.2.packed.mine.refs_0_), channel_id=1, source_target_pairs={{0,4},{4,8},{8,12},{12,0},{1,5},{5,9},{9,13},{13,1},{2,6},{6,10},{... | collective-permute-start | bytes 1204232 | tf_op jit(solution)/shard_map/ppermute | solution.py:317
  4.3 3.2 %copy-start.4 = (f32[256]{0:T(256)S(1)}, f32[256]{0:T(256)}, u32[]{:S(2)}) copy-start(f32[256]{0:T(256)} %param.8) | copy-start | bytes 3076
  5.9 1.6 %copy-start.3 = (s32[2,7]{1,0:T(2,128)S(1)}, s32[2,7]{1,0:T(2,128)}, u32[]{:S(2)}) copy-start(s32[2,7]{1,0:T(2,128)} %cols.1) | copy-start | bytes 172
  5.9 10.8 %collective-permute-start.4 = (f32[392,256]{1,0:T(8,128)S(1)}, f32[392,256]{1,0:T(8,128)S(1)}, u32[]{:S(2)}, u32[]{:S(2)}) collective-permute-start(f32[392,256]{1,0:T(8,128)S(1)} %pack.3), channel_id=1, source_target_pairs={{0,2},{2,0},{1,3},{3,1},{4,6},{6,4},{5,7},{7,5},{8,10},{10,8},{9,1... | collective-permute-start | bytes 1204232 | tf_op jit(solution)/shard_map/ppermute | solution.py:317
  7.4 2.7 %copy-start = (f32[1,8,128,128]{3,2,1,0:T(8,128)S(1)}, f32[1,8,128,128]{3,2,1,0:T(8,128)}, u32[]{:S(2)}) copy-start(f32[1,8,128,128]{3,2,1,0:T(8,128)} %param.11) | copy-start | bytes 1572868
  7.5 2.7 %copy-start.1 = (f32[256,256]{1,0:T(8,128)S(1)}, f32[256,256]{1,0:T(8,128)}, u32[]{:S(2)}) copy-start(f32[256,256]{1,0:T(8,128)} %field.5) | copy-start | bytes 786436
  8.6 1.4 %collective-permute-start.1 = (f32[256,128]{1,0:T(8,128)S(1)}, f32[256,128]{1,0:T(8,128)S(1)}, u32[]{:S(2)}, u32[]{:S(2)}) collective-permute-start(f32[256,128]{1,0:T(8,128)S(1)} %get-tuple-element.31), channel_id=1, source_target_pairs={{0,1},{1,0},{2,3},{3,2},{4,5},{5,4},{6,7},{7,6},{8,9},{9,8},{10,11... | collective-permute-start | bytes 393224 | tf_op jit(solution)/shard_map/ppermute | solution.py:340
  8.6 1.5 %collective-permute-start.2 = (f32[256,128]{1,0:T(8,128)S(1)}, f32[256,128]{1,0:T(8,128)S(1)}, u32[]{:S(2)}, u32[]{:S(2)}) collective-permute-start(f32[256,128]{1,0:T(8,128)S(1)} %get-tuple-element.32), channel_id=1, source_target_pairs={{0,1},{1,0},{2,3},{3,2},{4,5},{5,4},{6,7},{7,6},{8,9},{9,8},{10,11... | collective-permute-start | bytes 393224 | tf_op jit(solution)/shard_map/ppermute | solution.py:340
  10.3 11.0 %collective-permute-start.5 = (f32[520,128]{1,0:T(8,128)S(1)}, f32[520,128]{1,0:T(8,128)S(1)}, u32[]{:S(2)}, u32[]{:S(2)}) collective-permute-start(f32[520,128]{1,0:T(8,128)S(1)} %get-tuple-element.37), channel_id=1, source_target_pairs={{4,0},{8,4},{12,8},{0,12},{5,1},{9,5},{13,9},{1,13},{6,2},{10,6},{... | collective-permute-start | bytes 798728 | tf_op jit(solution)/shard_map/ppermute | solution.py:346
  12.6 1.9 %collective-permute-start = (f32[256,256]{1,0:T(8,128)S(1)}, f32[256,256]{1,0:T(8,128)S(1)}, u32[]{:S(2)}, u32[]{:S(2)}) collective-permute-start(f32[256,256]{1,0:T(8,128)S(1)} %copy-done.1), channel_id=1, source_target_pairs={{0,1},{1,0},{2,3},{3,2},{4,5},{5,4},{6,7},{7,6},{8,9},{9,8},{10,11... | collective-permute-start | bytes 786440 | tf_op jit(solution)/shard_map/ppermute | solution.py:319
  12.6 11.5 %collective-permute-start.6 = (f32[264,128]{1,0:T(8,128)S(1)}, f32[264,128]{1,0:T(8,128)S(1)}, u32[]{:S(2)}, u32[]{:S(2)}) collective-permute-start(f32[264,128]{1,0:T(8,128)S(1)} %get-tuple-element.40), channel_id=1, source_target_pairs={{4,0},{8,4},{12,8},{0,12},{5,1},{9,5},{13,9},{1,13},{6,2},{10,6},{... | collective-permute-start | bytes 405512 | tf_op jit(solution)/shard_map/ppermute | solution.py:346
  21.7 10.1 %collective-permute-start.9 = (f32[256,256]{1,0:T(8,128)S(1)}, f32[256,256]{1,0:T(8,128)S(1)}, u32[]{:S(2)}, u32[]{:S(2)}) collective-permute-start(f32[256,256]{1,0:T(8,128)S(1)} %get-tuple-element.50), channel_id=1, source_target_pairs={{0,4},{4,8},{8,12},{12,0},{1,5},{5,9},{9,13},{13,1},{2,6},{6,10},{... | collective-permute-start | bytes 786440 | tf_op jit(solution)/shard_map/ppermute | solution.py:355
  22.3 5.2 %collective-permute-start.10 = (f32[264,128]{1,0:T(8,128)S(1)}, f32[264,128]{1,0:T(8,128)S(1)}, u32[]{:S(2)}, u32[]{:S(2)}) collective-permute-start(f32[264,128]{1,0:T(8,128)S(1)} %get-tuple-element.52), channel_id=1, source_target_pairs={{0,2},{2,0},{1,3},{3,1},{4,6},{6,4},{5,7},{7,5},{8,10},{10,8},{9,1... | collective-permute-start | bytes 405512 | tf_op jit(solution)/shard_map/ppermute | solution.py:365
  24.4 1.4 %collective-permute-start.8 = (f32[256,128]{1,0:T(8,128)S(1)}, f32[256,128]{1,0:T(8,128)S(1)}, u32[]{:S(2)}, u32[]{:S(2)}) collective-permute-start(f32[256,128]{1,0:T(8,128)S(1)} %get-tuple-element.43), channel_id=1, source_target_pairs={{0,1},{1,0},{2,3},{3,2},{4,5},{5,4},{6,7},{7,6},{8,9},{9,8},{10,11... | collective-permute-start | bytes 393224 | tf_op jit(solution)/shard_map/ppermute | solution.py:357
  24.5 1.5 %collective-permute-start.7 = (f32[256,128]{1,0:T(8,128)S(1)}, f32[256,128]{1,0:T(8,128)S(1)}, u32[]{:S(2)}, u32[]{:S(2)}) collective-permute-start(f32[256,128]{1,0:T(8,128)S(1)} %get-tuple-element.38.half), channel_id=1, source_target_pairs={{0,1},{1,0},{2,3},{3,2},{4,5},{5,4},{6,7},{7,6},{8,9},{9,8},{10,11... | collective-permute-start | bytes 393224 | tf_op jit(solution)/shard_map/ppermute | solution.py:357
  32.3 3.2 %collective-permute-start.13 = (f32[8,256]{1,0:T(8,128)S(1)}, f32[8,256]{1,0:T(8,128)S(1)}, u32[]{:S(2)}, u32[]{:S(2)}) collective-permute-start(f32[8,256]{1,0:T(8,128)S(1)} %far.1.refs_0_), channel_id=1, source_target_pairs={{0,3},{1,2},{2,1},{3,0},{4,7},{5,6},{6,5},{7,4},{8,11},{9,10},{10,... | collective-permute-start | bytes 24584 | tf_op jit(solution)/shard_map/ppermute | solution.py:46
  32.3 3.7 %collective-permute-start.12 = (f32[8,256]{1,0:T(8,128)S(1)}, f32[8,256]{1,0:T(8,128)S(1)}, u32[]{:S(2)}, u32[]{:S(2)}) collective-permute-start(f32[8,256]{1,0:T(8,128)S(1)} %far.1.refs_0_), channel_id=1, source_target_pairs={{0,2},{1,3},{2,0},{3,1},{4,6},{5,7},{6,4},{7,5},{8,10},{9,11},{10,... | collective-permute-start | bytes 24584 | tf_op jit(solution)/shard_map/ppermute | solution.py:46
  33.9 2.2 %collective-permute-start.11 = (f32[8,256]{1,0:T(8,128)S(1)}, f32[8,256]{1,0:T(8,128)S(1)}, u32[]{:S(2)}, u32[]{:S(2)}) collective-permute-start(f32[8,256]{1,0:T(8,128)S(1)} %far.1.refs_0_), channel_id=1, source_target_pairs={{0,1},{1,0},{2,3},{3,2},{4,5},{5,4},{6,7},{7,6},{8,9},{9,8},{10,11... | collective-permute-start | bytes 24584 | tf_op jit(solution)/shard_map/ppermute | solution.py:46
  36.1 5.5 %collective-permute-start.16 = (f32[8,256]{1,0:T(8,128)S(1)}, f32[8,256]{1,0:T(8,128)S(1)}, u32[]{:S(2)}, u32[]{:S(2)}) collective-permute-start(f32[8,256]{1,0:T(8,128)S(1)} %merge.2.refs_0_), channel_id=1, source_target_pairs={{0,12},{1,13},{2,14},{3,15},{4,8},{5,9},{6,10},{7,11},{8,4},{9,5},... | collective-permute-start | bytes 24584 | tf_op jit(solution)/shard_map/ppermute | solution.py:46
  37.6 4.5 %collective-permute-start.15 = (f32[8,256]{1,0:T(8,128)S(1)}, f32[8,256]{1,0:T(8,128)S(1)}, u32[]{:S(2)}, u32[]{:S(2)}) collective-permute-start(f32[8,256]{1,0:T(8,128)S(1)} %merge.2.refs_0_), channel_id=1, source_target_pairs={{0,8},{1,9},{2,10},{3,11},{4,12},{5,13},{6,14},{7,15},{8,0},{9,1},... | collective-permute-start | bytes 24584 | tf_op jit(solution)/shard_map/ppermute | solution.py:46
  37.6 4.6 %collective-permute-start.14 = (f32[8,256]{1,0:T(8,128)S(1)}, f32[8,256]{1,0:T(8,128)S(1)}, u32[]{:S(2)}, u32[]{:S(2)}) collective-permute-start(f32[8,256]{1,0:T(8,128)S(1)} %merge.2.refs_0_), channel_id=1, source_target_pairs={{0,4},{1,5},{2,6},{3,7},{4,0},{5,1},{6,2},{7,3},{8,12},{9,13},{10,... | collective-permute-start | bytes 24584 | tf_op jit(solution)/shard_map/ppermute | solution.py:46

commit v14 on v13

--- a/solution.py
+++ b/solution.py
@@ -94,18 +94,6 @@
         copy.wait()
 
 
-def pack_right_kernel(mine, field, border, low, high, pay, other):
-    width = field.shape[0]
-    bs = border.shape[1]
-    last = mine.shape[0] - TAIL
-    toward = mine[pl.ds(last + 2, 1), pl.ds(0, 1)]
-    pay[pl.ds(0, width), :] = columns(field, toward, True)
-    for s in range(SIDE):
-        pay[pl.ds(width + s * bs, bs), :] = border[s]
-    pay[pl.ds(width + SIDE * bs, TAIL), :] = mine[pl.ds(last, TAIL), pl.ds(0, bs)]
-    other[pl.ds(0, width), :] = columns(field, toward, False)
-
-
 def prep_kernel(cols, marks, diag, local, packed, own, pair, low, high):
     nblocks, nonzeros, bs, _ = local.shape
     width = nblocks * bs
@@ -166,13 +154,16 @@
     image[...] = dot(own[...], mine[pl.ds(0, width), :]) + dot(coup[...], mate[...])
 
 
-def left_kernel(mine, part, border, pay, image, once, coup, back):
+def left_kernel(mine, part, border, pay, image, once, coup, back, out, other):
     width = part.shape[0]
+    toward = mine[pl.ds(mine.shape[0] - TAIL + 2, 1), pl.ds(0, 1)]
     coup[...] = edge(0, width, mine, pay, border)
+    back[...] = dot(coup[...].T, mine[pl.ds(0, width), :])
+    out[pl.ds(0, width), :] = columns(back, toward, True)
+    other[pl.ds(0, width), :] = columns(back, toward, False)
     term = dot(coup[...], pay[pl.ds(0, width), :])
     image[...] = part[...] + term
     once[...] = part[...] + 2.0 * term
-    back[...] = dot(coup[...].T, mine[pl.ds(0, width), :])
 
 
 def turn(mine, width):
@@ -197,11 +188,10 @@
     return jnp.where((toward == 3.0) == out, ref[:, middle:], ref[:, :middle])
 
 
-def right_kernel(mine, part, border, pay, half, across, coup, pass_on):
+def right_kernel(mine, part, out, half, across, pass_on):
     width = part.shape[0]
     toward = mine[pl.ds(mine.shape[0] - TAIL + 2, 1), pl.ds(0, 1)]
-    coup[...] = edge(1, width, mine, pay, border)
-    half[...] = columns(part, toward, True) + dot(coup[...], pay[pl.ds(0, width), :])
+    half[...] = columns(part, toward, True) + out[pl.ds(0, width), :]
     across[pl.ds(0, width), :] = half[...]
     across[pl.ds(width, EXTRA), :] = jnp.zeros((EXTRA, half.shape[1]), F32)
     pass_on[...] = part[...]
@@ -213,9 +203,9 @@
     return jnp.concatenate([low, high], axis=1)
 
 
-def whole_kernel(mine, part, half, coup, pay, image, other):
-    toward = mine[pl.ds(mine.shape[0] - TAIL + 2, 1), pl.ds(0, 1)]
-    other[...] = columns(part, toward, False) + dot(coup[...], pay[pl.ds(0, part.shape[0]), :])
+def whole_kernel(mine, part, half, rest, image, other):
+    toward = mine[pl.ds(mine.shape[0] - TAIL + 2, 1), pl.ds(0, 1)]
+    other[...] = columns(part, toward, False) + rest[pl.ds(0, part.shape[0]), :]
     image[...] = joined(toward, half[...], other[...])
 
 
@@ -293,8 +283,7 @@
     def smem(n):
         return [pl.BlockSpec(memory_space=pltpu.SMEM)] * n
 
-    wider = width + EXTRA
-    full, blocks, half = (width + bs + TAIL, ncols), (width + SIDE * bs + TAIL, ncols // 2), (width, ncols // 2)
+    full, half, longer = (width + bs + TAIL, ncols), (width, ncols // 2), (width + EXTRA, ncols // 2)
 
     def pack(gives):
         count = len(gives)
@@ -340,20 +329,17 @@
     mate_pair = [lax.ppermute(piece, "nd", swap) for piece in pieces]
 
     part, coup = call(base_kernel, "base", [field, square])(mine, own, pair, mate, *mate_pair)
-    to_left = call(pack_right_kernel, "pack_right", [blocks, (wider, ncols // 2)])(
-        mine, right_side, border, *mate_pair
+    part, once, left_coup, back, *to_left = call(left_kernel, "left", [field, field, square, field] + [longer] * 2)(
+        mine, part, border, pays[0]
     )
-    from_right = [lax.ppermute(pay, "gx", left) for pay in to_left]
-    part, once, left_coup, back = call(left_kernel, "left", [field, field, square, field])(mine, part, border, pays[0])
+    from_right = [lax.ppermute(piece, "gx", left) for piece in to_left]
     side_coup = []
     for (_, take, weight), pay in zip(sides, pays[1:]):
         part, once, block = call(partial(gy_kernel, take, weight), "gy", [field, field, square])(mine, part, once, border, pay)
         side_coup.append(block)
-    half_w, across, right_coup, pass_on = call(right_kernel, "right", [half, (wider, ncols // 2), square, field])(
-        mine, part, border, from_right[0]
-    )
+    half_w, across, pass_on = call(right_kernel, "right", [half, longer, field])(mine, part, from_right[0])
     left_w = lax.ppermute(pass_on, "gx", right)
-    image, other_w = call(whole_kernel, "whole", [field, half])(mine, part, half_w, right_coup, from_right[1])
+    image, other_w = call(whole_kernel, "whole", [field, half])(mine, part, half_w, from_right[1])
     mate_w = [lax.ppermute(w, "nd", swap) for w in (half_w, other_w)]
     part, lift, state = call(near_kernel, "near", [field, field, (TAIL, ncols)])(
         mine, right_side, image, once, mate, *mate_w, own, coup, pays[0], back

time: 43.2 us -> 42.7 us (0.988)
  waiting for transfers between devices: 16.6 us -> 19.2 us
  starting transfers between devices: 18.4 us -> 15.9 us
  Pallas kernels: 7.02 us -> 6.47 us
    ppermute x2, waiting for transfers between devices: 1.28 us -> 4.61 us  [shards(): lax.ppermute(pay, axis, perm)]
    ppermute x2, starting transfers between devices: 4.11 us -> 2.24 us  [shards(): from_right = [lax.ppermute(piece, 'gx', left) for piece in to_left]]
    ppermute x1, waiting for transfers between devices: 4.23 us -> 3.12 us  [shards(): left_w = lax.ppermute(pass_on, 'gx', right)]
    ppermute x6, waiting for transfers between devices: 3.51 us -> 4.11 us  [join(): lax.ppermute(state, AXES, [(i, i ^ m) for i in range(count)])]
    ppermute x1, starting transfers between devices: 0.62 us -> 0.06 us  [shards(): left_w = lax.ppermute(pass_on, 'gx', right)]
    pallas_call x10 -> x9, Pallas kernels: 3.23 us -> 2.68 us  [run(): pl.pallas_call(kernel, name=name, in_specs=[vmem()] * len(args), out_spec...]
    ppermute x1, waiting for transfers between devices: 0.96 us -> 0.5 us  [shards(): lax.ppermute(across if take is None else image, 'gy', perm)]
  transfers between devices with their start and end apart: 17 -> 17, of which waited for: 15 -> 13; matrix products, arithmetic and copies ran while one was open for 0% -> 0% of each run, Pallas kernels for 12% -> 11%
where the time goes in v14:
time: 42.7 us; the launch traced here: 42.6 us
  waiting for transfers between devices  19.2 us (45%)
  starting transfers between devices  15.9 us (37%)
  Pallas kernels  6.47 us (15%)
  other arithmetic  0.85 us (2%)
    ppermute x6, starting transfers between devices, join(): lax.ppermute(state, AXES, [(i, i ^ m) for i in range(count)])  6.39 us
    ppermute x2, starting transfers between devices, shards(): lax.ppermute(pay, axis, perm)  4.63 us
    ppermute x2, waiting for transfers between devices, shards(): lax.ppermute(pay, axis, perm)  4.61 us
    ppermute x2, waiting for transfers between devices, shards(): from_right = [lax.ppermute(piece, 'gx', left) for piece in to_left]  4.61 us
    ppermute x6, waiting for transfers between devices, join(): lax.ppermute(state, AXES, [(i, i ^ m) for i in range(count)])  4.11 us
    ppermute x1, waiting for transfers between devices, shards(): left_w = lax.ppermute(pass_on, 'gx', right)  3.12 us
    pallas_call x2, Pallas kernels, pack(): pl.pallas_call(partial(pack_kernel, gives), name='pack', in_specs=smem(le...  2.7 us
    pallas_call x9, Pallas kernels, run(): pl.pallas_call(kernel, name=name, in_specs=[vmem()] * len(args), out_spec...  2.68 us
  transfers between devices with their start and end apart: 17, of which 13 were waited for; matrix products, arithmetic and copies ran while one was open for 0% of the time, Pallas kernels for 11%

profile of v14, /device:TPU:0, one launch (start us, length us, event | category | flops | bytes accessed | tf_op | source)
XLA Modules:
  0.0 42.6 jit_solution(16875896741267466257)
XLA Ops:
  0.0 1.1 %pack.2.packed.mine.refs_0_ = f32[392,256]{1,0:T(8,128)S(1)} custom-call(f32[256,256]{1,0:T(8,128)} %field.3, f32[8,128,128]{2,1,0:T(8,128)} %bitcast.6, s32[1,8]{1,0:T(1,128)} %refs_3_.3, s32[1,8]{1,0:T(1,128)} %refs_4_.1, s32[1,8]{1,0:T(1,128)S(1)} %broadcast_in_dim.3.refs_4_.refs_5_), custom_call_target="tpu_custom_call" | custom-call | tf_op jit(solution)/shard_map/pack/pallas_call | solution.py:291
  1.1 3.1 %collective-permute-start.3 = (f32[392,256]{1,0:T(8,128)S(1)}, f32[392,256]{1,0:T(8,128)S(1)}, u32[]{:S(2)}, u32[]{:S(2)}) collective-permute-start(f32[392,256]{1,0:T(8,128)S(1)} %pack.2.packed.mine.refs_0_), channel_id=1, source_target_pairs={{0,4},{4,8},{8,12},{12,0},{1,5},{5,9},{9,13},{13,1},{2,6},{6,10},{... | collective-permute-start | bytes 1204232 | tf_op jit(solution)/shard_map/ppermute | solution.py:306
  4.3 1.6 %pack.3 = f32[392,256]{1,0:T(8,128)S(1)} custom-call(s32[2]{0:T(128)S(1)} %pad_add_fusion.marks.refs_0_, f32[256,256]{1,0:T(8,128)} %field.3, f32[8,128,128]{2,1,0:T(8,128)} %bitcast.7, s32[1,8]{1,0:T(1,128)} %refs_3_.3, s32[1,8]{1,0:T(1,128)} %refs_4_.1, s32[1,8]{1,0:T(1,128)S(1)} %broadcast_in_dim.3.refs_4_.refs_5_), custom_call_target="tpu_custom_call" | custom-call | tf_op jit(solution)/shard_map/pack/pallas_call | solution.py:291
  5.9 1.6 %collective-permute-start.4 = (f32[392,256]{1,0:T(8,128)S(1)}, f32[392,256]{1,0:T(8,128)S(1)}, u32[]{:S(2)}, u32[]{:S(2)}) collective-permute-start(f32[392,256]{1,0:T(8,128)S(1)} %pack.3), channel_id=1, source_target_pairs={{0,2},{2,0},{1,3},{3,1},{4,6},{6,4},{5,7},{7,5},{8,10},{10,8},{9,1... | collective-permute-start | bytes 1204232 | tf_op jit(solution)/shard_map/ppermute | solution.py:306
  7.5 1.1 %prep.1 = (f32[256,256]{1,0:T(8,128)S(1)}, f32[256,256]{1,0:T(8,128)S(1)}, f32[256,128]{1,0:T(8,128)S(1)}, f32[256,128]{1,0:T(8,128)S(1)}) custom-call(s32[2,7]{1,0:T(2,128)S(1)} %copy-done.3, s32[2]{0:T(128)S(1)} %pad_add_fusion.marks.refs_0_, f32[1,256]{1,0:T(1,128)S(1)} %bitcast.10, f32[2,7,128,128]{3,2,1,0:T(8,128)S(1)} %copy-done.2, ...), custom_call_target="tpu_custom_call" | custom-call | flops 16777216 | bytes 1048576 | tf_op jit(solution)/shard_map/prep/pallas_call | solution.py:313
  8.6 0.6 %collective-permute-start.1 = (f32[256,128]{1,0:T(8,128)S(1)}, f32[256,128]{1,0:T(8,128)S(1)}, u32[]{:S(2)}, u32[]{:S(2)}) collective-permute-start(f32[256,128]{1,0:T(8,128)S(1)} %get-tuple-element.30), channel_id=1, source_target_pairs={{0,1},{1,0},{2,3},{3,2},{4,5},{5,4},{6,7},{7,6},{8,9},{9,8},{10,11... | collective-permute-start | bytes 393224 | tf_op jit(solution)/shard_map/ppermute | solution.py:329
  9.2 0.9 %collective-permute-done.1.low = f32[256,128]{1,0:T(8,128)S(1)} collective-permute-done((f32[256,128]{1,0:T(8,128)S(1)}, f32[256,128]{1,0:T(8,128)S(1)}, u32[]{:S(2)}, u32[]{:S(2)}) %collective-permute-start.1) | collective-permute-done | bytes 131104 | tf_op jit(solution)/shard_map/ppermute | solution.py:329
  10.9 4.6 %collective-permute-done.3.pay = f32[392,256]{1,0:T(8,128)S(1)} collective-permute-done((f32[392,256]{1,0:T(8,128)S(1)}, f32[392,256]{1,0:T(8,128)S(1)}, u32[]{:S(2)}, u32[]{:S(2)}) %collective-permute-start.3) | collective-permute-done | bytes 401440 | tf_op jit(solution)/shard_map/ppermute | solution.py:306
  15.5 0.6 %left.1 = (f32[256,256]{1,0:T(8,128)S(1)}, f32[256,256]{1,0:T(8,128)S(1)}, f32[256,256]{1,0:T(8,128)S(1)}, f32[256,256]{1,0:T(8,128)S(1)}, f32[264,128]{1,0:T(8,128)S(1)}, /*index=5*/f32[264,128]{1,0:T(8,128)S(1)}) custom-call(f32[392,256]{1,0:T(8,128)S(1)} %pack.2.packed.mine.refs_0_, f32[256,256]{1,0:T(8,128)S(1)} %get-tuple-element.32.part, ...), custom_call_target="tpu_custom_call" | custom-call | tf_op jit(solution)/shard_map/left/pallas_call | solution.py:26
  16.1 1.8 %collective-permute-start.5 = (f32[264,128]{1,0:T(8,128)S(1)}, f32[264,128]{1,0:T(8,128)S(1)}, u32[]{:S(2)}, u32[]{:S(2)}) collective-permute-start(f32[264,128]{1,0:T(8,128)S(1)} %get-tuple-element.36), channel_id=1, source_target_pairs={{4,0},{8,4},{12,8},{0,12},{5,1},{9,5},{13,9},{1,13},{6,2},{10,6},{... | collective-permute-start | bytes 405512 | tf_op jit(solution)/shard_map/ppermute | solution.py:335
  18.7 3.6 %collective-permute-done.5.out = f32[264,128]{1,0:T(8,128)S(1)} collective-permute-done((f32[264,128]{1,0:T(8,128)S(1)}, f32[264,128]{1,0:T(8,128)S(1)}, u32[]{:S(2)}, u32[]{:S(2)}) %collective-permute-start.5) | collective-permute-done | bytes 135200 | tf_op jit(solution)/shard_map/ppermute | solution.py:335
  22.5 1.3 %collective-permute-start.10 = (f32[264,128]{1,0:T(8,128)S(1)}, f32[264,128]{1,0:T(8,128)S(1)}, u32[]{:S(2)}, u32[]{:S(2)}) collective-permute-start(f32[264,128]{1,0:T(8,128)S(1)} %get-tuple-element.50), channel_id=1, source_target_pairs={{0,2},{2,0},{1,3},{3,1},{4,6},{6,4},{5,7},{7,5},{8,10},{10,8},{9,1... | collective-permute-start | bytes 405512 | tf_op jit(solution)/shard_map/ppermute | solution.py:351
  23.9 1.0 %collective-permute-done.6.rest = f32[264,128]{1,0:T(8,128)S(1)} collective-permute-done((f32[264,128]{1,0:T(8,128)S(1)}, f32[264,128]{1,0:T(8,128)S(1)}, u32[]{:S(2)}, u32[]{:S(2)}) %collective-permute-start.6) | collective-permute-done | bytes 135200 | tf_op jit(solution)/shard_map/ppermute | solution.py:335
  25.5 0.8 %collective-permute-done.8.mate_other = f32[256,128]{1,0:T(8,128)S(1)} collective-permute-done((f32[256,128]{1,0:T(8,128)S(1)}, f32[256,128]{1,0:T(8,128)S(1)}, u32[]{:S(2)}, u32[]{:S(2)}) %collective-permute-start.8) | collective-permute-done | bytes 131104 | tf_op jit(solution)/shard_map/ppermute | solution.py:343
  26.5 0.6 %near.1 = (f32[256,256]{1,0:T(8,128)S(1)}, f32[256,256]{1,0:T(8,128)S(1)}, f32[8,256]{1,0:T(8,128)S(1)}) custom-call(f32[392,256]{1,0:T(8,128)S(1)} %pack.2.packed.mine.refs_0_, f32[256,256]{1,0:T(8,128)S(1)} %copy-done.1, f32[256,256]{1,0:T(8,128)S(1)} %get-tuple-element.39.image, f32[256,256]{1,0:T(8,128)S(1)} %get-tuple-element.40.once, ...), custom_call_target="tpu_custom_call" | custom-call | tf_op jit(solution)/shard_map/near/pallas_call | solution.py:26
  27.6 3.1 %collective-permute-done.9.left = f32[256,256]{1,0:T(8,128)S(1)} collective-permute-done((f32[256,256]{1,0:T(8,128)S(1)}, f32[256,256]{1,0:T(8,128)S(1)}, u32[]{:S(2)}, u32[]{:S(2)}) %collective-permute-start.9) | collective-permute-done | bytes 262176 | tf_op jit(solution)/shard_map/ppermute | solution.py:341
  31.3 1.6 %collective-permute-start.12 = (f32[8,256]{1,0:T(8,128)S(1)}, f32[8,256]{1,0:T(8,128)S(1)}, u32[]{:S(2)}, u32[]{:S(2)}) collective-permute-start(f32[8,256]{1,0:T(8,128)S(1)} %far.1.refs_0_), channel_id=1, source_target_pairs={{0,2},{1,3},{2,0},{3,1},{4,6},{5,7},{6,4},{7,5},{8,10},{9,11},{10,... | collective-permute-start | bytes 24584 | tf_op jit(solution)/shard_map/ppermute | solution.py:46
  33.2 1.3 %collective-permute-done.13.refs_3_ = f32[8,256]{1,0:T(8,128)S(1)} collective-permute-done((f32[8,256]{1,0:T(8,128)S(1)}, f32[8,256]{1,0:T(8,128)S(1)}, u32[]{:S(2)}, u32[]{:S(2)}) %collective-permute-start.13) | collective-permute-done | bytes 8224 | tf_op jit(solution)/shard_map/ppermute | solution.py:46
  34.4 0.6 %collective-permute-done.12.refs_2_ = f32[8,256]{1,0:T(8,128)S(1)} collective-permute-done((f32[8,256]{1,0:T(8,128)S(1)}, f32[8,256]{1,0:T(8,128)S(1)}, u32[]{:S(2)}, u32[]{:S(2)}) %collective-permute-start.12) | collective-permute-done | bytes 8224 | tf_op jit(solution)/shard_map/ppermute | solution.py:46
  35.1 2.2 %collective-permute-start.16 = (f32[8,256]{1,0:T(8,128)S(1)}, f32[8,256]{1,0:T(8,128)S(1)}, u32[]{:S(2)}, u32[]{:S(2)}) collective-permute-start(f32[8,256]{1,0:T(8,128)S(1)} %merge.2.refs_0_), channel_id=1, source_target_pairs={{0,12},{1,13},{2,14},{3,15},{4,8},{5,9},{6,10},{7,11},{8,4},{9,5},... | collective-permute-start | bytes 24584 | tf_op jit(solution)/shard_map/ppermute | solution.py:46
  37.2 2.3 %collective-permute-start.14 = (f32[8,256]{1,0:T(8,128)S(1)}, f32[8,256]{1,0:T(8,128)S(1)}, u32[]{:S(2)}, u32[]{:S(2)}) collective-permute-start(f32[8,256]{1,0:T(8,128)S(1)} %merge.2.refs_0_), channel_id=1, source_target_pairs={{0,4},{1,5},{2,6},{3,7},{4,0},{5,1},{6,2},{7,3},{8,12},{9,13},{10,... | collective-permute-start | bytes 24584 | tf_op jit(solution)/shard_map/ppermute | solution.py:46
  39.5 1.1 %collective-permute-done.16.refs_3_ = f32[8,256]{1,0:T(8,128)S(1)} collective-permute-done((f32[8,256]{1,0:T(8,128)S(1)}, f32[8,256]{1,0:T(8,128)S(1)}, u32[]{:S(2)}, u32[]{:S(2)}) %collective-permute-start.16) | collective-permute-done | bytes 8224 | tf_op jit(solution)/shard_map/ppermute | solution.py:46
  40.6 1.2 %collective-permute-done.15.refs_2_ = f32[8,256]{1,0:T(8,128)S(1)} collective-permute-done((f32[8,256]{1,0:T(8,128)S(1)}, f32[8,256]{1,0:T(8,128)S(1)}, u32[]{:S(2)}, u32[]{:S(2)}) %collective-permute-start.15) | collective-permute-done | bytes 8224 | tf_op jit(solution)/shard_map/ppermute | solution.py:46
  41.9 0.7 %multiply_subtract_fusion = f32[256,256]{1,0:T(8,128)} fusion(f32[256,256]{1,0:T(8,128)S(1)} %get-tuple-element.39.image, f32[256,256]{1,0:T(8,128)S(1)} %copy-done.1, f32[256]{0:T(256)S(1)} %bitcast.12, f32[256]{0:T(256)S(1)} %bitcast.11), kind=kLoop, calls=%fused_computation | loop fusion | flops 196608 | bytes 788480 | tf_op jit(solution)/shard_map/sub | solution.py:359
  (37 shorter events, 4.3 us)
Async XLA Ops:
  0.0 7.4 %copy-start.2 = (f32[2,7,128,128]{3,2,1,0:T(8,128)S(1)}, f32[2,7,128,128]{3,2,1,0:T(8,128)}, u32[]{:S(2)}) copy-start(f32[2,7,128,128]{3,2,1,0:T(8,128)} %local.1) | copy-start | bytes 2752516
  1.1 14.4 %collective-permute-start.3 = (f32[392,256]{1,0:T(8,128)S(1)}, f32[392,256]{1,0:T(8,128)S(1)}, u32[]{:S(2)}, u32[]{:S(2)}) collective-permute-start(f32[392,256]{1,0:T(8,128)S(1)} %pack.2.packed.mine.refs_0_), channel_id=1, source_target_pairs={{0,4},{4,8},{8,12},{12,0},{1,5},{5,9},{9,13},{13,1},{2,6},{6,10},{... | collective-permute-start | bytes 1204232 | tf_op jit(solution)/shard_map/ppermute | solution.py:306
  4.3 3.2 %copy-start.1 = (f32[256,256]{1,0:T(8,128)S(1)}, f32[256,256]{1,0:T(8,128)}, u32[]{:S(2)}) copy-start(f32[256,256]{1,0:T(8,128)} %field.3) | copy-start | bytes 786436
  4.3 3.2 %copy-start.4 = (f32[256]{0:T(256)S(1)}, f32[256]{0:T(256)}, u32[]{:S(2)}) copy-start(f32[256]{0:T(256)} %param.8) | copy-start | bytes 3076
  5.9 1.6 %copy-start.3 = (s32[2,7]{1,0:T(2,128)S(1)}, s32[2,7]{1,0:T(2,128)}, u32[]{:S(2)}) copy-start(s32[2,7]{1,0:T(2,128)} %cols.1) | copy-start | bytes 172
  5.9 12.5 %collective-permute-start.4 = (f32[392,256]{1,0:T(8,128)S(1)}, f32[392,256]{1,0:T(8,128)S(1)}, u32[]{:S(2)}, u32[]{:S(2)}) collective-permute-start(f32[392,256]{1,0:T(8,128)S(1)} %pack.3), channel_id=1, source_target_pairs={{0,2},{2,0},{1,3},{3,1},{4,6},{6,4},{5,7},{7,5},{8,10},{10,8},{9,1... | collective-permute-start | bytes 1204232 | tf_op jit(solution)/shard_map/ppermute | solution.py:306
  7.4 3.0 %collective-permute-start = (f32[256,256]{1,0:T(8,128)S(1)}, f32[256,256]{1,0:T(8,128)S(1)}, u32[]{:S(2)}, u32[]{:S(2)}) collective-permute-start(f32[256,256]{1,0:T(8,128)S(1)} %copy-done.1), channel_id=1, source_target_pairs={{0,1},{1,0},{2,3},{3,2},{4,5},{5,4},{6,7},{7,6},{8,9},{9,8},{10,11... | collective-permute-start | bytes 786440 | tf_op jit(solution)/shard_map/ppermute | solution.py:308
  8.6 1.5 %collective-permute-start.1 = (f32[256,128]{1,0:T(8,128)S(1)}, f32[256,128]{1,0:T(8,128)S(1)}, u32[]{:S(2)}, u32[]{:S(2)}) collective-permute-start(f32[256,128]{1,0:T(8,128)S(1)} %get-tuple-element.30), channel_id=1, source_target_pairs={{0,1},{1,0},{2,3},{3,2},{4,5},{5,4},{6,7},{7,6},{8,9},{9,8},{10,11... | collective-permute-start | bytes 393224 | tf_op jit(solution)/shard_map/ppermute | solution.py:329
  9.1 1.3 %collective-permute-start.2 = (f32[256,128]{1,0:T(8,128)S(1)}, f32[256,128]{1,0:T(8,128)S(1)}, u32[]{:S(2)}, u32[]{:S(2)}) collective-permute-start(f32[256,128]{1,0:T(8,128)S(1)} %get-tuple-element.31), channel_id=1, source_target_pairs={{0,1},{1,0},{2,3},{3,2},{4,5},{5,4},{6,7},{7,6},{8,9},{9,8},{10,11... | collective-permute-start | bytes 393224 | tf_op jit(solution)/shard_map/ppermute | solution.py:329
  10.5 5.0 %copy-start = (f32[1,8,128,128]{3,2,1,0:T(8,128)S(1)}, f32[1,8,128,128]{3,2,1,0:T(8,128)}, u32[]{:S(2)}) copy-start(f32[1,8,128,128]{3,2,1,0:T(8,128)} %param.11) | copy-start | bytes 1572868
  16.1 6.3 %collective-permute-start.5 = (f32[264,128]{1,0:T(8,128)S(1)}, f32[264,128]{1,0:T(8,128)S(1)}, u32[]{:S(2)}, u32[]{:S(2)}) collective-permute-start(f32[264,128]{1,0:T(8,128)S(1)} %get-tuple-element.36), channel_id=1, source_target_pairs={{4,0},{8,4},{12,8},{0,12},{5,1},{9,5},{13,9},{1,13},{6,2},{10,6},{... | collective-permute-start | bytes 405512 | tf_op jit(solution)/shard_map/ppermute | solution.py:335
  17.9 7.0 %collective-permute-start.6 = (f32[264,128]{1,0:T(8,128)S(1)}, f32[264,128]{1,0:T(8,128)S(1)}, u32[]{:S(2)}, u32[]{:S(2)}) collective-permute-start(f32[264,128]{1,0:T(8,128)S(1)} %get-tuple-element.38), channel_id=1, source_target_pairs={{4,0},{8,4},{12,8},{0,12},{5,1},{9,5},{13,9},{1,13},{6,2},{10,6},{... | collective-permute-start | bytes 405512 | tf_op jit(solution)/shard_map/ppermute | solution.py:335
  22.5 8.3 %collective-permute-start.9 = (f32[256,256]{1,0:T(8,128)S(1)}, f32[256,256]{1,0:T(8,128)S(1)}, u32[]{:S(2)}, u32[]{:S(2)}) collective-permute-start(f32[256,256]{1,0:T(8,128)S(1)} %get-tuple-element.48), channel_id=1, source_target_pairs={{0,4},{4,8},{8,12},{12,0},{1,5},{5,9},{9,13},{13,1},{2,6},{6,10},{... | collective-permute-start | bytes 786440 | tf_op jit(solution)/shard_map/ppermute | solution.py:341
  22.5 5.1 %collective-permute-start.10 = (f32[264,128]{1,0:T(8,128)S(1)}, f32[264,128]{1,0:T(8,128)S(1)}, u32[]{:S(2)}, u32[]{:S(2)}) collective-permute-start(f32[264,128]{1,0:T(8,128)S(1)} %get-tuple-element.50), channel_id=1, source_target_pairs={{0,2},{2,0},{1,3},{3,1},{4,6},{6,4},{5,7},{7,5},{8,10},{10,8},{9,1... | collective-permute-start | bytes 405512 | tf_op jit(solution)/shard_map/ppermute | solution.py:351
  24.9 1.4 %collective-permute-start.8 = (f32[256,128]{1,0:T(8,128)S(1)}, f32[256,128]{1,0:T(8,128)S(1)}, u32[]{:S(2)}, u32[]{:S(2)}) collective-permute-start(f32[256,128]{1,0:T(8,128)S(1)} %get-tuple-element.41), channel_id=1, source_target_pairs={{0,1},{1,0},{2,3},{3,2},{4,5},{5,4},{6,7},{7,6},{8,9},{9,8},{10,11... | collective-permute-start | bytes 393224 | tf_op jit(solution)/shard_map/ppermute | solution.py:343
  25.0 1.5 %collective-permute-start.7 = (f32[256,128]{1,0:T(8,128)S(1)}, f32[256,128]{1,0:T(8,128)S(1)}, u32[]{:S(2)}, u32[]{:S(2)}) collective-permute-start(f32[256,128]{1,0:T(8,128)S(1)} %get-tuple-element.37.half), channel_id=1, source_target_pairs={{0,1},{1,0},{2,3},{3,2},{4,5},{5,4},{6,7},{7,6},{8,9},{9,8},{10,11... | collective-permute-start | bytes 393224 | tf_op jit(solution)/shard_map/ppermute | solution.py:343
  31.2 3.2 %collective-permute-start.13 = (f32[8,256]{1,0:T(8,128)S(1)}, f32[8,256]{1,0:T(8,128)S(1)}, u32[]{:S(2)}, u32[]{:S(2)}) collective-permute-start(f32[8,256]{1,0:T(8,128)S(1)} %far.1.refs_0_), channel_id=1, source_target_pairs={{0,3},{1,2},{2,1},{3,0},{4,7},{5,6},{6,5},{7,4},{8,11},{9,10},{10,... | collective-permute-start | bytes 24584 | tf_op jit(solution)/shard_map/ppermute | solution.py:46
  31.3 3.7 %collective-permute-start.12 = (f32[8,256]{1,0:T(8,128)S(1)}, f32[8,256]{1,0:T(8,128)S(1)}, u32[]{:S(2)}, u32[]{:S(2)}) collective-permute-start(f32[8,256]{1,0:T(8,128)S(1)} %far.1.refs_0_), channel_id=1, source_target_pairs={{0,2},{1,3},{2,0},{3,1},{4,6},{5,7},{6,4},{7,5},{8,10},{9,11},{10,... | collective-permute-start | bytes 24584 | tf_op jit(solution)/shard_map/ppermute | solution.py:46
  32.9 2.2 %collective-permute-start.11 = (f32[8,256]{1,0:T(8,128)S(1)}, f32[8,256]{1,0:T(8,128)S(1)}, u32[]{:S(2)}, u32[]{:S(2)}) collective-permute-start(f32[8,256]{1,0:T(8,128)S(1)} %far.1.refs_0_), channel_id=1, source_target_pairs={{0,1},{1,0},{2,3},{3,2},{4,5},{5,4},{6,7},{7,6},{8,9},{9,8},{10,11... | collective-permute-start | bytes 24584 | tf_op jit(solution)/shard_map/ppermute | solution.py:46
  35.1 5.5 %collective-permute-start.16 = (f32[8,256]{1,0:T(8,128)S(1)}, f32[8,256]{1,0:T(8,128)S(1)}, u32[]{:S(2)}, u32[]{:S(2)}) collective-permute-start(f32[8,256]{1,0:T(8,128)S(1)} %merge.2.refs_0_), channel_id=1, source_target_pairs={{0,12},{1,13},{2,14},{3,15},{4,8},{5,9},{6,10},{7,11},{8,4},{9,5},... | collective-permute-start | bytes 24584 | tf_op jit(solution)/shard_map/ppermute | solution.py:46
  37.2 4.5 %collective-permute-start.15 = (f32[8,256]{1,0:T(8,128)S(1)}, f32[8,256]{1,0:T(8,128)S(1)}, u32[]{:S(2)}, u32[]{:S(2)}) collective-permute-start(f32[8,256]{1,0:T(8,128)S(1)} %merge.2.refs_0_), channel_id=1, source_target_pairs={{0,8},{1,9},{2,10},{3,11},{4,12},{5,13},{6,14},{7,15},{8,0},{9,1},... | collective-permute-start | bytes 24584 | tf_op jit(solution)/shard_map/ppermute | solution.py:46
  37.2 4.5 %collective-permute-start.14 = (f32[8,256]{1,0:T(8,128)S(1)}, f32[8,256]{1,0:T(8,128)S(1)}, u32[]{:S(2)}, u32[]{:S(2)}) collective-permute-start(f32[8,256]{1,0:T(8,128)S(1)} %merge.2.refs_0_), channel_id=1, source_target_pairs={{0,4},{1,5},{2,6},{3,7},{4,0},{5,1},{6,2},{7,3},{8,12},{9,13},{10,... | collective-permute-start | bytes 24584 | tf_op jit(solution)/shard_map/ppermute | solution.py:46

commit v15 on v14

--- a/solution.py
+++ b/solution.py
@@ -188,13 +188,12 @@
     return jnp.where((toward == 3.0) == out, ref[:, middle:], ref[:, :middle])
 
 
-def right_kernel(mine, part, out, half, across, pass_on):
+def right_kernel(mine, part, out, half, across):
     width = part.shape[0]
     toward = mine[pl.ds(mine.shape[0] - TAIL + 2, 1), pl.ds(0, 1)]
     half[...] = columns(part, toward, True) + out[pl.ds(0, width), :]
     across[pl.ds(0, width), :] = half[...]
     across[pl.ds(width, EXTRA), :] = jnp.zeros((EXTRA, half.shape[1]), F32)
-    pass_on[...] = part[...]
 
 
 def joined(toward, out, other):
@@ -337,8 +336,8 @@
     for (_, take, weight), pay in zip(sides, pays[1:]):
         part, once, block = call(partial(gy_kernel, take, weight), "gy", [field, field, square])(mine, part, once, border, pay)
         side_coup.append(block)
-    half_w, across, pass_on = call(right_kernel, "right", [half, longer, field])(mine, part, from_right[0])
-    left_w = lax.ppermute(pass_on, "gx", right)
+    left_w = lax.ppermute(part, "gx", right)
+    half_w, across = call(right_kernel, "right", [half, longer])(mine, part, from_right[0])
     image, other_w = call(whole_kernel, "whole", [field, half])(mine, part, half_w, from_right[1])
     mate_w = [lax.ppermute(w, "nd", swap) for w in (half_w, other_w)]
     part, lift, state = call(near_kernel, "near", [field, field, (TAIL, ncols)])(

time: 42.7 us -> 42.9 us (level)
  starting transfers between devices: 15.9 us -> 16.6 us
  waiting for transfers between devices: 19.2 us -> 18.6 us
    ppermute x2, waiting for transfers between devices: 4.61 us -> 7.91 us  [shards(): from_right = [lax.ppermute(piece, 'gx', left) for piece in to_left]]
    ppermute x1, waiting for transfers between devices: 3.12 us -> 0.01 us  [shards(): left_w = lax.ppermute(part, 'gx', right)]
    ppermute x1, starting transfers between devices: 0.06 us -> 1.63 us  [shards(): left_w = lax.ppermute(part, 'gx', right)]
    ppermute x6, waiting for transfers between devices: 4.11 us -> 3.5 us  [join(): lax.ppermute(state, AXES, [(i, i ^ m) for i in range(count)])]
    ppermute x2, starting transfers between devices: 0.57 us -> 0.07 us  [shards(): mate_w = [lax.ppermute(w, 'nd', swap) for w in (half_w, other_w)]]
    ppermute x1, waiting for transfers between devices: 0.5 us -> 0.01 us  [shards(): lax.ppermute(across if take is None else image, 'gy', perm)]
  transfers between devices with their start and end apart: 17 -> 17, of which waited for: 13 -> 11; matrix products, arithmetic and copies ran while one was open for 0% -> 0% of each run, Pallas kernels for 11% -> 11%
where the time goes in v15:
time: 42.9 us; the launch traced here: 42.8 us
  waiting for transfers between devices  18.6 us (43%)
  starting transfers between devices  16.6 us (39%)
  Pallas kernels  6.5 us (15%)
  other arithmetic  0.85 us (2%)
    ppermute x2, waiting for transfers between devices, shards(): from_right = [lax.ppermute(piece, 'gx', left) for piece in to_left]  7.91 us
    ppermute x6, starting transfers between devices, join(): lax.ppermute(state, AXES, [(i, i ^ m) for i in range(count)])  6.37 us
    ppermute x2, starting transfers between devices, shards(): lax.ppermute(pay, axis, perm)  4.63 us
    ppermute x2, waiting for transfers between devices, shards(): lax.ppermute(pay, axis, perm)  4.61 us
    ppermute x6, waiting for transfers between devices, join(): lax.ppermute(state, AXES, [(i, i ^ m) for i in range(count)])  3.5 us
    pallas_call x9, Pallas kernels, run(): pl.pallas_call(kernel, name=name, in_specs=[vmem()] * len(args), out_spec...  2.71 us
    pallas_call x2, Pallas kernels, pack(): pl.pallas_call(partial(pack_kernel, gives), name='pack', in_specs=smem(le...  2.7 us
    ppermute x2, starting transfers between devices, shards(): from_right = [lax.ppermute(piece, 'gx', left) for piece in to_left]  2.24 us
  transfers between devices with their start and end apart: 17, of which 11 were waited for; matrix products, arithmetic and copies ran while one was open for 0% of the time, Pallas kernels for 11%

profile of v15, /device:TPU:0, one launch (start us, length us, event | category | flops | bytes accessed | tf_op | source)
XLA Modules:
  0.0 42.8 jit_solution(18065174712142936475)
XLA Ops:
  0.0 1.1 %pack.2.packed.mine.refs_0_ = f32[392,256]{1,0:T(8,128)S(1)} custom-call(f32[256,256]{1,0:T(8,128)} %field.3, f32[8,128,128]{2,1,0:T(8,128)} %bitcast.6, s32[1,8]{1,0:T(1,128)} %refs_3_.3, s32[1,8]{1,0:T(1,128)} %refs_4_.1, s32[1,8]{1,0:T(1,128)S(1)} %broadcast_in_dim.3.refs_4_.refs_5_), custom_call_target="tpu_custom_call" | custom-call | tf_op jit(solution)/shard_map/pack/pallas_call | solution.py:290
  1.1 3.1 %collective-permute-start.3 = (f32[392,256]{1,0:T(8,128)S(1)}, f32[392,256]{1,0:T(8,128)S(1)}, u32[]{:S(2)}, u32[]{:S(2)}) collective-permute-start(f32[392,256]{1,0:T(8,128)S(1)} %pack.2.packed.mine.refs_0_), channel_id=1, source_target_pairs={{0,4},{4,8},{8,12},{12,0},{1,5},{5,9},{9,13},{13,1},{2,6},{6,10},{... | collective-permute-start | bytes 1204232 | tf_op jit(solution)/shard_map/ppermute | solution.py:305
  4.3 1.6 %pack.3 = f32[392,256]{1,0:T(8,128)S(1)} custom-call(s32[2]{0:T(128)S(1)} %pad_add_fusion.marks.refs_0_, f32[256,256]{1,0:T(8,128)} %field.3, f32[8,128,128]{2,1,0:T(8,128)} %bitcast.7, s32[1,8]{1,0:T(1,128)} %refs_3_.3, s32[1,8]{1,0:T(1,128)} %refs_4_.1, s32[1,8]{1,0:T(1,128)S(1)} %broadcast_in_dim.3.refs_4_.refs_5_), custom_call_target="tpu_custom_call" | custom-call | tf_op jit(solution)/shard_map/pack/pallas_call | solution.py:290
  5.9 1.6 %collective-permute-start.4 = (f32[392,256]{1,0:T(8,128)S(1)}, f32[392,256]{1,0:T(8,128)S(1)}, u32[]{:S(2)}, u32[]{:S(2)}) collective-permute-start(f32[392,256]{1,0:T(8,128)S(1)} %pack.3), channel_id=1, source_target_pairs={{0,2},{2,0},{1,3},{3,1},{4,6},{6,4},{5,7},{7,5},{8,10},{10,8},{9,1... | collective-permute-start | bytes 1204232 | tf_op jit(solution)/shard_map/ppermute | solution.py:305
  7.5 1.1 %prep.1 = (f32[256,256]{1,0:T(8,128)S(1)}, f32[256,256]{1,0:T(8,128)S(1)}, f32[256,128]{1,0:T(8,128)S(1)}, f32[256,128]{1,0:T(8,128)S(1)}) custom-call(s32[2,7]{1,0:T(2,128)S(1)} %copy-done.3, s32[2]{0:T(128)S(1)} %pad_add_fusion.marks.refs_0_, f32[1,256]{1,0:T(1,128)S(1)} %bitcast.10, f32[2,7,128,128]{3,2,1,0:T(8,128)S(1)} %copy-done.2, ...), custom_call_target="tpu_custom_call" | custom-call | flops 16777216 | bytes 1048576 | tf_op jit(solution)/shard_map/prep/pallas_call | solution.py:312
  8.6 0.6 %collective-permute-start.1 = (f32[256,128]{1,0:T(8,128)S(1)}, f32[256,128]{1,0:T(8,128)S(1)}, u32[]{:S(2)}, u32[]{:S(2)}) collective-permute-start(f32[256,128]{1,0:T(8,128)S(1)} %get-tuple-element.29), channel_id=1, source_target_pairs={{0,1},{1,0},{2,3},{3,2},{4,5},{5,4},{6,7},{7,6},{8,9},{9,8},{10,11... | collective-permute-start | bytes 393224 | tf_op jit(solution)/shard_map/ppermute | solution.py:328
  9.2 0.9 %collective-permute-done.1.low = f32[256,128]{1,0:T(8,128)S(1)} collective-permute-done((f32[256,128]{1,0:T(8,128)S(1)}, f32[256,128]{1,0:T(8,128)S(1)}, u32[]{:S(2)}, u32[]{:S(2)}) %collective-permute-start.1) | collective-permute-done | bytes 131104 | tf_op jit(solution)/shard_map/ppermute | solution.py:328
  10.9 4.6 %collective-permute-done.3.pay = f32[392,256]{1,0:T(8,128)S(1)} collective-permute-done((f32[392,256]{1,0:T(8,128)S(1)}, f32[392,256]{1,0:T(8,128)S(1)}, u32[]{:S(2)}, u32[]{:S(2)}) %collective-permute-start.3) | collective-permute-done | bytes 401440 | tf_op jit(solution)/shard_map/ppermute | solution.py:305
  15.5 0.6 %left.1 = (f32[256,256]{1,0:T(8,128)S(1)}, f32[256,256]{1,0:T(8,128)S(1)}, f32[256,256]{1,0:T(8,128)S(1)}, f32[256,256]{1,0:T(8,128)S(1)}, f32[264,128]{1,0:T(8,128)S(1)}, /*index=5*/f32[264,128]{1,0:T(8,128)S(1)}) custom-call(f32[392,256]{1,0:T(8,128)S(1)} %pack.2.packed.mine.refs_0_, f32[256,256]{1,0:T(8,128)S(1)} %get-tuple-element.31.part, ...), custom_call_target="tpu_custom_call" | custom-call | tf_op jit(solution)/shard_map/left/pallas_call | solution.py:26
  16.1 1.8 %collective-permute-start.5 = (f32[264,128]{1,0:T(8,128)S(1)}, f32[264,128]{1,0:T(8,128)S(1)}, u32[]{:S(2)}, u32[]{:S(2)}) collective-permute-start(f32[264,128]{1,0:T(8,128)S(1)} %get-tuple-element.35), channel_id=1, source_target_pairs={{4,0},{8,4},{12,8},{0,12},{5,1},{9,5},{13,9},{1,13},{6,2},{10,6},{... | collective-permute-start | bytes 405512 | tf_op jit(solution)/shard_map/ppermute | solution.py:334
  18.7 1.6 %collective-permute-start.9 = (f32[256,256]{1,0:T(8,128)S(1)}, f32[256,256]{1,0:T(8,128)S(1)}, u32[]{:S(2)}, u32[]{:S(2)}) collective-permute-start(f32[256,256]{1,0:T(8,128)S(1)} %get-tuple-element.34.part), channel_id=1, source_target_pairs={{0,4},{4,8},{8,12},{12,0},{1,5},{5,9},{9,13},{13,1},{2,6},{6,10},{... | collective-permute-start | bytes 786440 | tf_op jit(solution)/shard_map/ppermute | solution.py:339
  20.4 2.8 %collective-permute-done.5.out = f32[264,128]{1,0:T(8,128)S(1)} collective-permute-done((f32[264,128]{1,0:T(8,128)S(1)}, f32[264,128]{1,0:T(8,128)S(1)}, u32[]{:S(2)}, u32[]{:S(2)}) %collective-permute-start.5) | collective-permute-done | bytes 135200 | tf_op jit(solution)/shard_map/ppermute | solution.py:334
  23.2 1.1 %collective-permute-start.10 = (f32[264,128]{1,0:T(8,128)S(1)}, f32[264,128]{1,0:T(8,128)S(1)}, u32[]{:S(2)}, u32[]{:S(2)}) collective-permute-start(f32[264,128]{1,0:T(8,128)S(1)} %get-tuple-element.48), channel_id=1, source_target_pairs={{0,2},{2,0},{1,3},{3,1},{4,6},{6,4},{5,7},{7,5},{8,10},{10,8},{9,1... | collective-permute-start | bytes 405512 | tf_op jit(solution)/shard_map/ppermute | solution.py:350
  24.3 5.1 %collective-permute-done.6.rest = f32[264,128]{1,0:T(8,128)S(1)} collective-permute-done((f32[264,128]{1,0:T(8,128)S(1)}, f32[264,128]{1,0:T(8,128)S(1)}, u32[]{:S(2)}, u32[]{:S(2)}) %collective-permute-start.6) | collective-permute-done | bytes 135200 | tf_op jit(solution)/shard_map/ppermute | solution.py:334
  29.6 1.3 %collective-permute-done.8.mate_other = f32[256,128]{1,0:T(8,128)S(1)} collective-permute-done((f32[256,128]{1,0:T(8,128)S(1)}, f32[256,128]{1,0:T(8,128)S(1)}, u32[]{:S(2)}, u32[]{:S(2)}) %collective-permute-start.8) | collective-permute-done | bytes 131104 | tf_op jit(solution)/shard_map/ppermute | solution.py:342
  31.0 0.6 %near.1 = (f32[256,256]{1,0:T(8,128)S(1)}, f32[256,256]{1,0:T(8,128)S(1)}, f32[8,256]{1,0:T(8,128)S(1)}) custom-call(f32[392,256]{1,0:T(8,128)S(1)} %pack.2.packed.mine.refs_0_, f32[256,256]{1,0:T(8,128)S(1)} %copy-done.1, f32[256,256]{1,0:T(8,128)S(1)} %get-tuple-element.38.image, f32[256,256]{1,0:T(8,128)S(1)} %get-tuple-element.39.once, ...), custom_call_target="tpu_custom_call" | custom-call | tf_op jit(solution)/shard_map/near/pallas_call | solution.py:26
  31.5 0.5 %far.1.refs_0_ = f32[8,256]{1,0:T(8,128)S(1)} custom-call(f32[256,256]{1,0:T(8,128)S(1)} %copy-done.1, f32[256,256]{1,0:T(8,128)S(1)} %get-tuple-element.38.image, f32[256,256]{1,0:T(8,128)S(1)} %get-tuple-element.43.part, f32[8,256]{1,0:T(8,128)S(1)} %get-tuple-element.44.near, f32[256,256]{1,0:T(8,128)S(1)} %get-tuple-element.45.lift, ...), custom_call_target="tpu_custom_call" | custom-call | tf_op jit(solution)/shard_map/far/pallas_call | solution.py:26
  32.1 1.8 %collective-permute-start.12 = (f32[8,256]{1,0:T(8,128)S(1)}, f32[8,256]{1,0:T(8,128)S(1)}, u32[]{:S(2)}, u32[]{:S(2)}) collective-permute-start(f32[8,256]{1,0:T(8,128)S(1)} %far.1.refs_0_), channel_id=1, source_target_pairs={{0,2},{1,3},{2,0},{3,1},{4,6},{5,7},{6,4},{7,5},{8,10},{9,11},{10,... | collective-permute-start | bytes 24584 | tf_op jit(solution)/shard_map/ppermute | solution.py:46
  34.0 1.2 %collective-permute-done.13.refs_3_ = f32[8,256]{1,0:T(8,128)S(1)} collective-permute-done((f32[8,256]{1,0:T(8,128)S(1)}, f32[8,256]{1,0:T(8,128)S(1)}, u32[]{:S(2)}, u32[]{:S(2)}) %collective-permute-start.13) | collective-permute-done | bytes 8224 | tf_op jit(solution)/shard_map/ppermute | solution.py:46
  35.2 0.7 %collective-permute-done.12.refs_2_ = f32[8,256]{1,0:T(8,128)S(1)} collective-permute-done((f32[8,256]{1,0:T(8,128)S(1)}, f32[8,256]{1,0:T(8,128)S(1)}, u32[]{:S(2)}, u32[]{:S(2)}) %collective-permute-start.12) | collective-permute-done | bytes 8224 | tf_op jit(solution)/shard_map/ppermute | solution.py:46
  35.9 1.4 %collective-permute-start.16 = (f32[8,256]{1,0:T(8,128)S(1)}, f32[8,256]{1,0:T(8,128)S(1)}, u32[]{:S(2)}, u32[]{:S(2)}) collective-permute-start(f32[8,256]{1,0:T(8,128)S(1)} %merge.2.refs_0_), channel_id=1, source_target_pairs={{0,12},{1,13},{2,14},{3,15},{4,8},{5,9},{6,10},{7,11},{8,4},{9,5},... | collective-permute-start | bytes 24584 | tf_op jit(solution)/shard_map/ppermute | solution.py:46
  37.3 3.0 %collective-permute-start.14 = (f32[8,256]{1,0:T(8,128)S(1)}, f32[8,256]{1,0:T(8,128)S(1)}, u32[]{:S(2)}, u32[]{:S(2)}) collective-permute-start(f32[8,256]{1,0:T(8,128)S(1)} %merge.2.refs_0_), channel_id=1, source_target_pairs={{0,4},{1,5},{2,6},{3,7},{4,0},{5,1},{6,2},{7,3},{8,12},{9,13},{10,... | collective-permute-start | bytes 24584 | tf_op jit(solution)/shard_map/ppermute | solution.py:46
  40.3 1.1 %collective-permute-done.16.refs_3_ = f32[8,256]{1,0:T(8,128)S(1)} collective-permute-done((f32[8,256]{1,0:T(8,128)S(1)}, f32[8,256]{1,0:T(8,128)S(1)}, u32[]{:S(2)}, u32[]{:S(2)}) %collective-permute-start.16) | collective-permute-done | bytes 8224 | tf_op jit(solution)/shard_map/ppermute | solution.py:46
  42.1 0.7 %multiply_subtract_fusion = f32[256,256]{1,0:T(8,128)} fusion(f32[256,256]{1,0:T(8,128)S(1)} %get-tuple-element.38.image, f32[256,256]{1,0:T(8,128)S(1)} %copy-done.1, f32[256]{0:T(256)S(1)} %bitcast.12, f32[256]{0:T(256)S(1)} %bitcast.11), kind=kLoop, calls=%fused_computation | loop fusion | flops 196608 | bytes 788480 | tf_op jit(solution)/shard_map/sub | solution.py:358
  (37 shorter events, 2.9 us)
Async XLA Ops:
  0.0 7.4 %copy-start.2 = (f32[2,7,128,128]{3,2,1,0:T(8,128)S(1)}, f32[2,7,128,128]{3,2,1,0:T(8,128)}, u32[]{:S(2)}) copy-start(f32[2,7,128,128]{3,2,1,0:T(8,128)} %local.1) | copy-start | bytes 2752516
  1.1 14.4 %collective-permute-start.3 = (f32[392,256]{1,0:T(8,128)S(1)}, f32[392,256]{1,0:T(8,128)S(1)}, u32[]{:S(2)}, u32[]{:S(2)}) collective-permute-start(f32[392,256]{1,0:T(8,128)S(1)} %pack.2.packed.mine.refs_0_), channel_id=1, source_target_pairs={{0,4},{4,8},{8,12},{12,0},{1,5},{5,9},{9,13},{13,1},{2,6},{6,10},{... | collective-permute-start | bytes 1204232 | tf_op jit(solution)/shard_map/ppermute | solution.py:305
  4.3 3.2 %copy-start.1 = (f32[256,256]{1,0:T(8,128)S(1)}, f32[256,256]{1,0:T(8,128)}, u32[]{:S(2)}) copy-start(f32[256,256]{1,0:T(8,128)} %field.3) | copy-start | bytes 786436
  4.3 3.2 %copy-start.4 = (f32[256]{0:T(256)S(1)}, f32[256]{0:T(256)}, u32[]{:S(2)}) copy-start(f32[256]{0:T(256)} %param.8) | copy-start | bytes 3076
  5.9 1.6 %copy-start.3 = (s32[2,7]{1,0:T(2,128)S(1)}, s32[2,7]{1,0:T(2,128)}, u32[]{:S(2)}) copy-start(s32[2,7]{1,0:T(2,128)} %cols.1) | copy-start | bytes 172
  5.9 12.5 %collective-permute-start.4 = (f32[392,256]{1,0:T(8,128)S(1)}, f32[392,256]{1,0:T(8,128)S(1)}, u32[]{:S(2)}, u32[]{:S(2)}) collective-permute-start(f32[392,256]{1,0:T(8,128)S(1)} %pack.3), channel_id=1, source_target_pairs={{0,2},{2,0},{1,3},{3,1},{4,6},{6,4},{5,7},{7,5},{8,10},{10,8},{9,1... | collective-permute-start | bytes 1204232 | tf_op jit(solution)/shard_map/ppermute | solution.py:305
  7.4 3.0 %collective-permute-start = (f32[256,256]{1,0:T(8,128)S(1)}, f32[256,256]{1,0:T(8,128)S(1)}, u32[]{:S(2)}, u32[]{:S(2)}) collective-permute-start(f32[256,256]{1,0:T(8,128)S(1)} %copy-done.1), channel_id=1, source_target_pairs={{0,1},{1,0},{2,3},{3,2},{4,5},{5,4},{6,7},{7,6},{8,9},{9,8},{10,11... | collective-permute-start | bytes 786440 | tf_op jit(solution)/shard_map/ppermute | solution.py:307
  8.6 1.5 %collective-permute-start.1 = (f32[256,128]{1,0:T(8,128)S(1)}, f32[256,128]{1,0:T(8,128)S(1)}, u32[]{:S(2)}, u32[]{:S(2)}) collective-permute-start(f32[256,128]{1,0:T(8,128)S(1)} %get-tuple-element.29), channel_id=1, source_target_pairs={{0,1},{1,0},{2,3},{3,2},{4,5},{5,4},{6,7},{7,6},{8,9},{9,8},{10,11... | collective-permute-start | bytes 393224 | tf_op jit(solution)/shard_map/ppermute | solution.py:328
  9.1 1.3 %collective-permute-start.2 = (f32[256,128]{1,0:T(8,128)S(1)}, f32[256,128]{1,0:T(8,128)S(1)}, u32[]{:S(2)}, u32[]{:S(2)}) collective-permute-start(f32[256,128]{1,0:T(8,128)S(1)} %get-tuple-element.30), channel_id=1, source_target_pairs={{0,1},{1,0},{2,3},{3,2},{4,5},{5,4},{6,7},{7,6},{8,9},{9,8},{10,11... | collective-permute-start | bytes 393224 | tf_op jit(solution)/shard_map/ppermute | solution.py:328
  10.5 5.0 %copy-start = (f32[1,8,128,128]{3,2,1,0:T(8,128)S(1)}, f32[1,8,128,128]{3,2,1,0:T(8,128)}, u32[]{:S(2)}) copy-start(f32[1,8,128,128]{3,2,1,0:T(8,128)} %param.11) | copy-start | bytes 1572868
  16.1 7.0 %collective-permute-start.5 = (f32[264,128]{1,0:T(8,128)S(1)}, f32[264,128]{1,0:T(8,128)S(1)}, u32[]{:S(2)}, u32[]{:S(2)}) collective-permute-start(f32[264,128]{1,0:T(8,128)S(1)} %get-tuple-element.35), channel_id=1, source_target_pairs={{4,0},{8,4},{12,8},{0,12},{5,1},{9,5},{13,9},{1,13},{6,2},{10,6},{... | collective-permute-start | bytes 405512 | tf_op jit(solution)/shard_map/ppermute | solution.py:334
  17.9 11.5 %collective-permute-start.6 = (f32[264,128]{1,0:T(8,128)S(1)}, f32[264,128]{1,0:T(8,128)S(1)}, u32[]{:S(2)}, u32[]{:S(2)}) collective-permute-start(f32[264,128]{1,0:T(8,128)S(1)} %get-tuple-element.37), channel_id=1, source_target_pairs={{4,0},{8,4},{12,8},{0,12},{5,1},{9,5},{13,9},{1,13},{6,2},{10,6},{... | collective-permute-start | bytes 405512 | tf_op jit(solution)/shard_map/ppermute | solution.py:334
  18.7 12.8 %collective-permute-start.9 = (f32[256,256]{1,0:T(8,128)S(1)}, f32[256,256]{1,0:T(8,128)S(1)}, u32[]{:S(2)}, u32[]{:S(2)}) collective-permute-start(f32[256,256]{1,0:T(8,128)S(1)} %get-tuple-element.34.part), channel_id=1, source_target_pairs={{0,4},{4,8},{8,12},{12,0},{1,5},{5,9},{9,13},{13,1},{2,6},{6,10},{... | collective-permute-start | bytes 786440 | tf_op jit(solution)/shard_map/ppermute | solution.py:339
  23.2 8.3 %collective-permute-start.10 = (f32[264,128]{1,0:T(8,128)S(1)}, f32[264,128]{1,0:T(8,128)S(1)}, u32[]{:S(2)}, u32[]{:S(2)}) collective-permute-start(f32[264,128]{1,0:T(8,128)S(1)} %get-tuple-element.48), channel_id=1, source_target_pairs={{0,2},{2,0},{1,3},{3,1},{4,6},{6,4},{5,7},{7,5},{8,10},{10,8},{9,1... | collective-permute-start | bytes 405512 | tf_op jit(solution)/shard_map/ppermute | solution.py:350
  24.3 5.3 %collective-permute-start.7 = (f32[256,128]{1,0:T(8,128)S(1)}, f32[256,128]{1,0:T(8,128)S(1)}, u32[]{:S(2)}, u32[]{:S(2)}) collective-permute-start(f32[256,128]{1,0:T(8,128)S(1)} %get-tuple-element.36.half), channel_id=1, source_target_pairs={{0,1},{1,0},{2,3},{3,2},{4,5},{5,4},{6,7},{7,6},{8,9},{9,8},{10,11... | collective-permute-start | bytes 393224 | tf_op jit(solution)/shard_map/ppermute | solution.py:342
  29.5 1.4 %collective-permute-start.8 = (f32[256,128]{1,0:T(8,128)S(1)}, f32[256,128]{1,0:T(8,128)S(1)}, u32[]{:S(2)}, u32[]{:S(2)}) collective-permute-start(f32[256,128]{1,0:T(8,128)S(1)} %get-tuple-element.40), channel_id=1, source_target_pairs={{0,1},{1,0},{2,3},{3,2},{4,5},{5,4},{6,7},{7,6},{8,9},{9,8},{10,11... | collective-permute-start | bytes 393224 | tf_op jit(solution)/shard_map/ppermute | solution.py:342
  32.1 3.1 %collective-permute-start.13 = (f32[8,256]{1,0:T(8,128)S(1)}, f32[8,256]{1,0:T(8,128)S(1)}, u32[]{:S(2)}, u32[]{:S(2)}) collective-permute-start(f32[8,256]{1,0:T(8,128)S(1)} %far.1.refs_0_), channel_id=1, source_target_pairs={{0,3},{1,2},{2,1},{3,0},{4,7},{5,6},{6,5},{7,4},{8,11},{9,10},{10,... | collective-permute-start | bytes 24584 | tf_op jit(solution)/shard_map/ppermute | solution.py:46
  32.1 3.7 %collective-permute-start.12 = (f32[8,256]{1,0:T(8,128)S(1)}, f32[8,256]{1,0:T(8,128)S(1)}, u32[]{:S(2)}, u32[]{:S(2)}) collective-permute-start(f32[8,256]{1,0:T(8,128)S(1)} %far.1.refs_0_), channel_id=1, source_target_pairs={{0,2},{1,3},{2,0},{3,1},{4,6},{5,7},{6,4},{7,5},{8,10},{9,11},{10,... | collective-permute-start | bytes 24584 | tf_op jit(solution)/shard_map/ppermute | solution.py:46
  33.9 1.9 %collective-permute-start.11 = (f32[8,256]{1,0:T(8,128)S(1)}, f32[8,256]{1,0:T(8,128)S(1)}, u32[]{:S(2)}, u32[]{:S(2)}) collective-permute-start(f32[8,256]{1,0:T(8,128)S(1)} %far.1.refs_0_), channel_id=1, source_target_pairs={{0,1},{1,0},{2,3},{3,2},{4,5},{5,4},{6,7},{7,6},{8,9},{9,8},{10,11... | collective-permute-start | bytes 24584 | tf_op jit(solution)/shard_map/ppermute | solution.py:46
  35.9 5.5 %collective-permute-start.16 = (f32[8,256]{1,0:T(8,128)S(1)}, f32[8,256]{1,0:T(8,128)S(1)}, u32[]{:S(2)}, u32[]{:S(2)}) collective-permute-start(f32[8,256]{1,0:T(8,128)S(1)} %merge.2.refs_0_), channel_id=1, source_target_pairs={{0,12},{1,13},{2,14},{3,15},{4,8},{5,9},{6,10},{7,11},{8,4},{9,5},... | collective-permute-start | bytes 24584 | tf_op jit(solution)/shard_map/ppermute | solution.py:46
  37.3 4.5 %collective-permute-start.15 = (f32[8,256]{1,0:T(8,128)S(1)}, f32[8,256]{1,0:T(8,128)S(1)}, u32[]{:S(2)}, u32[]{:S(2)}) collective-permute-start(f32[8,256]{1,0:T(8,128)S(1)} %merge.2.refs_0_), channel_id=1, source_target_pairs={{0,8},{1,9},{2,10},{3,11},{4,12},{5,13},{6,14},{7,15},{8,0},{9,1},... | collective-permute-start | bytes 24584 | tf_op jit(solution)/shard_map/ppermute | solution.py:46
  37.3 4.6 %collective-permute-start.14 = (f32[8,256]{1,0:T(8,128)S(1)}, f32[8,256]{1,0:T(8,128)S(1)}, u32[]{:S(2)}, u32[]{:S(2)}) collective-permute-start(f32[8,256]{1,0:T(8,128)S(1)} %merge.2.refs_0_), channel_id=1, source_target_pairs={{0,4},{1,5},{2,6},{3,7},{4,0},{5,1},{6,2},{7,3},{8,12},{9,13},{10,... | collective-permute-start | bytes 24584 | tf_op jit(solution)/shard_map/ppermute | solution.py:46

commit v16 on v15

--- a/solution.py
+++ b/solution.py
@@ -71,16 +71,14 @@
 
 def pack_kernel(gives, *refs):
     marks, refs = (refs[0], refs[1:]) if gives != [1] else (None, refs)
-    field, border, send, rows, toward, *pays, sems, table, table_sems = refs
-    width = field.shape[0]
+    border, send, rows, toward, *pays, sems, table, table_sems = refs
     bs = border.shape[1]
     tables = [pltpu.make_async_copy(ref, table.at[n], table_sems.at[n]) for n, ref in enumerate((rows, send, toward))]
     copies = []
     for n, (give, pay) in enumerate(zip(gives, pays)):
         give = marks[0] if give is None else give
-        copies.append(pltpu.make_async_copy(field, pay.at[pl.ds(0, width), :], sems.at[n, SIDE]))
         for s in range(SIDE):
-            block = pay.at[pl.ds(width, bs), pl.ds(s * bs, bs)]
+            block = pay.at[pl.ds(0, bs), pl.ds(s * bs, bs)]
             copies.append(pltpu.make_async_copy(border.at[give * SIDE + s], block, sems.at[n, s]))
     for copy in tables + copies:
         copy.start()
@@ -89,7 +87,7 @@
     count = table.shape[2]
     for pay in pays:
         for n in range(3):
-            pay[pl.ds(pay.shape[0] - TAIL + n, 1), pl.ds(0, count)] = table[n].astype(F32)
+            pay[pl.ds(bs + n, 1), pl.ds(0, count)] = table[n].astype(F32)
     for copy in copies:
         copy.wait()
 
@@ -135,8 +133,7 @@
 
     blocks = [[0.0] * (width // bs) for _ in range(width // bs)]
     for s in range(SIDE):
-        beside = pay.shape[1] > bs
-        turned = (pay[pl.ds(width, bs), pl.ds(s * bs, bs)] if beside else pay[pl.ds(width + s * bs, bs), :]).T
+        turned = pay[pl.ds(0, bs), pl.ds(s * bs, bs)].T
         pairs = [
             (pick(lambda t: border[t * SIDE + s]), pick(lambda t: number(mine, 0, t)), pick(lambda t: number(pay, 1, t))),
             (turned, pick(lambda t: number(mine, 1, t ^ 1)), pick(lambda t: number(pay, 0, t ^ 1))),
@@ -148,20 +145,22 @@
     return jnp.concatenate([jnp.concatenate(line, axis=1) for line in blocks], axis=0)
 
 
-def base_kernel(mine, own, pair, mate, low, high, image, coup):
-    width = mate.shape[0]
+def base_kernel(field, own, pair, mate, low, high, image, coup):
     coup[...] = pair[...] + jnp.concatenate([low[...].T, high[...].T], axis=0)
-    image[...] = dot(own[...], mine[pl.ds(0, width), :]) + dot(coup[...], mate[...])
-
-
-def left_kernel(mine, part, border, pay, image, once, coup, back, out, other):
-    width = part.shape[0]
+    image[...] = dot(own[...], field[...]) + dot(coup[...], mate[...])
+
+
+def back_kernel(mine, field, border, pay, coup, back, out, other):
+    width = field.shape[0]
     toward = mine[pl.ds(mine.shape[0] - TAIL + 2, 1), pl.ds(0, 1)]
     coup[...] = edge(0, width, mine, pay, border)
-    back[...] = dot(coup[...].T, mine[pl.ds(0, width), :])
+    back[...] = dot(coup[...].T, field[...])
     out[pl.ds(0, width), :] = columns(back, toward, True)
     other[pl.ds(0, width), :] = columns(back, toward, False)
-    term = dot(coup[...], pay[pl.ds(0, width), :])
+
+
+def left_kernel(part, coup, there, image, once):
+    term = dot(coup[...], there[...])
     image[...] = part[...] + term
     once[...] = part[...] + 2.0 * term
 
@@ -173,11 +172,11 @@
     return jnp.where(toward == 3.0, first, 1.0 - first)
 
 
-def gy_kernel(take, weight, mine, part, single, border, pay, image, once, coup):
+def gy_kernel(take, weight, mine, part, single, border, pay, there, image, once, coup):
     width = coup.shape[0]
     toward = mine[pl.ds(mine.shape[0] - TAIL + 2, 1), pl.ds(0, 1)]
     coup[...] = edge(toward if take is None else take, width, mine, pay, border)
-    term = dot(coup[...], pay[pl.ds(0, width), :])
+    term = dot(coup[...], there[...])
     image[...] = part[...] + term
     scale = weight * turn(mine, width) if take is None else weight
     once[...] = single[...] + scale * term
@@ -208,7 +207,7 @@
     image[...] = joined(toward, half[...], other[...])
 
 
-def near_kernel(mine, field, image, once, mate, mate_out, mate_other, own, coup, pay, back, part, lift, state):
+def near_kernel(mine, field, image, once, mate, mate_out, mate_other, own, coup, there, back, part, lift, state):
     b = field[...]
     toward = mine[pl.ds(mine.shape[0] - TAIL + 2, 1), pl.ds(0, 1)]
     mate_w = joined(toward, mate_out[...], mate_other[...])
@@ -216,7 +215,7 @@
     c = jnp.where(norm > 0.0, col_sum(b, image[...]) / jnp.where(norm > 0.0, norm, 1.0), 0.0)
     g = image[...] - c * b
     part[...] = dot(own[...], g) + dot(coup[...], mate_w - c * mate[...])
-    lift[...] = back[...] - c * pay[pl.ds(0, b.shape[0]), :]
+    lift[...] = back[...] - c * there[...]
     rows = [(0, norm), (1, c), (2, col_sum(g, g)), (4, -col_sum(g, once[...])), (5, col_sum(b, once[...]))]
     state[...] = stack_rows(rows, state.shape)
 
@@ -228,15 +227,15 @@
     c = near[1:2, :]
     acc = part[...] + 2.0 * dot(coup[...], left[...] + lift[...])
     if sides:
-        mine, coup_gy, pay, side = sides
+        mine, coup_gy, there, side = sides
         if take is None:
             toward = mine[pl.ds(mine.shape[0] - TAIL + 2, 1), pl.ds(0, 1)]
             middle = b.shape[1] // 2
-            shift = c * pay[pl.ds(0, width), :]
+            shift = c * there[...]
             term = dot(coup_gy[...], side[pl.ds(0, width), :] - jnp.where(toward == 3.0, shift[:, :middle], shift[:, middle:]))
             acc += 2.0 * turn(mine, width) * jnp.concatenate([term, term], axis=1)
         else:
-            acc += 2.0 * dot(coup_gy[...], side[...] - c * pay[pl.ds(0, width), :])
+            acc += 2.0 * dot(coup_gy[...], side[...] - c * there[...])
     state[...] = near[...] + stack_rows([(3, col_sum(image[...] - c * b, acc)), (4, -col_sum(b, acc))], state.shape)
 
 
@@ -282,7 +281,7 @@
     def smem(n):
         return [pl.BlockSpec(memory_space=pltpu.SMEM)] * n
 
-    full, half, longer = (width + bs + TAIL, ncols), (width, ncols // 2), (width + EXTRA, ncols // 2)
+    full, half, longer = (bs + TAIL, ncols), (width, ncols // 2), (width + EXTRA, ncols // 2)
 
     def pack(gives):
         count = len(gives)
@@ -290,20 +289,21 @@
         return pl.pallas_call(
             partial(pack_kernel, gives),
             name="pack",
-            in_specs=smem(len(tables)) + [pl.BlockSpec(memory_space=pl.ANY)] * 5,
+            in_specs=smem(len(tables)) + [pl.BlockSpec(memory_space=pl.ANY)] * 4,
             out_specs=[vmem()] * count,
             out_shape=[pltpu.VMEM(full, F32)] * count,
             scratch_shapes=[
-                pltpu.SemaphoreType.DMA((count, SIDE + 1)),
+                pltpu.SemaphoreType.DMA((count, SIDE)),
                 pltpu.VMEM((3, 1, 4 * SIDE), jnp.int32),
                 pltpu.SemaphoreType.DMA((3,)),
             ],
             compiler_params=pltpu.CompilerParams(vmem_limit_bytes=LIMIT),
-        )(*tables, *[pltpu.with_memory_space_constraint(a, pltpu.HBM) for a in (right_side, border, border_send, border_rows)], toward)
+        )(*tables, *[pltpu.with_memory_space_constraint(a, pltpu.HBM) for a in (border, border_send, border_rows)], toward)
 
     packed = [*pack(gives[:1]), *(pack(gives[1:]) if sides else [])]
     pays = [lax.ppermute(pay, axis, perm) for pay, (axis, perm) in zip(packed, sends)]
     mine = packed[0]
+    fields = [lax.ppermute(right_side, axis, perm) for axis, perm in sends]
     mate = lax.ppermute(right_side, "nd", swap)
 
     def tabled(kernel, name, tables, shapes, flops=None):
@@ -327,27 +327,26 @@
     )
     mate_pair = [lax.ppermute(piece, "nd", swap) for piece in pieces]
 
-    part, coup = call(base_kernel, "base", [field, square])(mine, own, pair, mate, *mate_pair)
-    part, once, left_coup, back, *to_left = call(left_kernel, "left", [field, field, square, field] + [longer] * 2)(
-        mine, part, border, pays[0]
-    )
+    part, coup = call(base_kernel, "base", [field, square])(right_side, own, pair, mate, *mate_pair)
+    left_coup, back, *to_left = call(back_kernel, "back", [square, field] + [longer] * 2)(mine, right_side, border, pays[0])
     from_right = [lax.ppermute(piece, "gx", left) for piece in to_left]
+    part, once = call(left_kernel, "left", [field] * 2)(part, left_coup, fields[0])
     side_coup = []
-    for (_, take, weight), pay in zip(sides, pays[1:]):
-        part, once, block = call(partial(gy_kernel, take, weight), "gy", [field, field, square])(mine, part, once, border, pay)
+    for (_, take, weight), pay, there in zip(sides, pays[1:], fields[1:]):
+        part, once, block = call(partial(gy_kernel, take, weight), "gy", [field, field, square])(mine, part, once, border, pay, there)
         side_coup.append(block)
     left_w = lax.ppermute(part, "gx", right)
     half_w, across = call(right_kernel, "right", [half, longer])(mine, part, from_right[0])
     image, other_w = call(whole_kernel, "whole", [field, half])(mine, part, half_w, from_right[1])
     mate_w = [lax.ppermute(w, "nd", swap) for w in (half_w, other_w)]
     part, lift, state = call(near_kernel, "near", [field, field, (TAIL, ncols)])(
-        mine, right_side, image, once, mate, *mate_w, own, coup, pays[0], back
+        mine, right_side, image, once, mate, *mate_w, own, coup, fields[0], back
     )
     far = []
     take = None
     if sides:
         perm, take, _ = sides[0]
-        far = [mine, side_coup[0], pays[1], lax.ppermute(across if take is None else image, "gy", perm)]
+        far = [mine, side_coup[0], fields[1], lax.ppermute(across if take is None else image, "gy", perm)]
     (state,) = call(partial(far_kernel, take), "far", [(TAIL, ncols)])(
         right_side, image, part, state, lift, left_coup, left_w, *far
     )

time: 42.9 us -> 43.3 us (level)
  waiting for transfers between devices: 18.6 us -> 13.8 us
  starting transfers between devices: 16.6 us -> 20 us
  local copies, waits for them, and re-layouts: 0.02 us -> 1.87 us
    ppermute x2, waiting for transfers between devices: 7.91 us -> 0.01 us  [shards(): from_right = [lax.ppermute(piece, 'gx', left) for piece in to_left]]
    ppermute x0 -> x2, starting transfers between devices: none -> 3.07 us  [shards(): fields = [lax.ppermute(right_side, axis, perm) for axis, perm in sends]]
    ppermute x2, waiting for transfers between devices: 4.61 us -> 1.94 us  [shards(): lax.ppermute(pay, axis, perm)]
    ppermute x1, waiting for transfers between devices: 0.01 us -> 2.18 us  [shards(): left_w = lax.ppermute(part, 'gx', right)]
    ppermute x6, waiting for transfers between devices: 3.5 us -> 5.64 us  [join(): lax.ppermute(state, AXES, [(i, i ^ m) for i in range(count)])]
    unnamed x10, local copies, waits for them, and re-layouts: 0.02 us -> 1.87 us
    ppermute x1, waiting for transfers between devices: 0.01 us -> 1.28 us  [shards(): lax.ppermute(across if take is None else image, 'gy', perm)]
    ppermute x2, starting transfers between devices: 4.63 us -> 3.68 us  [shards(): lax.ppermute(pay, axis, perm)]
  transfers between devices with their start and end apart: 17 -> 19, of which waited for: 11 -> 11; matrix products, arithmetic and copies ran while one was open for 0% -> 0% of each run, Pallas kernels for 11% -> 11%
where the time goes in v16:
time: 43.3 us; the launch traced here: 43 us
  starting transfers between devices  20 us (46%)
  waiting for transfers between devices  13.8 us (32%)
  Pallas kernels  6.39 us (15%)
  local copies, waits for them, and re-layouts  1.87 us (4%)
  other arithmetic  0.85 us (2%)
    ppermute x6, starting transfers between devices, join(): lax.ppermute(state, AXES, [(i, i ^ m) for i in range(count)])  6.39 us
    ppermute x6, waiting for transfers between devices, join(): lax.ppermute(state, AXES, [(i, i ^ m) for i in range(count)])  5.64 us
    ppermute x2, starting transfers between devices, shards(): lax.ppermute(pay, axis, perm)  3.68 us
    ppermute x2, starting transfers between devices, shards(): fields = [lax.ppermute(right_side, axis, perm) for axis, perm in sends]  3.07 us
    pallas_call x10, Pallas kernels, run(): pl.pallas_call(kernel, name=name, in_specs=[vmem()] * len(args), out_spec...  2.86 us
    ppermute x2, starting transfers between devices, shards(): from_right = [lax.ppermute(piece, 'gx', left) for piece in to_left]  2.5 us
    pallas_call x2, Pallas kernels, pack(): pl.pallas_call(partial(pack_kernel, gives), name='pack', in_specs=smem(le...  2.44 us
    ppermute x1, waiting for transfers between devices, shards(): left_w = lax.ppermute(part, 'gx', right)  2.18 us
  transfers between devices with their start and end apart: 19, of which 11 were waited for; matrix products, arithmetic and copies ran while one was open for 0% of the time, Pallas kernels for 11%

profile of v16, /device:TPU:0, one launch (start us, length us, event | category | flops | bytes accessed | tf_op | source)
XLA Modules:
  0.0 43.0 jit_solution(7161305521592176183)
XLA Ops:
  0.0 0.9 %pack.2.packed.mine.refs_0_ = f32[136,256]{1,0:T(8,128)S(1)} custom-call(f32[8,128,128]{2,1,0:T(8,128)} %bitcast.6, s32[1,8]{1,0:T(1,128)} %refs_2_.3, s32[1,8]{1,0:T(1,128)} %refs_3_.1, s32[1,8]{1,0:T(1,128)S(1)} %broadcast_in_dim.3.refs_3_.refs_4_), custom_call_target="tpu_custom_call" | custom-call | tf_op jit(solution)/shard_map/pack/pallas_call | solution.py:289
  1.0 3.1 %collective-permute-start.3 = (f32[136,256]{1,0:T(8,128)S(1)}, f32[136,256]{1,0:T(8,128)S(1)}, u32[]{:S(2)}, u32[]{:S(2)}) collective-permute-start(f32[136,256]{1,0:T(8,128)S(1)} %pack.2.packed.mine.refs_0_), channel_id=1, source_target_pairs={{0,4},{4,8},{8,12},{12,0},{1,5},{5,9},{9,13},{13,1},{2,6},{6,10},{... | collective-permute-start | bytes 417800 | tf_op jit(solution)/shard_map/ppermute | solution.py:304
  4.8 1.2 %copy-done.2 = f32[2,7,128,128]{3,2,1,0:T(8,128)S(1)} copy-done((f32[2,7,128,128]{3,2,1,0:T(8,128)S(1)}, f32[2,7,128,128]{3,2,1,0:T(8,128)}, u32[]{:S(2)}) %copy-start.2) | copy-done | bytes 917528
  6.0 1.1 %prep.1 = (f32[256,256]{1,0:T(8,128)S(1)}, f32[256,256]{1,0:T(8,128)S(1)}, f32[256,128]{1,0:T(8,128)S(1)}, f32[256,128]{1,0:T(8,128)S(1)}) custom-call(s32[2,7]{1,0:T(2,128)S(1)} %copy-done.3, s32[2]{0:T(128)S(1)} %pad_add_fusion.marks.refs_0_, f32[1,256]{1,0:T(1,128)S(1)} %bitcast.10, f32[2,7,128,128]{3,2,1,0:T(8,128)S(1)} %copy-done.2, ...), custom_call_target="tpu_custom_call" | custom-call | flops 16777216 | bytes 1048576 | tf_op jit(solution)/shard_map/prep/pallas_call | solution.py:312
  7.7 1.6 %collective-permute-start.4 = (f32[256,256]{1,0:T(8,128)S(1)}, f32[256,256]{1,0:T(8,128)S(1)}, u32[]{:S(2)}, u32[]{:S(2)}) collective-permute-start(f32[256,256]{1,0:T(8,128)S(1)} %copy-done.1), channel_id=1, source_target_pairs={{0,4},{4,8},{8,12},{12,0},{1,5},{5,9},{9,13},{13,1},{2,6},{6,10},{... | collective-permute-start | bytes 786440 | tf_op jit(solution)/shard_map/ppermute | solution.py:306
  9.2 1.5 %collective-permute-start.6 = (f32[256,256]{1,0:T(8,128)S(1)}, f32[256,256]{1,0:T(8,128)S(1)}, u32[]{:S(2)}, u32[]{:S(2)}) collective-permute-start(f32[256,256]{1,0:T(8,128)S(1)} %copy-done.1), channel_id=1, source_target_pairs={{0,2},{2,0},{1,3},{3,1},{4,6},{6,4},{5,7},{7,5},{8,10},{10,8},{9,1... | collective-permute-start | bytes 786440 | tf_op jit(solution)/shard_map/ppermute | solution.py:306
  10.7 1.5 %pack.3 = f32[136,256]{1,0:T(8,128)S(1)} custom-call(s32[2]{0:T(128)S(1)} %pad_add_fusion.marks.refs_0_, f32[8,128,128]{2,1,0:T(8,128)} %bitcast.7, s32[1,8]{1,0:T(1,128)} %refs_2_.3, s32[1,8]{1,0:T(1,128)} %refs_3_.1, s32[1,8]{1,0:T(1,128)S(1)} %broadcast_in_dim.3.refs_3_.refs_4_), custom_call_target="tpu_custom_call" | custom-call | tf_op jit(solution)/shard_map/pack/pallas_call | solution.py:289
  13.3 0.9 %collective-permute-done.2.high = f32[256,128]{1,0:T(8,128)S(1)} collective-permute-done((f32[256,128]{1,0:T(8,128)S(1)}, f32[256,128]{1,0:T(8,128)S(1)}, u32[]{:S(2)}, u32[]{:S(2)}) %collective-permute-start.2) | collective-permute-done | bytes 131104 | tf_op jit(solution)/shard_map/ppermute | solution.py:328
  14.2 2.2 %collective-permute-start.7 = (f32[264,128]{1,0:T(8,128)S(1)}, f32[264,128]{1,0:T(8,128)S(1)}, u32[]{:S(2)}, u32[]{:S(2)}) collective-permute-start(f32[264,128]{1,0:T(8,128)S(1)} %get-tuple-element.36), channel_id=1, source_target_pairs={{4,0},{8,4},{12,8},{0,12},{5,1},{9,5},{13,9},{1,13},{6,2},{10,6},{... | collective-permute-start | bytes 405512 | tf_op jit(solution)/shard_map/ppermute | solution.py:332
  17.1 0.9 %collective-permute-done.4.there = f32[256,256]{1,0:T(8,128)S(1)} collective-permute-done((f32[256,256]{1,0:T(8,128)S(1)}, f32[256,256]{1,0:T(8,128)S(1)}, u32[]{:S(2)}, u32[]{:S(2)}) %collective-permute-start.4) | collective-permute-done | bytes 262176 | tf_op jit(solution)/shard_map/ppermute | solution.py:306
  18.3 1.9 %collective-permute-done.5.pay = f32[136,256]{1,0:T(8,128)S(1)} collective-permute-done((f32[136,256]{1,0:T(8,128)S(1)}, f32[136,256]{1,0:T(8,128)S(1)}, u32[]{:S(2)}, u32[]{:S(2)}) %collective-permute-start.5) | collective-permute-done | bytes 139296 | tf_op jit(solution)/shard_map/ppermute | solution.py:304
  20.6 1.6 %collective-permute-start.11 = (f32[256,256]{1,0:T(8,128)S(1)}, f32[256,256]{1,0:T(8,128)S(1)}, u32[]{:S(2)}, u32[]{:S(2)}) collective-permute-start(f32[256,256]{1,0:T(8,128)S(1)} %get-tuple-element.35.part), channel_id=1, source_target_pairs={{0,4},{4,8},{8,12},{12,0},{1,5},{5,9},{9,13},{13,1},{2,6},{6,10},{... | collective-permute-start | bytes 786440 | tf_op jit(solution)/shard_map/ppermute | solution.py:338
  22.4 1.6 %collective-permute-start.12 = (f32[264,128]{1,0:T(8,128)S(1)}, f32[264,128]{1,0:T(8,128)S(1)}, u32[]{:S(2)}, u32[]{:S(2)}) collective-permute-start(f32[264,128]{1,0:T(8,128)S(1)} %get-tuple-element.48), channel_id=1, source_target_pairs={{0,2},{2,0},{1,3},{3,1},{4,6},{6,4},{5,7},{7,5},{8,10},{10,8},{9,1... | collective-permute-start | bytes 405512 | tf_op jit(solution)/shard_map/ppermute | solution.py:349
  24.6 0.7 %collective-permute-done.9.mate_out = f32[256,128]{1,0:T(8,128)S(1)} collective-permute-done((f32[256,128]{1,0:T(8,128)S(1)}, f32[256,128]{1,0:T(8,128)S(1)}, u32[]{:S(2)}, u32[]{:S(2)}) %collective-permute-start.9) | collective-permute-done | bytes 131104 | tf_op jit(solution)/shard_map/ppermute | solution.py:341
  26.2 1.3 %collective-permute-done.12.refs_3_ = f32[264,128]{1,0:T(8,128)S(1)} collective-permute-done((f32[264,128]{1,0:T(8,128)S(1)}, f32[264,128]{1,0:T(8,128)S(1)}, u32[]{:S(2)}, u32[]{:S(2)}) %collective-permute-start.12) | collective-permute-done | bytes 135200 | tf_op jit(solution)/shard_map/ppermute | solution.py:349
  27.4 2.2 %collective-permute-done.11.left = f32[256,256]{1,0:T(8,128)S(1)} collective-permute-done((f32[256,256]{1,0:T(8,128)S(1)}, f32[256,256]{1,0:T(8,128)S(1)}, u32[]{:S(2)}, u32[]{:S(2)}) %collective-permute-start.11) | collective-permute-done | bytes 262176 | tf_op jit(solution)/shard_map/ppermute | solution.py:338
  30.2 1.6 %collective-permute-start.14 = (f32[8,256]{1,0:T(8,128)S(1)}, f32[8,256]{1,0:T(8,128)S(1)}, u32[]{:S(2)}, u32[]{:S(2)}) collective-permute-start(f32[8,256]{1,0:T(8,128)S(1)} %far.1.refs_0_), channel_id=1, source_target_pairs={{0,2},{1,3},{2,0},{3,1},{4,6},{5,7},{6,4},{7,5},{8,10},{9,11},{10,... | collective-permute-start | bytes 24584 | tf_op jit(solution)/shard_map/ppermute | solution.py:46
  32.1 1.3 %collective-permute-done.15.refs_3_ = f32[8,256]{1,0:T(8,128)S(1)} collective-permute-done((f32[8,256]{1,0:T(8,128)S(1)}, f32[8,256]{1,0:T(8,128)S(1)}, u32[]{:S(2)}, u32[]{:S(2)}) %collective-permute-start.15) | collective-permute-done | bytes 8224 | tf_op jit(solution)/shard_map/ppermute | solution.py:46
  33.3 0.6 %collective-permute-done.14.refs_2_ = f32[8,256]{1,0:T(8,128)S(1)} collective-permute-done((f32[8,256]{1,0:T(8,128)S(1)}, f32[8,256]{1,0:T(8,128)S(1)}, u32[]{:S(2)}, u32[]{:S(2)}) %collective-permute-start.14) | collective-permute-done | bytes 8224 | tf_op jit(solution)/shard_map/ppermute | solution.py:46
  34.0 3.7 %collective-permute-start.18 = (f32[8,256]{1,0:T(8,128)S(1)}, f32[8,256]{1,0:T(8,128)S(1)}, u32[]{:S(2)}, u32[]{:S(2)}) collective-permute-start(f32[8,256]{1,0:T(8,128)S(1)} %merge.2.refs_0_), channel_id=1, source_target_pairs={{0,12},{1,13},{2,14},{3,15},{4,8},{5,9},{6,10},{7,11},{8,4},{9,5},... | collective-permute-start | bytes 24584 | tf_op jit(solution)/shard_map/ppermute | solution.py:46
  37.7 0.8 %collective-permute-start.16 = (f32[8,256]{1,0:T(8,128)S(1)}, f32[8,256]{1,0:T(8,128)S(1)}, u32[]{:S(2)}, u32[]{:S(2)}) collective-permute-start(f32[8,256]{1,0:T(8,128)S(1)} %merge.2.refs_0_), channel_id=1, source_target_pairs={{0,4},{1,5},{2,6},{3,7},{4,0},{5,1},{6,2},{7,3},{8,12},{9,13},{10,... | collective-permute-start | bytes 24584 | tf_op jit(solution)/shard_map/ppermute | solution.py:46
  38.4 1.1 %collective-permute-done.18.refs_3_ = f32[8,256]{1,0:T(8,128)S(1)} collective-permute-done((f32[8,256]{1,0:T(8,128)S(1)}, f32[8,256]{1,0:T(8,128)S(1)}, u32[]{:S(2)}, u32[]{:S(2)}) %collective-permute-start.18) | collective-permute-done | bytes 8224 | tf_op jit(solution)/shard_map/ppermute | solution.py:46
  39.5 2.7 %collective-permute-done.17.refs_2_ = f32[8,256]{1,0:T(8,128)S(1)} collective-permute-done((f32[8,256]{1,0:T(8,128)S(1)}, f32[8,256]{1,0:T(8,128)S(1)}, u32[]{:S(2)}, u32[]{:S(2)}) %collective-permute-start.17) | collective-permute-done | bytes 8224 | tf_op jit(solution)/shard_map/ppermute | solution.py:46
  42.3 0.7 %multiply_subtract_fusion = f32[256,256]{1,0:T(8,128)} fusion(f32[256,256]{1,0:T(8,128)S(1)} %get-tuple-element.39.image, f32[256,256]{1,0:T(8,128)S(1)} %copy-done.1, f32[256]{0:T(256)S(1)} %bitcast.12, f32[256]{0:T(256)S(1)} %bitcast.11), kind=kLoop, calls=%fused_computation | loop fusion | flops 196608 | bytes 788480 | tf_op jit(solution)/shard_map/sub | solution.py:357
  (42 shorter events, 6.4 us)
Async XLA Ops:
  1.0 11.9 %collective-permute-start.3 = (f32[136,256]{1,0:T(8,128)S(1)}, f32[136,256]{1,0:T(8,128)S(1)}, u32[]{:S(2)}, u32[]{:S(2)}) collective-permute-start(f32[136,256]{1,0:T(8,128)S(1)} %pack.2.packed.mine.refs_0_), channel_id=1, source_target_pairs={{0,4},{4,8},{8,12},{12,0},{1,5},{5,9},{9,13},{13,1},{2,6},{6,10},{... | collective-permute-start | bytes 417800 | tf_op jit(solution)/shard_map/ppermute | solution.py:304
  4.0 0.7 %copy-start.4 = (f32[256]{0:T(256)S(1)}, f32[256]{0:T(256)}, u32[]{:S(2)}) copy-start(f32[256]{0:T(256)} %param.8) | copy-start | bytes 3076
  4.1 0.7 %copy-start.3 = (s32[2,7]{1,0:T(2,128)S(1)}, s32[2,7]{1,0:T(2,128)}, u32[]{:S(2)}) copy-start(s32[2,7]{1,0:T(2,128)} %cols.1) | copy-start | bytes 172
  4.8 1.2 %copy-start.2 = (f32[2,7,128,128]{3,2,1,0:T(8,128)S(1)}, f32[2,7,128,128]{3,2,1,0:T(8,128)}, u32[]{:S(2)}) copy-start(f32[2,7,128,128]{3,2,1,0:T(8,128)} %local.1) | copy-start | bytes 2752516
  6.0 1.2 %copy-start.1 = (f32[256,256]{1,0:T(8,128)S(1)}, f32[256,256]{1,0:T(8,128)}, u32[]{:S(2)}) copy-start(f32[256,256]{1,0:T(8,128)} %field.7) | copy-start | bytes 786436
  7.1 5.8 %copy-start = (f32[1,8,128,128]{3,2,1,0:T(8,128)S(1)}, f32[1,8,128,128]{3,2,1,0:T(8,128)}, u32[]{:S(2)}) copy-start(f32[1,8,128,128]{3,2,1,0:T(8,128)} %param.11) | copy-start | bytes 1572868
  7.1 5.1 %collective-permute-start.1 = (f32[256,128]{1,0:T(8,128)S(1)}, f32[256,128]{1,0:T(8,128)S(1)}, u32[]{:S(2)}, u32[]{:S(2)}) collective-permute-start(f32[256,128]{1,0:T(8,128)S(1)} %get-tuple-element.29), channel_id=1, source_target_pairs={{0,1},{1,0},{2,3},{3,2},{4,5},{5,4},{6,7},{7,6},{8,9},{9,8},{10,11... | collective-permute-start | bytes 393224 | tf_op jit(solution)/shard_map/ppermute | solution.py:328
  7.2 9.3 %collective-permute-start = (f32[256,256]{1,0:T(8,128)S(1)}, f32[256,256]{1,0:T(8,128)S(1)}, u32[]{:S(2)}, u32[]{:S(2)}) collective-permute-start(f32[256,256]{1,0:T(8,128)S(1)} %copy-done.1), channel_id=1, source_target_pairs={{0,1},{1,0},{2,3},{3,2},{4,5},{5,4},{6,7},{7,6},{8,9},{9,8},{10,11... | collective-permute-start | bytes 786440 | tf_op jit(solution)/shard_map/ppermute | solution.py:307
  7.7 10.3 %collective-permute-start.4 = (f32[256,256]{1,0:T(8,128)S(1)}, f32[256,256]{1,0:T(8,128)S(1)}, u32[]{:S(2)}, u32[]{:S(2)}) collective-permute-start(f32[256,256]{1,0:T(8,128)S(1)} %copy-done.1), channel_id=1, source_target_pairs={{0,4},{4,8},{8,12},{12,0},{1,5},{5,9},{9,13},{13,1},{2,6},{6,10},{... | collective-permute-start | bytes 786440 | tf_op jit(solution)/shard_map/ppermute | solution.py:306
  9.2 11.0 %collective-permute-start.6 = (f32[256,256]{1,0:T(8,128)S(1)}, f32[256,256]{1,0:T(8,128)S(1)}, u32[]{:S(2)}, u32[]{:S(2)}) collective-permute-start(f32[256,256]{1,0:T(8,128)S(1)} %copy-done.1), channel_id=1, source_target_pairs={{0,2},{2,0},{1,3},{3,1},{4,6},{6,4},{5,7},{7,5},{8,10},{10,8},{9,1... | collective-permute-start | bytes 786440 | tf_op jit(solution)/shard_map/ppermute | solution.py:306
  12.2 8.0 %collective-permute-start.5 = (f32[136,256]{1,0:T(8,128)S(1)}, f32[136,256]{1,0:T(8,128)S(1)}, u32[]{:S(2)}, u32[]{:S(2)}) collective-permute-start(f32[136,256]{1,0:T(8,128)S(1)} %pack.3), channel_id=1, source_target_pairs={{0,2},{2,0},{1,3},{3,1},{4,6},{6,4},{5,7},{7,5},{8,10},{10,8},{9,1... | collective-permute-start | bytes 417800 | tf_op jit(solution)/shard_map/ppermute | solution.py:304
  12.8 1.3 %collective-permute-start.2 = (f32[256,128]{1,0:T(8,128)S(1)}, f32[256,128]{1,0:T(8,128)S(1)}, u32[]{:S(2)}, u32[]{:S(2)}) collective-permute-start(f32[256,128]{1,0:T(8,128)S(1)} %get-tuple-element.30), channel_id=1, source_target_pairs={{0,1},{1,0},{2,3},{3,2},{4,5},{5,4},{6,7},{7,6},{8,9},{9,8},{10,11... | collective-permute-start | bytes 393224 | tf_op jit(solution)/shard_map/ppermute | solution.py:328
  14.2 8.1 %collective-permute-start.7 = (f32[264,128]{1,0:T(8,128)S(1)}, f32[264,128]{1,0:T(8,128)S(1)}, u32[]{:S(2)}, u32[]{:S(2)}) collective-permute-start(f32[264,128]{1,0:T(8,128)S(1)} %get-tuple-element.36), channel_id=1, source_target_pairs={{4,0},{8,4},{12,8},{0,12},{5,1},{9,5},{13,9},{1,13},{6,2},{10,6},{... | collective-permute-start | bytes 405512 | tf_op jit(solution)/shard_map/ppermute | solution.py:332
  16.4 7.5 %collective-permute-start.8 = (f32[264,128]{1,0:T(8,128)S(1)}, f32[264,128]{1,0:T(8,128)S(1)}, u32[]{:S(2)}, u32[]{:S(2)}) collective-permute-start(f32[264,128]{1,0:T(8,128)S(1)} %get-tuple-element.38), channel_id=1, source_target_pairs={{4,0},{8,4},{12,8},{0,12},{5,1},{9,5},{13,9},{1,13},{6,2},{10,6},{... | collective-permute-start | bytes 405512 | tf_op jit(solution)/shard_map/ppermute | solution.py:332
  20.6 9.0 %collective-permute-start.11 = (f32[256,256]{1,0:T(8,128)S(1)}, f32[256,256]{1,0:T(8,128)S(1)}, u32[]{:S(2)}, u32[]{:S(2)}) collective-permute-start(f32[256,256]{1,0:T(8,128)S(1)} %get-tuple-element.35.part), channel_id=1, source_target_pairs={{0,4},{4,8},{8,12},{12,0},{1,5},{5,9},{9,13},{13,1},{2,6},{6,10},{... | collective-permute-start | bytes 786440 | tf_op jit(solution)/shard_map/ppermute | solution.py:338
  22.4 5.1 %collective-permute-start.12 = (f32[264,128]{1,0:T(8,128)S(1)}, f32[264,128]{1,0:T(8,128)S(1)}, u32[]{:S(2)}, u32[]{:S(2)}) collective-permute-start(f32[264,128]{1,0:T(8,128)S(1)} %get-tuple-element.48), channel_id=1, source_target_pairs={{0,2},{2,0},{1,3},{3,1},{4,6},{6,4},{5,7},{7,5},{8,10},{10,8},{9,1... | collective-permute-start | bytes 405512 | tf_op jit(solution)/shard_map/ppermute | solution.py:349
  23.9 1.3 %collective-permute-start.9 = (f32[256,128]{1,0:T(8,128)S(1)}, f32[256,128]{1,0:T(8,128)S(1)}, u32[]{:S(2)}, u32[]{:S(2)}) collective-permute-start(f32[256,128]{1,0:T(8,128)S(1)} %get-tuple-element.37.half), channel_id=1, source_target_pairs={{0,1},{1,0},{2,3},{3,2},{4,5},{5,4},{6,7},{7,6},{8,9},{9,8},{10,11... | collective-permute-start | bytes 393224 | tf_op jit(solution)/shard_map/ppermute | solution.py:341
  24.0 1.6 %collective-permute-start.10 = (f32[256,128]{1,0:T(8,128)S(1)}, f32[256,128]{1,0:T(8,128)S(1)}, u32[]{:S(2)}, u32[]{:S(2)}) collective-permute-start(f32[256,128]{1,0:T(8,128)S(1)} %get-tuple-element.41), channel_id=1, source_target_pairs={{0,1},{1,0},{2,3},{3,2},{4,5},{5,4},{6,7},{7,6},{8,9},{9,8},{10,11... | collective-permute-start | bytes 393224 | tf_op jit(solution)/shard_map/ppermute | solution.py:341
  30.1 3.2 %collective-permute-start.15 = (f32[8,256]{1,0:T(8,128)S(1)}, f32[8,256]{1,0:T(8,128)S(1)}, u32[]{:S(2)}, u32[]{:S(2)}) collective-permute-start(f32[8,256]{1,0:T(8,128)S(1)} %far.1.refs_0_), channel_id=1, source_target_pairs={{0,3},{1,2},{2,1},{3,0},{4,7},{5,6},{6,5},{7,4},{8,11},{9,10},{10,... | collective-permute-start | bytes 24584 | tf_op jit(solution)/shard_map/ppermute | solution.py:46
  30.2 3.7 %collective-permute-start.14 = (f32[8,256]{1,0:T(8,128)S(1)}, f32[8,256]{1,0:T(8,128)S(1)}, u32[]{:S(2)}, u32[]{:S(2)}) collective-permute-start(f32[8,256]{1,0:T(8,128)S(1)} %far.1.refs_0_), channel_id=1, source_target_pairs={{0,2},{1,3},{2,0},{3,1},{4,6},{5,7},{6,4},{7,5},{8,10},{9,11},{10,... | collective-permute-start | bytes 24584 | tf_op jit(solution)/shard_map/ppermute | solution.py:46
  31.8 2.2 %collective-permute-start.13 = (f32[8,256]{1,0:T(8,128)S(1)}, f32[8,256]{1,0:T(8,128)S(1)}, u32[]{:S(2)}, u32[]{:S(2)}) collective-permute-start(f32[8,256]{1,0:T(8,128)S(1)} %far.1.refs_0_), channel_id=1, source_target_pairs={{0,1},{1,0},{2,3},{3,2},{4,5},{5,4},{6,7},{7,6},{8,9},{9,8},{10,11... | collective-permute-start | bytes 24584 | tf_op jit(solution)/shard_map/ppermute | solution.py:46
  34.0 5.5 %collective-permute-start.18 = (f32[8,256]{1,0:T(8,128)S(1)}, f32[8,256]{1,0:T(8,128)S(1)}, u32[]{:S(2)}, u32[]{:S(2)}) collective-permute-start(f32[8,256]{1,0:T(8,128)S(1)} %merge.2.refs_0_), channel_id=1, source_target_pairs={{0,12},{1,13},{2,14},{3,15},{4,8},{5,9},{6,10},{7,11},{8,4},{9,5},... | collective-permute-start | bytes 24584 | tf_op jit(solution)/shard_map/ppermute | solution.py:46
  37.7 4.5 %collective-permute-start.17 = (f32[8,256]{1,0:T(8,128)S(1)}, f32[8,256]{1,0:T(8,128)S(1)}, u32[]{:S(2)}, u32[]{:S(2)}) collective-permute-start(f32[8,256]{1,0:T(8,128)S(1)} %merge.2.refs_0_), channel_id=1, source_target_pairs={{0,8},{1,9},{2,10},{3,11},{4,12},{5,13},{6,14},{7,15},{8,0},{9,1},... | collective-permute-start | bytes 24584 | tf_op jit(solution)/shard_map/ppermute | solution.py:46
  37.7 4.5 %collective-permute-start.16 = (f32[8,256]{1,0:T(8,128)S(1)}, f32[8,256]{1,0:T(8,128)S(1)}, u32[]{:S(2)}, u32[]{:S(2)}) collective-permute-start(f32[8,256]{1,0:T(8,128)S(1)} %merge.2.refs_0_), channel_id=1, source_target_pairs={{0,4},{1,5},{2,6},{3,7},{4,0},{5,1},{6,2},{7,3},{8,12},{9,13},{10,... | collective-permute-start | bytes 24584 | tf_op jit(solution)/shard_map/ppermute | solution.py:46

commit v17 on v16

--- a/solution.py
+++ b/solution.py
@@ -300,7 +300,7 @@
             compiler_params=pltpu.CompilerParams(vmem_limit_bytes=LIMIT),
         )(*tables, *[pltpu.with_memory_space_constraint(a, pltpu.HBM) for a in (border, border_send, border_rows)], toward)
 
-    packed = [*pack(gives[:1]), *(pack(gives[1:]) if sides else [])]
+    packed = pack(gives)
     pays = [lax.ppermute(pay, axis, perm) for pay, (axis, perm) in zip(packed, sends)]
     mine = packed[0]
     fields = [lax.ppermute(right_side, axis, perm) for axis, perm in sends]

time: 43.3 us -> 41 us (0.947)
  waiting for transfers between devices: 13.8 us -> 12.6 us
  Pallas kernels: 6.39 us -> 5.52 us
  local copies, waits for them, and re-layouts: 1.87 us -> 1.2 us
  starting transfers between devices: 20 us -> 20.5 us
    ppermute x6, waiting for transfers between devices: 5.64 us -> 3.5 us  [join(): lax.ppermute(state, AXES, [(i, i ^ m) for i in range(count)])]
    ppermute x2, waiting for transfers between devices: 0.89 us -> 2.47 us  [shards(): fields = [lax.ppermute(right_side, axis, perm) for axis, perm in sends]]
    pallas_call x2 -> x1, Pallas kernels: 2.44 us -> 1.57 us  [pack(): pl.pallas_call(partial(pack_kernel, gives), name='pack', in_specs=smem(le...]
    unnamed x10, local copies, waits for them, and re-layouts: 1.87 us -> 1.2 us
    ppermute x2, waiting for transfers between devices: 1.94 us -> 1.33 us  [shards(): lax.ppermute(pay, axis, perm)]
    ppermute x2, starting transfers between devices: 2.5 us -> 3.09 us  [shards(): from_right = [lax.ppermute(piece, 'gx', left) for piece in to_left]]
  transfers between devices with their start and end apart: 19 -> 19, of which waited for: 11 -> 12; matrix products, arithmetic and copies ran while one was open for 0% -> 0% of each run, Pallas kernels for 11% -> 8%
where the time goes in v17:
time: 41 us; the launch traced here: 40.8 us
  starting transfers between devices  20.5 us (50%)
  waiting for transfers between devices  12.6 us (31%)
  Pallas kernels  5.52 us (13%)
  local copies, waits for them, and re-layouts  1.2 us (3%)
  other arithmetic  0.85 us (2%)
    ppermute x6, starting transfers between devices, join(): lax.ppermute(state, AXES, [(i, i ^ m) for i in range(count)])  6.39 us
    ppermute x2, starting transfers between devices, shards(): lax.ppermute(pay, axis, perm)  3.61 us
    ppermute x6, waiting for transfers between devices, join(): lax.ppermute(state, AXES, [(i, i ^ m) for i in range(count)])  3.5 us
    ppermute x2, starting transfers between devices, shards(): from_right = [lax.ppermute(piece, 'gx', left) for piece in to_left]  3.09 us
    ppermute x2, starting transfers between devices, shards(): fields = [lax.ppermute(right_side, axis, perm) for axis, perm in sends]  3.07 us
    pallas_call x10, Pallas kernels, run(): pl.pallas_call(kernel, name=name, in_specs=[vmem()] * len(args), out_spec...  2.87 us
    ppermute x2, waiting for transfers between devices, shards(): fields = [lax.ppermute(right_side, axis, perm) for axis, perm in sends]  2.47 us
    ppermute x1, waiting for transfers between devices, shards(): left_w = lax.ppermute(part, 'gx', right)  2.18 us
  transfers between devices with their start and end apart: 19, of which 12 were waited for; matrix products, arithmetic and copies ran while one was open for 0% of the time, Pallas kernels for 8%

profile of v17, /device:TPU:0, one launch (start us, length us, event | category | flops | bytes accessed | tf_op | source)
XLA Modules:
  0.0 40.8 jit_solution(14857264668149176218)
XLA Ops:
  0.1 1.6 %pack.1 = (f32[136,256]{1,0:T(8,128)S(1)}, f32[136,256]{1,0:T(8,128)S(1)}) custom-call(s32[2]{0:T(128)S(1)} %pad_add_fusion.refs_0_.marks, f32[8,128,128]{2,1,0:T(8,128)} %bitcast.6, s32[1,8]{1,0:T(1,128)} %refs_2_.1, s32[1,8]{1,0:T(1,128)} %refs_3_.1, s32[1,8]{1,0:T(1,128)S(1)} %broadcast_in_dim.3.refs_4_), custom_call_target="tpu_custom_call" | custom-call | tf_op jit(solution)/shard_map/pack/pallas_call | solution.py:289
  1.7 3.1 %collective-permute-start.3 = (f32[136,256]{1,0:T(8,128)S(1)}, f32[136,256]{1,0:T(8,128)S(1)}, u32[]{:S(2)}, u32[]{:S(2)}) collective-permute-start(f32[136,256]{1,0:T(8,128)S(1)} %get-tuple-element.29.packed.mine.refs_0_), channel_id=1, source_target_pairs={{0,4},{4,8},{8,12},{12,0},{1,5},{5,9},{9,13},{13,1},{2,6},{6,10},{... | collective-permute-start | bytes 417800 | tf_op jit(solution)/shard_map/ppermute | solution.py:304
  4.8 1.2 %copy-done.2 = f32[2,7,128,128]{3,2,1,0:T(8,128)S(1)} copy-done((f32[2,7,128,128]{3,2,1,0:T(8,128)S(1)}, f32[2,7,128,128]{3,2,1,0:T(8,128)}, u32[]{:S(2)}) %copy-start.2) | copy-done | bytes 917528
  5.9 1.1 %prep.1 = (f32[256,256]{1,0:T(8,128)S(1)}, f32[256,256]{1,0:T(8,128)S(1)}, f32[256,128]{1,0:T(8,128)S(1)}, f32[256,128]{1,0:T(8,128)S(1)}) custom-call(s32[2,7]{1,0:T(2,128)S(1)} %copy-done.3, s32[2]{0:T(128)S(1)} %pad_add_fusion.refs_0_.marks, f32[1,256]{1,0:T(1,128)S(1)} %bitcast.9, f32[2,7,128,128]{3,2,1,0:T(8,128)S(1)} %copy-done.2, ...), custom_call_target="tpu_custom_call" | custom-call | flops 16777216 | bytes 1048576 | tf_op jit(solution)/shard_map/prep/pallas_call | solution.py:312
  7.6 1.6 %collective-permute-start.4 = (f32[256,256]{1,0:T(8,128)S(1)}, f32[256,256]{1,0:T(8,128)S(1)}, u32[]{:S(2)}, u32[]{:S(2)}) collective-permute-start(f32[256,256]{1,0:T(8,128)S(1)} %copy-done), channel_id=1, source_target_pairs={{0,4},{4,8},{8,12},{12,0},{1,5},{5,9},{9,13},{13,1},{2,6},{6,10},{... | collective-permute-start | bytes 786440 | tf_op jit(solution)/shard_map/ppermute | solution.py:306
  9.2 1.5 %collective-permute-start.6 = (f32[256,256]{1,0:T(8,128)S(1)}, f32[256,256]{1,0:T(8,128)S(1)}, u32[]{:S(2)}, u32[]{:S(2)}) collective-permute-start(f32[256,256]{1,0:T(8,128)S(1)} %copy-done), channel_id=1, source_target_pairs={{0,2},{2,0},{1,3},{3,1},{4,6},{6,4},{5,7},{7,5},{8,10},{10,8},{9,1... | collective-permute-start | bytes 786440 | tf_op jit(solution)/shard_map/ppermute | solution.py:306
  11.7 0.9 %collective-permute-done.2.high = f32[256,128]{1,0:T(8,128)S(1)} collective-permute-done((f32[256,128]{1,0:T(8,128)S(1)}, f32[256,128]{1,0:T(8,128)S(1)}, u32[]{:S(2)}, u32[]{:S(2)}) %collective-permute-start.2) | collective-permute-done | bytes 131104 | tf_op jit(solution)/shard_map/ppermute | solution.py:328
  12.6 2.2 %collective-permute-start.7 = (f32[264,128]{1,0:T(8,128)S(1)}, f32[264,128]{1,0:T(8,128)S(1)}, u32[]{:S(2)}, u32[]{:S(2)}) collective-permute-start(f32[264,128]{1,0:T(8,128)S(1)} %get-tuple-element.40), channel_id=1, source_target_pairs={{4,0},{8,4},{12,8},{0,12},{5,1},{9,5},{13,9},{1,13},{6,2},{10,6},{... | collective-permute-start | bytes 405512 | tf_op jit(solution)/shard_map/ppermute | solution.py:332
  14.8 0.8 %collective-permute-start.8 = (f32[264,128]{1,0:T(8,128)S(1)}, f32[264,128]{1,0:T(8,128)S(1)}, u32[]{:S(2)}, u32[]{:S(2)}) collective-permute-start(f32[264,128]{1,0:T(8,128)S(1)} %get-tuple-element.42), channel_id=1, source_target_pairs={{4,0},{8,4},{12,8},{0,12},{5,1},{9,5},{13,9},{1,13},{6,2},{10,6},{... | collective-permute-start | bytes 405512 | tf_op jit(solution)/shard_map/ppermute | solution.py:332
  16.1 2.5 %collective-permute-done.4.there = f32[256,256]{1,0:T(8,128)S(1)} collective-permute-done((f32[256,256]{1,0:T(8,128)S(1)}, f32[256,256]{1,0:T(8,128)S(1)}, u32[]{:S(2)}, u32[]{:S(2)}) %collective-permute-start.4) | collective-permute-done | bytes 262176 | tf_op jit(solution)/shard_map/ppermute | solution.py:306
  18.9 1.3 %collective-permute-done.5.pay = f32[136,256]{1,0:T(8,128)S(1)} collective-permute-done((f32[136,256]{1,0:T(8,128)S(1)}, f32[136,256]{1,0:T(8,128)S(1)}, u32[]{:S(2)}, u32[]{:S(2)}) %collective-permute-start.5) | collective-permute-done | bytes 139296 | tf_op jit(solution)/shard_map/ppermute | solution.py:304
  20.6 1.6 %collective-permute-start.11 = (f32[256,256]{1,0:T(8,128)S(1)}, f32[256,256]{1,0:T(8,128)S(1)}, u32[]{:S(2)}, u32[]{:S(2)}) collective-permute-start(f32[256,256]{1,0:T(8,128)S(1)} %get-tuple-element.39.part), channel_id=1, source_target_pairs={{0,4},{4,8},{8,12},{12,0},{1,5},{5,9},{9,13},{13,1},{2,6},{6,10},{... | collective-permute-start | bytes 786440 | tf_op jit(solution)/shard_map/ppermute | solution.py:338
  22.3 1.6 %collective-permute-start.12 = (f32[264,128]{1,0:T(8,128)S(1)}, f32[264,128]{1,0:T(8,128)S(1)}, u32[]{:S(2)}, u32[]{:S(2)}) collective-permute-start(f32[264,128]{1,0:T(8,128)S(1)} %get-tuple-element.52), channel_id=1, source_target_pairs={{0,2},{2,0},{1,3},{3,1},{4,6},{6,4},{5,7},{7,5},{8,10},{10,8},{9,1... | collective-permute-start | bytes 405512 | tf_op jit(solution)/shard_map/ppermute | solution.py:349
  24.0 0.6 %collective-permute-start.10 = (f32[256,128]{1,0:T(8,128)S(1)}, f32[256,128]{1,0:T(8,128)S(1)}, u32[]{:S(2)}, u32[]{:S(2)}) collective-permute-start(f32[256,128]{1,0:T(8,128)S(1)} %get-tuple-element.45), channel_id=1, source_target_pairs={{0,1},{1,0},{2,3},{3,2},{4,5},{5,4},{6,7},{7,6},{8,9},{9,8},{10,11... | collective-permute-start | bytes 393224 | tf_op jit(solution)/shard_map/ppermute | solution.py:341
  24.6 0.7 %collective-permute-done.9.mate_out = f32[256,128]{1,0:T(8,128)S(1)} collective-permute-done((f32[256,128]{1,0:T(8,128)S(1)}, f32[256,128]{1,0:T(8,128)S(1)}, u32[]{:S(2)}, u32[]{:S(2)}) %collective-permute-start.9) | collective-permute-done | bytes 131104 | tf_op jit(solution)/shard_map/ppermute | solution.py:341
  26.1 1.3 %collective-permute-done.12.refs_3_ = f32[264,128]{1,0:T(8,128)S(1)} collective-permute-done((f32[264,128]{1,0:T(8,128)S(1)}, f32[264,128]{1,0:T(8,128)S(1)}, u32[]{:S(2)}, u32[]{:S(2)}) %collective-permute-start.12) | collective-permute-done | bytes 135200 | tf_op jit(solution)/shard_map/ppermute | solution.py:349
  27.4 2.2 %collective-permute-done.11.left = f32[256,256]{1,0:T(8,128)S(1)} collective-permute-done((f32[256,256]{1,0:T(8,128)S(1)}, f32[256,256]{1,0:T(8,128)S(1)}, u32[]{:S(2)}, u32[]{:S(2)}) %collective-permute-start.11) | collective-permute-done | bytes 262176 | tf_op jit(solution)/shard_map/ppermute | solution.py:338
  30.2 1.6 %collective-permute-start.14 = (f32[8,256]{1,0:T(8,128)S(1)}, f32[8,256]{1,0:T(8,128)S(1)}, u32[]{:S(2)}, u32[]{:S(2)}) collective-permute-start(f32[8,256]{1,0:T(8,128)S(1)} %far.1.refs_0_), channel_id=1, source_target_pairs={{0,2},{1,3},{2,0},{3,1},{4,6},{5,7},{6,4},{7,5},{8,10},{9,11},{10,... | collective-permute-start | bytes 24584 | tf_op jit(solution)/shard_map/ppermute | solution.py:46
  32.0 1.3 %collective-permute-done.15.refs_3_ = f32[8,256]{1,0:T(8,128)S(1)} collective-permute-done((f32[8,256]{1,0:T(8,128)S(1)}, f32[8,256]{1,0:T(8,128)S(1)}, u32[]{:S(2)}, u32[]{:S(2)}) %collective-permute-start.15) | collective-permute-done | bytes 8224 | tf_op jit(solution)/shard_map/ppermute | solution.py:46
  33.3 0.6 %collective-permute-done.14.refs_2_ = f32[8,256]{1,0:T(8,128)S(1)} collective-permute-done((f32[8,256]{1,0:T(8,128)S(1)}, f32[8,256]{1,0:T(8,128)S(1)}, u32[]{:S(2)}, u32[]{:S(2)}) %collective-permute-start.14) | collective-permute-done | bytes 8224 | tf_op jit(solution)/shard_map/ppermute | solution.py:46
  33.9 1.3 %collective-permute-start.18 = (f32[8,256]{1,0:T(8,128)S(1)}, f32[8,256]{1,0:T(8,128)S(1)}, u32[]{:S(2)}, u32[]{:S(2)}) collective-permute-start(f32[8,256]{1,0:T(8,128)S(1)} %merge.2.refs_0_), channel_id=1, source_target_pairs={{0,12},{1,13},{2,14},{3,15},{4,8},{5,9},{6,10},{7,11},{8,4},{9,5},... | collective-permute-start | bytes 24584 | tf_op jit(solution)/shard_map/ppermute | solution.py:46
  35.3 3.1 %collective-permute-start.16 = (f32[8,256]{1,0:T(8,128)S(1)}, f32[8,256]{1,0:T(8,128)S(1)}, u32[]{:S(2)}, u32[]{:S(2)}) collective-permute-start(f32[8,256]{1,0:T(8,128)S(1)} %merge.2.refs_0_), channel_id=1, source_target_pairs={{0,4},{1,5},{2,6},{3,7},{4,0},{5,1},{6,2},{7,3},{8,12},{9,13},{10,... | collective-permute-start | bytes 24584 | tf_op jit(solution)/shard_map/ppermute | solution.py:46
  38.4 1.1 %collective-permute-done.18.refs_3_ = f32[8,256]{1,0:T(8,128)S(1)} collective-permute-done((f32[8,256]{1,0:T(8,128)S(1)}, f32[8,256]{1,0:T(8,128)S(1)}, u32[]{:S(2)}, u32[]{:S(2)}) %collective-permute-start.18) | collective-permute-done | bytes 8224 | tf_op jit(solution)/shard_map/ppermute | solution.py:46
  40.1 0.7 %multiply_subtract_fusion = f32[256,256]{1,0:T(8,128)} fusion(f32[256,256]{1,0:T(8,128)S(1)} %get-tuple-element.43.image, f32[256,256]{1,0:T(8,128)S(1)} %copy-done, f32[256]{0:T(256)S(1)} %bitcast.11, f32[256]{0:T(256)S(1)} %bitcast.10), kind=kLoop, calls=%fused_computation | loop fusion | flops 196608 | bytes 788480 | tf_op jit(solution)/shard_map/sub | solution.py:357
  (41 shorter events, 5.4 us)
Async XLA Ops:
  1.7 3.1 %copy-start.4 = (f32[256]{0:T(256)S(1)}, f32[256]{0:T(256)}, u32[]{:S(2)}) copy-start(f32[256]{0:T(256)} %param.8) | copy-start | bytes 3076
  1.7 3.1 %copy-start.3 = (s32[2,7]{1,0:T(2,128)S(1)}, s32[2,7]{1,0:T(2,128)}, u32[]{:S(2)}) copy-start(s32[2,7]{1,0:T(2,128)} %cols.1) | copy-start | bytes 172
  1.7 9.5 %collective-permute-start.3 = (f32[136,256]{1,0:T(8,128)S(1)}, f32[136,256]{1,0:T(8,128)S(1)}, u32[]{:S(2)}, u32[]{:S(2)}) collective-permute-start(f32[136,256]{1,0:T(8,128)S(1)} %get-tuple-element.29.packed.mine.refs_0_), channel_id=1, source_target_pairs={{0,4},{4,8},{8,12},{12,0},{1,5},{5,9},{9,13},{13,1},{2,6},{6,10},{... | collective-permute-start | bytes 417800 | tf_op jit(solution)/shard_map/ppermute | solution.py:304
  4.8 1.2 %copy-start.2 = (f32[2,7,128,128]{3,2,1,0:T(8,128)S(1)}, f32[2,7,128,128]{3,2,1,0:T(8,128)}, u32[]{:S(2)}) copy-start(f32[2,7,128,128]{3,2,1,0:T(8,128)} %local.1) | copy-start | bytes 2752516
  5.9 1.2 %copy-start = (f32[256,256]{1,0:T(8,128)S(1)}, f32[256,256]{1,0:T(8,128)}, u32[]{:S(2)}) copy-start(f32[256,256]{1,0:T(8,128)} %field.7) | copy-start | bytes 786436
  5.9 5.3 %copy-start.1 = (f32[1,8,128,128]{3,2,1,0:T(8,128)S(1)}, f32[1,8,128,128]{3,2,1,0:T(8,128)}, u32[]{:S(2)}) copy-start(f32[1,8,128,128]{3,2,1,0:T(8,128)} %param.11) | copy-start | bytes 1572868
  7.0 3.6 %collective-permute-start.1 = (f32[256,128]{1,0:T(8,128)S(1)}, f32[256,128]{1,0:T(8,128)S(1)}, u32[]{:S(2)}, u32[]{:S(2)}) collective-permute-start(f32[256,128]{1,0:T(8,128)S(1)} %get-tuple-element.32), channel_id=1, source_target_pairs={{0,1},{1,0},{2,3},{3,2},{4,5},{5,4},{6,7},{7,6},{8,9},{9,8},{10,11... | collective-permute-start | bytes 393224 | tf_op jit(solution)/shard_map/ppermute | solution.py:328
  7.1 7.7 %collective-permute-start = (f32[256,256]{1,0:T(8,128)S(1)}, f32[256,256]{1,0:T(8,128)S(1)}, u32[]{:S(2)}, u32[]{:S(2)}) collective-permute-start(f32[256,256]{1,0:T(8,128)S(1)} %copy-done), channel_id=1, source_target_pairs={{0,1},{1,0},{2,3},{3,2},{4,5},{5,4},{6,7},{7,6},{8,9},{9,8},{10,11... | collective-permute-start | bytes 786440 | tf_op jit(solution)/shard_map/ppermute | solution.py:307
  7.6 11.0 %collective-permute-start.4 = (f32[256,256]{1,0:T(8,128)S(1)}, f32[256,256]{1,0:T(8,128)S(1)}, u32[]{:S(2)}, u32[]{:S(2)}) collective-permute-start(f32[256,256]{1,0:T(8,128)S(1)} %copy-done), channel_id=1, source_target_pairs={{0,4},{4,8},{8,12},{12,0},{1,5},{5,9},{9,13},{13,1},{2,6},{6,10},{... | collective-permute-start | bytes 786440 | tf_op jit(solution)/shard_map/ppermute | solution.py:306
  9.2 11.0 %collective-permute-start.6 = (f32[256,256]{1,0:T(8,128)S(1)}, f32[256,256]{1,0:T(8,128)S(1)}, u32[]{:S(2)}, u32[]{:S(2)}) collective-permute-start(f32[256,256]{1,0:T(8,128)S(1)} %copy-done), channel_id=1, source_target_pairs={{0,2},{2,0},{1,3},{3,1},{4,6},{6,4},{5,7},{7,5},{8,10},{10,8},{9,1... | collective-permute-start | bytes 786440 | tf_op jit(solution)/shard_map/ppermute | solution.py:306
  10.7 9.5 %collective-permute-start.5 = (f32[136,256]{1,0:T(8,128)S(1)}, f32[136,256]{1,0:T(8,128)S(1)}, u32[]{:S(2)}, u32[]{:S(2)}) collective-permute-start(f32[136,256]{1,0:T(8,128)S(1)} %get-tuple-element.38), channel_id=1, source_target_pairs={{0,2},{2,0},{1,3},{3,1},{4,6},{6,4},{5,7},{7,5},{8,10},{10,8},{9,1... | collective-permute-start | bytes 417800 | tf_op jit(solution)/shard_map/ppermute | solution.py:304
  11.2 1.3 %collective-permute-start.2 = (f32[256,128]{1,0:T(8,128)S(1)}, f32[256,128]{1,0:T(8,128)S(1)}, u32[]{:S(2)}, u32[]{:S(2)}) collective-permute-start(f32[256,128]{1,0:T(8,128)S(1)} %get-tuple-element.33), channel_id=1, source_target_pairs={{0,1},{1,0},{2,3},{3,2},{4,5},{5,4},{6,7},{7,6},{8,9},{9,8},{10,11... | collective-permute-start | bytes 393224 | tf_op jit(solution)/shard_map/ppermute | solution.py:328
  12.6 9.7 %collective-permute-start.7 = (f32[264,128]{1,0:T(8,128)S(1)}, f32[264,128]{1,0:T(8,128)S(1)}, u32[]{:S(2)}, u32[]{:S(2)}) collective-permute-start(f32[264,128]{1,0:T(8,128)S(1)} %get-tuple-element.40), channel_id=1, source_target_pairs={{4,0},{8,4},{12,8},{0,12},{5,1},{9,5},{13,9},{1,13},{6,2},{10,6},{... | collective-permute-start | bytes 405512 | tf_op jit(solution)/shard_map/ppermute | solution.py:332
  14.8 9.1 %collective-permute-start.8 = (f32[264,128]{1,0:T(8,128)S(1)}, f32[264,128]{1,0:T(8,128)S(1)}, u32[]{:S(2)}, u32[]{:S(2)}) collective-permute-start(f32[264,128]{1,0:T(8,128)S(1)} %get-tuple-element.42), channel_id=1, source_target_pairs={{4,0},{8,4},{12,8},{0,12},{5,1},{9,5},{13,9},{1,13},{6,2},{10,6},{... | collective-permute-start | bytes 405512 | tf_op jit(solution)/shard_map/ppermute | solution.py:332
  20.6 9.0 %collective-permute-start.11 = (f32[256,256]{1,0:T(8,128)S(1)}, f32[256,256]{1,0:T(8,128)S(1)}, u32[]{:S(2)}, u32[]{:S(2)}) collective-permute-start(f32[256,256]{1,0:T(8,128)S(1)} %get-tuple-element.39.part), channel_id=1, source_target_pairs={{0,4},{4,8},{8,12},{12,0},{1,5},{5,9},{9,13},{13,1},{2,6},{6,10},{... | collective-permute-start | bytes 786440 | tf_op jit(solution)/shard_map/ppermute | solution.py:338
  22.3 5.1 %collective-permute-start.12 = (f32[264,128]{1,0:T(8,128)S(1)}, f32[264,128]{1,0:T(8,128)S(1)}, u32[]{:S(2)}, u32[]{:S(2)}) collective-permute-start(f32[264,128]{1,0:T(8,128)S(1)} %get-tuple-element.52), channel_id=1, source_target_pairs={{0,2},{2,0},{1,3},{3,1},{4,6},{6,4},{5,7},{7,5},{8,10},{10,8},{9,1... | collective-permute-start | bytes 405512 | tf_op jit(solution)/shard_map/ppermute | solution.py:349
  23.9 1.3 %collective-permute-start.9 = (f32[256,128]{1,0:T(8,128)S(1)}, f32[256,128]{1,0:T(8,128)S(1)}, u32[]{:S(2)}, u32[]{:S(2)}) collective-permute-start(f32[256,128]{1,0:T(8,128)S(1)} %get-tuple-element.41.half), channel_id=1, source_target_pairs={{0,1},{1,0},{2,3},{3,2},{4,5},{5,4},{6,7},{7,6},{8,9},{9,8},{10,11... | collective-permute-start | bytes 393224 | tf_op jit(solution)/shard_map/ppermute | solution.py:341
  24.0 1.6 %collective-permute-start.10 = (f32[256,128]{1,0:T(8,128)S(1)}, f32[256,128]{1,0:T(8,128)S(1)}, u32[]{:S(2)}, u32[]{:S(2)}) collective-permute-start(f32[256,128]{1,0:T(8,128)S(1)} %get-tuple-element.45), channel_id=1, source_target_pairs={{0,1},{1,0},{2,3},{3,2},{4,5},{5,4},{6,7},{7,6},{8,9},{9,8},{10,11... | collective-permute-start | bytes 393224 | tf_op jit(solution)/shard_map/ppermute | solution.py:341
  30.1 3.2 %collective-permute-start.15 = (f32[8,256]{1,0:T(8,128)S(1)}, f32[8,256]{1,0:T(8,128)S(1)}, u32[]{:S(2)}, u32[]{:S(2)}) collective-permute-start(f32[8,256]{1,0:T(8,128)S(1)} %far.1.refs_0_), channel_id=1, source_target_pairs={{0,3},{1,2},{2,1},{3,0},{4,7},{5,6},{6,5},{7,4},{8,11},{9,10},{10,... | collective-permute-start | bytes 24584 | tf_op jit(solution)/shard_map/ppermute | solution.py:46
  30.2 3.7 %collective-permute-start.14 = (f32[8,256]{1,0:T(8,128)S(1)}, f32[8,256]{1,0:T(8,128)S(1)}, u32[]{:S(2)}, u32[]{:S(2)}) collective-permute-start(f32[8,256]{1,0:T(8,128)S(1)} %far.1.refs_0_), channel_id=1, source_target_pairs={{0,2},{1,3},{2,0},{3,1},{4,6},{5,7},{6,4},{7,5},{8,10},{9,11},{10,... | collective-permute-start | bytes 24584 | tf_op jit(solution)/shard_map/ppermute | solution.py:46
  31.7 2.2 %collective-permute-start.13 = (f32[8,256]{1,0:T(8,128)S(1)}, f32[8,256]{1,0:T(8,128)S(1)}, u32[]{:S(2)}, u32[]{:S(2)}) collective-permute-start(f32[8,256]{1,0:T(8,128)S(1)} %far.1.refs_0_), channel_id=1, source_target_pairs={{0,1},{1,0},{2,3},{3,2},{4,5},{5,4},{6,7},{7,6},{8,9},{9,8},{10,11... | collective-permute-start | bytes 24584 | tf_op jit(solution)/shard_map/ppermute | solution.py:46
  33.9 5.5 %collective-permute-start.18 = (f32[8,256]{1,0:T(8,128)S(1)}, f32[8,256]{1,0:T(8,128)S(1)}, u32[]{:S(2)}, u32[]{:S(2)}) collective-permute-start(f32[8,256]{1,0:T(8,128)S(1)} %merge.2.refs_0_), channel_id=1, source_target_pairs={{0,12},{1,13},{2,14},{3,15},{4,8},{5,9},{6,10},{7,11},{8,4},{9,5},... | collective-permute-start | bytes 24584 | tf_op jit(solution)/shard_map/ppermute | solution.py:46
  35.2 4.5 %collective-permute-start.17 = (f32[8,256]{1,0:T(8,128)S(1)}, f32[8,256]{1,0:T(8,128)S(1)}, u32[]{:S(2)}, u32[]{:S(2)}) collective-permute-start(f32[8,256]{1,0:T(8,128)S(1)} %merge.2.refs_0_), channel_id=1, source_target_pairs={{0,8},{1,9},{2,10},{3,11},{4,12},{5,13},{6,14},{7,15},{8,0},{9,1},... | collective-permute-start | bytes 24584 | tf_op jit(solution)/shard_map/ppermute | solution.py:46
  35.3 4.8 %collective-permute-start.16 = (f32[8,256]{1,0:T(8,128)S(1)}, f32[8,256]{1,0:T(8,128)S(1)}, u32[]{:S(2)}, u32[]{:S(2)}) collective-permute-start(f32[8,256]{1,0:T(8,128)S(1)} %merge.2.refs_0_), channel_id=1, source_target_pairs={{0,4},{1,5},{2,6},{3,7},{4,0},{5,1},{6,2},{7,3},{8,12},{9,13},{10,... | collective-permute-start | bytes 24584 | tf_op jit(solution)/shard_map/ppermute | solution.py:46

commit v18 on v17

--- a/solution.py
+++ b/solution.py
@@ -150,10 +150,15 @@
     image[...] = dot(own[...], field[...]) + dot(coup[...], mate[...])
 
 
-def back_kernel(mine, field, border, pay, coup, back, out, other):
+def back_kernel(takes, mine, field, border, *refs):
+    count = len(takes)
+    *pays, pay = refs[: count + 1]
+    coup, back, out, other, *coups = refs[count + 1 :]
     width = field.shape[0]
     toward = mine[pl.ds(mine.shape[0] - TAIL + 2, 1), pl.ds(0, 1)]
     coup[...] = edge(0, width, mine, pay, border)
+    for take, gy_pay, gy_coup in zip(takes, pays, coups):
+        gy_coup[...] = edge(toward if take is None else take, width, mine, gy_pay, border)
     back[...] = dot(coup[...].T, field[...])
     out[pl.ds(0, width), :] = columns(back, toward, True)
     other[pl.ds(0, width), :] = columns(back, toward, False)
@@ -172,14 +177,10 @@
     return jnp.where(toward == 3.0, first, 1.0 - first)
 
 
-def gy_kernel(take, weight, mine, part, single, border, pay, there, image, once, coup):
-    width = coup.shape[0]
-    toward = mine[pl.ds(mine.shape[0] - TAIL + 2, 1), pl.ds(0, 1)]
-    coup[...] = edge(toward if take is None else take, width, mine, pay, border)
+def gy_kernel(take, weight, mine, part, single, coup, there, image, once):
     term = dot(coup[...], there[...])
     image[...] = part[...] + term
-    scale = weight * turn(mine, width) if take is None else weight
-    once[...] = single[...] + scale * term
+    once[...] = single[...] + (weight * turn(mine, part.shape[0]) if take is None else weight) * term
 
 
 def columns(ref, toward, out):
@@ -328,13 +329,15 @@
     mate_pair = [lax.ppermute(piece, "nd", swap) for piece in pieces]
 
     part, coup = call(base_kernel, "base", [field, square])(right_side, own, pair, mate, *mate_pair)
-    left_coup, back, *to_left = call(back_kernel, "back", [square, field] + [longer] * 2)(mine, right_side, border, pays[0])
+    kernel = partial(back_kernel, [take for _, take, _ in sides])
+    left_coup, back, *to_left = call(kernel, "back", [square, field] + [longer] * 2 + [square] * len(sides))(
+        mine, right_side, border, *pays[1:], pays[0]
+    )
+    to_left, side_coup = to_left[:2], to_left[2:]
     from_right = [lax.ppermute(piece, "gx", left) for piece in to_left]
     part, once = call(left_kernel, "left", [field] * 2)(part, left_coup, fields[0])
-    side_coup = []
-    for (_, take, weight), pay, there in zip(sides, pays[1:], fields[1:]):
-        part, once, block = call(partial(gy_kernel, take, weight), "gy", [field, field, square])(mine, part, once, border, pay, there)
-        side_coup.append(block)
+    for (_, take, weight), block, there in zip(sides, side_coup, fields[1:]):
+        part, once = call(partial(gy_kernel, take, weight), "gy", [field] * 2)(mine, part, once, block, there)
     left_w = lax.ppermute(part, "gx", right)
     half_w, across = call(right_kernel, "right", [half, longer])(mine, part, from_right[0])
     image, other_w = call(whole_kernel, "whole", [field, half])(mine, part, half_w, from_right[1])

time: 41 us -> 41.7 us (1.017)
  waiting for transfers between devices: 12.6 us -> 16.2 us
  starting transfers between devices: 20.5 us -> 17.7 us
    ppermute x2, waiting for transfers between devices: 0.01 us -> 4.2 us  [shards(): from_right = [lax.ppermute(piece, 'gx', left) for piece in to_left]]
    ppermute x6, waiting for transfers between devices: 3.5 us -> 5.11 us  [join(): lax.ppermute(state, AXES, [(i, i ^ m) for i in range(count)])]
    ppermute x2, waiting for transfers between devices: 2.47 us -> 1.04 us  [shards(): fields = [lax.ppermute(right_side, axis, perm) for axis, perm in sends]]
    ppermute x1, starting transfers between devices: 1.63 us -> 0.28 us  [shards(): left_w = lax.ppermute(part, 'gx', right)]
    ppermute x2, starting transfers between devices: 3.61 us -> 4.58 us  [shards(): lax.ppermute(pay, axis, perm)]
    ppermute x2, starting transfers between devices: 3.07 us -> 2.11 us  [shards(): fields = [lax.ppermute(right_side, axis, perm) for axis, perm in sends]]
    ppermute x1, waiting for transfers between devices: 1.28 us -> 0.33 us  [shards(): lax.ppermute(across if take is None else image, 'gy', perm)]
    ppermute x1, starting transfers between devices: 1.56 us -> 0.63 us  [shards(): lax.ppermute(across if take is None else image, 'gy', perm)]
  transfers between devices with their start and end apart: 19 -> 19, of which waited for: 12 -> 11; matrix products, arithmetic and copies ran while one was open for 0% -> 0% of each run, Pallas kernels for 8% -> 8%
where the time goes in v18:
time: 41.7 us; the launch traced here: 41.5 us
  starting transfers between devices  17.7 us (42%)
  waiting for transfers between devices  16.2 us (39%)
  Pallas kernels  5.45 us (13%)
  local copies, waits for them, and re-layouts  1.2 us (3%)
  other arithmetic  0.85 us (2%)
    ppermute x6, starting transfers between devices, join(): lax.ppermute(state, AXES, [(i, i ^ m) for i in range(count)])  6.37 us
    ppermute x6, waiting for transfers between devices, join(): lax.ppermute(state, AXES, [(i, i ^ m) for i in range(count)])  5.11 us
    ppermute x2, starting transfers between devices, shards(): lax.ppermute(pay, axis, perm)  4.58 us
    ppermute x2, waiting for transfers between devices, shards(): from_right = [lax.ppermute(piece, 'gx', left) for piece in to_left]  4.2 us
    ppermute x2, starting transfers between devices, shards(): from_right = [lax.ppermute(piece, 'gx', left) for piece in to_left]  3.55 us
    ppermute x1, waiting for transfers between devices, shards(): left_w = lax.ppermute(part, 'gx', right)  2.79 us
    pallas_call x10, Pallas kernels, run(): pl.pallas_call(kernel, name=name, in_specs=[vmem()] * len(args), out_spec...  2.79 us
    ppermute x2, starting transfers between devices, shards(): fields = [lax.ppermute(right_side, axis, perm) for axis, perm in sends]  2.11 us
  transfers between devices with their start and end apart: 19, of which 11 were waited for; matrix products, arithmetic and copies ran while one was open for 0% of the time, Pallas kernels for 8%

profile of v18, /device:TPU:0, one launch (start us, length us, event | category | flops | bytes accessed | tf_op | source)
XLA Modules:
  0.0 41.5 jit_solution(13891674976079301601)
XLA Ops:
  0.1 1.6 %pack.1 = (f32[136,256]{1,0:T(8,128)S(1)}, f32[136,256]{1,0:T(8,128)S(1)}) custom-call(s32[2]{0:T(128)S(1)} %pad_add_fusion.refs_0_.marks, f32[8,128,128]{2,1,0:T(8,128)} %bitcast.6, s32[1,8]{1,0:T(1,128)} %refs_2_.1, s32[1,8]{1,0:T(1,128)} %refs_3_.1, s32[1,8]{1,0:T(1,128)S(1)} %broadcast_in_dim.3.refs_4_), custom_call_target="tpu_custom_call" | custom-call | tf_op jit(solution)/shard_map/pack/pallas_call | solution.py:290
  1.7 3.0 %collective-permute-start.3 = (f32[136,256]{1,0:T(8,128)S(1)}, f32[136,256]{1,0:T(8,128)S(1)}, u32[]{:S(2)}, u32[]{:S(2)}) collective-permute-start(f32[136,256]{1,0:T(8,128)S(1)} %get-tuple-element.35), channel_id=1, source_target_pairs={{0,2},{2,0},{1,3},{3,1},{4,6},{6,4},{5,7},{7,5},{8,10},{10,8},{9,1... | collective-permute-start | bytes 417800 | tf_op jit(solution)/shard_map/ppermute | solution.py:305
  4.7 1.6 %collective-permute-start.4 = (f32[136,256]{1,0:T(8,128)S(1)}, f32[136,256]{1,0:T(8,128)S(1)}, u32[]{:S(2)}, u32[]{:S(2)}) collective-permute-start(f32[136,256]{1,0:T(8,128)S(1)} %get-tuple-element.29.packed.mine.refs_0_), channel_id=1, source_target_pairs={{0,4},{4,8},{8,12},{12,0},{1,5},{5,9},{9,13},{13,1},{2,6},{6,10},{... | collective-permute-start | bytes 417800 | tf_op jit(solution)/shard_map/ppermute | solution.py:305
  6.2 1.6 %collective-permute-start.5 = (f32[256,256]{1,0:T(8,128)S(1)}, f32[256,256]{1,0:T(8,128)S(1)}, u32[]{:S(2)}, u32[]{:S(2)}) collective-permute-start(f32[256,256]{1,0:T(8,128)S(1)} %copy-done), channel_id=1, source_target_pairs={{0,4},{4,8},{8,12},{12,0},{1,5},{5,9},{9,13},{13,1},{2,6},{6,10},{... | collective-permute-start | bytes 786440 | tf_op jit(solution)/shard_map/ppermute | solution.py:307
  8.4 1.2 %copy-done.2 = f32[2,7,128,128]{3,2,1,0:T(8,128)S(1)} copy-done((f32[2,7,128,128]{3,2,1,0:T(8,128)S(1)}, f32[2,7,128,128]{3,2,1,0:T(8,128)}, u32[]{:S(2)}) %copy-start.2) | copy-done | bytes 917528
  9.5 1.1 %prep.1 = (f32[256,256]{1,0:T(8,128)S(1)}, f32[256,256]{1,0:T(8,128)S(1)}, f32[256,128]{1,0:T(8,128)S(1)}, f32[256,128]{1,0:T(8,128)S(1)}) custom-call(s32[2,7]{1,0:T(2,128)S(1)} %copy-done.3, s32[2]{0:T(128)S(1)} %pad_add_fusion.refs_0_.marks, f32[1,256]{1,0:T(1,128)S(1)} %bitcast.8, f32[2,7,128,128]{3,2,1,0:T(8,128)S(1)} %copy-done.2, ...), custom_call_target="tpu_custom_call" | custom-call | flops 16777216 | bytes 1048576 | tf_op jit(solution)/shard_map/prep/pallas_call | solution.py:313
  10.7 1.4 %collective-permute-done.4.refs_1_ = f32[136,256]{1,0:T(8,128)S(1)} collective-permute-done((f32[136,256]{1,0:T(8,128)S(1)}, f32[136,256]{1,0:T(8,128)S(1)}, u32[]{:S(2)}, u32[]{:S(2)}) %collective-permute-start.4) | collective-permute-done | bytes 139296 | tf_op jit(solution)/shard_map/ppermute | solution.py:305
  12.7 2.8 %collective-permute-start.7 = (f32[264,128]{1,0:T(8,128)S(1)}, f32[264,128]{1,0:T(8,128)S(1)}, u32[]{:S(2)}, u32[]{:S(2)}) collective-permute-start(f32[264,128]{1,0:T(8,128)S(1)} %get-tuple-element.41), channel_id=1, source_target_pairs={{4,0},{8,4},{12,8},{0,12},{5,1},{9,5},{13,9},{1,13},{6,2},{10,6},{... | collective-permute-start | bytes 405512 | tf_op jit(solution)/shard_map/ppermute | solution.py:337
  15.4 0.8 %collective-permute-start.8 = (f32[264,128]{1,0:T(8,128)S(1)}, f32[264,128]{1,0:T(8,128)S(1)}, u32[]{:S(2)}, u32[]{:S(2)}) collective-permute-start(f32[264,128]{1,0:T(8,128)S(1)} %get-tuple-element.43), channel_id=1, source_target_pairs={{4,0},{8,4},{12,8},{0,12},{5,1},{9,5},{13,9},{1,13},{6,2},{10,6},{... | collective-permute-start | bytes 405512 | tf_op jit(solution)/shard_map/ppermute | solution.py:337
  16.7 1.0 %collective-permute-done.5.there = f32[256,256]{1,0:T(8,128)S(1)} collective-permute-done((f32[256,256]{1,0:T(8,128)S(1)}, f32[256,256]{1,0:T(8,128)S(1)}, u32[]{:S(2)}, u32[]{:S(2)}) %collective-permute-start.5) | collective-permute-done | bytes 262176 | tf_op jit(solution)/shard_map/ppermute | solution.py:307
  18.5 1.7 %collective-permute-done.7.out = f32[264,128]{1,0:T(8,128)S(1)} collective-permute-done((f32[264,128]{1,0:T(8,128)S(1)}, f32[264,128]{1,0:T(8,128)S(1)}, u32[]{:S(2)}, u32[]{:S(2)}) %collective-permute-start.7) | collective-permute-done | bytes 135200 | tf_op jit(solution)/shard_map/ppermute | solution.py:337
  20.3 0.6 %collective-permute-start.12 = (f32[264,128]{1,0:T(8,128)S(1)}, f32[264,128]{1,0:T(8,128)S(1)}, u32[]{:S(2)}, u32[]{:S(2)}) collective-permute-start(f32[264,128]{1,0:T(8,128)S(1)} %get-tuple-element.52), channel_id=1, source_target_pairs={{0,2},{2,0},{1,3},{3,1},{4,6},{6,4},{5,7},{7,5},{8,10},{10,8},{9,1... | collective-permute-start | bytes 405512 | tf_op jit(solution)/shard_map/ppermute | solution.py:352
  20.9 2.5 %collective-permute-done.8.rest = f32[264,128]{1,0:T(8,128)S(1)} collective-permute-done((f32[264,128]{1,0:T(8,128)S(1)}, f32[264,128]{1,0:T(8,128)S(1)}, u32[]{:S(2)}, u32[]{:S(2)}) %collective-permute-start.8) | collective-permute-done | bytes 135200 | tf_op jit(solution)/shard_map/ppermute | solution.py:337
  23.7 1.3 %collective-permute-done.10.mate_other = f32[256,128]{1,0:T(8,128)S(1)} collective-permute-done((f32[256,128]{1,0:T(8,128)S(1)}, f32[256,128]{1,0:T(8,128)S(1)}, u32[]{:S(2)}, u32[]{:S(2)}) %collective-permute-start.10) | collective-permute-done | bytes 131104 | tf_op jit(solution)/shard_map/ppermute | solution.py:344
  25.9 2.8 %collective-permute-done.11.left = f32[256,256]{1,0:T(8,128)S(1)} collective-permute-done((f32[256,256]{1,0:T(8,128)S(1)}, f32[256,256]{1,0:T(8,128)S(1)}, u32[]{:S(2)}, u32[]{:S(2)}) %collective-permute-start.11) | collective-permute-done | bytes 262176 | tf_op jit(solution)/shard_map/ppermute | solution.py:341
  29.3 1.0 %collective-permute-start.14 = (f32[8,256]{1,0:T(8,128)S(1)}, f32[8,256]{1,0:T(8,128)S(1)}, u32[]{:S(2)}, u32[]{:S(2)}) collective-permute-start(f32[8,256]{1,0:T(8,128)S(1)} %far.1.refs_0_), channel_id=1, source_target_pairs={{0,2},{1,3},{2,0},{3,1},{4,6},{5,7},{6,4},{7,5},{8,10},{9,11},{10,... | collective-permute-start | bytes 24584 | tf_op jit(solution)/shard_map/ppermute | solution.py:46
  30.3 0.8 %collective-permute-start.13 = (f32[8,256]{1,0:T(8,128)S(1)}, f32[8,256]{1,0:T(8,128)S(1)}, u32[]{:S(2)}, u32[]{:S(2)}) collective-permute-start(f32[8,256]{1,0:T(8,128)S(1)} %far.1.refs_0_), channel_id=1, source_target_pairs={{0,1},{1,0},{2,3},{3,2},{4,5},{5,4},{6,7},{7,6},{8,9},{9,8},{10,11... | collective-permute-start | bytes 24584 | tf_op jit(solution)/shard_map/ppermute | solution.py:46
  31.1 1.2 %collective-permute-done.15.refs_3_ = f32[8,256]{1,0:T(8,128)S(1)} collective-permute-done((f32[8,256]{1,0:T(8,128)S(1)}, f32[8,256]{1,0:T(8,128)S(1)}, u32[]{:S(2)}, u32[]{:S(2)}) %collective-permute-start.15) | collective-permute-done | bytes 8224 | tf_op jit(solution)/shard_map/ppermute | solution.py:46
  32.3 0.7 %collective-permute-done.14.refs_2_ = f32[8,256]{1,0:T(8,128)S(1)} collective-permute-done((f32[8,256]{1,0:T(8,128)S(1)}, f32[8,256]{1,0:T(8,128)S(1)}, u32[]{:S(2)}, u32[]{:S(2)}) %collective-permute-start.14) | collective-permute-done | bytes 8224 | tf_op jit(solution)/shard_map/ppermute | solution.py:46
  33.0 3.1 %collective-permute-start.18 = (f32[8,256]{1,0:T(8,128)S(1)}, f32[8,256]{1,0:T(8,128)S(1)}, u32[]{:S(2)}, u32[]{:S(2)}) collective-permute-start(f32[8,256]{1,0:T(8,128)S(1)} %merge.2.refs_0_), channel_id=1, source_target_pairs={{0,12},{1,13},{2,14},{3,15},{4,8},{5,9},{6,10},{7,11},{8,4},{9,5},... | collective-permute-start | bytes 24584 | tf_op jit(solution)/shard_map/ppermute | solution.py:46
  36.2 1.3 %collective-permute-start.16 = (f32[8,256]{1,0:T(8,128)S(1)}, f32[8,256]{1,0:T(8,128)S(1)}, u32[]{:S(2)}, u32[]{:S(2)}) collective-permute-start(f32[8,256]{1,0:T(8,128)S(1)} %merge.2.refs_0_), channel_id=1, source_target_pairs={{0,4},{1,5},{2,6},{3,7},{4,0},{5,1},{6,2},{7,3},{8,12},{9,13},{10,... | collective-permute-start | bytes 24584 | tf_op jit(solution)/shard_map/ppermute | solution.py:46
  37.5 1.1 %collective-permute-done.18.refs_3_ = f32[8,256]{1,0:T(8,128)S(1)} collective-permute-done((f32[8,256]{1,0:T(8,128)S(1)}, f32[8,256]{1,0:T(8,128)S(1)}, u32[]{:S(2)}, u32[]{:S(2)}) %collective-permute-start.18) | collective-permute-done | bytes 8224 | tf_op jit(solution)/shard_map/ppermute | solution.py:46
  38.5 2.2 %collective-permute-done.17.refs_2_ = f32[8,256]{1,0:T(8,128)S(1)} collective-permute-done((f32[8,256]{1,0:T(8,128)S(1)}, f32[8,256]{1,0:T(8,128)S(1)}, u32[]{:S(2)}, u32[]{:S(2)}) %collective-permute-start.17) | collective-permute-done | bytes 8224 | tf_op jit(solution)/shard_map/ppermute | solution.py:46
  40.8 0.7 %multiply_subtract_fusion = f32[256,256]{1,0:T(8,128)} fusion(f32[256,256]{1,0:T(8,128)S(1)} %get-tuple-element.44.image, f32[256,256]{1,0:T(8,128)S(1)} %copy-done, f32[256]{0:T(256)S(1)} %bitcast.10, f32[256]{0:T(256)S(1)} %bitcast.9), kind=kLoop, calls=%fused_computation | loop fusion | flops 196608 | bytes 788480 | tf_op jit(solution)/shard_map/sub | solution.py:360
  (41 shorter events, 4.3 us)
Async XLA Ops:
  0.1 6.2 %copy-start = (f32[256,256]{1,0:T(8,128)S(1)}, f32[256,256]{1,0:T(8,128)}, u32[]{:S(2)}) copy-start(f32[256,256]{1,0:T(8,128)} %field.7) | copy-start | bytes 786436
  1.7 9.0 %collective-permute-start.3 = (f32[136,256]{1,0:T(8,128)S(1)}, f32[136,256]{1,0:T(8,128)S(1)}, u32[]{:S(2)}, u32[]{:S(2)}) collective-permute-start(f32[136,256]{1,0:T(8,128)S(1)} %get-tuple-element.35), channel_id=1, source_target_pairs={{0,2},{2,0},{1,3},{3,1},{4,6},{6,4},{5,7},{7,5},{8,10},{10,8},{9,1... | collective-permute-start | bytes 417800 | tf_op jit(solution)/shard_map/ppermute | solution.py:305
  4.7 3.7 %copy-start.4 = (f32[256]{0:T(256)S(1)}, f32[256]{0:T(256)}, u32[]{:S(2)}) copy-start(f32[256]{0:T(256)} %param.8) | copy-start | bytes 3076
  4.7 3.7 %copy-start.3 = (s32[2,7]{1,0:T(2,128)S(1)}, s32[2,7]{1,0:T(2,128)}, u32[]{:S(2)}) copy-start(s32[2,7]{1,0:T(2,128)} %cols.1) | copy-start | bytes 172
  4.7 7.5 %collective-permute-start.4 = (f32[136,256]{1,0:T(8,128)S(1)}, f32[136,256]{1,0:T(8,128)S(1)}, u32[]{:S(2)}, u32[]{:S(2)}) collective-permute-start(f32[136,256]{1,0:T(8,128)S(1)} %get-tuple-element.29.packed.mine.refs_0_), channel_id=1, source_target_pairs={{0,4},{4,8},{8,12},{12,0},{1,5},{5,9},{9,13},{13,1},{2,6},{6,10},{... | collective-permute-start | bytes 417800 | tf_op jit(solution)/shard_map/ppermute | solution.py:305
  6.2 10.0 %collective-permute-start = (f32[256,256]{1,0:T(8,128)S(1)}, f32[256,256]{1,0:T(8,128)S(1)}, u32[]{:S(2)}, u32[]{:S(2)}) collective-permute-start(f32[256,256]{1,0:T(8,128)S(1)} %copy-done), channel_id=1, source_target_pairs={{0,1},{1,0},{2,3},{3,2},{4,5},{5,4},{6,7},{7,6},{8,9},{9,8},{10,11... | collective-permute-start | bytes 786440 | tf_op jit(solution)/shard_map/ppermute | solution.py:308
  6.2 11.4 %collective-permute-start.5 = (f32[256,256]{1,0:T(8,128)S(1)}, f32[256,256]{1,0:T(8,128)S(1)}, u32[]{:S(2)}, u32[]{:S(2)}) collective-permute-start(f32[256,256]{1,0:T(8,128)S(1)} %copy-done), channel_id=1, source_target_pairs={{0,4},{4,8},{8,12},{12,0},{1,5},{5,9},{9,13},{13,1},{2,6},{6,10},{... | collective-permute-start | bytes 786440 | tf_op jit(solution)/shard_map/ppermute | solution.py:307
  7.8 10.1 %collective-permute-start.6 = (f32[256,256]{1,0:T(8,128)S(1)}, f32[256,256]{1,0:T(8,128)S(1)}, u32[]{:S(2)}, u32[]{:S(2)}) collective-permute-start(f32[256,256]{1,0:T(8,128)S(1)} %copy-done), channel_id=1, source_target_pairs={{0,2},{2,0},{1,3},{3,1},{4,6},{6,4},{5,7},{7,5},{8,10},{10,8},{9,1... | collective-permute-start | bytes 786440 | tf_op jit(solution)/shard_map/ppermute | solution.py:307
  8.4 1.2 %copy-start.2 = (f32[2,7,128,128]{3,2,1,0:T(8,128)S(1)}, f32[2,7,128,128]{3,2,1,0:T(8,128)}, u32[]{:S(2)}) copy-start(f32[2,7,128,128]{3,2,1,0:T(8,128)} %local.1) | copy-start | bytes 2752516
  9.5 2.6 %copy-start.1 = (f32[1,8,128,128]{3,2,1,0:T(8,128)S(1)}, f32[1,8,128,128]{3,2,1,0:T(8,128)}, u32[]{:S(2)}) copy-start(f32[1,8,128,128]{3,2,1,0:T(8,128)} %param.11) | copy-start | bytes 1572868
  10.7 2.0 %collective-permute-start.1 = (f32[256,128]{1,0:T(8,128)S(1)}, f32[256,128]{1,0:T(8,128)S(1)}, u32[]{:S(2)}, u32[]{:S(2)}) collective-permute-start(f32[256,128]{1,0:T(8,128)S(1)} %get-tuple-element.32), channel_id=1, source_target_pairs={{0,1},{1,0},{2,3},{3,2},{4,5},{5,4},{6,7},{7,6},{8,9},{9,8},{10,11... | collective-permute-start | bytes 393224 | tf_op jit(solution)/shard_map/ppermute | solution.py:329
  12.1 3.3 %collective-permute-start.2 = (f32[256,128]{1,0:T(8,128)S(1)}, f32[256,128]{1,0:T(8,128)S(1)}, u32[]{:S(2)}, u32[]{:S(2)}) collective-permute-start(f32[256,128]{1,0:T(8,128)S(1)} %get-tuple-element.33), channel_id=1, source_target_pairs={{0,1},{1,0},{2,3},{3,2},{4,5},{5,4},{6,7},{7,6},{8,9},{9,8},{10,11... | collective-permute-start | bytes 393224 | tf_op jit(solution)/shard_map/ppermute | solution.py:329
  12.7 7.5 %collective-permute-start.7 = (f32[264,128]{1,0:T(8,128)S(1)}, f32[264,128]{1,0:T(8,128)S(1)}, u32[]{:S(2)}, u32[]{:S(2)}) collective-permute-start(f32[264,128]{1,0:T(8,128)S(1)} %get-tuple-element.41), channel_id=1, source_target_pairs={{4,0},{8,4},{12,8},{0,12},{5,1},{9,5},{13,9},{1,13},{6,2},{10,6},{... | collective-permute-start | bytes 405512 | tf_op jit(solution)/shard_map/ppermute | solution.py:337
  15.4 8.0 %collective-permute-start.8 = (f32[264,128]{1,0:T(8,128)S(1)}, f32[264,128]{1,0:T(8,128)S(1)}, u32[]{:S(2)}, u32[]{:S(2)}) collective-permute-start(f32[264,128]{1,0:T(8,128)S(1)} %get-tuple-element.43), channel_id=1, source_target_pairs={{4,0},{8,4},{12,8},{0,12},{5,1},{9,5},{13,9},{1,13},{6,2},{10,6},{... | collective-permute-start | bytes 405512 | tf_op jit(solution)/shard_map/ppermute | solution.py:337
  18.3 10.4 %collective-permute-start.11 = (f32[256,256]{1,0:T(8,128)S(1)}, f32[256,256]{1,0:T(8,128)S(1)}, u32[]{:S(2)}, u32[]{:S(2)}) collective-permute-start(f32[256,256]{1,0:T(8,128)S(1)} %get-tuple-element.40.part), channel_id=1, source_target_pairs={{0,4},{4,8},{8,12},{12,0},{1,5},{5,9},{9,13},{13,1},{2,6},{6,10},{... | collective-permute-start | bytes 786440 | tf_op jit(solution)/shard_map/ppermute | solution.py:341
  20.3 5.6 %collective-permute-start.12 = (f32[264,128]{1,0:T(8,128)S(1)}, f32[264,128]{1,0:T(8,128)S(1)}, u32[]{:S(2)}, u32[]{:S(2)}) collective-permute-start(f32[264,128]{1,0:T(8,128)S(1)} %get-tuple-element.52), channel_id=1, source_target_pairs={{0,2},{2,0},{1,3},{3,1},{4,6},{6,4},{5,7},{7,5},{8,10},{10,8},{9,1... | collective-permute-start | bytes 405512 | tf_op jit(solution)/shard_map/ppermute | solution.py:352
  20.9 2.7 %collective-permute-start.9 = (f32[256,128]{1,0:T(8,128)S(1)}, f32[256,128]{1,0:T(8,128)S(1)}, u32[]{:S(2)}, u32[]{:S(2)}) collective-permute-start(f32[256,128]{1,0:T(8,128)S(1)} %get-tuple-element.42.half), channel_id=1, source_target_pairs={{0,1},{1,0},{2,3},{3,2},{4,5},{5,4},{6,7},{7,6},{8,9},{9,8},{10,11... | collective-permute-start | bytes 393224 | tf_op jit(solution)/shard_map/ppermute | solution.py:344
  23.6 1.4 %collective-permute-start.10 = (f32[256,128]{1,0:T(8,128)S(1)}, f32[256,128]{1,0:T(8,128)S(1)}, u32[]{:S(2)}, u32[]{:S(2)}) collective-permute-start(f32[256,128]{1,0:T(8,128)S(1)} %get-tuple-element.46), channel_id=1, source_target_pairs={{0,1},{1,0},{2,3},{3,2},{4,5},{5,4},{6,7},{7,6},{8,9},{9,8},{10,11... | collective-permute-start | bytes 393224 | tf_op jit(solution)/shard_map/ppermute | solution.py:344
  29.2 3.1 %collective-permute-start.15 = (f32[8,256]{1,0:T(8,128)S(1)}, f32[8,256]{1,0:T(8,128)S(1)}, u32[]{:S(2)}, u32[]{:S(2)}) collective-permute-start(f32[8,256]{1,0:T(8,128)S(1)} %far.1.refs_0_), channel_id=1, source_target_pairs={{0,3},{1,2},{2,1},{3,0},{4,7},{5,6},{6,5},{7,4},{8,11},{9,10},{10,... | collective-permute-start | bytes 24584 | tf_op jit(solution)/shard_map/ppermute | solution.py:46
  29.3 3.7 %collective-permute-start.14 = (f32[8,256]{1,0:T(8,128)S(1)}, f32[8,256]{1,0:T(8,128)S(1)}, u32[]{:S(2)}, u32[]{:S(2)}) collective-permute-start(f32[8,256]{1,0:T(8,128)S(1)} %far.1.refs_0_), channel_id=1, source_target_pairs={{0,2},{1,3},{2,0},{3,1},{4,6},{5,7},{6,4},{7,5},{8,10},{9,11},{10,... | collective-permute-start | bytes 24584 | tf_op jit(solution)/shard_map/ppermute | solution.py:46
  30.3 2.7 %collective-permute-start.13 = (f32[8,256]{1,0:T(8,128)S(1)}, f32[8,256]{1,0:T(8,128)S(1)}, u32[]{:S(2)}, u32[]{:S(2)}) collective-permute-start(f32[8,256]{1,0:T(8,128)S(1)} %far.1.refs_0_), channel_id=1, source_target_pairs={{0,1},{1,0},{2,3},{3,2},{4,5},{5,4},{6,7},{7,6},{8,9},{9,8},{10,11... | collective-permute-start | bytes 24584 | tf_op jit(solution)/shard_map/ppermute | solution.py:46
  33.0 5.5 %collective-permute-start.18 = (f32[8,256]{1,0:T(8,128)S(1)}, f32[8,256]{1,0:T(8,128)S(1)}, u32[]{:S(2)}, u32[]{:S(2)}) collective-permute-start(f32[8,256]{1,0:T(8,128)S(1)} %merge.2.refs_0_), channel_id=1, source_target_pairs={{0,12},{1,13},{2,14},{3,15},{4,8},{5,9},{6,10},{7,11},{8,4},{9,5},... | collective-permute-start | bytes 24584 | tf_op jit(solution)/shard_map/ppermute | solution.py:46
  36.2 4.5 %collective-permute-start.17 = (f32[8,256]{1,0:T(8,128)S(1)}, f32[8,256]{1,0:T(8,128)S(1)}, u32[]{:S(2)}, u32[]{:S(2)}) collective-permute-start(f32[8,256]{1,0:T(8,128)S(1)} %merge.2.refs_0_), channel_id=1, source_target_pairs={{0,8},{1,9},{2,10},{3,11},{4,12},{5,13},{6,14},{7,15},{8,0},{9,1},... | collective-permute-start | bytes 24584 | tf_op jit(solution)/shard_map/ppermute | solution.py:46
  36.2 4.5 %collective-permute-start.16 = (f32[8,256]{1,0:T(8,128)S(1)}, f32[8,256]{1,0:T(8,128)S(1)}, u32[]{:S(2)}, u32[]{:S(2)}) collective-permute-start(f32[8,256]{1,0:T(8,128)S(1)} %merge.2.refs_0_), channel_id=1, source_target_pairs={{0,4},{1,5},{2,6},{3,7},{4,0},{5,1},{6,2},{7,3},{8,12},{9,13},{10,... | collective-permute-start | bytes 24584 | tf_op jit(solution)/shard_map/ppermute | solution.py:46

commit v19 on v17

--- a/solution.py
+++ b/solution.py
@@ -70,13 +70,14 @@
 
 
 def pack_kernel(gives, *refs):
-    marks, refs = (refs[0], refs[1:]) if gives != [1] else (None, refs)
-    border, send, rows, toward, *pays, sems, table, table_sems = refs
+    border, send, rows, toward, *pays, sems, table, table_sems, both = refs
     bs = border.shape[1]
     tables = [pltpu.make_async_copy(ref, table.at[n], table_sems.at[n]) for n, ref in enumerate((rows, send, toward))]
     copies = []
     for n, (give, pay) in enumerate(zip(gives, pays)):
-        give = marks[0] if give is None else give
+        if give is None:
+            copies.append(pltpu.make_async_copy(border.at[pl.ds(2 * SIDE, 2 * SIDE)], both, sems.at[n, 0]))
+            continue
         for s in range(SIDE):
             block = pay.at[pl.ds(0, bs), pl.ds(s * bs, bs)]
             copies.append(pltpu.make_async_copy(border.at[give * SIDE + s], block, sems.at[n, s]))
@@ -90,6 +91,11 @@
             pay[pl.ds(bs + n, 1), pl.ds(0, count)] = table[n].astype(F32)
     for copy in copies:
         copy.wait()
+    facing = table[2][:, 0:1]
+    for give, pay in zip(gives, pays):
+        if give is None:
+            for s in range(SIDE):
+                pay[pl.ds(0, bs), pl.ds(s * bs, bs)] = jnp.where(facing == 3, both[SIDE + s], both[s])
 
 
 def prep_kernel(cols, marks, diag, local, packed, own, pair, low, high):
@@ -285,20 +291,20 @@
 
     def pack(gives):
         count = len(gives)
-        tables = [marks] if gives != [1] else []
         return pl.pallas_call(
             partial(pack_kernel, gives),
             name="pack",
-            in_specs=smem(len(tables)) + [pl.BlockSpec(memory_space=pl.ANY)] * 4,
+            in_specs=[pl.BlockSpec(memory_space=pl.ANY)] * 4,
             out_specs=[vmem()] * count,
             out_shape=[pltpu.VMEM(full, F32)] * count,
             scratch_shapes=[
                 pltpu.SemaphoreType.DMA((count, SIDE)),
                 pltpu.VMEM((3, 1, 4 * SIDE), jnp.int32),
                 pltpu.SemaphoreType.DMA((3,)),
+                pltpu.VMEM((2 * SIDE, bs, bs), F32),
             ],
             compiler_params=pltpu.CompilerParams(vmem_limit_bytes=LIMIT),
-        )(*tables, *[pltpu.with_memory_space_constraint(a, pltpu.HBM) for a in (border, border_send, border_rows)], toward)
+        )(*[pltpu.with_memory_space_constraint(a, pltpu.HBM) for a in (border, border_send, border_rows)], toward)
 
     packed = pack(gives)
     pays = [lax.ppermute(pay, axis, perm) for pay, (axis, perm) in zip(packed, sends)]

time: 41 us -> 41.3 us (level)
  local copies, waits for them, and re-layouts: 1.2 us -> 1.87 us
    unnamed x10, local copies, waits for them, and re-layouts: 1.2 us -> 1.87 us
where the time goes in v19:
time: 41.3 us; the launch traced here: 41.1 us
  starting transfers between devices  20.2 us (49%)
  waiting for transfers between devices  13 us (31%)
  Pallas kernels  5.14 us (12%)
  local copies, waits for them, and re-layouts  1.87 us (5%)
  other arithmetic  0.85 us (2%)
    ppermute x6, starting transfers between devices, join(): lax.ppermute(state, AXES, [(i, i ^ m) for i in range(count)])  6.39 us
    ppermute x2, starting transfers between devices, shards(): lax.ppermute(pay, axis, perm)  3.61 us
    ppermute x6, waiting for transfers between devices, join(): lax.ppermute(state, AXES, [(i, i ^ m) for i in range(count)])  3.5 us
    ppermute x2, starting transfers between devices, shards(): fields = [lax.ppermute(right_side, axis, perm) for axis, perm in sends]  3.07 us
    pallas_call x10, Pallas kernels, run(): pl.pallas_call(kernel, name=name, in_specs=[vmem()] * len(args), out_spec...  2.86 us
    ppermute x2, waiting for transfers between devices, shards(): fields = [lax.ppermute(right_side, axis, perm) for axis, perm in sends]  2.8 us
    ppermute x2, starting transfers between devices, shards(): from_right = [lax.ppermute(piece, 'gx', left) for piece in to_left]  2.77 us
    ppermute x1, waiting for transfers between devices, shards(): left_w = lax.ppermute(part, 'gx', right)  2.18 us
  transfers between devices with their start and end apart: 19, of which 12 were waited for; matrix products, arithmetic and copies ran while one was open for 0% of the time, Pallas kernels for 8%

profile of v19, /device:TPU:0, one launch (start us, length us, event | category | flops | bytes accessed | tf_op | source)
XLA Modules:
  0.0 41.1 jit_solution(7862023615449590995)
XLA Ops:
  0.0 1.2 %pack.1 = (f32[136,256]{1,0:T(8,128)S(1)}, f32[136,256]{1,0:T(8,128)S(1)}) custom-call(f32[8,128,128]{2,1,0:T(8,128)} %bitcast.6, s32[1,8]{1,0:T(1,128)} %refs_1_.1, s32[1,8]{1,0:T(1,128)} %refs_2_.1, s32[1,8]{1,0:T(1,128)S(1)} %broadcast_in_dim.3.refs_3_), custom_call_target="tpu_custom_call" | custom-call | tf_op jit(solution)/shard_map/pack/pallas_call | solution.py:294
  1.2 3.1 %collective-permute-start.3 = (f32[136,256]{1,0:T(8,128)S(1)}, f32[136,256]{1,0:T(8,128)S(1)}, u32[]{:S(2)}, u32[]{:S(2)}) collective-permute-start(f32[136,256]{1,0:T(8,128)S(1)} %get-tuple-element.29.packed.mine.refs_0_), channel_id=1, source_target_pairs={{0,4},{4,8},{8,12},{12,0},{1,5},{5,9},{9,13},{13,1},{2,6},{6,10},{... | collective-permute-start | bytes 417800 | tf_op jit(solution)/shard_map/ppermute | solution.py:310
  4.4 0.6 %copy-done.4 = f32[256]{0:T(256)S(1)} copy-done((f32[256]{0:T(256)S(1)}, f32[256]{0:T(256)}, u32[]{:S(2)}) %copy-start.4) | copy-done | bytes 1048
  5.0 1.2 %copy-done.2 = f32[2,7,128,128]{3,2,1,0:T(8,128)S(1)} copy-done((f32[2,7,128,128]{3,2,1,0:T(8,128)S(1)}, f32[2,7,128,128]{3,2,1,0:T(8,128)}, u32[]{:S(2)}) %copy-start.2) | copy-done | bytes 917528
  6.2 1.1 %prep.1 = (f32[256,256]{1,0:T(8,128)S(1)}, f32[256,256]{1,0:T(8,128)S(1)}, f32[256,128]{1,0:T(8,128)S(1)}, f32[256,128]{1,0:T(8,128)S(1)}) custom-call(s32[2,7]{1,0:T(2,128)S(1)} %copy-done.3, s32[2]{0:T(128)S(1)} %pad_add_fusion.marks, f32[1,256]{1,0:T(1,128)S(1)} %bitcast.9, f32[2,7,128,128]{3,2,1,0:T(8,128)S(1)} %copy-done.2, ...), custom_call_target="tpu_custom_call" | custom-call | flops 16777216 | bytes 1048576 | tf_op jit(solution)/shard_map/prep/pallas_call | solution.py:318
  7.9 1.6 %collective-permute-start.4 = (f32[256,256]{1,0:T(8,128)S(1)}, f32[256,256]{1,0:T(8,128)S(1)}, u32[]{:S(2)}, u32[]{:S(2)}) collective-permute-start(f32[256,256]{1,0:T(8,128)S(1)} %copy-done), channel_id=1, source_target_pairs={{0,4},{4,8},{8,12},{12,0},{1,5},{5,9},{9,13},{13,1},{2,6},{6,10},{... | collective-permute-start | bytes 786440 | tf_op jit(solution)/shard_map/ppermute | solution.py:312
  9.5 1.5 %collective-permute-start.6 = (f32[256,256]{1,0:T(8,128)S(1)}, f32[256,256]{1,0:T(8,128)S(1)}, u32[]{:S(2)}, u32[]{:S(2)}) collective-permute-start(f32[256,256]{1,0:T(8,128)S(1)} %copy-done), channel_id=1, source_target_pairs={{0,2},{2,0},{1,3},{3,1},{4,6},{6,4},{5,7},{7,5},{8,10},{10,8},{9,1... | collective-permute-start | bytes 786440 | tf_op jit(solution)/shard_map/ppermute | solution.py:312
  12.0 0.9 %collective-permute-done.2.high = f32[256,128]{1,0:T(8,128)S(1)} collective-permute-done((f32[256,128]{1,0:T(8,128)S(1)}, f32[256,128]{1,0:T(8,128)S(1)}, u32[]{:S(2)}, u32[]{:S(2)}) %collective-permute-start.2) | collective-permute-done | bytes 131104 | tf_op jit(solution)/shard_map/ppermute | solution.py:334
  12.9 2.2 %collective-permute-start.7 = (f32[264,128]{1,0:T(8,128)S(1)}, f32[264,128]{1,0:T(8,128)S(1)}, u32[]{:S(2)}, u32[]{:S(2)}) collective-permute-start(f32[264,128]{1,0:T(8,128)S(1)} %get-tuple-element.40), channel_id=1, source_target_pairs={{4,0},{8,4},{12,8},{0,12},{5,1},{9,5},{13,9},{1,13},{6,2},{10,6},{... | collective-permute-start | bytes 405512 | tf_op jit(solution)/shard_map/ppermute | solution.py:338
  16.1 2.8 %collective-permute-done.4.there = f32[256,256]{1,0:T(8,128)S(1)} collective-permute-done((f32[256,256]{1,0:T(8,128)S(1)}, f32[256,256]{1,0:T(8,128)S(1)}, u32[]{:S(2)}, u32[]{:S(2)}) %collective-permute-start.4) | collective-permute-done | bytes 262176 | tf_op jit(solution)/shard_map/ppermute | solution.py:312
  19.1 1.3 %collective-permute-done.5.pay = f32[136,256]{1,0:T(8,128)S(1)} collective-permute-done((f32[136,256]{1,0:T(8,128)S(1)}, f32[136,256]{1,0:T(8,128)S(1)}, u32[]{:S(2)}, u32[]{:S(2)}) %collective-permute-start.5) | collective-permute-done | bytes 139296 | tf_op jit(solution)/shard_map/ppermute | solution.py:310
  20.9 1.6 %collective-permute-start.11 = (f32[256,256]{1,0:T(8,128)S(1)}, f32[256,256]{1,0:T(8,128)S(1)}, u32[]{:S(2)}, u32[]{:S(2)}) collective-permute-start(f32[256,256]{1,0:T(8,128)S(1)} %get-tuple-element.39.part), channel_id=1, source_target_pairs={{0,4},{4,8},{8,12},{12,0},{1,5},{5,9},{9,13},{13,1},{2,6},{6,10},{... | collective-permute-start | bytes 786440 | tf_op jit(solution)/shard_map/ppermute | solution.py:344
  22.6 1.6 %collective-permute-start.12 = (f32[264,128]{1,0:T(8,128)S(1)}, f32[264,128]{1,0:T(8,128)S(1)}, u32[]{:S(2)}, u32[]{:S(2)}) collective-permute-start(f32[264,128]{1,0:T(8,128)S(1)} %get-tuple-element.52), channel_id=1, source_target_pairs={{0,2},{2,0},{1,3},{3,1},{4,6},{6,4},{5,7},{7,5},{8,10},{10,8},{9,1... | collective-permute-start | bytes 405512 | tf_op jit(solution)/shard_map/ppermute | solution.py:355
  24.3 0.6 %collective-permute-start.10 = (f32[256,128]{1,0:T(8,128)S(1)}, f32[256,128]{1,0:T(8,128)S(1)}, u32[]{:S(2)}, u32[]{:S(2)}) collective-permute-start(f32[256,128]{1,0:T(8,128)S(1)} %get-tuple-element.45), channel_id=1, source_target_pairs={{0,1},{1,0},{2,3},{3,2},{4,5},{5,4},{6,7},{7,6},{8,9},{9,8},{10,11... | collective-permute-start | bytes 393224 | tf_op jit(solution)/shard_map/ppermute | solution.py:347
  24.9 0.7 %collective-permute-done.9.mate_out = f32[256,128]{1,0:T(8,128)S(1)} collective-permute-done((f32[256,128]{1,0:T(8,128)S(1)}, f32[256,128]{1,0:T(8,128)S(1)}, u32[]{:S(2)}, u32[]{:S(2)}) %collective-permute-start.9) | collective-permute-done | bytes 131104 | tf_op jit(solution)/shard_map/ppermute | solution.py:347
  26.4 1.3 %collective-permute-done.12.refs_3_ = f32[264,128]{1,0:T(8,128)S(1)} collective-permute-done((f32[264,128]{1,0:T(8,128)S(1)}, f32[264,128]{1,0:T(8,128)S(1)}, u32[]{:S(2)}, u32[]{:S(2)}) %collective-permute-start.12) | collective-permute-done | bytes 135200 | tf_op jit(solution)/shard_map/ppermute | solution.py:355
  27.7 2.2 %collective-permute-done.11.left = f32[256,256]{1,0:T(8,128)S(1)} collective-permute-done((f32[256,256]{1,0:T(8,128)S(1)}, f32[256,256]{1,0:T(8,128)S(1)}, u32[]{:S(2)}, u32[]{:S(2)}) %collective-permute-start.11) | collective-permute-done | bytes 262176 | tf_op jit(solution)/shard_map/ppermute | solution.py:344
  30.5 1.6 %collective-permute-start.14 = (f32[8,256]{1,0:T(8,128)S(1)}, f32[8,256]{1,0:T(8,128)S(1)}, u32[]{:S(2)}, u32[]{:S(2)}) collective-permute-start(f32[8,256]{1,0:T(8,128)S(1)} %far.1.refs_0_), channel_id=1, source_target_pairs={{0,2},{1,3},{2,0},{3,1},{4,6},{5,7},{6,4},{7,5},{8,10},{9,11},{10,... | collective-permute-start | bytes 24584 | tf_op jit(solution)/shard_map/ppermute | solution.py:46
  32.3 1.3 %collective-permute-done.15.refs_3_ = f32[8,256]{1,0:T(8,128)S(1)} collective-permute-done((f32[8,256]{1,0:T(8,128)S(1)}, f32[8,256]{1,0:T(8,128)S(1)}, u32[]{:S(2)}, u32[]{:S(2)}) %collective-permute-start.15) | collective-permute-done | bytes 8224 | tf_op jit(solution)/shard_map/ppermute | solution.py:46
  33.6 0.6 %collective-permute-done.14.refs_2_ = f32[8,256]{1,0:T(8,128)S(1)} collective-permute-done((f32[8,256]{1,0:T(8,128)S(1)}, f32[8,256]{1,0:T(8,128)S(1)}, u32[]{:S(2)}, u32[]{:S(2)}) %collective-permute-start.14) | collective-permute-done | bytes 8224 | tf_op jit(solution)/shard_map/ppermute | solution.py:46
  34.2 1.3 %collective-permute-start.18 = (f32[8,256]{1,0:T(8,128)S(1)}, f32[8,256]{1,0:T(8,128)S(1)}, u32[]{:S(2)}, u32[]{:S(2)}) collective-permute-start(f32[8,256]{1,0:T(8,128)S(1)} %merge.2.refs_0_), channel_id=1, source_target_pairs={{0,12},{1,13},{2,14},{3,15},{4,8},{5,9},{6,10},{7,11},{8,4},{9,5},... | collective-permute-start | bytes 24584 | tf_op jit(solution)/shard_map/ppermute | solution.py:46
  35.5 3.1 %collective-permute-start.16 = (f32[8,256]{1,0:T(8,128)S(1)}, f32[8,256]{1,0:T(8,128)S(1)}, u32[]{:S(2)}, u32[]{:S(2)}) collective-permute-start(f32[8,256]{1,0:T(8,128)S(1)} %merge.2.refs_0_), channel_id=1, source_target_pairs={{0,4},{1,5},{2,6},{3,7},{4,0},{5,1},{6,2},{7,3},{8,12},{9,13},{10,... | collective-permute-start | bytes 24584 | tf_op jit(solution)/shard_map/ppermute | solution.py:46
  38.7 1.1 %collective-permute-done.18.refs_3_ = f32[8,256]{1,0:T(8,128)S(1)} collective-permute-done((f32[8,256]{1,0:T(8,128)S(1)}, f32[8,256]{1,0:T(8,128)S(1)}, u32[]{:S(2)}, u32[]{:S(2)}) %collective-permute-start.18) | collective-permute-done | bytes 8224 | tf_op jit(solution)/shard_map/ppermute | solution.py:46
  40.4 0.7 %multiply_subtract_fusion = f32[256,256]{1,0:T(8,128)} fusion(f32[256,256]{1,0:T(8,128)S(1)} %get-tuple-element.43.image, f32[256,256]{1,0:T(8,128)S(1)} %copy-done, f32[256]{0:T(256)S(1)} %bitcast.11, f32[256]{0:T(256)S(1)} %bitcast.10), kind=kLoop, calls=%fused_computation | loop fusion | flops 196608 | bytes 788480 | tf_op jit(solution)/shard_map/sub | solution.py:363
  (41 shorter events, 6.0 us)
Async XLA Ops:
  1.2 10.3 %collective-permute-start.3 = (f32[136,256]{1,0:T(8,128)S(1)}, f32[136,256]{1,0:T(8,128)S(1)}, u32[]{:S(2)}, u32[]{:S(2)}) collective-permute-start(f32[136,256]{1,0:T(8,128)S(1)} %get-tuple-element.29.packed.mine.refs_0_), channel_id=1, source_target_pairs={{0,4},{4,8},{8,12},{12,0},{1,5},{5,9},{9,13},{13,1},{2,6},{6,10},{... | collective-permute-start | bytes 417800 | tf_op jit(solution)/shard_map/ppermute | solution.py:310
  4.3 0.7 %copy-start.4 = (f32[256]{0:T(256)S(1)}, f32[256]{0:T(256)}, u32[]{:S(2)}) copy-start(f32[256]{0:T(256)} %param.8) | copy-start | bytes 3076
  4.4 0.7 %copy-start.3 = (s32[2,7]{1,0:T(2,128)S(1)}, s32[2,7]{1,0:T(2,128)}, u32[]{:S(2)}) copy-start(s32[2,7]{1,0:T(2,128)} %cols.1) | copy-start | bytes 172
  5.0 1.2 %copy-start.2 = (f32[2,7,128,128]{3,2,1,0:T(8,128)S(1)}, f32[2,7,128,128]{3,2,1,0:T(8,128)}, u32[]{:S(2)}) copy-start(f32[2,7,128,128]{3,2,1,0:T(8,128)} %local.1) | copy-start | bytes 2752516
  6.2 1.2 %copy-start = (f32[256,256]{1,0:T(8,128)S(1)}, f32[256,256]{1,0:T(8,128)}, u32[]{:S(2)}) copy-start(f32[256,256]{1,0:T(8,128)} %field.7) | copy-start | bytes 786436
  6.2 5.3 %copy-start.1 = (f32[1,8,128,128]{3,2,1,0:T(8,128)S(1)}, f32[1,8,128,128]{3,2,1,0:T(8,128)}, u32[]{:S(2)}) copy-start(f32[1,8,128,128]{3,2,1,0:T(8,128)} %param.11) | copy-start | bytes 1572868
  7.3 3.6 %collective-permute-start.1 = (f32[256,128]{1,0:T(8,128)S(1)}, f32[256,128]{1,0:T(8,128)S(1)}, u32[]{:S(2)}, u32[]{:S(2)}) collective-permute-start(f32[256,128]{1,0:T(8,128)S(1)} %get-tuple-element.32), channel_id=1, source_target_pairs={{0,1},{1,0},{2,3},{3,2},{4,5},{5,4},{6,7},{7,6},{8,9},{9,8},{10,11... | collective-permute-start | bytes 393224 | tf_op jit(solution)/shard_map/ppermute | solution.py:334
  7.4 7.7 %collective-permute-start = (f32[256,256]{1,0:T(8,128)S(1)}, f32[256,256]{1,0:T(8,128)S(1)}, u32[]{:S(2)}, u32[]{:S(2)}) collective-permute-start(f32[256,256]{1,0:T(8,128)S(1)} %copy-done), channel_id=1, source_target_pairs={{0,1},{1,0},{2,3},{3,2},{4,5},{5,4},{6,7},{7,6},{8,9},{9,8},{10,11... | collective-permute-start | bytes 786440 | tf_op jit(solution)/shard_map/ppermute | solution.py:313
  7.9 11.0 %collective-permute-start.4 = (f32[256,256]{1,0:T(8,128)S(1)}, f32[256,256]{1,0:T(8,128)S(1)}, u32[]{:S(2)}, u32[]{:S(2)}) collective-permute-start(f32[256,256]{1,0:T(8,128)S(1)} %copy-done), channel_id=1, source_target_pairs={{0,4},{4,8},{8,12},{12,0},{1,5},{5,9},{9,13},{13,1},{2,6},{6,10},{... | collective-permute-start | bytes 786440 | tf_op jit(solution)/shard_map/ppermute | solution.py:312
  9.5 11.0 %collective-permute-start.6 = (f32[256,256]{1,0:T(8,128)S(1)}, f32[256,256]{1,0:T(8,128)S(1)}, u32[]{:S(2)}, u32[]{:S(2)}) collective-permute-start(f32[256,256]{1,0:T(8,128)S(1)} %copy-done), channel_id=1, source_target_pairs={{0,2},{2,0},{1,3},{3,1},{4,6},{6,4},{5,7},{7,5},{8,10},{10,8},{9,1... | collective-permute-start | bytes 786440 | tf_op jit(solution)/shard_map/ppermute | solution.py:312
  11.0 9.5 %collective-permute-start.5 = (f32[136,256]{1,0:T(8,128)S(1)}, f32[136,256]{1,0:T(8,128)S(1)}, u32[]{:S(2)}, u32[]{:S(2)}) collective-permute-start(f32[136,256]{1,0:T(8,128)S(1)} %get-tuple-element.38), channel_id=1, source_target_pairs={{0,2},{2,0},{1,3},{3,1},{4,6},{6,4},{5,7},{7,5},{8,10},{10,8},{9,1... | collective-permute-start | bytes 417800 | tf_op jit(solution)/shard_map/ppermute | solution.py:310
  11.5 1.3 %collective-permute-start.2 = (f32[256,128]{1,0:T(8,128)S(1)}, f32[256,128]{1,0:T(8,128)S(1)}, u32[]{:S(2)}, u32[]{:S(2)}) collective-permute-start(f32[256,128]{1,0:T(8,128)S(1)} %get-tuple-element.33), channel_id=1, source_target_pairs={{0,1},{1,0},{2,3},{3,2},{4,5},{5,4},{6,7},{7,6},{8,9},{9,8},{10,11... | collective-permute-start | bytes 393224 | tf_op jit(solution)/shard_map/ppermute | solution.py:334
  12.9 9.7 %collective-permute-start.7 = (f32[264,128]{1,0:T(8,128)S(1)}, f32[264,128]{1,0:T(8,128)S(1)}, u32[]{:S(2)}, u32[]{:S(2)}) collective-permute-start(f32[264,128]{1,0:T(8,128)S(1)} %get-tuple-element.40), channel_id=1, source_target_pairs={{4,0},{8,4},{12,8},{0,12},{5,1},{9,5},{13,9},{1,13},{6,2},{10,6},{... | collective-permute-start | bytes 405512 | tf_op jit(solution)/shard_map/ppermute | solution.py:338
  15.1 9.1 %collective-permute-start.8 = (f32[264,128]{1,0:T(8,128)S(1)}, f32[264,128]{1,0:T(8,128)S(1)}, u32[]{:S(2)}, u32[]{:S(2)}) collective-permute-start(f32[264,128]{1,0:T(8,128)S(1)} %get-tuple-element.42), channel_id=1, source_target_pairs={{4,0},{8,4},{12,8},{0,12},{5,1},{9,5},{13,9},{1,13},{6,2},{10,6},{... | collective-permute-start | bytes 405512 | tf_op jit(solution)/shard_map/ppermute | solution.py:338
  20.9 9.0 %collective-permute-start.11 = (f32[256,256]{1,0:T(8,128)S(1)}, f32[256,256]{1,0:T(8,128)S(1)}, u32[]{:S(2)}, u32[]{:S(2)}) collective-permute-start(f32[256,256]{1,0:T(8,128)S(1)} %get-tuple-element.39.part), channel_id=1, source_target_pairs={{0,4},{4,8},{8,12},{12,0},{1,5},{5,9},{9,13},{13,1},{2,6},{6,10},{... | collective-permute-start | bytes 786440 | tf_op jit(solution)/shard_map/ppermute | solution.py:344
  22.6 5.1 %collective-permute-start.12 = (f32[264,128]{1,0:T(8,128)S(1)}, f32[264,128]{1,0:T(8,128)S(1)}, u32[]{:S(2)}, u32[]{:S(2)}) collective-permute-start(f32[264,128]{1,0:T(8,128)S(1)} %get-tuple-element.52), channel_id=1, source_target_pairs={{0,2},{2,0},{1,3},{3,1},{4,6},{6,4},{5,7},{7,5},{8,10},{10,8},{9,1... | collective-permute-start | bytes 405512 | tf_op jit(solution)/shard_map/ppermute | solution.py:355
  24.2 1.3 %collective-permute-start.9 = (f32[256,128]{1,0:T(8,128)S(1)}, f32[256,128]{1,0:T(8,128)S(1)}, u32[]{:S(2)}, u32[]{:S(2)}) collective-permute-start(f32[256,128]{1,0:T(8,128)S(1)} %get-tuple-element.41.half), channel_id=1, source_target_pairs={{0,1},{1,0},{2,3},{3,2},{4,5},{5,4},{6,7},{7,6},{8,9},{9,8},{10,11... | collective-permute-start | bytes 393224 | tf_op jit(solution)/shard_map/ppermute | solution.py:347
  24.3 1.6 %collective-permute-start.10 = (f32[256,128]{1,0:T(8,128)S(1)}, f32[256,128]{1,0:T(8,128)S(1)}, u32[]{:S(2)}, u32[]{:S(2)}) collective-permute-start(f32[256,128]{1,0:T(8,128)S(1)} %get-tuple-element.45), channel_id=1, source_target_pairs={{0,1},{1,0},{2,3},{3,2},{4,5},{5,4},{6,7},{7,6},{8,9},{9,8},{10,11... | collective-permute-start | bytes 393224 | tf_op jit(solution)/shard_map/ppermute | solution.py:347
  30.4 3.2 %collective-permute-start.15 = (f32[8,256]{1,0:T(8,128)S(1)}, f32[8,256]{1,0:T(8,128)S(1)}, u32[]{:S(2)}, u32[]{:S(2)}) collective-permute-start(f32[8,256]{1,0:T(8,128)S(1)} %far.1.refs_0_), channel_id=1, source_target_pairs={{0,3},{1,2},{2,1},{3,0},{4,7},{5,6},{6,5},{7,4},{8,11},{9,10},{10,... | collective-permute-start | bytes 24584 | tf_op jit(solution)/shard_map/ppermute | solution.py:46
  30.5 3.7 %collective-permute-start.14 = (f32[8,256]{1,0:T(8,128)S(1)}, f32[8,256]{1,0:T(8,128)S(1)}, u32[]{:S(2)}, u32[]{:S(2)}) collective-permute-start(f32[8,256]{1,0:T(8,128)S(1)} %far.1.refs_0_), channel_id=1, source_target_pairs={{0,2},{1,3},{2,0},{3,1},{4,6},{5,7},{6,4},{7,5},{8,10},{9,11},{10,... | collective-permute-start | bytes 24584 | tf_op jit(solution)/shard_map/ppermute | solution.py:46
  32.0 2.2 %collective-permute-start.13 = (f32[8,256]{1,0:T(8,128)S(1)}, f32[8,256]{1,0:T(8,128)S(1)}, u32[]{:S(2)}, u32[]{:S(2)}) collective-permute-start(f32[8,256]{1,0:T(8,128)S(1)} %far.1.refs_0_), channel_id=1, source_target_pairs={{0,1},{1,0},{2,3},{3,2},{4,5},{5,4},{6,7},{7,6},{8,9},{9,8},{10,11... | collective-permute-start | bytes 24584 | tf_op jit(solution)/shard_map/ppermute | solution.py:46
  34.2 5.5 %collective-permute-start.18 = (f32[8,256]{1,0:T(8,128)S(1)}, f32[8,256]{1,0:T(8,128)S(1)}, u32[]{:S(2)}, u32[]{:S(2)}) collective-permute-start(f32[8,256]{1,0:T(8,128)S(1)} %merge.2.refs_0_), channel_id=1, source_target_pairs={{0,12},{1,13},{2,14},{3,15},{4,8},{5,9},{6,10},{7,11},{8,4},{9,5},... | collective-permute-start | bytes 24584 | tf_op jit(solution)/shard_map/ppermute | solution.py:46
  35.5 4.5 %collective-permute-start.17 = (f32[8,256]{1,0:T(8,128)S(1)}, f32[8,256]{1,0:T(8,128)S(1)}, u32[]{:S(2)}, u32[]{:S(2)}) collective-permute-start(f32[8,256]{1,0:T(8,128)S(1)} %merge.2.refs_0_), channel_id=1, source_target_pairs={{0,8},{1,9},{2,10},{3,11},{4,12},{5,13},{6,14},{7,15},{8,0},{9,1},... | collective-permute-start | bytes 24584 | tf_op jit(solution)/shard_map/ppermute | solution.py:46
  35.5 4.8 %collective-permute-start.16 = (f32[8,256]{1,0:T(8,128)S(1)}, f32[8,256]{1,0:T(8,128)S(1)}, u32[]{:S(2)}, u32[]{:S(2)}) collective-permute-start(f32[8,256]{1,0:T(8,128)S(1)} %merge.2.refs_0_), channel_id=1, source_target_pairs={{0,4},{1,5},{2,6},{3,7},{4,0},{5,1},{6,2},{7,3},{8,12},{9,13},{10,... | collective-permute-start | bytes 24584 | tf_op jit(solution)/shard_map/ppermute | solution.py:46

commit v20 on v18

--- a/solution.py
+++ b/solution.py
@@ -70,13 +70,14 @@
 
 
 def pack_kernel(gives, *refs):
-    marks, refs = (refs[0], refs[1:]) if gives != [1] else (None, refs)
-    border, send, rows, toward, *pays, sems, table, table_sems = refs
+    border, send, rows, toward, *pays, sems, table, table_sems, both = refs
     bs = border.shape[1]
     tables = [pltpu.make_async_copy(ref, table.at[n], table_sems.at[n]) for n, ref in enumerate((rows, send, toward))]
     copies = []
     for n, (give, pay) in enumerate(zip(gives, pays)):
-        give = marks[0] if give is None else give
+        if give is None:
+            copies.append(pltpu.make_async_copy(border.at[pl.ds(2 * SIDE, 2 * SIDE)], both, sems.at[n, 0]))
+            continue
         for s in range(SIDE):
             block = pay.at[pl.ds(0, bs), pl.ds(s * bs, bs)]
             copies.append(pltpu.make_async_copy(border.at[give * SIDE + s], block, sems.at[n, s]))
@@ -90,6 +91,11 @@
             pay[pl.ds(bs + n, 1), pl.ds(0, count)] = table[n].astype(F32)
     for copy in copies:
         copy.wait()
+    facing = table[2][:, 0:1]
+    for give, pay in zip(gives, pays):
+        if give is None:
+            for s in range(SIDE):
+                pay[pl.ds(0, bs), pl.ds(s * bs, bs)] = jnp.where(facing == 3, both[SIDE + s], both[s])
 
 
 def prep_kernel(cols, marks, diag, local, packed, own, pair, low, high):
@@ -286,20 +292,20 @@
 
     def pack(gives):
         count = len(gives)
-        tables = [marks] if gives != [1] else []
         return pl.pallas_call(
             partial(pack_kernel, gives),
             name="pack",
-            in_specs=smem(len(tables)) + [pl.BlockSpec(memory_space=pl.ANY)] * 4,
+            in_specs=[pl.BlockSpec(memory_space=pl.ANY)] * 4,
             out_specs=[vmem()] * count,
             out_shape=[pltpu.VMEM(full, F32)] * count,
             scratch_shapes=[
                 pltpu.SemaphoreType.DMA((count, SIDE)),
                 pltpu.VMEM((3, 1, 4 * SIDE), jnp.int32),
                 pltpu.SemaphoreType.DMA((3,)),
+                pltpu.VMEM((2 * SIDE, bs, bs), F32),
             ],
             compiler_params=pltpu.CompilerParams(vmem_limit_bytes=LIMIT),
-        )(*tables, *[pltpu.with_memory_space_constraint(a, pltpu.HBM) for a in (border, border_send, border_rows)], toward)
+        )(*[pltpu.with_memory_space_constraint(a, pltpu.HBM) for a in (border, border_send, border_rows)], toward)
 
     packed = pack(gives)
     pays = [lax.ppermute(pay, axis, perm) for pay, (axis, perm) in zip(packed, sends)]

time: 41.7 us -> 41.9 us (level)
  local copies, waits for them, and re-layouts: 1.2 us -> 1.87 us
    ppermute x2, waiting for transfers between devices: 1.41 us -> 0.67 us  [shards(): lax.ppermute(pay, axis, perm)]
    unnamed x10, local copies, waits for them, and re-layouts: 1.19 us -> 1.87 us
  transfers between devices with their start and end apart: 19 -> 19, of which waited for: 11 -> 13; matrix products, arithmetic and copies ran while one was open for 0% -> 0% of each run, Pallas kernels for 8% -> 8%
where the time goes in v20:
time: 41.9 us; the launch traced here: 41.8 us
  starting transfers between devices  17.7 us (42%)
  waiting for transfers between devices  16.1 us (38%)
  Pallas kernels  5.1 us (12%)
  local copies, waits for them, and re-layouts  1.87 us (4%)
  other arithmetic  0.85 us (2%)
    ppermute x6, starting transfers between devices, join(): lax.ppermute(state, AXES, [(i, i ^ m) for i in range(count)])  6.59 us
    ppermute x6, waiting for transfers between devices, join(): lax.ppermute(state, AXES, [(i, i ^ m) for i in range(count)])  5.52 us
    ppermute x2, starting transfers between devices, shards(): lax.ppermute(pay, axis, perm)  4.58 us
    ppermute x2, waiting for transfers between devices, shards(): from_right = [lax.ppermute(piece, 'gx', left) for piece in to_left]  4.21 us
    ppermute x2, starting transfers between devices, shards(): from_right = [lax.ppermute(piece, 'gx', left) for piece in to_left]  3.39 us
    ppermute x1, waiting for transfers between devices, shards(): left_w = lax.ppermute(part, 'gx', right)  2.8 us
    pallas_call x10, Pallas kernels, run(): pl.pallas_call(kernel, name=name, in_specs=[vmem()] * len(args), out_spec...  2.78 us
    ppermute x2, starting transfers between devices, shards(): fields = [lax.ppermute(right_side, axis, perm) for axis, perm in sends]  2.11 us
  transfers between devices with their start and end apart: 19, of which 13 were waited for; matrix products, arithmetic and copies ran while one was open for 0% of the time, Pallas kernels for 8%

profile of v20, /device:TPU:0, one launch (start us, length us, event | category | flops | bytes accessed | tf_op | source)
XLA Modules:
  0.0 41.8 jit_solution(13595791127563593150)
XLA Ops:
  0.0 1.2 %pack.1 = (f32[136,256]{1,0:T(8,128)S(1)}, f32[136,256]{1,0:T(8,128)S(1)}) custom-call(f32[8,128,128]{2,1,0:T(8,128)} %bitcast.6, s32[1,8]{1,0:T(1,128)} %refs_1_.1, s32[1,8]{1,0:T(1,128)} %refs_2_.1, s32[1,8]{1,0:T(1,128)S(1)} %broadcast_in_dim.3.refs_3_), custom_call_target="tpu_custom_call" | custom-call | tf_op jit(solution)/shard_map/pack/pallas_call | solution.py:295
  1.2 3.0 %collective-permute-start.3 = (f32[136,256]{1,0:T(8,128)S(1)}, f32[136,256]{1,0:T(8,128)S(1)}, u32[]{:S(2)}, u32[]{:S(2)}) collective-permute-start(f32[136,256]{1,0:T(8,128)S(1)} %get-tuple-element.35), channel_id=1, source_target_pairs={{0,2},{2,0},{1,3},{3,1},{4,6},{6,4},{5,7},{7,5},{8,10},{10,8},{9,1... | collective-permute-start | bytes 417800 | tf_op jit(solution)/shard_map/ppermute | solution.py:311
  4.2 1.6 %collective-permute-start.4 = (f32[136,256]{1,0:T(8,128)S(1)}, f32[136,256]{1,0:T(8,128)S(1)}, u32[]{:S(2)}, u32[]{:S(2)}) collective-permute-start(f32[136,256]{1,0:T(8,128)S(1)} %get-tuple-element.29.packed.mine.refs_0_), channel_id=1, source_target_pairs={{0,4},{4,8},{8,12},{12,0},{1,5},{5,9},{9,13},{13,1},{2,6},{6,10},{... | collective-permute-start | bytes 417800 | tf_op jit(solution)/shard_map/ppermute | solution.py:311
  5.8 1.6 %collective-permute-start.5 = (f32[256,256]{1,0:T(8,128)S(1)}, f32[256,256]{1,0:T(8,128)S(1)}, u32[]{:S(2)}, u32[]{:S(2)}) collective-permute-start(f32[256,256]{1,0:T(8,128)S(1)} %copy-done), channel_id=1, source_target_pairs={{0,4},{4,8},{8,12},{12,0},{1,5},{5,9},{9,13},{13,1},{2,6},{6,10},{... | collective-permute-start | bytes 786440 | tf_op jit(solution)/shard_map/ppermute | solution.py:313
  8.7 1.2 %copy-done.2 = f32[2,7,128,128]{3,2,1,0:T(8,128)S(1)} copy-done((f32[2,7,128,128]{3,2,1,0:T(8,128)S(1)}, f32[2,7,128,128]{3,2,1,0:T(8,128)}, u32[]{:S(2)}) %copy-start.2) | copy-done | bytes 917528
  9.9 1.1 %prep.1 = (f32[256,256]{1,0:T(8,128)S(1)}, f32[256,256]{1,0:T(8,128)S(1)}, f32[256,128]{1,0:T(8,128)S(1)}, f32[256,128]{1,0:T(8,128)S(1)}) custom-call(s32[2,7]{1,0:T(2,128)S(1)} %copy-done.3, s32[2]{0:T(128)S(1)} %pad_add_fusion.marks, f32[1,256]{1,0:T(1,128)S(1)} %bitcast.8, f32[2,7,128,128]{3,2,1,0:T(8,128)S(1)} %copy-done.2, ...), custom_call_target="tpu_custom_call" | custom-call | flops 16777216 | bytes 1048576 | tf_op jit(solution)/shard_map/prep/pallas_call | solution.py:319
  11.1 0.7 %collective-permute-done.4.refs_1_ = f32[136,256]{1,0:T(8,128)S(1)} collective-permute-done((f32[136,256]{1,0:T(8,128)S(1)}, f32[136,256]{1,0:T(8,128)S(1)}, u32[]{:S(2)}, u32[]{:S(2)}) %collective-permute-start.4) | collective-permute-done | bytes 139296 | tf_op jit(solution)/shard_map/ppermute | solution.py:311
  12.4 2.6 %collective-permute-start.7 = (f32[264,128]{1,0:T(8,128)S(1)}, f32[264,128]{1,0:T(8,128)S(1)}, u32[]{:S(2)}, u32[]{:S(2)}) collective-permute-start(f32[264,128]{1,0:T(8,128)S(1)} %get-tuple-element.41), channel_id=1, source_target_pairs={{4,0},{8,4},{12,8},{0,12},{5,1},{9,5},{13,9},{1,13},{6,2},{10,6},{... | collective-permute-start | bytes 405512 | tf_op jit(solution)/shard_map/ppermute | solution.py:343
  15.0 0.8 %collective-permute-start.8 = (f32[264,128]{1,0:T(8,128)S(1)}, f32[264,128]{1,0:T(8,128)S(1)}, u32[]{:S(2)}, u32[]{:S(2)}) collective-permute-start(f32[264,128]{1,0:T(8,128)S(1)} %get-tuple-element.43), channel_id=1, source_target_pairs={{4,0},{8,4},{12,8},{0,12},{5,1},{9,5},{13,9},{1,13},{6,2},{10,6},{... | collective-permute-start | bytes 405512 | tf_op jit(solution)/shard_map/ppermute | solution.py:343
  16.2 1.0 %collective-permute-done.5.there = f32[256,256]{1,0:T(8,128)S(1)} collective-permute-done((f32[256,256]{1,0:T(8,128)S(1)}, f32[256,256]{1,0:T(8,128)S(1)}, u32[]{:S(2)}, u32[]{:S(2)}) %collective-permute-start.5) | collective-permute-done | bytes 262176 | tf_op jit(solution)/shard_map/ppermute | solution.py:313
  18.1 1.7 %collective-permute-done.7.out = f32[264,128]{1,0:T(8,128)S(1)} collective-permute-done((f32[264,128]{1,0:T(8,128)S(1)}, f32[264,128]{1,0:T(8,128)S(1)}, u32[]{:S(2)}, u32[]{:S(2)}) %collective-permute-start.7) | collective-permute-done | bytes 135200 | tf_op jit(solution)/shard_map/ppermute | solution.py:343
  19.9 0.6 %collective-permute-start.12 = (f32[264,128]{1,0:T(8,128)S(1)}, f32[264,128]{1,0:T(8,128)S(1)}, u32[]{:S(2)}, u32[]{:S(2)}) collective-permute-start(f32[264,128]{1,0:T(8,128)S(1)} %get-tuple-element.52), channel_id=1, source_target_pairs={{0,2},{2,0},{1,3},{3,1},{4,6},{6,4},{5,7},{7,5},{8,10},{10,8},{9,1... | collective-permute-start | bytes 405512 | tf_op jit(solution)/shard_map/ppermute | solution.py:358
  20.5 2.5 %collective-permute-done.8.rest = f32[264,128]{1,0:T(8,128)S(1)} collective-permute-done((f32[264,128]{1,0:T(8,128)S(1)}, f32[264,128]{1,0:T(8,128)S(1)}, u32[]{:S(2)}, u32[]{:S(2)}) %collective-permute-start.8) | collective-permute-done | bytes 135200 | tf_op jit(solution)/shard_map/ppermute | solution.py:343
  23.3 1.3 %collective-permute-done.10.mate_other = f32[256,128]{1,0:T(8,128)S(1)} collective-permute-done((f32[256,128]{1,0:T(8,128)S(1)}, f32[256,128]{1,0:T(8,128)S(1)}, u32[]{:S(2)}, u32[]{:S(2)}) %collective-permute-start.10) | collective-permute-done | bytes 131104 | tf_op jit(solution)/shard_map/ppermute | solution.py:350
  25.5 2.8 %collective-permute-done.11.left = f32[256,256]{1,0:T(8,128)S(1)} collective-permute-done((f32[256,256]{1,0:T(8,128)S(1)}, f32[256,256]{1,0:T(8,128)S(1)}, u32[]{:S(2)}, u32[]{:S(2)}) %collective-permute-start.11) | collective-permute-done | bytes 262176 | tf_op jit(solution)/shard_map/ppermute | solution.py:347
  28.9 1.0 %collective-permute-start.14 = (f32[8,256]{1,0:T(8,128)S(1)}, f32[8,256]{1,0:T(8,128)S(1)}, u32[]{:S(2)}, u32[]{:S(2)}) collective-permute-start(f32[8,256]{1,0:T(8,128)S(1)} %far.1.refs_0_), channel_id=1, source_target_pairs={{0,2},{1,3},{2,0},{3,1},{4,6},{5,7},{6,4},{7,5},{8,10},{9,11},{10,... | collective-permute-start | bytes 24584 | tf_op jit(solution)/shard_map/ppermute | solution.py:46
  29.9 0.8 %collective-permute-start.13 = (f32[8,256]{1,0:T(8,128)S(1)}, f32[8,256]{1,0:T(8,128)S(1)}, u32[]{:S(2)}, u32[]{:S(2)}) collective-permute-start(f32[8,256]{1,0:T(8,128)S(1)} %far.1.refs_0_), channel_id=1, source_target_pairs={{0,1},{1,0},{2,3},{3,2},{4,5},{5,4},{6,7},{7,6},{8,9},{9,8},{10,11... | collective-permute-start | bytes 24584 | tf_op jit(solution)/shard_map/ppermute | solution.py:46
  30.7 1.2 %collective-permute-done.15.refs_3_ = f32[8,256]{1,0:T(8,128)S(1)} collective-permute-done((f32[8,256]{1,0:T(8,128)S(1)}, f32[8,256]{1,0:T(8,128)S(1)}, u32[]{:S(2)}, u32[]{:S(2)}) %collective-permute-start.15) | collective-permute-done | bytes 8224 | tf_op jit(solution)/shard_map/ppermute | solution.py:46
  31.9 0.7 %collective-permute-done.14.refs_2_ = f32[8,256]{1,0:T(8,128)S(1)} collective-permute-done((f32[8,256]{1,0:T(8,128)S(1)}, f32[8,256]{1,0:T(8,128)S(1)}, u32[]{:S(2)}, u32[]{:S(2)}) %collective-permute-start.14) | collective-permute-done | bytes 8224 | tf_op jit(solution)/shard_map/ppermute | solution.py:46
  32.6 3.4 %collective-permute-start.18 = (f32[8,256]{1,0:T(8,128)S(1)}, f32[8,256]{1,0:T(8,128)S(1)}, u32[]{:S(2)}, u32[]{:S(2)}) collective-permute-start(f32[8,256]{1,0:T(8,128)S(1)} %merge.2.refs_0_), channel_id=1, source_target_pairs={{0,12},{1,13},{2,14},{3,15},{4,8},{5,9},{6,10},{7,11},{8,4},{9,5},... | collective-permute-start | bytes 24584 | tf_op jit(solution)/shard_map/ppermute | solution.py:46
  36.0 1.3 %collective-permute-start.17 = (f32[8,256]{1,0:T(8,128)S(1)}, f32[8,256]{1,0:T(8,128)S(1)}, u32[]{:S(2)}, u32[]{:S(2)}) collective-permute-start(f32[8,256]{1,0:T(8,128)S(1)} %merge.2.refs_0_), channel_id=1, source_target_pairs={{0,8},{1,9},{2,10},{3,11},{4,12},{5,13},{6,14},{7,15},{8,0},{9,1},... | collective-permute-start | bytes 24584 | tf_op jit(solution)/shard_map/ppermute | solution.py:46
  37.3 0.9 %collective-permute-done.18.refs_3_ = f32[8,256]{1,0:T(8,128)S(1)} collective-permute-done((f32[8,256]{1,0:T(8,128)S(1)}, f32[8,256]{1,0:T(8,128)S(1)}, u32[]{:S(2)}, u32[]{:S(2)}) %collective-permute-start.18) | collective-permute-done | bytes 8224 | tf_op jit(solution)/shard_map/ppermute | solution.py:46
  38.2 2.3 %collective-permute-done.17.refs_2_ = f32[8,256]{1,0:T(8,128)S(1)} collective-permute-done((f32[8,256]{1,0:T(8,128)S(1)}, f32[8,256]{1,0:T(8,128)S(1)}, u32[]{:S(2)}, u32[]{:S(2)}) %collective-permute-start.17) | collective-permute-done | bytes 8224 | tf_op jit(solution)/shard_map/ppermute | solution.py:46
  41.0 0.7 %multiply_subtract_fusion = f32[256,256]{1,0:T(8,128)} fusion(f32[256,256]{1,0:T(8,128)S(1)} %get-tuple-element.44.image, f32[256,256]{1,0:T(8,128)S(1)} %copy-done, f32[256]{0:T(256)S(1)} %bitcast.10, f32[256]{0:T(256)S(1)} %bitcast.9), kind=kLoop, calls=%fused_computation | loop fusion | flops 196608 | bytes 788480 | tf_op jit(solution)/shard_map/sub | solution.py:366
  (41 shorter events, 5.5 us)
Async XLA Ops:
  0.0 5.8 %copy-start = (f32[256,256]{1,0:T(8,128)S(1)}, f32[256,256]{1,0:T(8,128)}, u32[]{:S(2)}) copy-start(f32[256,256]{1,0:T(8,128)} %field.7) | copy-start | bytes 786436
  1.2 9.7 %collective-permute-start.3 = (f32[136,256]{1,0:T(8,128)S(1)}, f32[136,256]{1,0:T(8,128)S(1)}, u32[]{:S(2)}, u32[]{:S(2)}) collective-permute-start(f32[136,256]{1,0:T(8,128)S(1)} %get-tuple-element.35), channel_id=1, source_target_pairs={{0,2},{2,0},{1,3},{3,1},{4,6},{6,4},{5,7},{7,5},{8,10},{10,8},{9,1... | collective-permute-start | bytes 417800 | tf_op jit(solution)/shard_map/ppermute | solution.py:311
  4.2 7.5 %collective-permute-start.4 = (f32[136,256]{1,0:T(8,128)S(1)}, f32[136,256]{1,0:T(8,128)S(1)}, u32[]{:S(2)}, u32[]{:S(2)}) collective-permute-start(f32[136,256]{1,0:T(8,128)S(1)} %get-tuple-element.29.packed.mine.refs_0_), channel_id=1, source_target_pairs={{0,4},{4,8},{8,12},{12,0},{1,5},{5,9},{9,13},{13,1},{2,6},{6,10},{... | collective-permute-start | bytes 417800 | tf_op jit(solution)/shard_map/ppermute | solution.py:311
  5.8 10.0 %collective-permute-start = (f32[256,256]{1,0:T(8,128)S(1)}, f32[256,256]{1,0:T(8,128)S(1)}, u32[]{:S(2)}, u32[]{:S(2)}) collective-permute-start(f32[256,256]{1,0:T(8,128)S(1)} %copy-done), channel_id=1, source_target_pairs={{0,1},{1,0},{2,3},{3,2},{4,5},{5,4},{6,7},{7,6},{8,9},{9,8},{10,11... | collective-permute-start | bytes 786440 | tf_op jit(solution)/shard_map/ppermute | solution.py:314
  5.8 11.4 %collective-permute-start.5 = (f32[256,256]{1,0:T(8,128)S(1)}, f32[256,256]{1,0:T(8,128)S(1)}, u32[]{:S(2)}, u32[]{:S(2)}) collective-permute-start(f32[256,256]{1,0:T(8,128)S(1)} %copy-done), channel_id=1, source_target_pairs={{0,4},{4,8},{8,12},{12,0},{1,5},{5,9},{9,13},{13,1},{2,6},{6,10},{... | collective-permute-start | bytes 786440 | tf_op jit(solution)/shard_map/ppermute | solution.py:313
  7.4 10.2 %collective-permute-start.6 = (f32[256,256]{1,0:T(8,128)S(1)}, f32[256,256]{1,0:T(8,128)S(1)}, u32[]{:S(2)}, u32[]{:S(2)}) collective-permute-start(f32[256,256]{1,0:T(8,128)S(1)} %copy-done), channel_id=1, source_target_pairs={{0,2},{2,0},{1,3},{3,1},{4,6},{6,4},{5,7},{7,5},{8,10},{10,8},{9,1... | collective-permute-start | bytes 786440 | tf_op jit(solution)/shard_map/ppermute | solution.py:313
  7.9 0.7 %copy-start.4 = (f32[256]{0:T(256)S(1)}, f32[256]{0:T(256)}, u32[]{:S(2)}) copy-start(f32[256]{0:T(256)} %param.8) | copy-start | bytes 3076
  8.0 0.7 %copy-start.3 = (s32[2,7]{1,0:T(2,128)S(1)}, s32[2,7]{1,0:T(2,128)}, u32[]{:S(2)}) copy-start(s32[2,7]{1,0:T(2,128)} %cols.1) | copy-start | bytes 172
  8.7 1.2 %copy-start.2 = (f32[2,7,128,128]{3,2,1,0:T(8,128)S(1)}, f32[2,7,128,128]{3,2,1,0:T(8,128)}, u32[]{:S(2)}) copy-start(f32[2,7,128,128]{3,2,1,0:T(8,128)} %local.1) | copy-start | bytes 2752516
  9.9 1.9 %copy-start.1 = (f32[1,8,128,128]{3,2,1,0:T(8,128)S(1)}, f32[1,8,128,128]{3,2,1,0:T(8,128)}, u32[]{:S(2)}) copy-start(f32[1,8,128,128]{3,2,1,0:T(8,128)} %param.11) | copy-start | bytes 1572868
  11.0 1.4 %collective-permute-start.1 = (f32[256,128]{1,0:T(8,128)S(1)}, f32[256,128]{1,0:T(8,128)S(1)}, u32[]{:S(2)}, u32[]{:S(2)}) collective-permute-start(f32[256,128]{1,0:T(8,128)S(1)} %get-tuple-element.32), channel_id=1, source_target_pairs={{0,1},{1,0},{2,3},{3,2},{4,5},{5,4},{6,7},{7,6},{8,9},{9,8},{10,11... | collective-permute-start | bytes 393224 | tf_op jit(solution)/shard_map/ppermute | solution.py:335
  11.7 3.3 %collective-permute-start.2 = (f32[256,128]{1,0:T(8,128)S(1)}, f32[256,128]{1,0:T(8,128)S(1)}, u32[]{:S(2)}, u32[]{:S(2)}) collective-permute-start(f32[256,128]{1,0:T(8,128)S(1)} %get-tuple-element.33), channel_id=1, source_target_pairs={{0,1},{1,0},{2,3},{3,2},{4,5},{5,4},{6,7},{7,6},{8,9},{9,8},{10,11... | collective-permute-start | bytes 393224 | tf_op jit(solution)/shard_map/ppermute | solution.py:335
  12.4 7.4 %collective-permute-start.7 = (f32[264,128]{1,0:T(8,128)S(1)}, f32[264,128]{1,0:T(8,128)S(1)}, u32[]{:S(2)}, u32[]{:S(2)}) collective-permute-start(f32[264,128]{1,0:T(8,128)S(1)} %get-tuple-element.41), channel_id=1, source_target_pairs={{4,0},{8,4},{12,8},{0,12},{5,1},{9,5},{13,9},{1,13},{6,2},{10,6},{... | collective-permute-start | bytes 405512 | tf_op jit(solution)/shard_map/ppermute | solution.py:343
  15.0 8.0 %collective-permute-start.8 = (f32[264,128]{1,0:T(8,128)S(1)}, f32[264,128]{1,0:T(8,128)S(1)}, u32[]{:S(2)}, u32[]{:S(2)}) collective-permute-start(f32[264,128]{1,0:T(8,128)S(1)} %get-tuple-element.43), channel_id=1, source_target_pairs={{4,0},{8,4},{12,8},{0,12},{5,1},{9,5},{13,9},{1,13},{6,2},{10,6},{... | collective-permute-start | bytes 405512 | tf_op jit(solution)/shard_map/ppermute | solution.py:343
  17.9 10.4 %collective-permute-start.11 = (f32[256,256]{1,0:T(8,128)S(1)}, f32[256,256]{1,0:T(8,128)S(1)}, u32[]{:S(2)}, u32[]{:S(2)}) collective-permute-start(f32[256,256]{1,0:T(8,128)S(1)} %get-tuple-element.40.part), channel_id=1, source_target_pairs={{0,4},{4,8},{8,12},{12,0},{1,5},{5,9},{9,13},{13,1},{2,6},{6,10},{... | collective-permute-start | bytes 786440 | tf_op jit(solution)/shard_map/ppermute | solution.py:347
  19.9 5.6 %collective-permute-start.12 = (f32[264,128]{1,0:T(8,128)S(1)}, f32[264,128]{1,0:T(8,128)S(1)}, u32[]{:S(2)}, u32[]{:S(2)}) collective-permute-start(f32[264,128]{1,0:T(8,128)S(1)} %get-tuple-element.52), channel_id=1, source_target_pairs={{0,2},{2,0},{1,3},{3,1},{4,6},{6,4},{5,7},{7,5},{8,10},{10,8},{9,1... | collective-permute-start | bytes 405512 | tf_op jit(solution)/shard_map/ppermute | solution.py:358
  20.5 2.7 %collective-permute-start.9 = (f32[256,128]{1,0:T(8,128)S(1)}, f32[256,128]{1,0:T(8,128)S(1)}, u32[]{:S(2)}, u32[]{:S(2)}) collective-permute-start(f32[256,128]{1,0:T(8,128)S(1)} %get-tuple-element.42.half), channel_id=1, source_target_pairs={{0,1},{1,0},{2,3},{3,2},{4,5},{5,4},{6,7},{7,6},{8,9},{9,8},{10,11... | collective-permute-start | bytes 393224 | tf_op jit(solution)/shard_map/ppermute | solution.py:350
  23.2 1.4 %collective-permute-start.10 = (f32[256,128]{1,0:T(8,128)S(1)}, f32[256,128]{1,0:T(8,128)S(1)}, u32[]{:S(2)}, u32[]{:S(2)}) collective-permute-start(f32[256,128]{1,0:T(8,128)S(1)} %get-tuple-element.46), channel_id=1, source_target_pairs={{0,1},{1,0},{2,3},{3,2},{4,5},{5,4},{6,7},{7,6},{8,9},{9,8},{10,11... | collective-permute-start | bytes 393224 | tf_op jit(solution)/shard_map/ppermute | solution.py:350
  28.8 3.1 %collective-permute-start.15 = (f32[8,256]{1,0:T(8,128)S(1)}, f32[8,256]{1,0:T(8,128)S(1)}, u32[]{:S(2)}, u32[]{:S(2)}) collective-permute-start(f32[8,256]{1,0:T(8,128)S(1)} %far.1.refs_0_), channel_id=1, source_target_pairs={{0,3},{1,2},{2,1},{3,0},{4,7},{5,6},{6,5},{7,4},{8,11},{9,10},{10,... | collective-permute-start | bytes 24584 | tf_op jit(solution)/shard_map/ppermute | solution.py:46
  28.9 3.7 %collective-permute-start.14 = (f32[8,256]{1,0:T(8,128)S(1)}, f32[8,256]{1,0:T(8,128)S(1)}, u32[]{:S(2)}, u32[]{:S(2)}) collective-permute-start(f32[8,256]{1,0:T(8,128)S(1)} %far.1.refs_0_), channel_id=1, source_target_pairs={{0,2},{1,3},{2,0},{3,1},{4,6},{5,7},{6,4},{7,5},{8,10},{9,11},{10,... | collective-permute-start | bytes 24584 | tf_op jit(solution)/shard_map/ppermute | solution.py:46
  29.9 2.7 %collective-permute-start.13 = (f32[8,256]{1,0:T(8,128)S(1)}, f32[8,256]{1,0:T(8,128)S(1)}, u32[]{:S(2)}, u32[]{:S(2)}) collective-permute-start(f32[8,256]{1,0:T(8,128)S(1)} %far.1.refs_0_), channel_id=1, source_target_pairs={{0,1},{1,0},{2,3},{3,2},{4,5},{5,4},{6,7},{7,6},{8,9},{9,8},{10,11... | collective-permute-start | bytes 24584 | tf_op jit(solution)/shard_map/ppermute | solution.py:46
  32.6 5.6 %collective-permute-start.18 = (f32[8,256]{1,0:T(8,128)S(1)}, f32[8,256]{1,0:T(8,128)S(1)}, u32[]{:S(2)}, u32[]{:S(2)}) collective-permute-start(f32[8,256]{1,0:T(8,128)S(1)} %merge.2.refs_0_), channel_id=1, source_target_pairs={{0,12},{1,13},{2,14},{3,15},{4,8},{5,9},{6,10},{7,11},{8,4},{9,5},... | collective-permute-start | bytes 24584 | tf_op jit(solution)/shard_map/ppermute | solution.py:46
  36.0 4.5 %collective-permute-start.17 = (f32[8,256]{1,0:T(8,128)S(1)}, f32[8,256]{1,0:T(8,128)S(1)}, u32[]{:S(2)}, u32[]{:S(2)}) collective-permute-start(f32[8,256]{1,0:T(8,128)S(1)} %merge.2.refs_0_), channel_id=1, source_target_pairs={{0,8},{1,9},{2,10},{3,11},{4,12},{5,13},{6,14},{7,15},{8,0},{9,1},... | collective-permute-start | bytes 24584 | tf_op jit(solution)/shard_map/ppermute | solution.py:46
  37.3 3.7 %collective-permute-start.16 = (f32[8,256]{1,0:T(8,128)S(1)}, f32[8,256]{1,0:T(8,128)S(1)}, u32[]{:S(2)}, u32[]{:S(2)}) collective-permute-start(f32[8,256]{1,0:T(8,128)S(1)} %merge.2.refs_0_), channel_id=1, source_target_pairs={{0,4},{1,5},{2,6},{3,7},{4,0},{5,1},{6,2},{7,3},{8,12},{9,13},{10,... | collective-permute-start | bytes 24584 | tf_op jit(solution)/shard_map/ppermute | solution.py:46

commit v21 on v17

--- a/solution.py
+++ b/solution.py
@@ -92,7 +92,7 @@
         copy.wait()
 
 
-def prep_kernel(cols, marks, diag, local, packed, own, pair, low, high):
+def prep_kernel(cols, marks, diag, local, packed, own, pair):
     nblocks, nonzeros, bs, _ = local.shape
     width = nblocks * bs
     patch_len = 2 * nblocks
@@ -117,8 +117,6 @@
     here = lax.broadcasted_iota(jnp.int32, (width, width), 0)
     there = lax.broadcasted_iota(jnp.int32, (width, width), 1)
     own[...] = lower + lower.T + jnp.where(here == there, diag[...], 0.0)
-    low[...] = pair[:, : width // 2]
-    high[...] = pair[:, width // 2 :]
 
 
 def edge(take, width, mine, pay, border):
@@ -145,8 +143,8 @@
     return jnp.concatenate([jnp.concatenate(line, axis=1) for line in blocks], axis=0)
 
 
-def base_kernel(field, own, pair, mate, low, high, image, coup):
-    coup[...] = pair[...] + jnp.concatenate([low[...].T, high[...].T], axis=0)
+def base_kernel(field, own, pair, mate, mate_pair, image, coup):
+    coup[...] = pair[...] + mate_pair[...].T
     image[...] = dot(own[...], field[...]) + dot(coup[...], mate[...])
 
 
@@ -322,12 +320,12 @@
         return run
 
     field, square = (width, ncols), (width, width)
-    own, pair, *pieces = tabled(prep_kernel, "prep", 2, [square] * 2 + [(width, width // 2)] * 2, 1 << 24)(
+    own, pair = tabled(prep_kernel, "prep", 2, [square] * 2, 1 << 24)(
         block_cols, marks, node_diag.reshape(1, width), local_coup, mine
     )
-    mate_pair = [lax.ppermute(piece, "nd", swap) for piece in pieces]
-
-    part, coup = call(base_kernel, "base", [field, square])(right_side, own, pair, mate, *mate_pair)
+    mate_pair = lax.ppermute(pair, "nd", swap)
+
+    part, coup = call(base_kernel, "base", [field, square])(right_side, own, pair, mate, mate_pair)
     left_coup, back, *to_left = call(back_kernel, "back", [square, field] + [longer] * 2)(mine, right_side, border, pays[0])
     from_right = [lax.ppermute(piece, "gx", left) for piece in to_left]
     part, once = call(left_kernel, "left", [field] * 2)(part, left_coup, fields[0])

time: 41 us -> 41.3 us (level)
  waiting for transfers between devices: 12.6 us -> 13.1 us
    ppermute x2, waiting for transfers between devices: 2.47 us -> 3.53 us  [shards(): fields = [lax.ppermute(right_side, axis, perm) for axis, perm in sends]]
    ppermute x2 -> x1, waiting for transfers between devices: 0.89 us -> 0.01 us  [shards(): mate_pair = lax.ppermute(pair, 'nd', swap)]
    ppermute x2, starting transfers between devices: 3.09 us -> 2.24 us  [shards(): from_right = [lax.ppermute(piece, 'gx', left) for piece in to_left]]
    ppermute x2, starting transfers between devices: 3.61 us -> 4.33 us  [shards(): lax.ppermute(pay, axis, perm)]
    ppermute x1, starting transfers between devices: 0.49 us -> 0.01 us  [shards(): mate = lax.ppermute(right_side, 'nd', swap)]
    ppermute x2 -> x1, starting transfers between devices: 0.07 us -> 0.56 us  [shards(): mate_pair = lax.ppermute(pair, 'nd', swap)]
  transfers between devices with their start and end apart: 19 -> 18, of which waited for: 12 -> 11; matrix products, arithmetic and copies ran while one was open for 0% -> 0% of each run, Pallas kernels for 8% -> 8%
where the time goes in v21:
time: 41.3 us; the launch traced here: 41.1 us
  starting transfers between devices  20.4 us (49%)
  waiting for transfers between devices  13.1 us (32%)
  Pallas kernels  5.5 us (13%)
  local copies, waits for them, and re-layouts  1.2 us (3%)
  other arithmetic  0.85 us (2%)
    ppermute x6, starting transfers between devices, join(): lax.ppermute(state, AXES, [(i, i ^ m) for i in range(count)])  6.39 us
    ppermute x2, starting transfers between devices, shards(): lax.ppermute(pay, axis, perm)  4.33 us
    ppermute x6, waiting for transfers between devices, join(): lax.ppermute(state, AXES, [(i, i ^ m) for i in range(count)])  3.82 us
    ppermute x2, waiting for transfers between devices, shards(): fields = [lax.ppermute(right_side, axis, perm) for axis, perm in sends]  3.53 us
    ppermute x2, starting transfers between devices, shards(): fields = [lax.ppermute(right_side, axis, perm) for axis, perm in sends]  3.07 us
    pallas_call x10, Pallas kernels, run(): pl.pallas_call(kernel, name=name, in_specs=[vmem()] * len(args), out_spec...  2.85 us
    ppermute x2, starting transfers between devices, shards(): from_right = [lax.ppermute(piece, 'gx', left) for piece in to_left]  2.24 us
    ppermute x1, waiting for transfers between devices, shards(): left_w = lax.ppermute(part, 'gx', right)  2.16 us
  transfers between devices with their start and end apart: 18, of which 11 were waited for; matrix products, arithmetic and copies ran while one was open for 0% of the time, Pallas kernels for 8%

profile of v21, /device:TPU:0, one launch (start us, length us, event | category | flops | bytes accessed | tf_op | source)
XLA Modules:
  0.0 41.1 jit_solution(12985074834709423689)
XLA Ops:
  0.1 1.6 %pack.1 = (f32[136,256]{1,0:T(8,128)S(1)}, f32[136,256]{1,0:T(8,128)S(1)}) custom-call(s32[2]{0:T(128)S(1)} %pad_add_fusion.refs_0_.marks, f32[8,128,128]{2,1,0:T(8,128)} %bitcast.6, s32[1,8]{1,0:T(1,128)} %refs_2_.1, s32[1,8]{1,0:T(1,128)} %refs_3_.1, s32[1,8]{1,0:T(1,128)S(1)} %broadcast_in_dim.3.refs_4_), custom_call_target="tpu_custom_call" | custom-call | tf_op jit(solution)/shard_map/pack/pallas_call | solution.py:287
  1.7 3.1 %collective-permute-start.2 = (f32[136,256]{1,0:T(8,128)S(1)}, f32[136,256]{1,0:T(8,128)S(1)}, u32[]{:S(2)}, u32[]{:S(2)}) collective-permute-start(f32[136,256]{1,0:T(8,128)S(1)} %get-tuple-element.27.packed.mine.refs_0_), channel_id=1, source_target_pairs={{0,4},{4,8},{8,12},{12,0},{1,5},{5,9},{9,13},{13,1},{2,6},{6,10},{... | collective-permute-start | bytes 417800 | tf_op jit(solution)/shard_map/ppermute | solution.py:302
  4.8 1.2 %copy-done.2 = f32[2,7,128,128]{3,2,1,0:T(8,128)S(1)} copy-done((f32[2,7,128,128]{3,2,1,0:T(8,128)S(1)}, f32[2,7,128,128]{3,2,1,0:T(8,128)}, u32[]{:S(2)}) %copy-start.2) | copy-done | bytes 917528
  6.0 1.1 %prep.1 = (f32[256,256]{1,0:T(8,128)S(1)}, f32[256,256]{1,0:T(8,128)S(1)}) custom-call(s32[2,7]{1,0:T(2,128)S(1)} %copy-done.3, s32[2]{0:T(128)S(1)} %pad_add_fusion.refs_0_.marks, f32[1,256]{1,0:T(1,128)S(1)} %bitcast.9, f32[2,7,128,128]{3,2,1,0:T(8,128)S(1)} %copy-done.2, f32[136,256]{1,0:T(8,128)S(1)} %get-tuple-element.27.packed.mine.refs_0_), custom_call_target="tpu_custom_call" | custom-call | flops 16777216 | bytes 1048576 | tf_op jit(solution)/shard_map/prep/pallas_call | solution.py:310
  7.6 1.6 %collective-permute-start.3 = (f32[256,256]{1,0:T(8,128)S(1)}, f32[256,256]{1,0:T(8,128)S(1)}, u32[]{:S(2)}, u32[]{:S(2)}) collective-permute-start(f32[256,256]{1,0:T(8,128)S(1)} %copy-done), channel_id=1, source_target_pairs={{0,4},{4,8},{8,12},{12,0},{1,5},{5,9},{9,13},{13,1},{2,6},{6,10},{... | collective-permute-start | bytes 786440 | tf_op jit(solution)/shard_map/ppermute | solution.py:304
  9.2 1.5 %collective-permute-start.5 = (f32[256,256]{1,0:T(8,128)S(1)}, f32[256,256]{1,0:T(8,128)S(1)}, u32[]{:S(2)}, u32[]{:S(2)}) collective-permute-start(f32[256,256]{1,0:T(8,128)S(1)} %copy-done), channel_id=1, source_target_pairs={{0,2},{2,0},{1,3},{3,1},{4,6},{6,4},{5,7},{7,5},{8,10},{10,8},{9,1... | collective-permute-start | bytes 786440 | tf_op jit(solution)/shard_map/ppermute | solution.py:304
  10.7 1.3 %collective-permute-start.4 = (f32[136,256]{1,0:T(8,128)S(1)}, f32[136,256]{1,0:T(8,128)S(1)}, u32[]{:S(2)}, u32[]{:S(2)}) collective-permute-start(f32[136,256]{1,0:T(8,128)S(1)} %get-tuple-element.34), channel_id=1, source_target_pairs={{0,2},{2,0},{1,3},{3,1},{4,6},{6,4},{5,7},{7,5},{8,10},{10,8},{9,1... | collective-permute-start | bytes 417800 | tf_op jit(solution)/shard_map/ppermute | solution.py:302
  12.4 1.8 %collective-permute-start.6 = (f32[264,128]{1,0:T(8,128)S(1)}, f32[264,128]{1,0:T(8,128)S(1)}, u32[]{:S(2)}, u32[]{:S(2)}) collective-permute-start(f32[264,128]{1,0:T(8,128)S(1)} %get-tuple-element.36), channel_id=1, source_target_pairs={{4,0},{8,4},{12,8},{0,12},{5,1},{9,5},{13,9},{1,13},{6,2},{10,6},{... | collective-permute-start | bytes 405512 | tf_op jit(solution)/shard_map/ppermute | solution.py:330
  15.1 3.5 %collective-permute-done.3.there = f32[256,256]{1,0:T(8,128)S(1)} collective-permute-done((f32[256,256]{1,0:T(8,128)S(1)}, f32[256,256]{1,0:T(8,128)S(1)}, u32[]{:S(2)}, u32[]{:S(2)}) %collective-permute-start.3) | collective-permute-done | bytes 262176 | tf_op jit(solution)/shard_map/ppermute | solution.py:304
  18.9 1.3 %collective-permute-done.4.pay = f32[136,256]{1,0:T(8,128)S(1)} collective-permute-done((f32[136,256]{1,0:T(8,128)S(1)}, f32[136,256]{1,0:T(8,128)S(1)}, u32[]{:S(2)}, u32[]{:S(2)}) %collective-permute-start.4) | collective-permute-done | bytes 139296 | tf_op jit(solution)/shard_map/ppermute | solution.py:302
  20.6 1.6 %collective-permute-start.10 = (f32[256,256]{1,0:T(8,128)S(1)}, f32[256,256]{1,0:T(8,128)S(1)}, u32[]{:S(2)}, u32[]{:S(2)}) collective-permute-start(f32[256,256]{1,0:T(8,128)S(1)} %get-tuple-element.35.part), channel_id=1, source_target_pairs={{0,4},{4,8},{8,12},{12,0},{1,5},{5,9},{9,13},{13,1},{2,6},{6,10},{... | collective-permute-start | bytes 786440 | tf_op jit(solution)/shard_map/ppermute | solution.py:336
  22.3 1.6 %collective-permute-start.11 = (f32[264,128]{1,0:T(8,128)S(1)}, f32[264,128]{1,0:T(8,128)S(1)}, u32[]{:S(2)}, u32[]{:S(2)}) collective-permute-start(f32[264,128]{1,0:T(8,128)S(1)} %get-tuple-element.48), channel_id=1, source_target_pairs={{0,2},{2,0},{1,3},{3,1},{4,6},{6,4},{5,7},{7,5},{8,10},{10,8},{9,1... | collective-permute-start | bytes 405512 | tf_op jit(solution)/shard_map/ppermute | solution.py:347
  24.0 0.6 %collective-permute-start.9 = (f32[256,128]{1,0:T(8,128)S(1)}, f32[256,128]{1,0:T(8,128)S(1)}, u32[]{:S(2)}, u32[]{:S(2)}) collective-permute-start(f32[256,128]{1,0:T(8,128)S(1)} %get-tuple-element.41), channel_id=1, source_target_pairs={{0,1},{1,0},{2,3},{3,2},{4,5},{5,4},{6,7},{7,6},{8,9},{9,8},{10,11... | collective-permute-start | bytes 393224 | tf_op jit(solution)/shard_map/ppermute | solution.py:339
  24.6 0.7 %collective-permute-done.8.mate_out = f32[256,128]{1,0:T(8,128)S(1)} collective-permute-done((f32[256,128]{1,0:T(8,128)S(1)}, f32[256,128]{1,0:T(8,128)S(1)}, u32[]{:S(2)}, u32[]{:S(2)}) %collective-permute-start.8) | collective-permute-done | bytes 131104 | tf_op jit(solution)/shard_map/ppermute | solution.py:339
  26.1 1.3 %collective-permute-done.11.refs_3_ = f32[264,128]{1,0:T(8,128)S(1)} collective-permute-done((f32[264,128]{1,0:T(8,128)S(1)}, f32[264,128]{1,0:T(8,128)S(1)}, u32[]{:S(2)}, u32[]{:S(2)}) %collective-permute-start.11) | collective-permute-done | bytes 135200 | tf_op jit(solution)/shard_map/ppermute | solution.py:347
  27.4 2.2 %collective-permute-done.10.left = f32[256,256]{1,0:T(8,128)S(1)} collective-permute-done((f32[256,256]{1,0:T(8,128)S(1)}, f32[256,256]{1,0:T(8,128)S(1)}, u32[]{:S(2)}, u32[]{:S(2)}) %collective-permute-start.10) | collective-permute-done | bytes 262176 | tf_op jit(solution)/shard_map/ppermute | solution.py:336
  30.1 1.6 %collective-permute-start.13 = (f32[8,256]{1,0:T(8,128)S(1)}, f32[8,256]{1,0:T(8,128)S(1)}, u32[]{:S(2)}, u32[]{:S(2)}) collective-permute-start(f32[8,256]{1,0:T(8,128)S(1)} %far.1.refs_0_), channel_id=1, source_target_pairs={{0,2},{1,3},{2,0},{3,1},{4,6},{5,7},{6,4},{7,5},{8,10},{9,11},{10,... | collective-permute-start | bytes 24584 | tf_op jit(solution)/shard_map/ppermute | solution.py:46
  32.0 1.3 %collective-permute-done.14.refs_3_ = f32[8,256]{1,0:T(8,128)S(1)} collective-permute-done((f32[8,256]{1,0:T(8,128)S(1)}, f32[8,256]{1,0:T(8,128)S(1)}, u32[]{:S(2)}, u32[]{:S(2)}) %collective-permute-start.14) | collective-permute-done | bytes 8224 | tf_op jit(solution)/shard_map/ppermute | solution.py:46
  33.2 0.6 %collective-permute-done.13.refs_2_ = f32[8,256]{1,0:T(8,128)S(1)} collective-permute-done((f32[8,256]{1,0:T(8,128)S(1)}, f32[8,256]{1,0:T(8,128)S(1)}, u32[]{:S(2)}, u32[]{:S(2)}) %collective-permute-start.13) | collective-permute-done | bytes 8224 | tf_op jit(solution)/shard_map/ppermute | solution.py:46
  33.9 1.4 %collective-permute-start.17 = (f32[8,256]{1,0:T(8,128)S(1)}, f32[8,256]{1,0:T(8,128)S(1)}, u32[]{:S(2)}, u32[]{:S(2)}) collective-permute-start(f32[8,256]{1,0:T(8,128)S(1)} %merge.2.refs_0_), channel_id=1, source_target_pairs={{0,12},{1,13},{2,14},{3,15},{4,8},{5,9},{6,10},{7,11},{8,4},{9,5},... | collective-permute-start | bytes 24584 | tf_op jit(solution)/shard_map/ppermute | solution.py:46
  35.3 1.4 %collective-permute-start.16 = (f32[8,256]{1,0:T(8,128)S(1)}, f32[8,256]{1,0:T(8,128)S(1)}, u32[]{:S(2)}, u32[]{:S(2)}) collective-permute-start(f32[8,256]{1,0:T(8,128)S(1)} %merge.2.refs_0_), channel_id=1, source_target_pairs={{0,8},{1,9},{2,10},{3,11},{4,12},{5,13},{6,14},{7,15},{8,0},{9,1},... | collective-permute-start | bytes 24584 | tf_op jit(solution)/shard_map/ppermute | solution.py:46
  36.7 1.7 %collective-permute-start.15 = (f32[8,256]{1,0:T(8,128)S(1)}, f32[8,256]{1,0:T(8,128)S(1)}, u32[]{:S(2)}, u32[]{:S(2)}) collective-permute-start(f32[8,256]{1,0:T(8,128)S(1)} %merge.2.refs_0_), channel_id=1, source_target_pairs={{0,4},{1,5},{2,6},{3,7},{4,0},{5,1},{6,2},{7,3},{8,12},{9,13},{10,... | collective-permute-start | bytes 24584 | tf_op jit(solution)/shard_map/ppermute | solution.py:46
  38.4 1.1 %collective-permute-done.17.refs_3_ = f32[8,256]{1,0:T(8,128)S(1)} collective-permute-done((f32[8,256]{1,0:T(8,128)S(1)}, f32[8,256]{1,0:T(8,128)S(1)}, u32[]{:S(2)}, u32[]{:S(2)}) %collective-permute-start.17) | collective-permute-done | bytes 8224 | tf_op jit(solution)/shard_map/ppermute | solution.py:46
  40.4 0.7 %multiply_subtract_fusion = f32[256,256]{1,0:T(8,128)} fusion(f32[256,256]{1,0:T(8,128)S(1)} %get-tuple-element.39.image, f32[256,256]{1,0:T(8,128)S(1)} %copy-done, f32[256]{0:T(256)S(1)} %bitcast.11, f32[256]{0:T(256)S(1)} %bitcast.10), kind=kLoop, calls=%fused_computation | loop fusion | flops 196608 | bytes 788480 | tf_op jit(solution)/shard_map/sub | solution.py:355
  (39 shorter events, 5.6 us)
Async XLA Ops:
  0.1 4.7 %copy-start = (f32[256,256]{1,0:T(8,128)S(1)}, f32[256,256]{1,0:T(8,128)}, u32[]{:S(2)}) copy-start(f32[256,256]{1,0:T(8,128)} %field.7) | copy-start | bytes 786436
  1.7 3.1 %copy-start.4 = (f32[256]{0:T(256)S(1)}, f32[256]{0:T(256)}, u32[]{:S(2)}) copy-start(f32[256]{0:T(256)} %param.8) | copy-start | bytes 3076
  1.7 3.1 %copy-start.3 = (s32[2,7]{1,0:T(2,128)S(1)}, s32[2,7]{1,0:T(2,128)}, u32[]{:S(2)}) copy-start(s32[2,7]{1,0:T(2,128)} %cols.1) | copy-start | bytes 172
  1.7 9.0 %collective-permute-start.2 = (f32[136,256]{1,0:T(8,128)S(1)}, f32[136,256]{1,0:T(8,128)S(1)}, u32[]{:S(2)}, u32[]{:S(2)}) collective-permute-start(f32[136,256]{1,0:T(8,128)S(1)} %get-tuple-element.27.packed.mine.refs_0_), channel_id=1, source_target_pairs={{0,4},{4,8},{8,12},{12,0},{1,5},{5,9},{9,13},{13,1},{2,6},{6,10},{... | collective-permute-start | bytes 417800 | tf_op jit(solution)/shard_map/ppermute | solution.py:302
  4.8 7.6 %collective-permute-start = (f32[256,256]{1,0:T(8,128)S(1)}, f32[256,256]{1,0:T(8,128)S(1)}, u32[]{:S(2)}, u32[]{:S(2)}) collective-permute-start(f32[256,256]{1,0:T(8,128)S(1)} %copy-done), channel_id=1, source_target_pairs={{0,1},{1,0},{2,3},{3,2},{4,5},{5,4},{6,7},{7,6},{8,9},{9,8},{10,11... | collective-permute-start | bytes 786440 | tf_op jit(solution)/shard_map/ppermute | solution.py:305
  4.8 1.2 %copy-start.2 = (f32[2,7,128,128]{3,2,1,0:T(8,128)S(1)}, f32[2,7,128,128]{3,2,1,0:T(8,128)}, u32[]{:S(2)}) copy-start(f32[2,7,128,128]{3,2,1,0:T(8,128)} %local.1) | copy-start | bytes 2752516
  6.0 6.0 %copy-start.1 = (f32[1,8,128,128]{3,2,1,0:T(8,128)S(1)}, f32[1,8,128,128]{3,2,1,0:T(8,128)}, u32[]{:S(2)}) copy-start(f32[1,8,128,128]{3,2,1,0:T(8,128)} %param.11) | copy-start | bytes 1572868
  7.1 7.2 %collective-permute-start.1 = (f32[256,256]{1,0:T(8,128)S(1)}, f32[256,256]{1,0:T(8,128)S(1)}, u32[]{:S(2)}, u32[]{:S(2)}) collective-permute-start(f32[256,256]{1,0:T(8,128)S(1)} %get-tuple-element.29.pair), channel_id=1, source_target_pairs={{0,1},{1,0},{2,3},{3,2},{4,5},{5,4},{6,7},{7,6},{8,9},{9,8},{10,11... | collective-permute-start | bytes 786440 | tf_op jit(solution)/shard_map/ppermute | solution.py:326
  7.6 11.0 %collective-permute-start.3 = (f32[256,256]{1,0:T(8,128)S(1)}, f32[256,256]{1,0:T(8,128)S(1)}, u32[]{:S(2)}, u32[]{:S(2)}) collective-permute-start(f32[256,256]{1,0:T(8,128)S(1)} %copy-done), channel_id=1, source_target_pairs={{0,4},{4,8},{8,12},{12,0},{1,5},{5,9},{9,13},{13,1},{2,6},{6,10},{... | collective-permute-start | bytes 786440 | tf_op jit(solution)/shard_map/ppermute | solution.py:304
  9.2 11.0 %collective-permute-start.5 = (f32[256,256]{1,0:T(8,128)S(1)}, f32[256,256]{1,0:T(8,128)S(1)}, u32[]{:S(2)}, u32[]{:S(2)}) collective-permute-start(f32[256,256]{1,0:T(8,128)S(1)} %copy-done), channel_id=1, source_target_pairs={{0,2},{2,0},{1,3},{3,1},{4,6},{6,4},{5,7},{7,5},{8,10},{10,8},{9,1... | collective-permute-start | bytes 786440 | tf_op jit(solution)/shard_map/ppermute | solution.py:304
  10.7 9.5 %collective-permute-start.4 = (f32[136,256]{1,0:T(8,128)S(1)}, f32[136,256]{1,0:T(8,128)S(1)}, u32[]{:S(2)}, u32[]{:S(2)}) collective-permute-start(f32[136,256]{1,0:T(8,128)S(1)} %get-tuple-element.34), channel_id=1, source_target_pairs={{0,2},{2,0},{1,3},{3,1},{4,6},{6,4},{5,7},{7,5},{8,10},{10,8},{9,1... | collective-permute-start | bytes 417800 | tf_op jit(solution)/shard_map/ppermute | solution.py:302
  12.4 9.8 %collective-permute-start.6 = (f32[264,128]{1,0:T(8,128)S(1)}, f32[264,128]{1,0:T(8,128)S(1)}, u32[]{:S(2)}, u32[]{:S(2)}) collective-permute-start(f32[264,128]{1,0:T(8,128)S(1)} %get-tuple-element.36), channel_id=1, source_target_pairs={{4,0},{8,4},{12,8},{0,12},{5,1},{9,5},{13,9},{1,13},{6,2},{10,6},{... | collective-permute-start | bytes 405512 | tf_op jit(solution)/shard_map/ppermute | solution.py:330
  14.2 9.7 %collective-permute-start.7 = (f32[264,128]{1,0:T(8,128)S(1)}, f32[264,128]{1,0:T(8,128)S(1)}, u32[]{:S(2)}, u32[]{:S(2)}) collective-permute-start(f32[264,128]{1,0:T(8,128)S(1)} %get-tuple-element.38), channel_id=1, source_target_pairs={{4,0},{8,4},{12,8},{0,12},{5,1},{9,5},{13,9},{1,13},{6,2},{10,6},{... | collective-permute-start | bytes 405512 | tf_op jit(solution)/shard_map/ppermute | solution.py:330
  20.6 9.0 %collective-permute-start.10 = (f32[256,256]{1,0:T(8,128)S(1)}, f32[256,256]{1,0:T(8,128)S(1)}, u32[]{:S(2)}, u32[]{:S(2)}) collective-permute-start(f32[256,256]{1,0:T(8,128)S(1)} %get-tuple-element.35.part), channel_id=1, source_target_pairs={{0,4},{4,8},{8,12},{12,0},{1,5},{5,9},{9,13},{13,1},{2,6},{6,10},{... | collective-permute-start | bytes 786440 | tf_op jit(solution)/shard_map/ppermute | solution.py:336
  22.3 5.1 %collective-permute-start.11 = (f32[264,128]{1,0:T(8,128)S(1)}, f32[264,128]{1,0:T(8,128)S(1)}, u32[]{:S(2)}, u32[]{:S(2)}) collective-permute-start(f32[264,128]{1,0:T(8,128)S(1)} %get-tuple-element.48), channel_id=1, source_target_pairs={{0,2},{2,0},{1,3},{3,1},{4,6},{6,4},{5,7},{7,5},{8,10},{10,8},{9,1... | collective-permute-start | bytes 405512 | tf_op jit(solution)/shard_map/ppermute | solution.py:347
  23.9 1.3 %collective-permute-start.8 = (f32[256,128]{1,0:T(8,128)S(1)}, f32[256,128]{1,0:T(8,128)S(1)}, u32[]{:S(2)}, u32[]{:S(2)}) collective-permute-start(f32[256,128]{1,0:T(8,128)S(1)} %get-tuple-element.37.half), channel_id=1, source_target_pairs={{0,1},{1,0},{2,3},{3,2},{4,5},{5,4},{6,7},{7,6},{8,9},{9,8},{10,11... | collective-permute-start | bytes 393224 | tf_op jit(solution)/shard_map/ppermute | solution.py:339
  24.0 1.6 %collective-permute-start.9 = (f32[256,128]{1,0:T(8,128)S(1)}, f32[256,128]{1,0:T(8,128)S(1)}, u32[]{:S(2)}, u32[]{:S(2)}) collective-permute-start(f32[256,128]{1,0:T(8,128)S(1)} %get-tuple-element.41), channel_id=1, source_target_pairs={{0,1},{1,0},{2,3},{3,2},{4,5},{5,4},{6,7},{7,6},{8,9},{9,8},{10,11... | collective-permute-start | bytes 393224 | tf_op jit(solution)/shard_map/ppermute | solution.py:339
  30.1 3.2 %collective-permute-start.14 = (f32[8,256]{1,0:T(8,128)S(1)}, f32[8,256]{1,0:T(8,128)S(1)}, u32[]{:S(2)}, u32[]{:S(2)}) collective-permute-start(f32[8,256]{1,0:T(8,128)S(1)} %far.1.refs_0_), channel_id=1, source_target_pairs={{0,3},{1,2},{2,1},{3,0},{4,7},{5,6},{6,5},{7,4},{8,11},{9,10},{10,... | collective-permute-start | bytes 24584 | tf_op jit(solution)/shard_map/ppermute | solution.py:46
  30.1 3.7 %collective-permute-start.13 = (f32[8,256]{1,0:T(8,128)S(1)}, f32[8,256]{1,0:T(8,128)S(1)}, u32[]{:S(2)}, u32[]{:S(2)}) collective-permute-start(f32[8,256]{1,0:T(8,128)S(1)} %far.1.refs_0_), channel_id=1, source_target_pairs={{0,2},{1,3},{2,0},{3,1},{4,6},{5,7},{6,4},{7,5},{8,10},{9,11},{10,... | collective-permute-start | bytes 24584 | tf_op jit(solution)/shard_map/ppermute | solution.py:46
  31.7 2.2 %collective-permute-start.12 = (f32[8,256]{1,0:T(8,128)S(1)}, f32[8,256]{1,0:T(8,128)S(1)}, u32[]{:S(2)}, u32[]{:S(2)}) collective-permute-start(f32[8,256]{1,0:T(8,128)S(1)} %far.1.refs_0_), channel_id=1, source_target_pairs={{0,1},{1,0},{2,3},{3,2},{4,5},{5,4},{6,7},{7,6},{8,9},{9,8},{10,11... | collective-permute-start | bytes 24584 | tf_op jit(solution)/shard_map/ppermute | solution.py:46
  33.9 5.6 %collective-permute-start.17 = (f32[8,256]{1,0:T(8,128)S(1)}, f32[8,256]{1,0:T(8,128)S(1)}, u32[]{:S(2)}, u32[]{:S(2)}) collective-permute-start(f32[8,256]{1,0:T(8,128)S(1)} %merge.2.refs_0_), channel_id=1, source_target_pairs={{0,12},{1,13},{2,14},{3,15},{4,8},{5,9},{6,10},{7,11},{8,4},{9,5},... | collective-permute-start | bytes 24584 | tf_op jit(solution)/shard_map/ppermute | solution.py:46
  35.3 4.5 %collective-permute-start.16 = (f32[8,256]{1,0:T(8,128)S(1)}, f32[8,256]{1,0:T(8,128)S(1)}, u32[]{:S(2)}, u32[]{:S(2)}) collective-permute-start(f32[8,256]{1,0:T(8,128)S(1)} %merge.2.refs_0_), channel_id=1, source_target_pairs={{0,8},{1,9},{2,10},{3,11},{4,12},{5,13},{6,14},{7,15},{8,0},{9,1},... | collective-permute-start | bytes 24584 | tf_op jit(solution)/shard_map/ppermute | solution.py:46
  36.7 3.7 %collective-permute-start.15 = (f32[8,256]{1,0:T(8,128)S(1)}, f32[8,256]{1,0:T(8,128)S(1)}, u32[]{:S(2)}, u32[]{:S(2)}) collective-permute-start(f32[8,256]{1,0:T(8,128)S(1)} %merge.2.refs_0_), channel_id=1, source_target_pairs={{0,4},{1,5},{2,6},{3,7},{4,0},{5,1},{6,2},{7,3},{8,12},{9,13},{10,... | collective-permute-start | bytes 24584 | tf_op jit(solution)/shard_map/ppermute | solution.py:46
